TPU v7x, 32 devices: a whole 2x2x4 slice. The times are simulated.
32 devices in a mesh: dp: 8 (over y, x, core), tensor: 4 (over z).
Axes of the slice: x: 2, y: 2, z: 4, core: 2. Of those that a mesh axis runs over, the one named last changes fastest.
Arguments:
- layer_in: bfloat16 [8192, 2048], P(('dp', 'tensor')), may hold values from -6 to 6
- teacher: bfloat16 [8192, 2048], P(('dp', 'tensor')), may hold values from -6 to 6
- lengths: int32 [8], replicated, may hold values from 256 to 1024, as said below
- input_gain: float32 [2048], replicated, may hold values from 0.5 to 1.5
- mixer_in_weight: bfloat16 [2048, 2, 3072], P('dp', None, 'tensor'), may hold values from -0.125 to 0.125
- step_weight: bfloat16 [2048, 48], P('dp', 'tensor'), may hold values from -0.125 to 0.125
- query_weight: bfloat16 [2048, 1024], P('dp', 'tensor'), may hold values from -0.125 to 0.125
- shared_weight: bfloat16 [2048, 1024], P(('dp', 'tensor')), may hold values from -0.125 to 0.125
- conv_inner: float32 [4, 3072], P(None, 'tensor'), may hold values from -3 to 3
- conv_shared: float32 [4, 512], replicated, may hold values from -3 to 3
- step_bias: float32 [48], P('tensor'), may hold values from -4 to -1
- decay_log: float32 [48], P('tensor'), may hold values from -7 to 0
- skip_gain: float32 [48], P('tensor'), may hold values from 0.5 to 1.5
- inner_gain: float32 [3072], P('tensor'), may hold values from 0.5 to 1.5
- mixer_out_weight: bfloat16 [2048, 3072], P('dp', 'tensor'), may hold values from -0.109375 to 0.109375
- attn_out_weight: bfloat16 [2048, 1024], P('dp', 'tensor'), may hold values from -1.5 to 1.5
- middle_gain: float32 [2048], replicated, may hold values from 0.5 to 1.5
- gate_up_weight: bfloat16 [2048, 2, 4096], P('dp', None, 'tensor'), may hold values from -0.125 to 0.125
- down_weight: bfloat16 [2048, 4096], P('dp', 'tensor'), may hold values from -0.09375 to 0.09375
Outputs:
- layer_out: bfloat16 [8192, 2048], P(('dp', 'tensor'))
- loss: float32 [], replicated
- input_grad: float32 [8192, 2048], P(('dp', 'tensor'))
- input_gain_grad: float32 [2048], replicated
- mixer_in_grad: float32 [2048, 2, 3072], P('dp', None, 'tensor')
- step_weight_grad: float32 [2048, 48], P('dp', 'tensor')
- query_weight_grad: float32 [2048, 1024], P('dp', 'tensor')
- shared_weight_grad: float32 [2048, 1024], P(('dp', 'tensor'))
- conv_inner_grad: float32 [4, 3072], P(None, 'tensor')
- conv_shared_grad: float32 [4, 512], replicated
- step_bias_grad: float32 [48], P('tensor')
- decay_log_grad: float32 [48], P('tensor')
- skip_gain_grad: float32 [48], P('tensor')
- inner_gain_grad: float32 [3072], P('tensor')
- mixer_out_grad: float32 [2048, 3072], P('dp', 'tensor')
- attn_out_grad: float32 [2048, 1024], P('dp', 'tensor')
- middle_gain_grad: float32 [2048], replicated
- gate_up_grad: float32 [2048, 2, 4096], P('dp', None, 'tensor')
- down_grad: float32 [2048, 4096], P('dp', 'tensor')
Inputs may be any that keep to these rules, and one draw needn't show every extreme that they name: Slot i holds one sequence of lengths[i] tokens at its start, the rest is padding; some slot is full (1024 tokens) and some holds exactly 256.
All inputs are finite; a program needn't handle non-finite values.
Results may differ from a plain program's by a relative error of at most 0.014.
Values may be sent and summed in bfloat16 or wider, within the bound.
A program may use at most 320 MiB of HBM per device.

v0:
```python
import jax
import jax.numpy as jnp
from jax import lax
from jax.sharding import PartitionSpec as P

H = 48
KC = 4
QH = 8
KVH = 2
HD = 128
DI = 3072
SSD_BLOCK = 256
ATT_BLOCK = 512


EPS = 1e-05
ROPE_BASE = 100000000000.0
NEG_FILL = -1e30


def rounding_tools():

    def value_low(v):
        return lax.optimization_barrier(v.astype(jnp.bfloat16)).astype(jnp.float32)

    def value_keep(v):
        return (value_low(v), None)

    def value_pass(kept, grad):
        return (grad,)

    round_value = jax.custom_vjp(value_low)
    round_value.defvjp(value_keep, value_pass)

    def grad_same(v):
        return v

    def grad_keep(v):
        return (v, None)

    def grad_round(kept, grad):
        return (value_low(grad),)

    round_grad = jax.custom_vjp(grad_same)
    round_grad.defvjp(grad_keep, grad_round)

    def plain_product(left, right):
        return jnp.dot(
            left.astype(jnp.bfloat16),
            right.astype(jnp.bfloat16),
            preferred_element_type=jnp.float32,
        )

    def product_keep(left, right):
        left_low = left.astype(jnp.bfloat16)
        right_low = right.astype(jnp.bfloat16)
        return (
            jnp.dot(left_low, right_low, preferred_element_type=jnp.float32),
            (left_low, right_low),
        )

    def product_back(kept, grad):
        left_low, right_low = kept
        grad_low = grad.astype(jnp.bfloat16)
        return (
            jnp.dot(grad_low, right_low.T, preferred_element_type=jnp.float32),
            jnp.dot(left_low.T, grad_low, preferred_element_type=jnp.float32),
        )

    product = jax.custom_vjp(plain_product)
    product.defvjp(product_keep, product_back)
    return (round_value, round_grad, product)


def rms_norm(values, gain):
    return values * lax.rsqrt(jnp.mean(values * values, axis=-1, keepdims=True) + EPS) * gain


def causal_conv(values, taps):
    length = values.shape[0]
    width = taps.shape[0]
    padded = jnp.pad(values, ((width - 1, 0), (0, 0)))
    total = padded[0:length] * taps[0]
    for offset in range(1, width):
        total = total + padded[offset : offset + length] * taps[offset]
    return total


def rotary(values, positions, head_size):
    half_size = head_size // 2
    freqs = jnp.exp(
        -jnp.log(ROPE_BASE) * 2.0 * jnp.arange(half_size, dtype=jnp.float32) / head_size
    )
    angles = positions[:, None] * freqs[None, :]
    cosine = jnp.cos(angles)[:, None, :]
    sine_part = jnp.sin(angles)[:, None, :]
    front_part = values[..., :half_size]
    back_part = values[..., half_size:]
    return jnp.concatenate(
        [front_part * cosine - back_part * sine_part, back_part * cosine + front_part * sine_part],
        axis=-1,
    )


def ssd_scan(inputs, b_mat, c_mat, log_decay, step_size, skip_gain, block_len):
    length, num_heads, head_dim = inputs.shape
    state_dim = b_mat.shape[1]
    num_blocks = length // block_len
    highest = lax.Precision.HIGHEST
    row_index = jnp.arange(block_len)
    lower_mask = (row_index[:, None] >= row_index[None, :])[:, :, None]

    def block_step(carry_state, pieces):
        x_blk, b_blk, c_blk, decay_blk, step_blk = pieces
        cum_decay = jnp.cumsum(decay_blk, axis=0)
        gap_decay = jnp.where(lower_mask, cum_decay[:, None, :] - cum_decay[None, :, :], 0.0)
        kernel = jnp.where(lower_mask, jnp.exp(gap_decay), 0.0)
        cross_terms = jnp.dot(c_blk, b_blk.T, precision=highest)
        weights = cross_terms[:, :, None] * kernel * step_blk[None, :, :]
        inner_out = jnp.einsum("ijh,jhp->ihp", weights, x_blk, precision=highest)
        carried = (
            jnp.einsum("in,hpn->ihp", c_blk, carry_state, precision=highest)
            * jnp.exp(cum_decay)[:, :, None]
        )
        tail_weight = jnp.exp(cum_decay[-1][None, :] - cum_decay) * step_blk
        new_state = carry_state * jnp.exp(cum_decay[-1])[:, None, None] + jnp.einsum(
            "jh,jhp,jn->hpn", tail_weight, x_blk, b_blk, precision=highest
        )
        return (new_state, inner_out + carried + skip_gain[None, :, None] * x_blk)

    start_state = jnp.zeros((num_heads, head_dim, state_dim), jnp.float32)
    pieces = (
        inputs.reshape(num_blocks, block_len, num_heads, head_dim),
        b_mat.reshape(num_blocks, block_len, state_dim),
        c_mat.reshape(num_blocks, block_len, state_dim),
        log_decay.reshape(num_blocks, block_len, num_heads),
        step_size.reshape(num_blocks, block_len, num_heads),
    )
    _, results = lax.scan(jax.checkpoint(block_step), start_state, pieces)
    return results.reshape(length, num_heads, head_dim)


def attend(queries, keys_in, values_in, att_block, tools):
    round_value, round_grad, product = tools
    length, num_queries, head_size = queries.shape
    query_low = round_value(queries)
    key_low_t = round_value(keys_in).T
    value_low = round_value(values_in)
    score_scale = head_size ** (-0.5)
    key_pos = jnp.arange(length)

    def one_block(row_start):
        query_rows = lax.dynamic_slice_in_dim(query_low, row_start, att_block, 0).reshape(
            att_block * num_queries, head_size
        )
        raw_scores = round_grad(product(query_rows, key_low_t))
        query_pos = row_start + jnp.arange(att_block * num_queries) // num_queries
        scores = jnp.where(
            key_pos[None, :] <= query_pos[:, None], raw_scores * score_scale, NEG_FILL
        )
        top_score = jnp.max(scores, axis=1, keepdims=True)
        weights_un = jnp.exp(scores - top_score)
        probs = weights_un / jnp.sum(weights_un, axis=1, keepdims=True)
        mixed_out = round_grad(product(round_value(probs), value_low))
        return round_value(mixed_out).reshape(att_block, num_queries * head_size)

    starts = jnp.arange(length // att_block) * att_block
    results = lax.map(jax.checkpoint(one_block), starts)
    return results.reshape(length, num_queries * head_size)


def mixer_group(
    proj_zx,
    proj_dt,
    proj_shared,
    proj_query,
    conv_inner,
    conv_shared,
    step_bias,
    decay_log,
    skip_gain,
    inner_gain,
    kv_index,
    head_size,
    kv_heads,
    ssd_block,
    att_block,
    tools,
):
    round_value = tools[0]
    length = proj_zx.shape[0]
    num_heads = proj_dt.shape[1]
    inner_width = proj_zx.shape[2]
    head_dim = inner_width // num_heads
    state_dim = conv_shared.shape[1] // 2
    gate_in = proj_zx[:, 0]
    conv_out = jax.nn.silu(causal_conv(proj_zx[:, 1], conv_inner))
    bc_out = jax.nn.silu(causal_conv(proj_shared[:, : 2 * state_dim], conv_shared))
    step_size = jax.nn.softplus(proj_dt + step_bias)
    log_decay = -jnp.exp(decay_log) * step_size
    scanned = ssd_scan(
        conv_out.reshape(length, num_heads, head_dim),
        bc_out[:, :state_dim],
        bc_out[:, state_dim:],
        log_decay,
        step_size,
        skip_gain,
        ssd_block,
    ).reshape(length, inner_width)
    mixer_normed = round_value(rms_norm(scanned * jax.nn.silu(gate_in), inner_gain))
    key_start = 2 * state_dim + kv_index * head_size
    keys_in = lax.dynamic_slice_in_dim(proj_shared, key_start, head_size, 1)
    values_in = lax.dynamic_slice_in_dim(
        proj_shared, key_start + kv_heads * head_size, head_size, 1
    )
    num_queries = proj_query.shape[1] // head_size
    positions = jnp.arange(length).astype(jnp.float32)
    queries = rotary(proj_query.reshape(length, num_queries, head_size), positions, head_size)
    keys_rot = rotary(keys_in.reshape(length, 1, head_size), positions, head_size).reshape(
        length, head_size
    )
    attn_heads = attend(queries, keys_rot, values_in, att_block, tools)
    return (mixer_normed, attn_heads)


def per_device(
    layer_in,
    teacher,
    lengths,
    input_gain,
    mixer_in_weight,
    step_weight,
    query_weight,
    shared_weight,
    conv_inner,
    conv_shared,
    step_bias,
    decay_log,
    skip_gain,
    inner_gain,
    mixer_out_weight,
    attn_out_weight,
    middle_gain,
    gate_up_weight,
    down_weight,
):
    f32 = jnp.float32
    bf16 = jnp.bfloat16
    tools = rounding_tools()
    contract_last = (((1,), (1,)), ((), ()))
    contract_first = (((0,), (0,)), ((), ()))
    rows_here = layer_in.shape[0]
    tensor_size = lax.axis_size("tensor")
    data_size = lax.axis_size("dp")
    tensor_pos = lax.axis_index("tensor")
    data_pos = lax.axis_index("dp")
    slot_len = rows_here * tensor_size
    share_rows = shared_weight.shape[0]
    inputs = layer_in.astype(f32)
    normed_in, norm_in_back = jax.vjp(rms_norm, inputs, input_gain)
    act_all, shared_quad = (
        lax.all_gather(normed_in.astype(bf16), "tensor", axis=0, tiled=True),
        lax.all_gather(shared_weight, "tensor", axis=0, tiled=True),
    )
    zx_all, step_all, query_all, mix_out_all, attn_out_all, gate_up_all, down_all, shared_all = (
        lax.all_gather(mixer_in_weight, "dp", axis=0, tiled=True),
        lax.all_gather(step_weight, "dp", axis=0, tiled=True),
        lax.all_gather(query_weight, "dp", axis=0, tiled=True),
        lax.all_gather(mixer_out_weight, "dp", axis=0, tiled=True),
        lax.all_gather(attn_out_weight, "dp", axis=0, tiled=True),
        lax.all_gather(gate_up_weight, "dp", axis=0, tiled=True),
        lax.all_gather(down_weight, "dp", axis=0, tiled=True),
        lax.all_gather(shared_quad, "dp", axis=0, tiled=True),
    )
    proj_zx = jnp.einsum("sd,dkc->skc", act_all, zx_all, preferred_element_type=f32)
    proj_dt = jnp.dot(act_all, step_all, preferred_element_type=f32)
    proj_shared = jnp.dot(act_all, shared_all, preferred_element_type=f32)
    proj_query = jnp.dot(act_all, query_all, preferred_element_type=f32)
    local_queries = query_all.shape[1] // HD
    kv_index = tensor_pos * local_queries // (QH // KVH)

    def group_fn(
        zx_in, dt_in, shared_in, query_in, convx_in, convs_in, bias_in, decay_in, skip_in, gain_in
    ):
        return mixer_group(
            zx_in,
            dt_in,
            shared_in,
            query_in,
            convx_in,
            convs_in,
            bias_in,
            decay_in,
            skip_in,
            gain_in,
            kv_index,
            HD,
            KVH,
            SSD_BLOCK,
            ATT_BLOCK,
            tools,
        )

    primals = (
        proj_zx,
        proj_dt,
        proj_shared,
        proj_query,
        conv_inner,
        conv_shared,
        step_bias,
        decay_log,
        skip_gain,
        inner_gain,
    )
    (mixer_normed, attn_heads), group_back = jax.vjp(group_fn, *primals)
    mixer_low = mixer_normed.astype(bf16)
    attn_low = attn_heads.astype(bf16)
    mix_part = lax.dot_general(mixer_low, mix_out_all, contract_last, preferred_element_type=f32)
    mix_part = mix_part + lax.dot_general(
        attn_low, attn_out_all, contract_last, preferred_element_type=f32
    )
    mixed = lax.psum_scatter(mix_part, "tensor", scatter_dimension=0, tiled=True)
    resid = inputs + mixed
    normed_mid, norm_mid_back = jax.vjp(rms_norm, resid, middle_gain)
    mid_all = lax.all_gather(normed_mid.astype(bf16), "tensor", axis=0, tiled=True)
    gate_up = jnp.einsum("sd,dkf->skf", mid_all, gate_up_all, preferred_element_type=f32)
    gate_val = gate_up[:, 0]
    up_val = gate_up[:, 1]
    sigmoid_gate = jax.nn.sigmoid(gate_val)
    hidden = (gate_val * sigmoid_gate * up_val).astype(bf16)
    mlp_part = lax.dot_general(hidden, down_all, contract_last, preferred_element_type=f32)
    mlp_out = lax.psum_scatter(
        mlp_part.astype(jnp.bfloat16), "tensor", scatter_dimension=0, tiled=True
    ).astype(jnp.float32)
    outputs = resid + mlp_out
    seq_len = lax.dynamic_index_in_dim(lengths, data_pos, keepdims=False)
    positions = tensor_pos * rows_here + jnp.arange(rows_here)
    live = (positions < seq_len).astype(f32)
    error = (outputs - teacher.astype(f32)) * live[:, None]
    err_local = 0.5 * jnp.sum(error * error)
    grad_all = lax.all_gather(error.astype(bf16), "tensor", axis=0, tiled=True)
    grad_hidden = jnp.dot(grad_all, down_all, preferred_element_type=f32)
    grad_down = lax.dot_general(grad_all, hidden, contract_first, preferred_element_type=f32)
    grad_gate = grad_hidden * up_val * sigmoid_gate * (1.0 + gate_val * (1.0 - sigmoid_gate))
    grad_up = grad_hidden * gate_val * sigmoid_gate
    grad_gu = jnp.stack([grad_gate, grad_up], axis=1).astype(bf16)
    grad_mid_part = jnp.einsum("skf,dkf->sd", grad_gu, gate_up_all, preferred_element_type=f32)
    grad_gate_up = jnp.einsum("sd,skf->dkf", mid_all, grad_gu, preferred_element_type=f32)
    grad_mid = lax.psum_scatter(grad_mid_part, "tensor", scatter_dimension=0, tiled=True)
    grad_resid_norm, grad_middle_gain = norm_mid_back(grad_mid)
    grad_resid = error + grad_resid_norm
    mix_grad_all = lax.all_gather(grad_resid.astype(bf16), "tensor", axis=0, tiled=True)
    grad_mixer = jnp.dot(mix_grad_all, mix_out_all, preferred_element_type=f32)
    grad_attn = jnp.dot(mix_grad_all, attn_out_all, preferred_element_type=f32)
    grad_mix_out = lax.dot_general(
        mix_grad_all, mixer_low, contract_first, preferred_element_type=f32
    )
    grad_attn_out = lax.dot_general(
        mix_grad_all, attn_low, contract_first, preferred_element_type=f32
    )
    (
        grad_zx,
        grad_dt,
        grad_shared,
        grad_query,
        grad_convx,
        grad_convs,
        grad_bias,
        grad_decay,
        grad_skip,
        grad_gain,
    ) = group_back((grad_mixer, grad_attn))
    low_zx = grad_zx.astype(bf16)
    low_dt = grad_dt.astype(bf16)
    low_shared = grad_shared.astype(bf16)
    low_query = grad_query.astype(bf16)
    grad_act_part = jnp.einsum("skc,dkc->sd", low_zx, zx_all, preferred_element_type=f32)
    grad_act_part = grad_act_part + lax.dot_general(
        low_dt, step_all, contract_last, preferred_element_type=f32
    )
    grad_act_part = grad_act_part + lax.dot_general(
        low_shared, shared_all, contract_last, preferred_element_type=f32
    )
    grad_act_part = grad_act_part + lax.dot_general(
        low_query, query_all, contract_last, preferred_element_type=f32
    )
    grad_zx_weight = jnp.einsum("sd,skc->dkc", act_all, low_zx, preferred_element_type=f32)
    grad_step_weight = lax.dot_general(act_all, low_dt, contract_first, preferred_element_type=f32)
    grad_query_weight = lax.dot_general(
        act_all, low_query, contract_first, preferred_element_type=f32
    )
    act_split = act_all.reshape(slot_len, data_size, tensor_size, share_rows)
    grad_shared_split = jnp.einsum(
        "sbtr,sk->tbrk", act_split, low_shared, preferred_element_type=f32
    )
    grad_shared_split = grad_shared_split.reshape(
        tensor_size, data_size * share_rows, grad_shared_split.shape[3]
    )
    grad_act, grad_shared_part = (
        lax.psum_scatter(
            grad_act_part.astype(jnp.bfloat16), "tensor", scatter_dimension=0, tiled=True
        ).astype(jnp.float32),
        lax.psum_scatter(
            grad_shared_split.astype(jnp.bfloat16), "tensor", scatter_dimension=0, tiled=True
        ).astype(jnp.float32),
    )
    grad_shared_weight = grad_shared_part.reshape(data_size * share_rows, grad_shared_part.shape[2])
    grad_input_norm, grad_input_gain = norm_in_back(grad_act)
    input_grad = grad_resid + grad_input_norm
    (
        grad_zx_weight,
        grad_step_weight,
        grad_query_weight,
        grad_shared_weight,
        grad_mix_out,
        grad_attn_out,
        grad_gate_up,
        grad_down,
    ) = (
        lax.psum_scatter(
            grad_zx_weight.astype(jnp.bfloat16), "dp", scatter_dimension=0, tiled=True
        ).astype(jnp.float32),
        lax.psum_scatter(
            grad_step_weight.astype(jnp.bfloat16), "dp", scatter_dimension=0, tiled=True
        ).astype(jnp.float32),
        lax.psum_scatter(
            grad_query_weight.astype(jnp.bfloat16), "dp", scatter_dimension=0, tiled=True
        ).astype(jnp.float32),
        lax.psum_scatter(
            grad_shared_weight.astype(jnp.bfloat16), "dp", scatter_dimension=0, tiled=True
        ).astype(jnp.float32),
        lax.psum_scatter(
            grad_mix_out.astype(jnp.bfloat16), "dp", scatter_dimension=0, tiled=True
        ).astype(jnp.float32),
        lax.psum_scatter(
            grad_attn_out.astype(jnp.bfloat16), "dp", scatter_dimension=0, tiled=True
        ).astype(jnp.float32),
        lax.psum_scatter(
            grad_gate_up.astype(jnp.bfloat16), "dp", scatter_dimension=0, tiled=True
        ).astype(jnp.float32),
        lax.psum_scatter(
            grad_down.astype(jnp.bfloat16), "dp", scatter_dimension=0, tiled=True
        ).astype(jnp.float32),
    )
    local_heads = step_bias.shape[0]
    local_inner = inner_gain.shape[0]
    convx_full = lax.dynamic_update_slice(
        jnp.zeros((KC, DI), f32), grad_convx, (0, tensor_pos * local_inner)
    )
    head_stack = jnp.stack([grad_bias, grad_decay, grad_skip], axis=0)
    heads_full = lax.dynamic_update_slice(
        jnp.zeros((3, H), f32), head_stack, (0, tensor_pos * local_heads)
    )
    gain_full = lax.dynamic_update_slice(
        jnp.zeros((DI,), f32), grad_gain, (tensor_pos * local_inner,)
    )
    sum_convx, sum_convs, sum_heads, sum_gain, sum_input_gain, sum_middle_gain, err_total = (
        lax.psum(
            (
                convx_full,
                grad_convs,
                heads_full,
                gain_full,
                grad_input_gain,
                grad_middle_gain,
                err_local,
            ),
            ("dp", "tensor"),
        )
    )
    conv_inner_grad = lax.dynamic_slice_in_dim(sum_convx, tensor_pos * local_inner, local_inner, 1)
    heads_local = lax.dynamic_slice_in_dim(sum_heads, tensor_pos * local_heads, local_heads, 1)
    inner_gain_grad = lax.dynamic_slice_in_dim(sum_gain, tensor_pos * local_inner, local_inner, 0)
    loss = err_total / jnp.sum(lengths).astype(f32)
    return (
        outputs.astype(bf16),
        loss,
        input_grad,
        sum_input_gain,
        grad_zx_weight,
        grad_step_weight,
        grad_query_weight,
        grad_shared_weight,
        conv_inner_grad,
        sum_convs,
        heads_local[0],
        heads_local[1],
        heads_local[2],
        inner_gain_grad,
        grad_mix_out,
        grad_attn_out,
        sum_middle_gain,
        grad_gate_up,
        grad_down,
    )


def solution(mesh):
    placed = (
        P(("dp", "tensor"), None),
        P(("dp", "tensor"), None),
        P(),
        P(),
        P("dp", None, "tensor"),
        P("dp", "tensor"),
        P("dp", "tensor"),
        P(("dp", "tensor"), None),
        P(None, "tensor"),
        P(),
        P("tensor"),
        P("tensor"),
        P("tensor"),
        P("tensor"),
        P("dp", "tensor"),
        P("dp", "tensor"),
        P(),
        P("dp", None, "tensor"),
        P("dp", "tensor"),
    )
    return jax.shard_map(
        per_device,
        mesh=mesh,
        in_specs=placed,
        out_specs=(
            P(("dp", "tensor"), None),
            P(),
            P(("dp", "tensor"), None),
            P(),
            P("dp", None, "tensor"),
            P("dp", "tensor"),
            P("dp", "tensor"),
            P(("dp", "tensor"), None),
            P(None, "tensor"),
            P(),
            P("tensor"),
            P("tensor"),
            P("tensor"),
            P("tensor"),
            P("dp", "tensor"),
            P("dp", "tensor"),
            P(),
            P("dp", None, "tensor"),
            P("dp", "tensor"),
        ),
        check_vma=False,
    )
```

profile of v0, /device:TPU:1, one launch (start us, length us, event | category | flops | bytes accessed | tf_op | source)
XLA Modules:
  0.0 1862.7 jit_solution(17265381262947243816)
XLA Ops:
  46.8 71.7 %all-gather.12.cloned.1.call-done = bf16[1024,2048]{1,0:T(8,128)(2,1)} async-done(((bf16[256,2048]{1,0:T(8,128)(2,1)}), bf16[1024,2048]{1,0:T(8,128)(2,1)}) %all-gather.12.cloned.1.call-update) | async-done | bytes 4194320 | tf_op jit(solution)/shard_map/all_gather | solution.py:262
  131.9 24.1 %all-gather.16.cloned.1.call-done = bf16[2048,1024]{1,0:T(8,128)(2,1)} async-done(((bf16[256,1024]{1,0:T(8,128)(2,1)}), bf16[2048,1024]{1,0:T(8,128)(2,1)}) %all-gather.16.cloned.1.call-update) | async-done | bytes 4194320 | tf_op jit(solution)/shard_map/all_gather | solution.py:273
  234.2 56.1 %while.80 = (s32[]{:T(128)}, f32[12,64,256]{2,1,0:T(8,128)S(1)}, f32[4,256,12,64]{1,3,2,0:T(8,128)}, f32[4,12,64,256]{3,2,1,0:T(8,128)}, f32[4,256,12]{1,2,0:T(8...) while((s32[]{:T(128)}, f32[12,64,256]{2,1,0:T(8,128)S(1)}, ...), condition=%wide.region_4.5_spmd.clone.clone, body=%wide.region_1.4_spmd.clone.clone.sunk | while | flops 2019563520 | bytes 10638533 | solution.py:139
  332.9 141.6 %reduce-scatter.14.cloned.1.call-done = f32[256,2048]{1,0:T(8,128)} async-done(((f32[1024,2048]{1,0:T(8,128)}), f32[256,2048]{1,0:T(8,128)}) %reduce-scatter.14.cloned.1.call-update) | async-done | bytes 2097168 | tf_op jit(solution)/shard_map/reduce_scatter | solution.py:323
  478.4 54.4 %all-gather.26.cloned.1.call-done = bf16[2048,2,1024]{2,0,1:T(8,128)(2,1)} async-done(((bf16[256,2,1024]{2,0,1:T(8,128)(2,1)}), bf16[2048,2,1024]{2,0,1:T(8,128)(2,1)}) %all-gather.26.cloned.1.call-update) | async-done | bytes 8388624 | tf_op jit(solution)/shard_map/all_gather | solution.py:271
  532.8 82.0 %all-gather.24.cloned.1.call-done = bf16[1024,2048]{1,0:T(8,128)(2,1)} async-done(((bf16[256,2048]{1,0:T(8,128)(2,1)}), bf16[1024,2048]{1,0:T(8,128)(2,1)}) %all-gather.24.cloned.1.call-update) | async-done | bytes 4194320 | tf_op jit(solution)/shard_map/all_gather | solution.py:326
  633.4 18.8 %all-gather.28.cloned.1.call-done = bf16[2048,1024]{1,0:T(8,128)(2,1)} async-done(((bf16[256,1024]{1,0:T(8,128)(2,1)}), bf16[2048,1024]{1,0:T(8,128)(2,1)}) %all-gather.28.cloned.1.call-update) | async-done | bytes 4194320 | tf_op jit(solution)/shard_map/all_gather | solution.py:272
  663.4 74.7 %reduce-scatter.16.cloned.1.call-done = bf16[256,2048]{1,0:T(8,128)(2,1)} async-done(((bf16[1024,2048]{1,0:T(8,128)(2,1)}), bf16[256,2048]{1,0:T(8,128)(2,1)}) %reduce-scatter.16.cloned.1.call-update) | async-done | bytes 1048592 | tf_op jit(solution)/shard_map/reduce_scatter | solution.py:333
  741.3 80.9 %all-gather.30.cloned.1.call-done = bf16[1024,2048]{1,0:T(8,128)(2,1)} async-done(((bf16[256,2048]{1,0:T(8,128)(2,1)}), bf16[1024,2048]{1,0:T(8,128)(2,1)}) %all-gather.30.cloned.1.call-update) | async-done | bytes 4194320 | tf_op jit(solution)/shard_map/all_gather | solution.py:342
  848.9 142.9 %reduce-scatter.18.cloned.1.call-done = f32[256,2048]{1,0:T(8,128)} async-done(((f32[1024,2048]{1,0:T(8,128)}), f32[256,2048]{1,0:T(8,128)}) %reduce-scatter.18.cloned.1.call-update) | async-done | bytes 2097168 | tf_op jit(solution)/shard_map/reduce_scatter | solution.py:350
  1024.1 56.3 %all-gather.32.cloned.1.call-done = bf16[1024,2048]{1,0:T(8,128)(2,1)} async-done(((bf16[256,2048]{1,0:T(8,128)(2,1)}), bf16[1024,2048]{1,0:T(8,128)(2,1)}) %all-gather.32.cloned.1.call-update) | async-done | bytes 4194320 | tf_op jit(solution)/shard_map/all_gather | solution.py:353
  1104.3 249.4 %while.78 = (s32[]{:T(128)}, f32[12]{0:T(128)}, f32[12,64,256]{2,1,0:T(8,128)}, f32[4,256,12,64]{1,0,3,2:T(4,128)}, f32[4,256,256]{2,1,0:T(8,128)}, /*index=5*/f...) while((s32[]{:T(128)}, f32[12]{0:T(128)}, ...), condition=%wide.region_32.33_spmd.clone, body=%wide.region_19.32_spmd.clone.sunk | while | flops 4852054016 | bytes 41091348 | solution.py:139
  1144.7 18.1 dynamic_update_slice.128
  1207.4 17.9 dynamic_update_slice.128
  1269.7 17.8 dynamic_update_slice.128
  1331.9 17.8 dynamic_update_slice.128
  1358.8 50.1 %while.79 = (s32[]{:T(128)}, f32[1024,2,128]{2,1,0:T(2,128)}, f32[128,1024]{1,0:T(8,128)}, f32[1024,128]{1,0:T(8,128)}, s32[2]{0:T(128)S(1)}, /*index=5*/bf16[2,...) while((s32[]{:T(128)}, f32[1024,2,128]{2,1,0:T(2,128)}, ...), condition=%wide.region_39.40_spmd.clone, body=%wide.region_33.39_spmd.clone.sunk | while | flops 1374299136 | bytes 99991904 | solution.py:168
  1539.4 39.2 %reduce-scatter.26.cloned.1.call-done = bf16[256,256]{1,0:T(8,128)(2,1)} async-done(((bf16[2048,256]{1,0:T(8,128)(2,1)}), bf16[256,256]{1,0:T(8,128)(2,1)}) %reduce-scatter.26.cloned.1.call-update) | async-done | bytes 131088 | tf_op jit(solution)/shard_map/reduce_scatter | solution.py:427
  1580.2 37.8 %reduce-scatter.34.cloned.1.call-done = bf16[256,256]{1,0:T(8,128)(2,1)} async-done(((bf16[2048,256]{1,0:T(8,128)(2,1)}), bf16[256,256]{1,0:T(8,128)(2,1)}) %reduce-scatter.34.cloned.1.call-update) | async-done | bytes 131088 | tf_op jit(solution)/shard_map/reduce_scatter | solution.py:436
  1619.6 48.5 %reduce-scatter.32.cloned.1.call-done = bf16[256,768]{1,0:T(8,128)(2,1)} async-done(((bf16[2048,768]{1,0:T(8,128)(2,1)}), bf16[256,768]{1,0:T(8,128)(2,1)}) %reduce-scatter.32.cloned.1.call-update) | async-done | bytes 393232 | tf_op jit(solution)/shard_map/reduce_scatter | solution.py:433
  1670.1 77.2 %reduce-scatter.20.cloned.1.call-done = bf16[256,2048]{1,0:T(8,128)(2,1)} async-done(((bf16[1024,2048]{1,0:T(8,128)(2,1)}), bf16[256,2048]{1,0:T(8,128)(2,1)}) %reduce-scatter.20.cloned.1.call-update) | async-done | bytes 1048592 | tf_op jit(solution)/shard_map/reduce_scatter | solution.py:401
  1749.5 43.0 %all-reduce.31 = (f32[]{:T(128)}, f32[2048]{0:T(1024)}, f32[4,3072]{1,0:T(4,128)S(1)}, f32[4,512]{1,0:T(4,128)}, f32[3,48]{1,0:T(4,128)S(1)}, /*index=5*/f32[3072]{0:T(1024)S(1)}, f32[2048]{0:T(1024)}) all-reduce(f32[]{:T(128)S(6)} %mul_shard_map.3, ...), channel_id=1, replica_groups=mesh['dp'=8,'tensor'=4] {'dp','tensor'}, use_global_device_ids=true, to_apply=%region_14.15 | all-reduce | flops 21649 | bytes 173192 | tf_op jit(solution)/shard_map/psum | solution.py:459
  1798.2 15.7 reduce-scatter.22.cloned.1.call-done
  1817.0 35.9 %reduce-scatter.30.cloned.1.call-done = bf16[64,1024]{1,0:T(8,128)(2,1)} async-done(((bf16[512,1024]{1,0:T(8,128)(2,1)}), bf16[64,1024]{1,0:T(8,128)(2,1)}) %reduce-scatter.30.cloned.1.call-update) | async-done | bytes 131088 | tf_op jit(solution)/shard_map/reduce_scatter | solution.py:430
  (913 shorter events, 731.9 us)
Async XLA Ops:
  7.2 39.6 %all-gather.20.cloned.1.call-start = ((), (), s32[]{:S(2)}) async-start(), calls=%async_computation.17 | async-start | bytes 1179648 | tf_op jit(solution)/shard_map/all_gather | solution.py:268
  7.9 110.5 %all-gather.12.cloned.1.call-start = ((), (), s32[]{:S(2)}) async-start(), calls=%async_computation.13 | async-start | bytes 5242880 | tf_op jit(solution)/shard_map/all_gather | solution.py:262
  13.1 142.9 %all-gather.16.cloned.1.call-start = ((), (), s32[]{:S(2)}) async-start(), calls=%async_computation.15 | async-start | bytes 4718592 | tf_op jit(solution)/shard_map/all_gather | solution.py:273
  28.9 175.0 %all-gather.14.cloned.1.call-start = ((), (), s32[]{:S(2)}) async-start(), calls=%async_computation.14 | async-start | bytes 7077888 | tf_op jit(solution)/shard_map/all_gather | solution.py:266
  30.0 283.0 %all-gather.18.cloned.1.call-start = ((), (), s32[]{:S(2)}) async-start(), calls=%async_computation.16 | async-start | bytes 3538944 | tf_op jit(solution)/shard_map/all_gather | solution.py:269
  30.6 291.6 %all-gather.22.cloned.1.call-start = ((), (), s32[]{:S(2)}) async-start(), calls=%async_computation.18 | async-start | bytes 1179648 | tf_op jit(solution)/shard_map/all_gather | solution.py:270
  31.1 443.4 %reduce-scatter.14.cloned.1.call-start = ((), (), s32[]{:S(2)}) async-start(), calls=%async_computation.19 | async-start | bytes 10485760 | tf_op jit(solution)/shard_map/reduce_scatter | solution.py:323
  330.4 202.4 %all-gather.26.cloned.1.call-start = ((), (), s32[]{:S(2)}) async-start(), calls=%async_computation.21 | async-start | bytes 9437184 | tf_op jit(solution)/shard_map/all_gather | solution.py:271
  332.9 281.9 %all-gather.24.cloned.1.call-start = ((), (), s32[]{:S(2)}) async-start(), calls=%async_computation.20 | async-start | bytes 5242880 | tf_op jit(solution)/shard_map/all_gather | solution.py:326
  477.8 174.4 %all-gather.28.cloned.1.call-start = ((), (), s32[]{:S(2)}) async-start(), calls=%async_computation.22 | async-start | bytes 4718592 | tf_op jit(solution)/shard_map/all_gather | solution.py:272
  478.4 259.7 %reduce-scatter.16.cloned.1.call-start = ((), (), s32[]{:S(2)}) async-start(), calls=%async_computation.23 | async-start | bytes 5242880 | tf_op jit(solution)/shard_map/reduce_scatter | solution.py:333
  661.6 160.6 %all-gather.30.cloned.1.call-start = ((), (), s32[]{:S(2)}) async-start(), calls=%async_computation.24 | async-start | bytes 5242880 | tf_op jit(solution)/shard_map/all_gather | solution.py:342
  740.8 251.0 %reduce-scatter.18.cloned.1.call-start = ((), (), s32[]{:S(2)}) async-start(), calls=%async_computation.25 | async-start | bytes 10485760 | tf_op jit(solution)/shard_map/reduce_scatter | solution.py:350
  848.8 231.6 %all-gather.32.cloned.1.call-start = ((), (), s32[]{:S(2)}) async-start(), calls=%async_computation.26 | async-start | bytes 5242880 | tf_op jit(solution)/shard_map/all_gather | solution.py:353
  998.6 520.3 %reduce-scatter.38.cloned.1.call-start = ((), (), s32[]{:S(2)}) async-start(), calls=%async_computation.36 | async-start | bytes 4718592 | tf_op jit(solution)/shard_map/reduce_scatter | solution.py:442
  1008.4 512.6 %reduce-scatter.36.cloned.1.call-start = ((), (), s32[]{:S(2)}) async-start(), calls=%async_computation.35 | async-start | bytes 9437184 | tf_op jit(solution)/shard_map/reduce_scatter | solution.py:439
  1024.0 501.6 %reduce-scatter.28.cloned.1.call-start = ((), (), s32[]{:S(2)}) async-start(), calls=%async_computation.31 | async-start | bytes 5242880 | tf_op jit(solution)/shard_map/reduce_scatter | solution.py:404
  1428.1 110.0 %reduce-scatter.24.cloned.1.call-start = ((), (), s32[]{:S(2)}) async-start(), calls=%async_computation.29 | async-start | bytes 73728 | tf_op jit(solution)/shard_map/reduce_scatter | solution.py:424
  1435.8 142.9 %reduce-scatter.26.cloned.1.call-start = ((), (), s32[]{:S(2)}) async-start(), calls=%async_computation.30 | async-start | bytes 1179648 | tf_op jit(solution)/shard_map/reduce_scatter | solution.py:427
  1440.6 177.4 %reduce-scatter.34.cloned.1.call-start = ((), (), s32[]{:S(2)}) async-start(), calls=%async_computation.34 | async-start | bytes 1179648 | tf_op jit(solution)/shard_map/reduce_scatter | solution.py:436
  1451.8 216.3 %reduce-scatter.32.cloned.1.call-start = ((), (), s32[]{:S(2)}) async-start(), calls=%async_computation.33 | async-start | bytes 3538944 | tf_op jit(solution)/shard_map/reduce_scatter | solution.py:433
  1468.0 279.2 %reduce-scatter.20.cloned.1.call-start = ((), (), s32[]{:S(2)}) async-start(), calls=%async_computation.27 | async-start | bytes 5242880 | tf_op jit(solution)/shard_map/reduce_scatter | solution.py:401
  1505.1 308.8 %reduce-scatter.22.cloned.1.call-start = ((), (), s32[]{:S(2)}) async-start(), calls=%async_computation.28 | async-start | bytes 7077888 | tf_op jit(solution)/shard_map/reduce_scatter | solution.py:421
  1516.9 335.9 %reduce-scatter.30.cloned.1.call-start = ((), (), s32[]{:S(2)}) async-start(), calls=%async_computation.32 | async-start | bytes 1179648 | tf_op jit(solution)/shard_map/reduce_scatter | solution.py:430
  (187 other events, 4174.2 us)
Sparse Core Ops, SparseCore 0:
  9.9 25.9 all-gather.19
  38.1 80.3 all-gather.11
  120.4 35.6 all-gather.15
  158.4 45.5 all-gather.13
  205.7 32.3 all-gather.17
  239.8 23.6 all-gather.21
  330.5 143.9 reduce-scatter.13
  477.1 55.7 all-gather.25
  534.4 80.3 all-gather.23
  616.5 35.6 all-gather.27
  661.7 76.3 reduce-scatter.15
  740.9 81.2 all-gather.29
  849.0 142.8 reduce-scatter.17
  998.7 81.6 all-gather.31
  1084.0 49.8 reduce-scatter.37
  1137.2 71.2 reduce-scatter.35
  1428.2 74.9 reduce-scatter.27
  1506.7 31.3 reduce-scatter.23
  1542.2 36.4 reduce-scatter.25
  1582.0 35.9 reduce-scatter.33
  1621.8 46.3 reduce-scatter.31
  1670.4 76.7 reduce-scatter.19
  1751.0 62.8 reduce-scatter.21
  1816.9 35.8 reduce-scatter.29
where the time goes:
time: 1870 us; the launch traced here: 1860 us
  waiting for transfers between devices  1030 us (55%)
  matrix products  346 us (19%)
  local copies, waits for them, and re-layouts  229 us (12%)
  other arithmetic  158 us (8%)
  blocking collectives  69.9 us (4%)
  between operations  19.4 us (1%)
    reduce_scatter x1, waiting for transfers between devices, per_device(): lax.psum_scatter(grad_mid_part, 'tensor', scatter_dimension=0, tiled=True)  143 us
    reduce_scatter x1, waiting for transfers between devices, per_device(): lax.psum_scatter(mix_part, 'tensor', scatter_dimension=0, tiled=True)  142 us
    dynamic_update_slice x24, local copies, waits for them, and re-layouts, ssd_scan(): _, results = lax.scan(jax.checkpoint(block_step), start_state, pieces)  89.2 us
    all_gather x1, waiting for transfers between devices, per_device(): lax.all_gather(normed_mid.astype(bf16), 'tensor', axis=0, tiled=True)  82 us
    all_gather x1, waiting for transfers between devices, per_device(): grad_all = lax.all_gather(error.astype(bf16), 'tensor', axis=0, tiled=True)  80.9 us
    reduce_scatter x1, waiting for transfers between devices, per_device(): lax.psum_scatter(grad_act_part.astype(jnp.bfloat16), 'tensor', scatter_di...  77.2 us
    reduce_scatter x1, waiting for transfers between devices, per_device(): lax.psum_scatter(mlp_part.astype(jnp.bfloat16), 'tensor', scatter_dimensi...  74.7 us
    all_gather x1, waiting for transfers between devices, per_device(): lax.all_gather(normed_in.astype(bf16), 'tensor', axis=0, tiled=True)  71.7 us
  transfers between devices with their start and end apart: 24, of which 18 were waited for; matrix products, arithmetic and copies ran while one was open for 35% of the time, Pallas kernels for 0%

commit v1 on v0

v1 whole, which is shorter than its diff:
```python
import jax
import jax.numpy as jnp
from jax import lax
from jax.experimental import pallas as pl
from jax.experimental.pallas import tpu as pltpu
from jax.sharding import PartitionSpec as P

H = 48
KC = 4
QH = 8
KVH = 2
HD = 128
DI = 3072

EPS = 1e-05
ROPE_BASE = 100000000000.0


def rms_norm(values, gain):
    return values * lax.rsqrt(jnp.mean(values * values, axis=-1, keepdims=True) + EPS) * gain


def low_dot(left, right, dims):
    return lax.dot_general(left, right, (dims, ((), ())), preferred_element_type=jnp.float32)


NN = ((1,), (0,))
NT = ((1,), (1,))
TN = ((0,), (0,))
CHUNK = 128
ROWS = 256
WIDE = 128
FAR = -1e30


def exact_dot(ones, values, parts=3):
    total = None
    for _ in range(parts):
        part = values.astype(jnp.bfloat16)
        values = values - part.astype(jnp.float32)
        term = low_dot(ones, part, NN)
        total = term if total is None else total + term
    return total


def split_dot(values, ones, parts=2):
    total = None
    for _ in range(parts):
        part = values.astype(jnp.bfloat16)
        values = values - part.astype(jnp.float32)
        term = low_dot(part, ones, NN)
        total = term if total is None else total + term
    return total


def sigmoid(v):
    return 1.0 / (1.0 + jnp.exp(-v))


def softplus(v):
    return jnp.maximum(v, 0.0) + jnp.log1p(jnp.exp(-jnp.abs(v)))


def iota(shape, axis):
    return lax.broadcasted_iota(jnp.int32, shape, axis)


def spin(values, cosine, sine):
    return values * cosine + pltpu.roll(values, HD // 2, 1) * sine


def unspin(values, cosine, sine):
    return values * cosine - pltpu.roll(values, HD // 2, 1) * sine


def attn_probs(query_low, key_low, first_row, scale):
    scores = low_dot(query_low, key_low, NT) * scale
    rows, keys = scores.shape
    allowed = iota((rows, keys), 1) <= iota((rows, keys), 0) + first_row
    scores = jnp.where(allowed, scores, FAR)
    top = jnp.max(scores, axis=1, keepdims=True)
    weights = jnp.exp(scores - top)
    return weights / jnp.sum(weights, axis=1, keepdims=True)


def attn_fwd_body(order, q_ref, kv_ref, cos_ref, sin_ref, out_ref, key_s, value_s):
    bf16 = jnp.bfloat16
    step = pl.program_id(0)
    cosine, sine = cos_ref[...], sin_ref[...]
    rows = pl.ds(pl.multiple_of(step * ROWS, ROWS), ROWS)
    key_s[rows, :] = spin(kv_ref[:, :HD], cosine, sine).astype(bf16)
    value_s[rows, :] = kv_ref[:, HD:].astype(bf16)
    heads = q_ref.shape[1] // HD
    blocks = key_s.shape[0] // ROWS
    for block in range(blocks):

        @pl.when(step == block)
        def _(block=block):
            keys = (block + 1) * ROWS
            for head in range(heads):
                lanes = slice(head * HD, (head + 1) * HD)
                query = spin(q_ref[:, lanes], cosine, sine).astype(bf16)
                probs = attn_probs(query, key_s[:keys, :], block * ROWS, HD**-0.5)
                out_ref[:, lanes] = low_dot(
                    probs.astype(bf16), value_s[:keys, :], NN
                ).astype(bf16)


def attn_bwd_body(
    order, q_ref, kv_ref, cos_ref, sin_ref, grad_ref, all_cos, all_sin, dq_ref, dkv_ref,
    key_s, value_s, dkey_s, dvalue_s,
):
    bf16, f32 = jnp.bfloat16, jnp.float32
    step = pl.program_id(0)

    @pl.when(step == 0)
    def _():
        dkey_s[...] = jnp.zeros_like(dkey_s)
        dvalue_s[...] = jnp.zeros_like(dvalue_s)

    cosine, sine = cos_ref[...], sin_ref[...]
    rows = pl.ds(pl.multiple_of(step * ROWS, ROWS), ROWS)
    key_s[rows, :] = spin(kv_ref[:, :HD], cosine, sine).astype(bf16)
    value_s[rows, :] = kv_ref[:, HD:].astype(bf16)
    heads = q_ref.shape[1] // HD
    blocks = key_s.shape[0] // ROWS
    scale = HD**-0.5
    for block in range(blocks):

        @pl.when(step == block)
        def _(block=block):
            keys = (block + 1) * ROWS
            for head in range(heads):
                lanes = slice(head * HD, (head + 1) * HD)
                query = spin(q_ref[:, lanes], cosine, sine).astype(bf16)
                probs = attn_probs(query, key_s[:keys, :], block * ROWS, scale)
                grad = grad_ref[:, lanes].astype(bf16)
                dprobs = low_dot(grad, value_s[:keys, :], NT)
                dvalue_s[:keys, :] += low_dot(probs.astype(bf16), grad, TN)
                inner = jnp.sum(dprobs * probs, axis=1, keepdims=True)
                dscores = (probs * (dprobs - inner) * scale).astype(bf16)
                dquery = low_dot(dscores, key_s[:keys, :], NN)
                dkey_s[:keys, :] += low_dot(dscores, query, TN)
                dq_ref[:, lanes] = unspin(dquery, cosine, sine).astype(bf16)

    @pl.when(step == blocks - 1)
    def _():
        dkv_ref[:, :HD] = unspin(dkey_s[...], all_cos[...], all_sin[...]).astype(bf16)
        dkv_ref[:, HD:] = dvalue_s[...].astype(bf16)


def conv_taps(ext, taps, first, width):
    rows = ext.shape[0] - 8
    total = None
    for tap in range(width):
        at = 8 - (width - 1) + tap
        term = ext[at : at + rows, :] * taps[first + tap : first + tap + 1, :]
        total = term if total is None else total + term
    return total


def decays(steps, head_params, tri):
    shifted = steps + head_params[0:1, :]
    dt = softplus(shifted)
    la = dt * head_params[1:2, :]
    cum = exact_dot(tri, la)
    return shifted, dt, la, cum


def spread_lanes(values, pair, first):
    rows = values.shape[0]
    a = jnp.broadcast_to(values[:, 2 * pair : 2 * pair + 1], (rows, WIDE))
    b = jnp.broadcast_to(values[:, 2 * pair + 1 : 2 * pair + 2], (rows, WIDE))
    return a, b, jnp.where(first, a, b)


def mixer_fwd_body(
    order, gate_ref, inner_ref, step_ref, bc_ref, attn_ref, lane_ref, conv_ref, head_ref,
    out_ref, y_ref, state_ref, ext_s, extbc_s, state_s, x_s,
):
    bf16, f32 = jnp.bfloat16, jnp.float32
    step = pl.program_id(0)
    width = inner_ref.shape[1]
    states = bc_ref.shape[1] // 2

    @pl.when(step == 0)
    def _():
        ext_s[0:8, :] = jnp.zeros((8, width), f32)
        extbc_s[0:8, :] = jnp.zeros((8, 2 * states), f32)
        state_s[...] = jnp.zeros_like(state_s)

    ext_s[8:, :] = inner_ref[...]
    extbc_s[8:, :] = bc_ref[...]
    pre = conv_taps(ext_s, lane_ref, 0, KC)
    x_s[...] = pre * sigmoid(pre)
    pre = conv_taps(extbc_s, conv_ref, 0, KC)
    bc = (pre * sigmoid(pre)).astype(bf16)
    ext_s[0:8, :] = ext_s[ROWS : ROWS + 8, :]
    extbc_s[0:8, :] = extbc_s[ROWS : ROWS + 8, :]
    row, col = iota((CHUNK, CHUNK), 0), iota((CHUNK, CHUNK), 1)
    causal = row >= col
    tri = jnp.where(causal, 1.0, 0.0).astype(bf16)
    first = iota((CHUNK, WIDE), 1) < WIDE // 2
    for sub in range(ROWS // CHUNK):
        lo = sub * CHUNK
        b_low = bc[lo : lo + CHUNK, :states]
        c_low = bc[lo : lo + CHUNK, states:]
        _, dt, _, cum = decays(step_ref[lo : lo + CHUNK, :], head_ref, tri)
        cum_t = cum.T
        cross = low_dot(c_low, b_low, NT)
        state_low = state_s[...].astype(bf16)
        state_ref[sub] = state_low
        b_t = b_low.T
        for pair in range(width // WIDE):
            lanes = slice(pair * WIDE, (pair + 1) * WIDE)
            cum_a, cum_b, cum_p = spread_lanes(cum, pair, first)
            _, _, dt_p = spread_lanes(dt, pair, first)
            weights = []
            for wide, head in ((cum_a, 2 * pair), (cum_b, 2 * pair + 1)):
                gap = jnp.where(causal, wide - cum_t[head : head + 1, :], FAR)
                weights.append((cross * jnp.exp(gap)).astype(bf16))
            x = x_s[lo : lo + CHUNK, lanes]
            scaled = x * dt_p
            zero = jnp.zeros_like(scaled)
            stacked = jnp.concatenate(
                [jnp.where(first, scaled, zero), jnp.where(first, zero, scaled)], axis=0
            ).astype(bf16)
            y = low_dot(jnp.concatenate(weights, axis=1), stacked, NN)
            y = y + jnp.exp(cum_p) * low_dot(c_low, state_low[:, lanes], NN)
            y_ref[lo : lo + CHUNK, lanes] = y + lane_ref[5:6, lanes] * x
            last = cum_p[CHUNK - 1 : CHUNK, :]
            ends = (scaled * jnp.exp(last - cum_p)).astype(bf16)
            state_s[:, lanes] = state_s[:, lanes] * jnp.exp(last) + low_dot(b_t, ends, NN)
    gate = gate_ref[...]
    gated = y_ref[...] * (gate * sigmoid(gate))
    scale = lax.rsqrt(jnp.mean(gated * gated, axis=1, keepdims=True) + EPS)
    out_ref[:, :width] = (gated * scale * lane_ref[4:5, :]).astype(bf16)
    out_ref[:, width:] = attn_ref[...]


def mixer_bwd_body(
    order, gate_ref, inner_ref, before_ref, step_ref, bc_ref, bcbefore_ref, y_ref, state_ref,
    grad_ref, dq_ref, dkv_ref, lane_ref, conv_ref, head_ref, seg_ref,
    low_ref, lowsh_ref, dlane_ref, dconv_ref, dhead_ref,
    ext_s, extbc_s, pre_s, prebc_s, x_s, bc_s, g_s, dx_s, dbc_s, dpre_s, dprebc_s, dstate_s,
    z_s, rows_s,
):
    bf16, f32 = jnp.bfloat16, jnp.float32
    step = pl.program_id(0)
    blocks = pl.num_programs(0)
    width = inner_ref.shape[1]
    states = bc_ref.shape[1] // 2
    query_width = dq_ref.shape[1]

    @pl.when(step == 0)
    def _():
        dlane_ref[...] = jnp.zeros_like(dlane_ref)
        dconv_ref[...] = jnp.zeros_like(dconv_ref)
        dhead_ref[...] = jnp.zeros_like(dhead_ref)
        dstate_s[...] = jnp.zeros_like(dstate_s)
        dpre_s[ROWS:, :] = jnp.zeros((8, width), f32)
        dprebc_s[ROWS:, :] = jnp.zeros((8, 2 * states), f32)
        z_s[...] = jnp.zeros_like(z_s)
        rows_s[...] = jnp.zeros_like(rows_s)

    keep = jnp.where(step == blocks - 1, 0.0, 1.0)
    ext_s[0:8, :] = before_ref[...] * keep
    extbc_s[0:8, :] = bcbefore_ref[...] * keep
    ext_s[8:, :] = inner_ref[...]
    extbc_s[8:, :] = bc_ref[...]
    pre = conv_taps(ext_s, lane_ref, 0, KC)
    pre_s[...] = pre
    x_s[...] = pre * sigmoid(pre)
    pre = conv_taps(extbc_s, conv_ref, 0, KC)
    prebc_s[...] = pre
    bc_s[...] = (pre * sigmoid(pre)).astype(bf16)

    gate = gate_ref[...]
    sig = sigmoid(gate)
    gate_act = gate * sig
    y = y_ref[...]
    gated = y * gate_act
    scale = lax.rsqrt(jnp.mean(gated * gated, axis=1, keepdims=True) + EPS)
    grad = grad_ref[...]
    dlane_ref[4:5, :] += jnp.sum(grad * gated * scale, axis=0, keepdims=True)
    grad = grad * lane_ref[4:5, :]
    mean = jnp.mean(grad * gated, axis=1, keepdims=True)
    dgated = scale * grad - gated * (scale * scale * scale * mean)
    g_s[...] = dgated * gate_act
    low_ref[:, :width] = (dgated * y * sig * (1.0 + gate * (1.0 - sig))).astype(bf16)

    row, col = iota((CHUNK, CHUNK), 0), iota((CHUNK, CHUNK), 1)
    tri = jnp.where(row >= col, 1.0, 0.0).astype(bf16)
    tri_up = jnp.where(row <= col, 1.0, 0.0).astype(bf16)
    later = row <= col
    first = iota((CHUNK, WIDE), 1) < WIDE // 2
    last_row = iota((CHUNK, WIDE), 0) == CHUNK - 1
    for sub in reversed(range(ROWS // CHUNK)):
        lo = sub * CHUNK
        b_low = bc_s[lo : lo + CHUNK, :states]
        c_low = bc_s[lo : lo + CHUNK, states:]
        shifted, dt, la, cum = decays(step_ref[lo : lo + CHUNK, :], head_ref, tri)
        cum_t = cum.T
        cross_t = low_dot(b_low, c_low, NT)
        c_t = c_low.T
        state_low = state_ref[sub]
        dstate_low = dstate_s[...].astype(bf16)
        dcross_t = jnp.zeros((CHUNK, CHUNK), f32)
        db = jnp.zeros((CHUNK, states), f32)
        dc = jnp.zeros((CHUNK, states), f32)
        for pair in range(width // WIDE):
            lanes = slice(pair * WIDE, (pair + 1) * WIDE)
            cum_a, cum_b, cum_p = spread_lanes(cum, pair, first)
            _, _, dt_p = spread_lanes(dt, pair, first)
            x = x_s[lo : lo + CHUNK, lanes]
            g = g_s[lo : lo + CHUNK, lanes]
            scaled = x * dt_p
            scaled_low = scaled.astype(bf16)
            zero = jnp.zeros_like(g)
            g_stack = jnp.concatenate(
                [jnp.where(first, g, zero), jnp.where(first, zero, g)], axis=0
            ).astype(bf16)
            dweights_t = low_dot(scaled_low, g_stack, NT)
            weights_t = []
            for place, wide, head in ((0, cum_a, 2 * pair), (1, cum_b, 2 * pair + 1)):
                gap = jnp.where(later, cum_t[head : head + 1, :] - wide, FAR)
                grow = jnp.exp(gap)
                weight = (cross_t * grow).astype(bf16)
                weights_t.append(weight)
                dweight = dweights_t[:, place * CHUNK : (place + 1) * CHUNK]
                dcross_t = dcross_t + dweight * grow
                rows_s[head : head + 1, :] = jnp.sum(
                    dweight * weight.astype(f32), axis=0, keepdims=True
                )
            dx_in = low_dot(jnp.concatenate(weights_t, axis=1), g_stack, NN)
            grown = jnp.exp(cum_p)
            last = cum_p[CHUNK - 1 : CHUNK, :]
            tail = jnp.exp(last - cum_p)
            last = jnp.exp(last)
            dx_tail = tail * low_dot(b_low, dstate_low[:, lanes], NN)
            dscaled = dx_in + dx_tail
            g_grown = g * grown
            g_low = g_grown.astype(bf16)
            ends = (scaled * tail).astype(bf16)
            carried = low_dot(c_low, state_low[:, lanes], NN)
            dc = dc + low_dot(g_low, state_low[:, lanes], NT)
            db = db + low_dot(ends, dstate_low[:, lanes], NT)
            dstate = dstate_s[:, lanes]
            kept = jnp.sum(dstate * state_low[:, lanes].astype(f32), axis=0, keepdims=True) * last
            dstate_s[:, lanes] = dstate * last + low_dot(c_t, g_low, NN)
            tails = scaled * dx_tail
            z_s[0:CHUNK, lanes] = g_grown * carried - tails - scaled_low.astype(f32) * dx_in
            z_s[CHUNK : 2 * CHUNK, lanes] = dscaled * x
            z_s[2 * CHUNK : 2 * CHUNK + 1, lanes] = (
                jnp.sum(tails, axis=0, keepdims=True) + kept
            )
            dx_s[lo : lo + CHUNK, lanes] = dscaled * dt_p + lane_ref[5:6, lanes] * g
            dlane_ref[5:6, lanes] += jnp.sum(g * x, axis=0, keepdims=True)
        sums = split_dot(z_s[...], seg_ref[...])
        dcum = sums[0:CHUNK, :] + rows_s[...].T
        dcum = dcum + jnp.where(last_row, sums[2 * CHUNK : 2 * CHUNK + 1, :], 0.0)
        dla = exact_dot(tri_up, dcum)
        ddt = sums[CHUNK : 2 * CHUNK, :] + dla * head_ref[1:2, :]
        dsteps = ddt * sigmoid(shifted)
        dhead_ref[0:1, :] += jnp.sum(dsteps, axis=0, keepdims=True)
        dhead_ref[1:2, :] += jnp.sum(dla * la, axis=0, keepdims=True)
        low_ref[lo : lo + CHUNK, 2 * width + query_width :] = dsteps.astype(bf16)
        dcross_low = dcross_t.astype(bf16)
        dbc_s[lo : lo + CHUNK, :states] = db + low_dot(dcross_low, c_low, NN)
        dbc_s[lo : lo + CHUNK, states:] = dc + low_dot(dcross_low, b_low, TN)

    def conv_back(pre_ref, dact, dpre_ref, ext, taps, dtaps_ref):
        pre = pre_ref[...]
        sig = sigmoid(pre)
        dpre = dact * (sig * (1.0 + pre * (1.0 - sig)))
        dpre_ref[0:ROWS, :] = dpre
        total = None
        for tap in range(KC):
            ahead = KC - 1 - tap
            term = dpre_ref[ahead : ahead + ROWS, :] * taps[tap : tap + 1, :]
            total = term if total is None else total + term
            at = 8 - (KC - 1) + tap
            dtaps_ref[tap : tap + 1, :] += jnp.sum(
                dpre * ext[at : at + ROWS, :], axis=0, keepdims=True
            )
        dpre_ref[ROWS:, :] = dpre_ref[0:8, :]
        return total

    dinner = conv_back(pre_s, dx_s[...], dpre_s, ext_s, lane_ref, dlane_ref)
    low_ref[:, width : 2 * width] = dinner.astype(bf16)
    dbc = conv_back(prebc_s, dbc_s[...], dprebc_s, extbc_s, conv_ref, dconv_ref)
    lowsh_ref[:, : 2 * states] = dbc.astype(bf16)
    lowsh_ref[:, 2 * states :] = dkv_ref[...]
    low_ref[:, 2 * width : 2 * width + query_width] = dq_ref[...]


def block_at(rows, cols, col):
    return pl.BlockSpec((rows, cols), lambda i, order: (order[i], col))


def whole_at(shape):
    return pl.BlockSpec(shape, lambda i, order: (0,) * len(shape))


def kernel_params():
    return pltpu.CompilerParams(
        dimension_semantics=("arbitrary",), vmem_limit_bytes=56 * 1024 * 1024
    )


def attn_forward(order, proj, proj_shared, cosine, sine, query_width, width, bc_width):
    slot = proj.shape[0]
    scratch = [pltpu.VMEM((slot, HD), jnp.bfloat16)] * 2
    return pl.pallas_call(
        attn_fwd_body,
        grid_spec=pltpu.PrefetchScalarGridSpec(
            num_scalar_prefetch=1,
            grid=(slot // ROWS,),
            in_specs=[
                block_at(ROWS, query_width, 2 * width // query_width),
                block_at(ROWS, 2 * HD, bc_width // (2 * HD)),
                pl.BlockSpec((ROWS, HD), lambda i, order: (i, 0)),
                pl.BlockSpec((ROWS, HD), lambda i, order: (i, 0)),
            ],
            out_specs=block_at(ROWS, query_width, 0),
            scratch_shapes=scratch,
        ),
        out_shape=jax.ShapeDtypeStruct((slot, query_width), jnp.bfloat16),
        compiler_params=kernel_params(),
        cost_estimate=pl.CostEstimate(
            flops=slot * slot * query_width * 3,
            bytes_accessed=slot * 4 * (query_width + 4 * HD),
            transcendentals=slot * slot * query_width // HD,
        ),
    )(order, proj, proj_shared, cosine, sine)


def attn_backward(order, proj, proj_shared, cosine, sine, grad_heads, query_width, width, bc_width):
    slot = proj.shape[0]
    return pl.pallas_call(
        attn_bwd_body,
        grid_spec=pltpu.PrefetchScalarGridSpec(
            num_scalar_prefetch=1,
            grid=(slot // ROWS,),
            in_specs=[
                block_at(ROWS, query_width, 2 * width // query_width),
                block_at(ROWS, 2 * HD, bc_width // (2 * HD)),
                pl.BlockSpec((ROWS, HD), lambda i, order: (i, 0)),
                pl.BlockSpec((ROWS, HD), lambda i, order: (i, 0)),
                block_at(ROWS, query_width, width // query_width),
                whole_at((slot, HD)),
                whole_at((slot, HD)),
            ],
            out_specs=[block_at(ROWS, query_width, 0), whole_at((slot, 2 * HD))],
            scratch_shapes=[pltpu.VMEM((slot, HD), jnp.bfloat16)] * 2
            + [pltpu.VMEM((slot, HD), jnp.float32)] * 2,
        ),
        out_shape=[
            jax.ShapeDtypeStruct((slot, query_width), jnp.bfloat16),
            jax.ShapeDtypeStruct((slot, 2 * HD), jnp.bfloat16),
        ],
        compiler_params=kernel_params(),
        cost_estimate=pl.CostEstimate(
            flops=slot * slot * query_width * 8,
            bytes_accessed=slot * 4 * (2 * query_width + 6 * HD),
            transcendentals=slot * slot * query_width // HD,
        ),
    )(order, proj, proj_shared, cosine, sine, grad_heads, cosine, sine)


def mixer_forward(order, proj, proj_shared, attn_low, lane_params, conv_shared, head_params):
    slot = proj.shape[0]
    f32, bf16 = jnp.float32, jnp.bfloat16
    width = lane_params.shape[1]
    bc_width = conv_shared.shape[1]
    query_width = attn_low.shape[1]
    chunks = ROWS // CHUNK
    return pl.pallas_call(
        mixer_fwd_body,
        grid_spec=pltpu.PrefetchScalarGridSpec(
            num_scalar_prefetch=1,
            grid=(slot // ROWS,),
            in_specs=[
                block_at(ROWS, width, 0),
                block_at(ROWS, width, 1),
                block_at(ROWS, WIDE, (2 * width + query_width) // WIDE),
                block_at(ROWS, bc_width, 0),
                block_at(ROWS, query_width, 0),
                whole_at(lane_params.shape),
                whole_at(conv_shared.shape),
                whole_at(head_params.shape),
            ],
            out_specs=[
                block_at(ROWS, width + query_width, 0),
                pl.BlockSpec((ROWS, width), lambda i, order: (i, 0)),
                pl.BlockSpec((chunks, bc_width // 2, width), lambda i, order: (i, 0, 0)),
            ],
            scratch_shapes=[
                pltpu.VMEM((ROWS + 8, width), f32),
                pltpu.VMEM((ROWS + 8, bc_width), f32),
                pltpu.VMEM((bc_width // 2, width), f32),
                pltpu.VMEM((ROWS, width), f32),
            ],
        ),
        out_shape=[
            jax.ShapeDtypeStruct((slot, width + query_width), bf16),
            jax.ShapeDtypeStruct((slot, width), f32),
            jax.ShapeDtypeStruct((slot // CHUNK, bc_width // 2, width), bf16),
        ],
        compiler_params=kernel_params(),
        cost_estimate=pl.CostEstimate(
            flops=slot * width * bc_width * 8,
            bytes_accessed=slot * width * 20,
            transcendentals=slot * width * 8,
        ),
    )(order, proj, proj, proj, proj_shared, attn_low, lane_params, conv_shared, head_params)


def mixer_backward(
    order, proj, proj_shared, y, states, grad_heads, dq, dkv, lane_params, conv_shared,
    head_params, seg, query_width,
):
    slot = proj.shape[0]
    f32, bf16 = jnp.float32, jnp.bfloat16
    width = lane_params.shape[1]
    bc_width = conv_shared.shape[1]
    blocks = slot // ROWS
    chunks = ROWS // CHUNK

    def back(rows, cols, col):
        return pl.BlockSpec((rows, cols), lambda i, order: (order[blocks - 1 - i], col))

    def straight(shape):
        return pl.BlockSpec(
            shape, lambda i, order: (blocks - 1 - i,) + (0,) * (len(shape) - 1)
        )

    def before(cols, col):
        return pl.BlockSpec(
            (8, cols),
            lambda i, order: (
                order[jnp.maximum(blocks - 2 - i, 0)] * (ROWS // 8) + ROWS // 8 - 1,
                col,
            ),
        )

    return pl.pallas_call(
        mixer_bwd_body,
        grid_spec=pltpu.PrefetchScalarGridSpec(
            num_scalar_prefetch=1,
            grid=(blocks,),
            in_specs=[
                back(ROWS, width, 0),
                back(ROWS, width, 1),
                before(width, 1),
                back(ROWS, WIDE, (2 * width + query_width) // WIDE),
                back(ROWS, bc_width, 0),
                before(bc_width, 0),
                straight((ROWS, width)),
                straight((chunks, bc_width // 2, width)),
                back(ROWS, width, 0),
                back(ROWS, query_width, 0),
                straight((ROWS, 2 * HD)),
                whole_at(lane_params.shape),
                whole_at(conv_shared.shape),
                whole_at(head_params.shape),
                whole_at(seg.shape),
            ],
            out_specs=[
                back(ROWS, 2 * width + query_width + WIDE, 0),
                back(ROWS, bc_width + 2 * HD, 0),
                whole_at((8, width)),
                whole_at((8, bc_width)),
                whole_at((8, WIDE)),
            ],
            scratch_shapes=[
                pltpu.VMEM((ROWS + 8, width), f32),
                pltpu.VMEM((ROWS + 8, bc_width), f32),
                pltpu.VMEM((ROWS, width), f32),
                pltpu.VMEM((ROWS, bc_width), f32),
                pltpu.VMEM((ROWS, width), f32),
                pltpu.VMEM((ROWS, bc_width), bf16),
                pltpu.VMEM((ROWS, width), f32),
                pltpu.VMEM((ROWS, width), f32),
                pltpu.VMEM((ROWS, bc_width), f32),
                pltpu.VMEM((ROWS + 8, width), f32),
                pltpu.VMEM((ROWS + 8, bc_width), f32),
                pltpu.VMEM((bc_width // 2, width), f32),
                pltpu.VMEM((2 * CHUNK + 8, width), f32),
                pltpu.VMEM((WIDE, CHUNK), f32),
            ],
        ),
        out_shape=[
            jax.ShapeDtypeStruct((slot, 2 * width + query_width + WIDE), bf16),
            jax.ShapeDtypeStruct((slot, bc_width + 2 * HD), bf16),
            jax.ShapeDtypeStruct((8, width), f32),
            jax.ShapeDtypeStruct((8, bc_width), f32),
            jax.ShapeDtypeStruct((8, WIDE), f32),
        ],
        compiler_params=kernel_params(),
        cost_estimate=pl.CostEstimate(
            flops=slot * width * bc_width * 20,
            bytes_accessed=slot * width * 40,
            transcendentals=slot * width * 16,
        ),
    )(
        order, proj, proj, proj, proj, proj_shared, proj_shared, y, states, grad_heads, dq, dkv,
        lane_params, conv_shared, head_params, seg,
    )


class Places:
    def __init__(self):
        self.dp = lax.axis_size("dp")
        self.tp = lax.axis_size("tensor")
        d = lax.axis_index("dp")
        t = lax.axis_index("tensor")
        self.d, self.t = d, t
        self.c = d % 2
        self.k = d // 2
        self.zq = t % 2
        self.home = self.c == t // 2
        self.quarter = 2 * self.c + self.zq
        self.column = self.zq + 2 * self.c
        self.slot = 2 * self.k + t // 2
        self.blocks = self.dp // 2
        self.bits = self.blocks.bit_length() - 1

    def pairs(self, where_to):
        out = []
        for d in range(self.dp):
            for t in range(self.tp):
                target = where_to(d, t)
                if target is not None:
                    out.append((d * self.tp + t, target[0] * self.tp + target[1]))
        return out

    def send(self, values, where_to):
        return lax.ppermute(values, ("dp", "tensor"), self.pairs(where_to))

    def over_core(self, values):
        return self.send(values, lambda d, t: (d ^ 1, t))

    def over_z(self, values):
        return self.send(values, lambda d, t: (d, t ^ 1))

    def over_far(self, values):
        return self.send(values, lambda d, t: (d, t ^ 2))

    def over_bit(self, values, bit):
        return self.send(values, lambda d, t: (d ^ (2 << bit), t))

    def swap_away(self, values):
        def where_to(d, t):
            if d % 2 == t // 2:
                return None
            return (d ^ 1, t ^ 2)

        return self.send(values, where_to)

    def column_out(self, values):
        def where_to(d, t):
            if d % 2 == t // 2:
                return (d, t ^ 2)
            return (d ^ 1, t)

        return self.send(values, where_to)

    def column_back(self, values):
        def where_to(d, t):
            if d % 2 == t // 2:
                return (d ^ 1, t)
            return (d, t ^ 2)

        return self.send(values, where_to)


def relocate(values, at):
    return jnp.where(at.home, values, at.swap_away(values))


def turn_features(values, at, axis):
    block = values.shape[axis] // at.blocks
    parts = [
        lax.slice_in_dim(values, place * block, (place + 1) * block, axis=axis)
        for place in range(at.blocks)
    ]
    for bit in range(at.bits):
        turned = (at.k >> bit) % 2 == 1
        parts = [
            jnp.where(turned, parts[place ^ (1 << bit)], parts[place])
            for place in range(at.blocks)
        ]
    return jnp.concatenate(parts, axis=axis)


def share_rows(values, at):
    far = at.over_z(values)
    core = at.over_core(values)
    both = at.over_core(far)
    return (values, core, far, both)


def sum_rows(pieces, at):
    own, core, far, both = pieces
    bf16 = jnp.bfloat16
    from_both = at.over_core(both.astype(bf16))
    passed = (far + from_both.astype(jnp.float32)).astype(bf16)
    from_far = at.over_z(passed)
    from_core = at.over_core(core.astype(bf16))
    return own + from_core.astype(jnp.float32) + from_far.astype(jnp.float32)


def spread(piece, at, upward):
    found = {0: piece}
    order = range(at.bits) if upward else reversed(range(at.bits))
    for bit in order:
        for place in sorted(found):
            found[place | (1 << bit)] = at.over_bit(found[place], bit)
    return found


def gather_weight(shard, at):
    first_in = at.column_out(shard)
    second_in = at.swap_away(shard)
    own = jnp.where(at.home, shard, first_in)
    other = jnp.where(at.home, first_in, second_in)
    low = jnp.where(at.c == 0, own, other)
    high = jnp.where(at.c == 0, other, own)
    lows = spread(low, at, True)
    highs = spread(high, at, False)
    return jnp.concatenate(
        [part for place in range(at.blocks) for part in (lows[place], highs[place])], axis=0
    )


def collect(piece_of, at, half):
    bf16 = jnp.bfloat16
    bits = list(range(at.bits))
    order = list(reversed(bits)) if half == 0 else bits
    arrived = {}
    places = list(range(at.blocks))

    def total(place):
        value = piece_of(place, half)
        for part in arrived.get(place, []):
            value = value + part.astype(jnp.float32)
        return value

    for bit in order:
        going = [place for place in places if (place >> bit) & 1]
        places = [place for place in places if not (place >> bit) & 1]
        for place in going:
            part = at.over_bit(total(place).astype(bf16), bit)
            arrived.setdefault(place ^ (1 << bit), []).append(part)
    return total(0)


def scatter_weight(piece_of, at):
    bf16 = jnp.bfloat16
    low = collect(piece_of, at, 0)
    high = collect(piece_of, at, 1)
    own = jnp.where(at.c == 0, low, high)
    other = jnp.where(at.c == 0, high, low)
    first_in = at.column_back(jnp.where(at.home, other, own).astype(bf16)).astype(jnp.float32)
    second_in = at.swap_away(other.astype(bf16)).astype(jnp.float32)
    return first_in + jnp.where(at.home, own, second_in)


def gather_shared(shard, at):
    rows, width = shard.shape
    half = width // 2
    mine = jnp.where(at.c == 0, shard[:, :half], shard[:, half:])
    theirs = jnp.where(at.c == 0, shard[:, half:], shard[:, :half])
    came = at.over_core(theirs)
    both = jnp.stack([jnp.where(at.c == 0, mine, came), jnp.where(at.c == 0, came, mine)])
    near = at.over_z(both)
    lowest = at.t % 2 == 0
    two = jnp.stack([jnp.where(lowest, both, near), jnp.where(lowest, near, both)], axis=1)
    far = at.over_far(two)
    lower = at.t // 2 == 0
    four = jnp.stack([jnp.where(lower, two, far), jnp.where(lower, far, two)], axis=1)
    line = four.reshape(2, rows * at.tp, half)
    lows = spread(line[0], at, True)
    highs = spread(line[1], at, False)
    part = jnp.concatenate(
        [piece for place in range(at.blocks) for piece in (lows[place], highs[place])], axis=0
    )
    other = at.over_core(part)
    return jnp.where(at.c == 0, part, other), jnp.where(at.c == 0, other, part)


def scatter_shared(grad_bc, grad_kv, at):
    f32, bf16 = jnp.float32, jnp.bfloat16
    first = at.c == 0
    bc_width = grad_bc.shape[1]
    going = jnp.where(
        first, jnp.pad(grad_kv, ((0, 0), (0, bc_width - grad_kv.shape[1]))), grad_bc
    )
    came = at.over_core(going.astype(bf16)).astype(f32)
    kept = jnp.concatenate(
        [came[:, :HD], grad_kv[:, :HD], came[:, HD : 2 * HD], grad_kv[:, HD:]], axis=1
    )
    total = jnp.where(first, grad_bc + came, kept)
    rows = total.shape[0] // (2 * at.blocks)
    parts = total.reshape(at.blocks, 2, rows, total.shape[1])
    low = collect(lambda place, half: parts[place, half], at, 0)
    high = collect(lambda place, half: parts[place, half], at, 1)
    piece = rows // at.tp
    line = jnp.stack([low, high]).reshape(2, 2, 2, piece, total.shape[1])
    lower = at.t // 2 == 0
    went = at.over_far(jnp.where(lower, line[:, 1], line[:, 0]).astype(bf16)).astype(f32)
    line = jnp.where(lower, line[:, 0], line[:, 1]) + went
    lowest = at.t % 2 == 0
    went = at.over_z(jnp.where(lowest, line[:, 1], line[:, 0]).astype(bf16)).astype(f32)
    line = jnp.where(lowest, line[:, 0], line[:, 1]) + went
    mine = jnp.where(first, line[0], line[1])
    came = at.over_core(jnp.where(first, line[1], line[0]).astype(bf16)).astype(f32)
    return jnp.concatenate([jnp.where(first, mine, came), jnp.where(first, came, mine)], axis=1)


def sum_everywhere(values, at):
    for bit in range(at.dp.bit_length() - 1):
        values = values + at.send(values, lambda d, t: (d ^ (1 << bit), t))
    for bit in range(at.tp.bit_length() - 1):
        values = values + at.send(values, lambda d, t: (d, t ^ (1 << bit)))
    return values


def per_device(
    layer_in,
    teacher,
    lengths,
    input_gain,
    mixer_in_weight,
    step_weight,
    query_weight,
    shared_weight,
    conv_inner,
    conv_shared,
    step_bias,
    decay_log,
    skip_gain,
    inner_gain,
    mixer_out_weight,
    attn_out_weight,
    middle_gain,
    gate_up_weight,
    down_weight,
):
    f32 = jnp.float32
    bf16 = jnp.bfloat16
    contract_last = (((1,), (1,)), ((), ()))
    contract_first = (((0,), (0,)), ((), ()))
    at = Places()
    rows_here, features = layer_in.shape
    slot_len = rows_here * at.tp
    local_heads = step_bias.shape[0]
    width = inner_gain.shape[0]
    head_dim = width // local_heads
    query_width = query_weight.shape[1]
    hidden_width = down_weight.shape[1]
    bc_width = conv_shared.shape[1]
    w_rows = step_weight.shape[0]

    inputs = turn_features(relocate(layer_in, at), at, 1).astype(f32)
    target = turn_features(relocate(teacher, at), at, 1).astype(f32)
    gain_in = turn_features(input_gain, at, 0)
    gain_mid = turn_features(middle_gain, at, 0)
    column_params = jnp.concatenate(
        [conv_inner.reshape(-1), inner_gain, step_bias, decay_log, skip_gain]
    )
    column_params = relocate(column_params, at)
    lane_params = jnp.concatenate(
        [
            column_params[: (KC + 1) * width].reshape(KC + 1, width),
            jnp.repeat(column_params[(KC + 1) * width + 2 * local_heads :], head_dim)[None],
            jnp.zeros((2, width), f32),
        ],
        axis=0,
    )
    head_rows = column_params[(KC + 1) * width :][: 2 * local_heads].reshape(2, local_heads)
    head_rows = jnp.concatenate([head_rows[:1], -jnp.exp(head_rows[1:])], axis=0)
    head_params = jnp.pad(head_rows, ((0, 6), (0, WIDE - local_heads)))
    seg = (
        lax.broadcasted_iota(jnp.int32, (width, WIDE), 0) // head_dim
        == lax.broadcasted_iota(jnp.int32, (width, WIDE), 1)
    ).astype(bf16)
    half = HD // 2
    freqs = jnp.exp(-jnp.log(ROPE_BASE) * 2.0 * jnp.arange(half, dtype=f32) / HD)
    angles = jnp.arange(slot_len).astype(f32)[:, None] * freqs[None, :]
    cosine, sine = jnp.cos(angles), jnp.sin(angles)
    cosine = jnp.concatenate([cosine, cosine], axis=1)
    sine = jnp.concatenate([-sine, sine], axis=1)
    quarters = jnp.arange(at.tp, dtype=jnp.int32)
    order = (at.c ^ (quarters // 2)) + 2 * (at.zq ^ (quarters % 2))

    left, right = gather_shared(shared_weight, at)
    kv_index = at.column * (query_width // HD) // (QH // KVH)
    second = kv_index == 1
    shared_all = jnp.concatenate(
        [
            left,
            jnp.where(second, right[:, HD : 2 * HD], right[:, :HD]),
            jnp.where(second, right[:, 3 * HD :], right[:, 2 * HD : 3 * HD]),
        ],
        axis=1,
    )
    in_pack = jnp.concatenate(
        [
            mixer_in_weight.reshape(w_rows, 2 * width),
            query_weight,
            step_weight,
            jnp.zeros((w_rows, WIDE - local_heads), bf16),
        ],
        axis=1,
    )
    in_all = gather_weight(in_pack, at)
    out_all = gather_weight(jnp.concatenate([mixer_out_weight, attn_out_weight], axis=1), at)
    gate_up_all = gather_weight(gate_up_weight.reshape(w_rows, 2 * hidden_width), at)
    down_all = gather_weight(down_weight, at)

    def row_split(values):
        return [values[i * rows_here : (i + 1) * rows_here] for i in range(at.tp)]

    normed_in, norm_in_back = jax.vjp(rms_norm, inputs, gain_in)
    act_all = jnp.concatenate(share_rows(normed_in.astype(bf16), at), axis=0)
    proj_shared = jnp.dot(act_all, shared_all, preferred_element_type=f32)
    proj = jnp.dot(act_all, in_all, preferred_element_type=f32)
    attn_low = attn_forward(order, proj, proj_shared, cosine, sine, query_width, width, bc_width)
    heads_all, y, states = mixer_forward(
        order, proj, proj_shared, attn_low, lane_params, conv_shared, head_params
    )
    mix_parts = [
        lax.dot_general(piece, out_all, contract_last, preferred_element_type=f32)
        for piece in row_split(heads_all)
    ]
    resid = inputs + sum_rows(mix_parts, at)
    normed_mid, norm_mid_back = jax.vjp(rms_norm, resid, gain_mid)
    mid_all = jnp.concatenate(share_rows(normed_mid.astype(bf16), at), axis=0)
    gate_up = jnp.dot(mid_all, gate_up_all, preferred_element_type=f32)
    gate_val = gate_up[:, :hidden_width]
    up_val = gate_up[:, hidden_width:]
    sigmoid_gate = jax.nn.sigmoid(gate_val)
    hidden = (gate_val * sigmoid_gate * up_val).astype(bf16)
    mlp_parts = [
        lax.dot_general(piece, down_all, contract_last, preferred_element_type=f32)
        for piece in row_split(hidden)
    ]
    outputs = resid + sum_rows(mlp_parts, at)
    seq_len = lax.dynamic_index_in_dim(lengths, at.slot, keepdims=False)
    positions = at.quarter * rows_here + jnp.arange(rows_here)
    live = (positions < seq_len).astype(f32)
    error = (outputs - target) * live[:, None]
    err_local = 0.5 * jnp.sum(error * error)
    layer_out = relocate(turn_features(outputs.astype(bf16), at, 1), at)

    grad_all = jnp.concatenate(share_rows(error.astype(bf16), at), axis=0)
    block = features // (2 * at.blocks)

    def columns_of(values, place, half):
        start = (2 * place + half) * block
        return values[:, start : start + block]

    def weight_grad(left, right):
        def piece_of(place, half):
            return lax.dot_general(
                columns_of(left, place, half), right, contract_first, preferred_element_type=f32
            )

        return scatter_weight(piece_of, at)

    grad_down = weight_grad(grad_all, hidden)
    grad_hidden = jnp.dot(grad_all, down_all, preferred_element_type=f32)
    grad_gate = grad_hidden * up_val * sigmoid_gate * (1.0 + gate_val * (1.0 - sigmoid_gate))
    grad_up = grad_hidden * gate_val * sigmoid_gate
    grad_gu = jnp.concatenate([grad_gate.astype(bf16), grad_up.astype(bf16)], axis=1)
    grad_mid_parts = [
        lax.dot_general(piece, gate_up_all, contract_last, preferred_element_type=f32)
        for piece in row_split(grad_gu)
    ]
    grad_gate_up = weight_grad(mid_all, grad_gu)
    grad_mid = sum_rows(grad_mid_parts, at)
    grad_resid_norm, grad_middle_gain = norm_mid_back(grad_mid)
    grad_resid = error + grad_resid_norm
    mix_grad_all = jnp.concatenate(share_rows(grad_resid.astype(bf16), at), axis=0)
    grad_heads = jnp.dot(mix_grad_all, out_all, preferred_element_type=f32)
    grad_out = weight_grad(mix_grad_all, heads_all)
    dq, dkv = attn_backward(
        order, proj, proj_shared, cosine, sine, grad_heads, query_width, width, bc_width
    )
    low_pack, low_shared, dlane, dconv, dhead = mixer_backward(
        order, proj, proj_shared, y, states, grad_heads, dq, dkv, lane_params, conv_shared,
        head_params, seg, query_width,
    )
    grad_bc = lax.dot_general(
        act_all, low_shared[:, :bc_width], contract_first, preferred_element_type=f32
    )
    grad_kv = lax.dot_general(
        act_all, low_shared[:, bc_width:], contract_first, preferred_element_type=f32
    )
    grad_shared_weight = scatter_shared(grad_bc, grad_kv, at)
    grad_in = weight_grad(act_all, low_pack)
    grad_act_parts = [
        lax.dot_general(a, in_all, contract_last, preferred_element_type=f32)
        + lax.dot_general(b, shared_all, contract_last, preferred_element_type=f32)
        for a, b in zip(row_split(low_pack), row_split(low_shared))
    ]
    grad_act = sum_rows(grad_act_parts, at)
    grad_input_norm, grad_input_gain = norm_in_back(grad_act)
    input_grad = grad_resid + grad_input_norm
    input_grad = relocate(turn_features(input_grad, at, 1), at)

    column = at.column
    convx_full = lax.dynamic_update_slice(
        jnp.zeros((KC + 1, DI), f32), dlane[: KC + 1], (0, column * width)
    )
    head_stack = jnp.concatenate(
        [dhead[:2, :local_heads], dlane[KC + 1].reshape(1, local_heads, head_dim).sum(2)], axis=0
    )
    heads_full = lax.dynamic_update_slice(
        jnp.zeros((3, H), f32), head_stack, (0, column * local_heads)
    )
    small = (
        convx_full,
        dconv[:KC],
        heads_full,
        turn_features(grad_input_gain, at, 0),
        turn_features(grad_middle_gain, at, 0),
        err_local,
    )
    flat = jnp.concatenate([part.reshape(-1) for part in small])
    length = flat.shape[0]
    padded = -(-length // 1024) * 1024
    flat = jnp.pad(flat, (0, padded - length)).reshape(-1, 128)
    flat = sum_everywhere(flat, at).reshape(-1)
    sums = []
    start = 0
    for part in small:
        sums.append(flat[start : start + part.size].reshape(part.shape))
        start += part.size
    sum_lanes, sum_convs, sum_heads, sum_input_gain, sum_middle_gain, err_total = sums
    lanes_local = lax.dynamic_slice_in_dim(sum_lanes, at.t * width, width, 1)
    heads_local = lax.dynamic_slice_in_dim(sum_heads, at.t * local_heads, local_heads, 1)
    loss = err_total / jnp.sum(lengths).astype(f32)
    query_from = 2 * width
    step_from = query_from + query_width
    return (
        layer_out,
        loss,
        input_grad,
        sum_input_gain,
        grad_in[:, :query_from].reshape(w_rows, 2, width),
        grad_in[:, step_from : step_from + local_heads],
        grad_in[:, query_from:step_from],
        grad_shared_weight,
        lanes_local[:KC],
        sum_convs,
        heads_local[0],
        heads_local[1],
        heads_local[2],
        lanes_local[KC],
        grad_out[:, :width],
        grad_out[:, width:],
        sum_middle_gain,
        grad_gate_up.reshape(w_rows, 2, hidden_width),
        grad_down,
    )


def solution(mesh):
    placed = (
        P(("dp", "tensor"), None),
        P(("dp", "tensor"), None),
        P(),
        P(),
        P("dp", None, "tensor"),
        P("dp", "tensor"),
        P("dp", "tensor"),
        P(("dp", "tensor"), None),
        P(None, "tensor"),
        P(),
        P("tensor"),
        P("tensor"),
        P("tensor"),
        P("tensor"),
        P("dp", "tensor"),
        P("dp", "tensor"),
        P(),
        P("dp", None, "tensor"),
        P("dp", "tensor"),
    )
    return jax.shard_map(
        per_device,
        mesh=mesh,
        in_specs=placed,
        out_specs=(
            P(("dp", "tensor"), None),
            P(),
            P(("dp", "tensor"), None),
            P(),
            P("dp", None, "tensor"),
            P("dp", "tensor"),
            P("dp", "tensor"),
            P(("dp", "tensor"), None),
            P(None, "tensor"),
            P(),
            P("tensor"),
            P("tensor"),
            P("tensor"),
            P("tensor"),
            P("dp", "tensor"),
            P("dp", "tensor"),
            P(),
            P("dp", None, "tensor"),
            P("dp", "tensor"),
        ),
        check_vma=False,
    )
```

time: 1870 us -> 1130 us (0.60)
  waiting for transfers between devices: 1030 us -> 527 us
  starting transfers between devices: 2.35 us -> 189 us
  local copies, waits for them, and re-layouts: 229 us -> 48.5 us
  matrix products: 346 us -> 207 us
  other arithmetic: 158 us -> 68.3 us
  blocking collectives: 69.9 us -> 0 us
  Pallas kernels: 0 us -> 69.3 us
    reduce_scatter x13 -> x0, waiting for transfers between devices: 625 us -> none  [the longest x1 143 us: per_device(): lax.psum_scatter(grad_mid_part, 'tensor', scatter_dimension=0, tiled=True)]
    ppermute x0 -> x118, waiting for transfers between devices: none -> 527 us  [send(): return lax.ppermute(values, ('dp', 'tensor'), self.pairs(where_to))]
    all_gather x11 -> x0, waiting for transfers between devices: 399 us -> none  [the longest x1 82 us: per_device(): lax.all_gather(normed_mid.astype(bf16), 'tensor', axis=0, tiled=True)]
    ppermute x0 -> x118, starting transfers between devices: none -> 189 us  [send(): return lax.ppermute(values, ('dp', 'tensor'), self.pairs(where_to))]
    dot_general x91 -> x57, matrix products: 323 us -> 192 us  [the longest x32 61.3 us: piece_of(): lax.dot_general(columns_of(left, place, half), right, contract_first, pre...]
    dynamic_update_slice x29 -> x2, local copies, waits for them, and re-layouts: 91.1 us -> 0.26 us  [the longest x1 0.25 us: per_device(): lax.dynamic_update_slice(jnp.zeros((3, H), f32), head_stack, (0, column *...]
    pallas_call x0 -> x4, Pallas kernels: none -> 69.3 us  [the longest x1 33.6 us: mixer_backward(): pl.pallas_call(mixer_bwd_body, grid_spec=pltpu.PrefetchScalarGridSpec(num...]
    psum x1 -> x0, blocking collectives: 43 us -> none  [per_device(): lax.psum((convx_full, grad_convs, heads_full, gain_full, grad_input_gain,...]
  transfers between devices with their start and end apart: 24 -> 118, of which waited for: 18 -> 48; matrix products, arithmetic and copies ran while one was open for 35% -> 17% of each run, Pallas kernels for 0% -> 2%
where the time goes in v1:
time: 1130 us; the launch traced here: 1120 us
  waiting for transfers between devices  527 us (47%)
  matrix products  207 us (18%)
  starting transfers between devices  189 us (17%)
  Pallas kernels  69.3 us (6%)
  other arithmetic  68.3 us (6%)
  local copies, waits for them, and re-layouts  48.5 us (4%)
    ppermute x118, waiting for transfers between devices, send(): return lax.ppermute(values, ('dp', 'tensor'), self.pairs(where_to))  527 us
    ppermute x118, starting transfers between devices, send(): return lax.ppermute(values, ('dp', 'tensor'), self.pairs(where_to))  189 us
    dot_general x32, matrix products, piece_of(): lax.dot_general(columns_of(left, place, half), right, contract_first, pre...  61.3 us
    pallas_call x1, Pallas kernels, mixer_backward(): pl.pallas_call(mixer_bwd_body, grid_spec=pltpu.PrefetchScalarGridSpec(num...  33.6 us
    dot_general x4, matrix products, per_device(): lax.dot_general(a, in_all, contract_last, preferred_element_type=f32)  30.1 us
    dot_general x4, matrix products, per_device(): lax.dot_general(piece, gate_up_all, contract_last, preferred_element_type...  27.5 us
    unnamed x244, local copies, waits for them, and re-layouts  25.7 us
  transfers between devices with their start and end apart: 118, of which 48 were waited for; matrix products, arithmetic and copies ran while one was open for 17% of the time, Pallas kernels for 2%

profile of v1, /device:TPU:1, one launch (start us, length us, event | category | flops | bytes accessed | tf_op | source)
XLA Modules:
  0.0 1115.6 jit_solution(17899873455302125101)
XLA Ops:
  28.8 43.1 %collective-permute-done.22 = f32[3876]{0:T(1024)} collective-permute-done((f32[3876]{0:T(1024)}, f32[3876]{0:T(1024)}, u32[]{:S(2)}, u32[]{:S(2)}) %collective-permute-start.22) | collective-permute-done | bytes 15536 | tf_op jit(solution)/shard_map/ppermute | solution.py:639
  127.3 22.9 %collective-permute-done.57 = bf16[256,2048]{1,0:T(8,128)(2,1)S(1)} collective-permute-done((bf16[256,2048]{1,0:T(8,128)(2,1)S(1)}, bf16[256,2048]{1,0:T(8,128)(2,1)S(1)}, u32[]{:S(2)}, u32[]{:S(2)}) %collective-permute-start.57) | collective-permute-done | bytes 1048608 | tf_op jit(solution)/shard_map/ppermute | solution.py:639
  173.2 16.6 %collective-permute-done.30 = bf16[256,1024]{1,0:T(8,128)(2,1)S(1)} collective-permute-done((bf16[256,1024]{1,0:T(8,128)(2,1)S(1)}, bf16[256,1024]{1,0:T(8,128)(2,1)S(1)}, u32[]{:S(2)}, u32[]{:S(2)}) %collective-permute-start.30) | collective-permute-done | bytes 524320 | tf_op jit(solution)/shard_map/ppermute | solution.py:639
  191.9 18.4 %collective-permute-done.7 = bf16[256,1920]{1,0:T(8,128)(2,1)S(1)} collective-permute-done((bf16[256,1920]{1,0:T(8,128)(2,1)S(1)}, bf16[256,1920]{1,0:T(8,128)(2,1)S(1)}, u32[]{:S(2)}, u32[]{:S(2)}) %collective-permute-start.7) | collective-permute-done | bytes 983072 | tf_op jit(solution)/shard_map/ppermute | solution.py:639
  214.1 11.4 %collective-permute-done.10 = bf16[256,1920]{1,0:T(8,128)(2,1)S(1)} collective-permute-done((bf16[256,1920]{1,0:T(8,128)(2,1)S(1)}, bf16[256,1920]{1,0:T(8,128)(2,1)S(1)}, u32[]{:S(2)}, u32[]{:S(2)}) %collective-permute-start.10) | collective-permute-done | bytes 983072 | tf_op jit(solution)/shard_map/ppermute | solution.py:639
  262.9 15.8 %shard_map.331 = (bf16[1024,1024]{1,0:T(8,128)(2,1)}, f32[1024,768]{1,0:T(8,128)}, bf16[8,256,768]{2,1,0:T(8,128)(2,1)}) custom-call(s32[4]{0:T(128)} %fusion.127.order, f32[1024,1920]{1,0:T(8,128)} %fusion.146.q_ref.gate_ref.inner_ref.step_ref.before_ref, f32[1024,1920]{1,0:T(8,128)} %fusion.146.q_ref.gate_ref.inner_ref.step_ref.before_ref, ...), custom_call_target="tpu_custom_call" | custom-call | flops 3221225472 | bytes 15728640 | tf_op jit(solution)/shard_map/pallas_call | solution.py:478
  295.4 21.6 %collective-permute-done.33 = bf16[256,2048]{1,0:T(8,128)(2,1)S(1)} collective-permute-done((bf16[256,2048]{1,0:T(8,128)(2,1)S(1)}, bf16[256,2048]{1,0:T(8,128)(2,1)S(1)}, u32[]{:S(2)}, u32[]{:S(2)}) %collective-permute-start.33) | collective-permute-done | bytes 1048608 | tf_op jit(solution)/shard_map/ppermute | solution.py:639
  325.2 31.1 %collective-permute-done.51 = bf16[256,1024]{1,0:T(8,128)(2,1)S(1)} collective-permute-done((bf16[256,1024]{1,0:T(8,128)(2,1)S(1)}, bf16[256,1024]{1,0:T(8,128)(2,1)S(1)}, u32[]{:S(2)}, u32[]{:S(2)}) %collective-permute-start.51) | collective-permute-done | bytes 524320 | tf_op jit(solution)/shard_map/ppermute | solution.py:639
  359.2 15.8 %collective-permute-done.40 = bf16[256,2048]{1,0:T(8,128)(2,1)S(1)} collective-permute-done((bf16[256,2048]{1,0:T(8,128)(2,1)S(1)}, bf16[256,2048]{1,0:T(8,128)(2,1)S(1)}, u32[]{:S(2)}, u32[]{:S(2)}) %collective-permute-start.40) | collective-permute-done | bytes 1048608 | tf_op jit(solution)/shard_map/ppermute | solution.py:639
  382.0 19.7 %collective-permute-done.43 = bf16[256,2048]{1,0:T(8,128)(2,1)S(1)} collective-permute-done((bf16[256,2048]{1,0:T(8,128)(2,1)S(1)}, bf16[256,2048]{1,0:T(8,128)(2,1)S(1)}, u32[]{:S(2)}, u32[]{:S(2)}) %collective-permute-start.43) | collective-permute-done | bytes 1048608 | tf_op jit(solution)/shard_map/ppermute | solution.py:639
  405.2 12.0 %fusion.139 = f32[1024,2048]{1,0:T(8,128)S(1)} fusion(bf16[2048,2048]{1,0:T(8,128)(2,1)} %copy-done.66, bf16[256,2048]{1,0:T(8,128)(2,1)S(1)} %collective-permute-done.36, bf16[256,2048]{1,0:T(8,128)(2,1)S(1)} %collective-permute-done.35, bf16[256,2048]{1,0:T(8,128)(2,1)S(1)} %collective-permute-done.34, bf16[256,2048]{1,0:T(8,128)(2,1)S(1)} %multiply_convert_fusion.3), kind=kOutput, calls=%fused_computation.439 | convolution fusion | flops 8606711808 | bytes 20971520 | tf_op jit(solution)/shard_map/dot_general | solution.py:941
  434.0 22.4 %collective-permute-done.55 = bf16[256,2048]{1,0:T(8,128)(2,1)} collective-permute-done((bf16[256,2048]{1,0:T(8,128)(2,1)}, bf16[256,2048]{1,0:T(8,128)(2,1)}, u32[]{:S(2)}, u32[]{:S(2)}) %collective-permute-start.55) | collective-permute-done | bytes 1048608 | tf_op jit(solution)/shard_map/ppermute | solution.py:639
  465.8 21.2 %collective-permute-done.59 = bf16[256,2048]{1,0:T(8,128)(2,1)} collective-permute-done((bf16[256,2048]{1,0:T(8,128)(2,1)}, bf16[256,2048]{1,0:T(8,128)(2,1)}, u32[]{:S(2)}, u32[]{:S(2)}) %collective-permute-start.59) | collective-permute-done | bytes 1048608 | tf_op jit(solution)/shard_map/ppermute | solution.py:639
  620.0 14.5 %collective-permute-done.107 = bf16[256,2048]{1,0:T(8,128)(2,1)} collective-permute-done((bf16[256,2048]{1,0:T(8,128)(2,1)}, bf16[256,2048]{1,0:T(8,128)(2,1)}, u32[]{:S(2)}, u32[]{:S(2)}) %collective-permute-start.107) | collective-permute-done | bytes 1048608 | tf_op jit(solution)/shard_map/ppermute | solution.py:639
  669.5 30.5 %collective-permute-done.109 = bf16[256,2048]{1,0:T(8,128)(2,1)S(1)} collective-permute-done((bf16[256,2048]{1,0:T(8,128)(2,1)}, bf16[256,2048]{1,0:T(8,128)(2,1)S(1)}, u32[]{:S(2)}, u32[]{:S(2)}) %collective-permute-start.109) | collective-permute-done | bytes 1048608 | tf_op jit(solution)/shard_map/ppermute | solution.py:639
  707.8 14.8 %collective-permute-done.56 = bf16[256,2048]{1,0:T(8,128)(2,1)} collective-permute-done((bf16[256,2048]{1,0:T(8,128)(2,1)}, bf16[256,2048]{1,0:T(8,128)(2,1)}, u32[]{:S(2)}, u32[]{:S(2)}) %collective-permute-start.56) | collective-permute-done | bytes 1048608 | tf_op jit(solution)/shard_map/ppermute | solution.py:639
  735.0 12.1 %shard_map.332 = (bf16[1024,256]{1,0:T(8,128)(2,1)}, bf16[1024,256]{1,0:T(8,128)(2,1)}) custom-call(s32[4]{0:T(128)} %fusion.127.order, f32[1024,1920]{1,0:T(8,128)} %fusion.146.q_ref.gate_ref.inner_ref.step_ref.before_ref, f32[1024,768]{1,0:T(8,128)} %fusion.140.kv_ref.bc_ref.bcbefore_ref, f32[1024,128]{1,0:T(8,128)} %get-tuple-element.173.cos_ref.all_cos, ...), custom_call_target="tpu_custom_call" | custom-call | flops 2147483648 | bytes 5242880 | tf_op jit(solution)/shard_map/pallas_call | solution.py:440
  747.1 33.6 %shard_map.333 = (bf16[1024,1920]{1,0:T(8,128)(2,1)}, bf16[1024,768]{1,0:T(8,128)(2,1)}, f32[8,768]{1,0:T(8,128)}, f32[8,512]{1,0:T(8,128)}, f32[8,128]{1,0:T(8,128)}) custom-call(s32[4]{0:T(128)} %fusion.127.order, f32[1024,1920]{1,0:T(8,128)} %fusion.146.q_ref.gate_ref.inner_ref.step_ref.before_ref, ...), custom_call_target="tpu_custom_call" | custom-call | flops 8053063680 | bytes 31457280 | tf_op jit(solution)/shard_map/pallas_call | solution.py:547
  853.3 24.5 %collective-permute-done.97 = bf16[256,1024]{1,0:T(8,128)(2,1)} collective-permute-done((bf16[256,1024]{1,0:T(8,128)(2,1)}, bf16[256,1024]{1,0:T(8,128)(2,1)}, u32[]{:S(2)}, u32[]{:S(2)}) %collective-permute-start.97) | collective-permute-done | bytes 524320 | tf_op jit(solution)/shard_map/ppermute | solution.py:639
  925.4 18.6 %collective-permute-done.81 = bf16[256,1920]{1,0:T(8,128)(2,1)S(1)} collective-permute-done((bf16[256,1920]{1,0:T(8,128)(2,1)S(1)}, bf16[256,1920]{1,0:T(8,128)(2,1)S(1)}, u32[]{:S(2)}, u32[]{:S(2)}) %collective-permute-start.81) | collective-permute-done | bytes 983072 | tf_op jit(solution)/shard_map/ppermute | solution.py:639
  965.1 12.2 %collective-permute-done.69 = bf16[256,2048]{1,0:T(8,128)(2,1)} collective-permute-done((bf16[256,2048]{1,0:T(8,128)(2,1)}, bf16[256,2048]{1,0:T(8,128)(2,1)}, u32[]{:S(2)}, u32[]{:S(2)}) %collective-permute-start.69) | collective-permute-done | bytes 1048608 | tf_op jit(solution)/shard_map/ppermute | solution.py:639
  1013.0 11.4 %collective-permute-done.74 = f32[176,128]{1,0:T(8,128)S(1)} collective-permute-done((f32[176,128]{1,0:T(8,128)S(1)}, f32[176,128]{1,0:T(8,128)S(1)}, u32[]{:S(2)}, u32[]{:S(2)}) %collective-permute-start.74) | collective-permute-done | bytes 90144 | tf_op jit(solution)/shard_map/ppermute | solution.py:639
  1039.5 31.6 %collective-permute-done.91 = bf16[2,2,64,512]{3,2,0,1:T(8,128)(2,1)S(1)} collective-permute-done((bf16[2,2,64,512]{3,2,0,1:T(8,128)(2,1)S(1)}, bf16[2,2,64,512]{3,2,0,1:T(8,128)(2,1)S(1)}, u32[]{:S(2)}, u32[]{:S(2)}) %collective-permute-start.91) | collective-permute-done | bytes 262176 | tf_op jit(solution)/shard_map/ppermute | solution.py:639
  1072.1 19.4 %collective-permute-start.92 = (bf16[2,64,512]{2,1,0:T(8,128)(2,1)S(1)}, bf16[2,64,512]{2,1,0:T(8,128)(2,1)}, u32[]{:S(2)}, u32[]{:S(2)}) collective-permute-start(bf16[2,64,512]{2,1,0:T(8,128)(2,1)S(1)} %fusion.118), channel_id=1, source_target_pairs={{0,1},{1,0},{2,3},{3,2},{4,5},{5,4},{6,7},{7,6},{8,9},{9,8},{10,11... | collective-permute-start | bytes 393224 | tf_op jit(solution)/shard_map/ppermute | solution.py:639
  (654 shorter events, 614.0 us)
Async XLA Ops:
  2.7 96.0 %collective-permute-start.23 = (bf16[256,1024]{1,0:T(8,128)(2,1)S(1)}, bf16[256,1024]{1,0:T(8,128)(2,1)}, u32[]{:S(2)}, u32[]{:S(2)}) collective-permute-start(bf16[256,1024]{1,0:T(8,128)(2,1)S(1)} %constant_dynamic-update-slice_fusion.16), channel_id=1, source_target_pairs={{0,2},{1,3},{2,6},{3,7},{4,0},{5,1},{6,4},{7,5},{8,10},{9,11},{10,... | collective-permute-start | bytes 1572872 | tf_op jit(solution)/shard_map/ppermute | solution.py:639
  2.8 96.2 %collective-permute-start.24 = (bf16[256,1024]{1,0:T(8,128)(2,1)S(1)}, bf16[256,1024]{1,0:T(8,128)(2,1)}, u32[]{:S(2)}, u32[]{:S(2)}) collective-permute-start(bf16[256,1024]{1,0:T(8,128)(2,1)S(1)} %constant_dynamic-update-slice_fusion.16), channel_id=1, source_target_pairs={{2,4},{3,5},{4,2},{5,3},{10,12},{11,13},{12,10},{13,11},{18,20},{1... | collective-permute-start | bytes 1572872 | tf_op jit(solution)/shard_map/ppermute | solution.py:639
  11.6 110.8 %collective-permute-start.4 = (bf16[256,1920]{1,0:T(8,128)(2,1)S(1)}, bf16[256,1920]{1,0:T(8,128)(2,1)S(1)}, u32[]{:S(2)}, u32[]{:S(2)}) collective-permute-start(bf16[256,1920]{1,0:T(8,128)(2,1)S(1)} %concatenate.88), channel_id=1, source_target_pairs={{0,2},{1,3},{2,6},{3,7},{4,0},{5,1},{6,4},{7,5},{8,10},{9,11},{10,... | collective-permute-start | bytes 2949128 | tf_op jit(solution)/shard_map/ppermute | solution.py:639
  11.6 112.1 %collective-permute-start.5 = (bf16[256,1920]{1,0:T(8,128)(2,1)S(1)}, bf16[256,1920]{1,0:T(8,128)(2,1)}, u32[]{:S(2)}, u32[]{:S(2)}) collective-permute-start(bf16[256,1920]{1,0:T(8,128)(2,1)S(1)} %concatenate.88), channel_id=1, source_target_pairs={{2,4},{3,5},{4,2},{5,3},{10,12},{11,13},{12,10},{13,11},{18,20},{1... | collective-permute-start | bytes 2949128 | tf_op jit(solution)/shard_map/ppermute | solution.py:639
  15.0 56.9 %collective-permute-start.22 = (f32[3876]{0:T(1024)}, f32[3876]{0:T(1024)}, u32[]{:S(2)}, u32[]{:S(2)}) collective-permute-start(f32[3876]{0:T(1024)} %concatenate.94), channel_id=1, source_target_pairs={{2,4},{3,5},{4,2},{5,3},{10,12},{11,13},{12,10},{13,11},{18,20},{1... | collective-permute-start | bytes 46520 | tf_op jit(solution)/shard_map/ppermute | solution.py:639
  173.2 57.8 %collective-permute-start.21 = (bf16[2048,512]{1,0:T(8,128)(2,1)S(1)}, bf16[2048,512]{1,0:T(8,128)(2,1)S(1)}, u32[]{:S(2)}, u32[]{:S(2)}) collective-permute-start(bf16[2048,512]{1,0:T(8,128)(2,1)S(1)} %constant_dynamic-update-slice_fusion.8), channel_id=1, source_target_pairs={{0,4},{1,5},{2,6},{3,7},{4,0},{5,1},{6,2},{7,3},{8,12},{9,13},{10,... | collective-permute-start | bytes 6291464 | tf_op jit(solution)/shard_map/ppermute | solution.py:639
  213.8 78.7 %collective-permute-start.37 = (bf16[256,2048]{1,0:T(8,128)(2,1)S(1)}, bf16[256,2048]{1,0:T(8,128)(2,1)S(1)}, u32[]{:S(2)}, u32[]{:S(2)}) collective-permute-start(bf16[256,2048]{1,0:T(8,128)(2,1)S(1)} %bitcast.147), channel_id=1, source_target_pairs={{0,2},{1,3},{2,6},{3,7},{4,0},{5,1},{6,4},{7,5},{8,10},{9,11},{10,... | collective-permute-start | bytes 3145736 | tf_op jit(solution)/shard_map/ppermute | solution.py:639
  225.5 67.1 %collective-permute-start.38 = (bf16[256,2048]{1,0:T(8,128)(2,1)S(1)}, bf16[256,2048]{1,0:T(8,128)(2,1)S(1)}, u32[]{:S(2)}, u32[]{:S(2)}) collective-permute-start(bf16[256,2048]{1,0:T(8,128)(2,1)S(1)} %bitcast.148), channel_id=1, source_target_pairs={{2,4},{3,5},{4,2},{5,3},{10,12},{11,13},{12,10},{13,11},{18,20},{1... | collective-permute-start | bytes 3145736 | tf_op jit(solution)/shard_map/ppermute | solution.py:639
  227.6 55.1 %collective-permute-start.45 = (bf16[256,1024]{1,0:T(8,128)(2,1)S(1)}, bf16[256,1024]{1,0:T(8,128)(2,1)S(1)}, u32[]{:S(2)}, u32[]{:S(2)}) collective-permute-start(bf16[256,1024]{1,0:T(8,128)(2,1)S(1)} %copy-done.35), channel_id=1, source_target_pairs={{0,2},{1,3},{2,6},{3,7},{4,0},{5,1},{6,4},{7,5},{8,10},{9,11},{10,... | collective-permute-start | bytes 1572872 | tf_op jit(solution)/shard_map/ppermute | solution.py:639
  233.3 50.9 %collective-permute-start.46 = (bf16[256,1024]{1,0:T(8,128)(2,1)S(1)}, bf16[256,1024]{1,0:T(8,128)(2,1)}, u32[]{:S(2)}, u32[]{:S(2)}) collective-permute-start(bf16[256,1024]{1,0:T(8,128)(2,1)S(1)} %copy-done.35), channel_id=1, source_target_pairs={{2,4},{3,5},{4,2},{5,3},{10,12},{11,13},{12,10},{13,11},{18,20},{1... | collective-permute-start | bytes 1572872 | tf_op jit(solution)/shard_map/ppermute | solution.py:639
  324.4 50.7 %collective-permute-start.40 = (bf16[256,2048]{1,0:T(8,128)(2,1)S(1)}, bf16[256,2048]{1,0:T(8,128)(2,1)S(1)}, u32[]{:S(2)}, u32[]{:S(2)}) collective-permute-start(bf16[256,2048]{1,0:T(8,128)(2,1)S(1)} %get-tuple-element.65), channel_id=1, source_target_pairs={{0,8},{1,9},{2,10},{3,11},{4,12},{5,13},{6,14},{7,15},{8,0},{9,1},... | collective-permute-start | bytes 3145736 | tf_op jit(solution)/shard_map/ppermute | solution.py:639
  529.0 62.9 %collective-permute-start.61 = (bf16[256,2048]{1,0:T(8,128)(2,1)S(1)}, bf16[256,2048]{1,0:T(8,128)(2,1)S(1)}, u32[]{:S(2)}, u32[]{:S(2)}) collective-permute-start(bf16[256,2048]{1,0:T(8,128)(2,1)S(1)} %convolution_convert_fusion.13), channel_id=1, source_target_pairs={{0,4},{1,5},{2,6},{3,7},{4,0},{5,1},{6,2},{7,3},{8,12},{9,13},{10,... | collective-permute-start | bytes 3145736 | tf_op jit(solution)/shard_map/ppermute | solution.py:639
  589.4 48.7 %collective-permute-start.102 = (bf16[256,2048]{1,0:T(8,128)(2,1)S(1)}, bf16[256,2048]{1,0:T(8,128)(2,1)}, u32[]{:S(2)}, u32[]{:S(2)}) collective-permute-start(bf16[256,2048]{1,0:T(8,128)(2,1)S(1)} %convolution_convert_fusion.7), channel_id=1, source_target_pairs={{0,8},{1,9},{2,10},{3,11},{4,12},{5,13},{6,14},{7,15},{8,0},{9,1},... | collective-permute-start | bytes 3145736 | tf_op jit(solution)/shard_map/ppermute | solution.py:639
  599.4 55.6 %collective-permute-start.117 = (bf16[256,1024]{1,0:T(8,128)(2,1)S(1)}, bf16[256,1024]{1,0:T(8,128)(2,1)S(1)}, u32[]{:S(2)}, u32[]{:S(2)}) collective-permute-start(bf16[256,1024]{1,0:T(8,128)(2,1)S(1)} %get-tuple-element.92), channel_id=1, source_target_pairs={{2,4},{3,5},{4,2},{5,3},{10,12},{11,13},{12,10},{13,11},{18,20},{1... | collective-permute-start | bytes 1572872 | tf_op jit(solution)/shard_map/ppermute | solution.py:639
  643.6 56.5 %collective-permute-start.109 = (bf16[256,2048]{1,0:T(8,128)(2,1)}, bf16[256,2048]{1,0:T(8,128)(2,1)S(1)}, u32[]{:S(2)}, u32[]{:S(2)}) collective-permute-start(bf16[256,2048]{1,0:T(8,128)(2,1)} %get-tuple-element.83), channel_id=1, source_target_pairs={{2,4},{3,5},{4,2},{5,3},{10,12},{11,13},{12,10},{13,11},{18,20},{1... | collective-permute-start | bytes 3145736 | tf_op jit(solution)/shard_map/ppermute | solution.py:639
  655.0 67.6 %collective-permute-start.56 = (bf16[256,2048]{1,0:T(8,128)(2,1)}, bf16[256,2048]{1,0:T(8,128)(2,1)}, u32[]{:S(2)}, u32[]{:S(2)}) collective-permute-start(bf16[256,2048]{1,0:T(8,128)(2,1)} %pad_maximum_fusion.8), channel_id=1, source_target_pairs={{2,4},{3,5},{4,2},{5,3},{10,12},{11,13},{12,10},{13,11},{18,20},{1... | collective-permute-start | bytes 3145736 | tf_op jit(solution)/shard_map/ppermute | solution.py:639
  658.2 67.2 %collective-permute-start.64 = (bf16[256,2048]{1,0:T(8,128)(2,1)S(1)}, bf16[256,2048]{1,0:T(8,128)(2,1)}, u32[]{:S(2)}, u32[]{:S(2)}) collective-permute-start(bf16[256,2048]{1,0:T(8,128)(2,1)S(1)} %get-tuple-element.62), channel_id=1, source_target_pairs={{0,4},{1,5},{2,6},{3,7},{4,0},{5,1},{6,2},{7,3},{8,12},{9,13},{10,... | collective-permute-start | bytes 3145736 | tf_op jit(solution)/shard_map/ppermute | solution.py:639
  665.5 59.9 %collective-permute-start.66 = (bf16[256,2048]{1,0:T(8,128)(2,1)}, bf16[256,2048]{1,0:T(8,128)(2,1)}, u32[]{:S(2)}, u32[]{:S(2)}) collective-permute-start(bf16[256,2048]{1,0:T(8,128)(2,1)} %collective-permute-done.65), channel_id=1, source_target_pairs={{0,4},{1,5},{2,6},{3,7},{4,0},{5,1},{6,2},{7,3},{8,12},{9,13},{10,... | collective-permute-start | bytes 3145736 | tf_op jit(solution)/shard_map/ppermute | solution.py:639
  831.6 57.6 %collective-permute-start.80 = (bf16[256,1920]{1,0:T(8,128)(2,1)}, bf16[256,1920]{1,0:T(8,128)(2,1)}, u32[]{:S(2)}, u32[]{:S(2)}) collective-permute-start(bf16[256,1920]{1,0:T(8,128)(2,1)} %convolution_convert_fusion), channel_id=1, source_target_pairs={{0,16},{1,17},{2,18},{3,19},{4,20},{5,21},{6,22},{7,23},{8,24},{9,... | collective-permute-start | bytes 2949128 | tf_op jit(solution)/shard_map/ppermute | solution.py:639
  834.3 46.6 %collective-permute-start.94 = (bf16[256,1024]{1,0:T(8,128)(2,1)}, bf16[256,1024]{1,0:T(8,128)(2,1)}, u32[]{:S(2)}, u32[]{:S(2)}) collective-permute-start(bf16[256,1024]{1,0:T(8,128)(2,1)} %convolution_convert_fusion.21), channel_id=1, source_target_pairs={{0,8},{1,9},{2,10},{3,11},{4,12},{5,13},{6,14},{7,15},{8,0},{9,1},... | collective-permute-start | bytes 1572872 | tf_op jit(solution)/shard_map/ppermute | solution.py:639
  904.0 54.6 %collective-permute-start.84 = (bf16[2048,512]{1,0:T(8,128)(2,1)S(1)}, bf16[2048,512]{1,0:T(8,128)(2,1)S(1)}, u32[]{:S(2)}, u32[]{:S(2)}) collective-permute-start(bf16[2048,512]{1,0:T(8,128)(2,1)S(1)} %copy-done.90), channel_id=1, source_target_pairs={{0,4},{1,5},{2,6},{3,7},{4,0},{5,1},{6,2},{7,3},{8,12},{9,13},{10,... | collective-permute-start | bytes 6291464 | tf_op jit(solution)/shard_map/ppermute | solution.py:639
  948.8 153.2 %collective-permute-start.83 = (bf16[256,1920]{1,0:T(8,128)(2,1)}, bf16[256,1920]{1,0:T(8,128)(2,1)}, u32[]{:S(2)}, u32[]{:S(2)}) collective-permute-start(bf16[256,1920]{1,0:T(8,128)(2,1)} %get-tuple-element.89), channel_id=1, source_target_pairs={{2,4},{3,5},{4,2},{5,3},{10,12},{11,13},{12,10},{13,11},{18,20},{1... | collective-permute-start | bytes 2949128 | tf_op jit(solution)/shard_map/ppermute | solution.py:639
  1001.0 101.0 %collective-permute-start.82 = (bf16[256,1920]{1,0:T(8,128)(2,1)}, bf16[256,1920]{1,0:T(8,128)(2,1)}, u32[]{:S(2)}, u32[]{:S(2)}) collective-permute-start(bf16[256,1920]{1,0:T(8,128)(2,1)} %get-tuple-element.88), channel_id=1, source_target_pairs={{0,4},{1,5},{2,0},{3,1},{4,6},{5,7},{6,2},{7,3},{8,12},{9,13},{10,... | collective-permute-start | bytes 2949128 | tf_op jit(solution)/shard_map/ppermute | solution.py:639
  1024.4 86.6 %collective-permute-start.75 = (f32[256,2048]{1,0:T(8,128)}, f32[256,2048]{1,0:T(8,128)}, u32[]{:S(2)}, u32[]{:S(2)}) collective-permute-start(f32[256,2048]{1,0:T(8,128)} %pad_maximum_fusion.6), channel_id=1, source_target_pairs={{2,4},{3,5},{4,2},{5,3},{10,12},{11,13},{12,10},{13,11},{18,20},{1... | collective-permute-start | bytes 6291464 | tf_op jit(solution)/shard_map/ppermute | solution.py:639
  (200 other events, 4616.3 us)

commit v2 on v1

--- a/solution.py
+++ b/solution.py
@@ -1,3 +1,5 @@
+import functools
+
 import jax
 import jax.numpy as jnp
 from jax import lax
@@ -679,19 +681,362 @@
     return jnp.where(at.home, values, at.swap_away(values))
 
 
-def turn_features(values, at, axis):
-    block = values.shape[axis] // at.blocks
-    parts = [
-        lax.slice_in_dim(values, place * block, (place + 1) * block, axis=axis)
-        for place in range(at.blocks)
-    ]
-    for bit in range(at.bits):
-        turned = (at.k >> bit) % 2 == 1
-        parts = [
-            jnp.where(turned, parts[place ^ (1 << bit)], parts[place])
-            for place in range(at.blocks)
-        ]
-    return jnp.concatenate(parts, axis=axis)
+MESH = pl.DeviceIdType.MESH
+
+
+class Lanes:
+    def __init__(self, blocks):
+        d = lax.axis_index("dp")
+        t = lax.axis_index("tensor")
+        self.c = lax.rem(d, 2)
+        self.k = lax.div(d, 2)
+        self.d, self.t = d, t
+        self.home = self.c == lax.div(t, 2)
+        self.away = self.c != lax.div(t, 2)
+        self.other = d + 1 - 2 * self.c
+        self.near = t + 1 - 2 * lax.rem(t, 2)
+        self.far = lax.rem(t + 2, 4)
+        self.blocks = blocks
+        self.bits = blocks.bit_length() - 1
+
+    def block(self, place):
+        value = self.k
+        for bit in range(self.bits):
+            if (place >> bit) & 1:
+                value = value + (1 << bit) * (1 - 2 * lax.rem(lax.div(self.k, 1 << bit), 2))
+        return value
+
+    def across(self, bit):
+        return (2 * self.block(1 << bit) + self.c, self.t)
+
+    def greet(self):
+        partners = [
+            (self.other, self.t),
+            (self.d, self.near),
+            (self.d, self.far),
+            (self.other, self.far),
+        ] + [self.across(bit) for bit in range(self.bits)]
+        barrier = pltpu.get_barrier_semaphore()
+        for partner in partners:
+            pl.semaphore_signal(barrier, inc=1, device_id=partner, device_id_type=MESH)
+        pl.semaphore_wait(barrier, len(partners))
+
+
+def remote(src, dst, send_sem, recv_sem, device):
+    return pltpu.make_async_remote_copy(
+        src_ref=src,
+        dst_ref=dst,
+        send_sem=send_sem,
+        recv_sem=recv_sem,
+        device_id=device,
+        device_id_type=MESH,
+    )
+
+
+def onward(place, half, bits):
+    if half == 0:
+        return [bit for bit in range(bits) if place < (1 << bit)]
+    return [bit for bit in reversed(range(bits)) if place % (2 << bit) == 0]
+
+
+class Spread:
+    def __init__(self, lanes, full, rows, chunks, send_sems, recv_sems):
+        self.lanes, self.full, self.rows, self.chunks = lanes, full, rows, chunks
+        self.piece = rows // chunks
+        self.send_sems, self.recv_sems = send_sems, recv_sems
+
+    def view(self, place, half, chunk):
+        start = self.lanes.block(place) * (2 * self.rows) + half * self.rows + chunk * self.piece
+        return self.full.at[pl.ds(pl.multiple_of(start, self.piece), self.piece), :]
+
+    def copy(self, place, half, chunk, bit):
+        view = self.view(place, half, chunk)
+        to = place | (1 << bit)
+        return remote(
+            view,
+            view,
+            self.send_sems.at[half, to, chunk],
+            self.recv_sems.at[half, to, chunk],
+            self.lanes.across(bit),
+        )
+
+    def give(self, place, half, chunk):
+        for bit in onward(place, half, self.lanes.bits):
+            self.copy(place, half, chunk, bit).start()
+
+    def take(self, place, half, chunk):
+        view = self.view(place, half, chunk)
+        remote(
+            view,
+            view,
+            self.send_sems.at[half, place, chunk],
+            self.recv_sems.at[half, place, chunk],
+            self.lanes.across(0),
+        ).wait_recv()
+
+    def pass_on(self, chunk):
+        for half in range(2):
+            places = range(1, self.lanes.blocks)
+            if half == 1:
+                key = lambda place: [-bit for bit in reversed(range(8)) if (place >> bit) & 1]
+                places = sorted(places, key=key)
+            for place in places:
+                if onward(place, half, self.lanes.bits):
+                    self.take(place, half, chunk)
+                    self.give(place, half, chunk)
+
+    def finish(self, chunk):
+        for half in range(2):
+            for place in range(1, self.lanes.blocks):
+                if not onward(place, half, self.lanes.bits):
+                    self.take(place, half, chunk)
+        for half in range(2):
+            for place in range(self.lanes.blocks):
+                for bit in onward(place, half, self.lanes.bits):
+                    self.copy(place, half, chunk, bit).wait_send()
+
+
+def front_body(
+    blocks, chunks, in_ref, out_ref, x_ref, gain_ref,
+    full_ref, pair_ref, act_ref, xr_ref,
+    x_s, act_s, home_sems, z_send, z_recv, o_sems, o_recv, send_sems, recv_sems, x_sems, a_send,
+    a_recv,
+):
+    lanes = Lanes(blocks)
+    rows = in_ref.shape[0]
+    piece = rows // chunks
+    here = x_ref.shape[0]
+    c, t = lanes.c, lanes.t
+    lanes.greet()
+    spread = Spread(lanes, full_ref, rows, chunks, send_sems, recv_sems)
+
+    def slot(chunk):
+        start = lanes.k * (2 * rows) + c * rows + chunk * piece
+        return full_ref.at[pl.ds(pl.multiple_of(start, piece), piece), :]
+
+    def first_copy(chunk, device):
+        return remote(
+            in_ref.at[pl.ds(chunk * piece, piece), :],
+            slot(chunk),
+            z_send.at[0, chunk],
+            z_recv.at[c, chunk],
+            device,
+        )
+
+    def second_copy(chunk):
+        return remote(
+            in_ref.at[pl.ds(chunk * piece, piece), :],
+            slot(chunk),
+            z_send.at[1, chunk],
+            z_recv.at[c, chunk],
+            (lanes.other, lanes.far),
+        )
+
+    def own_copy(chunk):
+        return pltpu.make_async_copy(
+            in_ref.at[pl.ds(chunk * piece, piece), :], slot(chunk), home_sems.at[chunk]
+        )
+
+    def out_slot():
+        return pair_ref.at[pl.ds(pl.multiple_of(c * rows, rows), rows), :]
+
+    def out_first(device):
+        return remote(out_ref, out_slot(), o_sems.at[0], o_recv.at[c], device)
+
+    def out_second():
+        return remote(out_ref, out_slot(), o_sems.at[1], o_recv.at[c], (lanes.other, lanes.far))
+
+    def x_away():
+        return remote(x_ref, x_s, x_sems.at[0], x_sems.at[1], (lanes.other, lanes.far))
+
+    def x_home():
+        return pltpu.make_async_copy(x_ref, x_s, x_sems.at[2])
+
+    def send_first(chunk):
+        @pl.when(lanes.home)
+        def _():
+            own_copy(chunk).start()
+            first_copy(chunk, (lanes.d, lanes.far)).start()
+
+        @pl.when(lanes.away)
+        def _():
+            first_copy(chunk, (lanes.other, t)).start()
+            second_copy(chunk).start()
+
+    early = max(chunks // 2, 1)
+    for chunk in range(early):
+        send_first(chunk)
+
+    @pl.when(lanes.home)
+    def _():
+        x_home().start()
+
+    @pl.when(lanes.away)
+    def _():
+        x_away().start()
+
+    for chunk in range(early, chunks):
+        send_first(chunk)
+
+    @pl.when(lanes.home)
+    def _():
+        out_first((lanes.d, lanes.far)).start()
+        pltpu.make_async_copy(out_ref, out_slot(), o_sems.at[2]).start()
+
+    @pl.when(lanes.away)
+    def _():
+        out_first((lanes.other, t)).start()
+        out_second().start()
+
+    def z_view(half, chunk):
+        start = lanes.k * (2 * rows) + half * rows + chunk * piece
+        return full_ref.at[pl.ds(pl.multiple_of(start, piece), piece), :]
+
+    def came(half, chunk):
+        view = z_view(half, chunk)
+        return remote(
+            view, view, z_send.at[0, chunk], z_recv.at[half, chunk], (lanes.other, t)
+        )
+
+    def arrive(chunk):
+        @pl.when(lanes.home)
+        def _():
+            own_copy(chunk).wait()
+            start = lanes.k * (2 * rows) + (1 - c) * rows + chunk * piece
+            view = full_ref.at[pl.ds(pl.multiple_of(start, piece), piece), :]
+            remote(
+                view, view, z_send.at[0, chunk], z_recv.at[1 - c, chunk], (lanes.other, t)
+            ).wait_recv()
+
+        @pl.when(lanes.away)
+        def _():
+            for half in range(2):
+                came(half, chunk).wait_recv()
+
+        for half in range(2):
+            spread.give(0, half, chunk)
+
+    def act_slot(index):
+        return act_ref.at[pl.ds(index * here, here), :]
+
+    def act_far():
+        return remote(act_s, act_slot(2), a_send.at[0], a_recv.at[0], (lanes.d, lanes.near))
+
+    def act_core():
+        return remote(act_s, act_slot(1), a_send.at[1], a_recv.at[1], (lanes.other, t))
+
+    def act_both():
+        return remote(act_slot(2), act_slot(3), a_send.at[2], a_recv.at[2], (lanes.other, t))
+
+    def norm():
+        @pl.when(lanes.home)
+        def _():
+            x_home().wait()
+
+        @pl.when(lanes.away)
+        def _():
+            x_away().wait_recv()
+
+        @pl.loop(0, here // 32)
+        def _(step):
+            part = pl.ds(pl.multiple_of(step * 32, 32), 32)
+            x = x_s[part, :].astype(jnp.float32)
+            scale = lax.rsqrt(jnp.mean(x * x, axis=1, keepdims=True) + EPS)
+            act_s[part, :] = (x * scale * gain_ref[...]).astype(jnp.bfloat16)
+
+        act_far().start()
+        act_core().start()
+        pltpu.make_async_copy(act_s, act_slot(0), a_send.at[3]).start()
+        pltpu.make_async_copy(x_s, xr_ref, x_sems.at[3]).start()
+
+    for chunk in range(chunks):
+        arrive(chunk)
+        if chunk >= 1:
+            spread.pass_on(chunk - 1)
+        if chunk == early:
+            norm()
+    if early >= chunks:
+        norm()
+    spread.pass_on(chunks - 1)
+    act_far().wait_recv()
+    act_both().start()
+    act_core().wait_recv()
+    for chunk in range(chunks):
+        spread.finish(chunk)
+    act_both().wait_recv()
+    act_far().wait_send()
+    act_core().wait_send()
+    act_both().wait_send()
+    pltpu.make_async_copy(act_s, act_slot(0), a_send.at[3]).wait()
+    pltpu.make_async_copy(x_s, xr_ref, x_sems.at[3]).wait()
+
+    @pl.when(lanes.home)
+    def _():
+        for chunk in range(chunks):
+            first_copy(chunk, (lanes.d, lanes.far)).wait_send()
+        out_first((lanes.d, lanes.far)).wait_send()
+        pltpu.make_async_copy(out_ref, out_slot(), o_sems.at[2]).wait()
+        start = (1 - c) * rows
+        view = pair_ref.at[pl.ds(pl.multiple_of(start, rows), rows), :]
+        remote(view, view, o_sems.at[0], o_recv.at[1 - c], (lanes.other, t)).wait_recv()
+
+    @pl.when(lanes.away)
+    def _():
+        x_away().wait_send()
+        for chunk in range(chunks):
+            first_copy(chunk, (lanes.other, t)).wait_send()
+            second_copy(chunk).wait_send()
+        out_first((lanes.other, t)).wait_send()
+        out_second().wait_send()
+        for half in range(2):
+            view = pair_ref.at[pl.ds(half * rows, rows), :]
+            remote(view, view, o_sems.at[0], o_recv.at[half], (lanes.other, t)).wait_recv()
+
+
+def front(in_pack, out_pack, layer_in, gain, at):
+    bf16 = jnp.bfloat16
+    rows = in_pack.shape[0]
+    blocks = at.blocks
+    chunks = 4 if rows >= 256 else 1
+    dma = pltpu.SemaphoreType.DMA
+    anywhere = pl.BlockSpec(memory_space=pl.ANY)
+    here, features = layer_in.shape
+    total = 2 * blocks * rows
+    return pl.pallas_call(
+        functools.partial(front_body, blocks, chunks),
+        in_specs=[anywhere, anywhere, anywhere, pl.BlockSpec(memory_space=pltpu.VMEM)],
+        out_specs=[anywhere] * 4,
+        out_shape=[
+            jax.ShapeDtypeStruct((total, in_pack.shape[1]), bf16),
+            jax.ShapeDtypeStruct((2 * rows, out_pack.shape[1]), bf16),
+            jax.ShapeDtypeStruct((4 * here, features), bf16),
+            jax.ShapeDtypeStruct((here, features), bf16),
+        ],
+        scratch_shapes=[
+            pltpu.VMEM((here, features), bf16),
+            pltpu.VMEM((here, features), bf16),
+            dma((chunks,)),
+            dma((2, chunks)),
+            dma((2, chunks)),
+            dma((3,)),
+            dma((2,)),
+            dma((2, blocks, chunks)),
+            dma((2, blocks, chunks)),
+            dma((4,)),
+            dma((4,)),
+            dma((3,)),
+        ],
+        compiler_params=pltpu.CompilerParams(
+            collective_id=1, has_side_effects=True, vmem_limit_bytes=16 * 1024 * 1024
+        ),
+        cost_estimate=pl.CostEstimate(
+            flops=here * features * 8, bytes_accessed=300_000_000, transcendentals=0
+        ),
+    )(in_pack, out_pack, layer_in, gain.reshape(1, -1))
+
+
+def after(values, *others):
+    return lax.optimization_barrier((values,) + others)[0]
 
 
 def share_rows(values, at):
@@ -711,60 +1056,47 @@
     return own + from_core.astype(jnp.float32) + from_far.astype(jnp.float32)
 
 
-def spread(piece, at, upward):
-    found = {0: piece}
-    order = range(at.bits) if upward else reversed(range(at.bits))
-    for bit in order:
-        for place in sorted(found):
-            found[place | (1 << bit)] = at.over_bit(found[place], bit)
-    return found
-
-
-def gather_weight(shard, at):
+def groups(at):
+    return [[d for d in range(at.dp) if d % 2 == c] for c in range(2)]
+
+
+def gather_blocks(block, at):
+    return lax.all_gather(block, "dp", axis=0, tiled=True, axis_index_groups=groups(at))
+
+
+def sum_blocks(values, at):
+    return lax.psum_scatter(
+        values, "dp", scatter_dimension=0, tiled=True, axis_index_groups=groups(at)
+    )
+
+
+def pair_up(own, other, at):
+    first = at.c == 0
+    return jnp.concatenate([jnp.where(first, own, other), jnp.where(first, other, own)], axis=0)
+
+
+def pair_weight(shard, at):
     first_in = at.column_out(shard)
     second_in = at.swap_away(shard)
     own = jnp.where(at.home, shard, first_in)
     other = jnp.where(at.home, first_in, second_in)
-    low = jnp.where(at.c == 0, own, other)
-    high = jnp.where(at.c == 0, other, own)
-    lows = spread(low, at, True)
-    highs = spread(high, at, False)
-    return jnp.concatenate(
-        [part for place in range(at.blocks) for part in (lows[place], highs[place])], axis=0
-    )
-
-
-def collect(piece_of, at, half):
-    bf16 = jnp.bfloat16
-    bits = list(range(at.bits))
-    order = list(reversed(bits)) if half == 0 else bits
-    arrived = {}
-    places = list(range(at.blocks))
-
-    def total(place):
-        value = piece_of(place, half)
-        for part in arrived.get(place, []):
-            value = value + part.astype(jnp.float32)
-        return value
-
-    for bit in order:
-        going = [place for place in places if (place >> bit) & 1]
-        places = [place for place in places if not (place >> bit) & 1]
-        for place in going:
-            part = at.over_bit(total(place).astype(bf16), bit)
-            arrived.setdefault(place ^ (1 << bit), []).append(part)
-    return total(0)
-
-
-def scatter_weight(piece_of, at):
-    bf16 = jnp.bfloat16
-    low = collect(piece_of, at, 0)
-    high = collect(piece_of, at, 1)
+    return pair_up(own, other, at)
+
+
+def gather_weight(shard, at):
+    return gather_blocks(pair_weight(shard, at), at)
+
+
+def scatter_weight(grad, at):
+    f32 = jnp.float32
+    mine = sum_blocks(grad, at)
+    rows = mine.shape[0] // 2
+    low, high = mine[:rows], mine[rows:]
     own = jnp.where(at.c == 0, low, high)
     other = jnp.where(at.c == 0, high, low)
-    first_in = at.column_back(jnp.where(at.home, other, own).astype(bf16)).astype(jnp.float32)
-    second_in = at.swap_away(other.astype(bf16)).astype(jnp.float32)
-    return first_in + jnp.where(at.home, own, second_in)
+    first_in = at.column_back(jnp.where(at.home, other, own)).astype(f32)
+    second_in = at.swap_away(other).astype(f32)
+    return first_in + jnp.where(at.home, own.astype(f32), second_in)
 
 
 def gather_shared(shard, at):
@@ -780,17 +1112,12 @@
     far = at.over_far(two)
     lower = at.t // 2 == 0
     four = jnp.stack([jnp.where(lower, two, far), jnp.where(lower, far, two)], axis=1)
-    line = four.reshape(2, rows * at.tp, half)
-    lows = spread(line[0], at, True)
-    highs = spread(line[1], at, False)
-    part = jnp.concatenate(
-        [piece for place in range(at.blocks) for piece in (lows[place], highs[place])], axis=0
-    )
+    part = gather_blocks(four.reshape(2 * rows * at.tp, half), at)
     other = at.over_core(part)
     return jnp.where(at.c == 0, part, other), jnp.where(at.c == 0, other, part)
 
 
-def scatter_shared(grad_bc, grad_kv, at):
+def scatter_shared(grad_bc, grad_kv, earlier, at):
     f32, bf16 = jnp.float32, jnp.bfloat16
     first = at.c == 0
     bc_width = grad_bc.shape[1]
@@ -802,12 +1129,9 @@
         [came[:, :HD], grad_kv[:, :HD], came[:, HD : 2 * HD], grad_kv[:, HD:]], axis=1
     )
     total = jnp.where(first, grad_bc + came, kept)
-    rows = total.shape[0] // (2 * at.blocks)
-    parts = total.reshape(at.blocks, 2, rows, total.shape[1])
-    low = collect(lambda place, half: parts[place, half], at, 0)
-    high = collect(lambda place, half: parts[place, half], at, 1)
-    piece = rows // at.tp
-    line = jnp.stack([low, high]).reshape(2, 2, 2, piece, total.shape[1])
+    mine = sum_blocks(after(total.astype(bf16), earlier), at)
+    piece = mine.shape[0] // (2 * at.tp)
+    line = mine.astype(f32).reshape(2, 2, 2, piece, total.shape[1])
     lower = at.t // 2 == 0
     went = at.over_far(jnp.where(lower, line[:, 1], line[:, 0]).astype(bf16)).astype(f32)
     line = jnp.where(lower, line[:, 0], line[:, 1]) + went
@@ -819,11 +1143,15 @@
     return jnp.concatenate([jnp.where(first, mine, came), jnp.where(first, came, mine)], axis=1)
 
 
-def sum_everywhere(values, at):
+def sum_tensor(values, at):
+    for bit in range(at.tp.bit_length() - 1):
+        values = values + at.send(values, lambda d, t: (d, t ^ (1 << bit)))
+    return values
+
+
+def sum_data(values, at):
     for bit in range(at.dp.bit_length() - 1):
         values = values + at.send(values, lambda d, t: (d ^ (1 << bit), t))
-    for bit in range(at.tp.bit_length() - 1):
-        values = values + at.send(values, lambda d, t: (d, t ^ (1 << bit)))
     return values
 
 
@@ -853,7 +1181,7 @@
     contract_last = (((1,), (1,)), ((), ()))
     contract_first = (((0,), (0,)), ((), ()))
     at = Places()
-    rows_here, features = layer_in.shape
+    rows_here = layer_in.shape[0]
     slot_len = rows_here * at.tp
     local_heads = step_bias.shape[0]
     width = inner_gain.shape[0]
@@ -863,10 +1191,6 @@
     bc_width = conv_shared.shape[1]
     w_rows = step_weight.shape[0]
 
-    inputs = turn_features(relocate(layer_in, at), at, 1).astype(f32)
-    target = turn_features(relocate(teacher, at), at, 1).astype(f32)
-    gain_in = turn_features(input_gain, at, 0)
-    gain_mid = turn_features(middle_gain, at, 0)
     column_params = jnp.concatenate(
         [conv_inner.reshape(-1), inner_gain, step_bias, decay_log, skip_gain]
     )
@@ -895,7 +1219,8 @@
     quarters = jnp.arange(at.tp, dtype=jnp.int32)
     order = (at.c ^ (quarters // 2)) + 2 * (at.zq ^ (quarters % 2))
 
-    left, right = gather_shared(shared_weight, at)
+    shared_full = lax.all_gather(shared_weight, ("dp", "tensor"), axis=0, tiled=True)
+    left, right = shared_full[:, :bc_width], shared_full[:, bc_width:]
     kv_index = at.column * (query_width // HD) // (QH // KVH)
     second = kv_index == 1
     shared_all = jnp.concatenate(
@@ -915,18 +1240,24 @@
         ],
         axis=1,
     )
-    in_all = gather_weight(in_pack, at)
-    out_all = gather_weight(jnp.concatenate([mixer_out_weight, attn_out_weight], axis=1), at)
-    gate_up_all = gather_weight(gate_up_weight.reshape(w_rows, 2 * hidden_width), at)
-    down_all = gather_weight(down_weight, at)
+    out_pack = jnp.concatenate([mixer_out_weight, attn_out_weight], axis=1)
+    in_all, out_pair, act_all, inputs = front(in_pack, out_pack, layer_in, input_gain, at)
+    inputs = inputs.astype(f32)
 
     def row_split(values):
         return [values[i * rows_here : (i + 1) * rows_here] for i in range(at.tp)]
 
-    normed_in, norm_in_back = jax.vjp(rms_norm, inputs, gain_in)
-    act_all = jnp.concatenate(share_rows(normed_in.astype(bf16), at), axis=0)
+    _, norm_in_back = jax.vjp(rms_norm, inputs, input_gain)
+    out_all = gather_blocks(out_pair, at)
+    rest = jnp.concatenate(
+        [gate_up_weight.reshape(w_rows, 2 * hidden_width), down_weight], axis=1
+    )
+    rest = pair_weight(after(rest, act_all), at)
+    gate_up_all = gather_blocks(rest[:, : 2 * hidden_width], at)
+    down_all = gather_blocks(rest[:, 2 * hidden_width :], at)
     proj_shared = jnp.dot(act_all, shared_all, preferred_element_type=f32)
     proj = jnp.dot(act_all, in_all, preferred_element_type=f32)
+    target = relocate(after(teacher, proj), at).astype(f32)
     attn_low = attn_forward(order, proj, proj_shared, cosine, sine, query_width, width, bc_width)
     heads_all, y, states = mixer_forward(
         order, proj, proj_shared, attn_low, lane_params, conv_shared, head_params
@@ -936,7 +1267,7 @@
         for piece in row_split(heads_all)
     ]
     resid = inputs + sum_rows(mix_parts, at)
-    normed_mid, norm_mid_back = jax.vjp(rms_norm, resid, gain_mid)
+    normed_mid, norm_mid_back = jax.vjp(rms_norm, resid, middle_gain)
     mid_all = jnp.concatenate(share_rows(normed_mid.astype(bf16), at), axis=0)
     gate_up = jnp.dot(mid_all, gate_up_all, preferred_element_type=f32)
     gate_val = gate_up[:, :hidden_width]
@@ -953,24 +1284,12 @@
     live = (positions < seq_len).astype(f32)
     error = (outputs - target) * live[:, None]
     err_local = 0.5 * jnp.sum(error * error)
-    layer_out = relocate(turn_features(outputs.astype(bf16), at, 1), at)
 
     grad_all = jnp.concatenate(share_rows(error.astype(bf16), at), axis=0)
-    block = features // (2 * at.blocks)
-
-    def columns_of(values, place, half):
-        start = (2 * place + half) * block
-        return values[:, start : start + block]
-
     def weight_grad(left, right):
-        def piece_of(place, half):
-            return lax.dot_general(
-                columns_of(left, place, half), right, contract_first, preferred_element_type=f32
-            )
-
-        return scatter_weight(piece_of, at)
-
-    grad_down = weight_grad(grad_all, hidden)
+        return lax.dot_general(left, right, contract_first, preferred_element_type=f32).astype(bf16)
+
+    part_down = weight_grad(grad_all, hidden)
     grad_hidden = jnp.dot(grad_all, down_all, preferred_element_type=f32)
     grad_gate = grad_hidden * up_val * sigmoid_gate * (1.0 + gate_val * (1.0 - sigmoid_gate))
     grad_up = grad_hidden * gate_val * sigmoid_gate
@@ -979,13 +1298,20 @@
         lax.dot_general(piece, gate_up_all, contract_last, preferred_element_type=f32)
         for piece in row_split(grad_gu)
     ]
-    grad_gate_up = weight_grad(mid_all, grad_gu)
+    part_gate_up = weight_grad(mid_all, grad_gu)
     grad_mid = sum_rows(grad_mid_parts, at)
+    grad_mid, part_down, part_gate_up = lax.optimization_barrier((grad_mid, part_down, part_gate_up))
+    grad_down = scatter_weight(part_down, at)
+    grad_gate_up = scatter_weight(part_gate_up, at)
     grad_resid_norm, grad_middle_gain = norm_mid_back(grad_mid)
     grad_resid = error + grad_resid_norm
     mix_grad_all = jnp.concatenate(share_rows(grad_resid.astype(bf16), at), axis=0)
     grad_heads = jnp.dot(mix_grad_all, out_all, preferred_element_type=f32)
-    grad_out = weight_grad(mix_grad_all, heads_all)
+    part_out = weight_grad(mix_grad_all, heads_all)
+    grad_heads, part_out = lax.optimization_barrier((grad_heads, part_out))
+    layer_out = relocate(after(outputs.astype(bf16), grad_heads), at)
+    part_out = after(part_out, grad_down)
+    grad_out = scatter_weight(part_out, at)
     dq, dkv = attn_backward(
         order, proj, proj_shared, cosine, sine, grad_heads, query_width, width, bc_width
     )
@@ -999,8 +1325,12 @@
     grad_kv = lax.dot_general(
         act_all, low_shared[:, bc_width:], contract_first, preferred_element_type=f32
     )
-    grad_shared_weight = scatter_shared(grad_bc, grad_kv, at)
-    grad_in = weight_grad(act_all, low_pack)
+    part_in = weight_grad(act_all, low_pack)
+    low_pack, low_shared, part_in, grad_bc, grad_kv = lax.optimization_barrier(
+        (low_pack, low_shared, part_in, grad_bc, grad_kv)
+    )
+    grad_in = scatter_weight(after(part_in, grad_gate_up), at)
+    grad_shared_weight = scatter_shared(grad_bc, grad_kv, grad_out, at)
     grad_act_parts = [
         lax.dot_general(a, in_all, contract_last, preferred_element_type=f32)
         + lax.dot_general(b, shared_all, contract_last, preferred_element_type=f32)
@@ -1009,7 +1339,6 @@
     grad_act = sum_rows(grad_act_parts, at)
     grad_input_norm, grad_input_gain = norm_in_back(grad_act)
     input_grad = grad_resid + grad_input_norm
-    input_grad = relocate(turn_features(input_grad, at, 1), at)
 
     column = at.column
     convx_full = lax.dynamic_update_slice(
@@ -1025,15 +1354,17 @@
         convx_full,
         dconv[:KC],
         heads_full,
-        turn_features(grad_input_gain, at, 0),
-        turn_features(grad_middle_gain, at, 0),
+        grad_input_gain,
+        grad_middle_gain,
         err_local,
     )
     flat = jnp.concatenate([part.reshape(-1) for part in small])
     length = flat.shape[0]
     padded = -(-length // 1024) * 1024
     flat = jnp.pad(flat, (0, padded - length)).reshape(-1, 128)
-    flat = sum_everywhere(flat, at).reshape(-1)
+    flat = sum_tensor(flat, at)
+    input_grad = relocate(after(input_grad.astype(bf16), flat), at).astype(f32)
+    flat = sum_data(flat, at).reshape(-1)
     sums = []
     start = 0
     for part in small:

time: 1130 us -> 1000 us (0.88)
  Pallas kernels: 69.3 us -> 194 us
  waiting for transfers between devices: 527 us -> 414 us
  starting transfers between devices: 189 us -> 76.1 us
  matrix products: 207 us -> 184 us
  between operations: 6.34 us -> 18.5 us
    ppermute x118 -> x44, waiting for transfers between devices: 527 us -> 365 us  [send(): return lax.ppermute(values, ('dp', 'tensor'), self.pairs(where_to))]
    pallas_call x0 -> x1, Pallas kernels: none -> 125 us  [front(): pl.pallas_call(functools.partial(front_body, blocks, chunks), in_specs=[a...]
    ppermute x118 -> x44, starting transfers between devices: 189 us -> 75.7 us  [send(): return lax.ppermute(values, ('dp', 'tensor'), self.pairs(where_to))]
    reduce_scatter x0 -> x5, waiting for transfers between devices: none -> 45.7 us  [sum_blocks(): lax.psum_scatter(values, 'dp', scatter_dimension=0, tiled=True, axis_inde...]
    dot_general x32 -> x4, matrix products: 61.3 us -> 42.3 us  [weight_grad(): lax.dot_general(left, right, contract_first, preferred_element_type=f32)]
    convert_element_type x2 -> x5, other arithmetic: 1.43 us -> 14.7 us  [the longest x2 6.9 us: per_device(): input_grad = relocate(after(input_grad.astype(bf16), flat), at).astype(f32)]
    unnamed x244 -> x164, local copies, waits for them, and re-layouts: 25.7 us -> 21 us
  transfers between devices with their start and end apart: 118 -> 53, of which waited for: 48 -> 26; matrix products, arithmetic and copies ran while one was open for 17% -> 24% of each run, Pallas kernels for 2% -> 19%
where the time goes in v2:
time: 1000 us; the launch traced here: 996 us
  waiting for transfers between devices  414 us (41%)
  Pallas kernels  194 us (19%)
  matrix products  184 us (18%)
  starting transfers between devices  76.1 us (8%)
  other arithmetic  68.9 us (7%)
  local copies, waits for them, and re-layouts  40.9 us (4%)
  between operations  18.5 us (2%)
    ppermute x44, waiting for transfers between devices, send(): return lax.ppermute(values, ('dp', 'tensor'), self.pairs(where_to))  365 us
    pallas_call x1, Pallas kernels, front(): pl.pallas_call(functools.partial(front_body, blocks, chunks), in_specs=[a...  125 us
    ppermute x44, starting transfers between devices, send(): return lax.ppermute(values, ('dp', 'tensor'), self.pairs(where_to))  75.7 us
    reduce_scatter x5, waiting for transfers between devices, sum_blocks(): lax.psum_scatter(values, 'dp', scatter_dimension=0, tiled=True, axis_inde...  45.7 us
    dot_general x4, matrix products, weight_grad(): lax.dot_general(left, right, contract_first, preferred_element_type=f32)  42.3 us
    pallas_call x1, Pallas kernels, mixer_backward(): pl.pallas_call(mixer_bwd_body, grid_spec=pltpu.PrefetchScalarGridSpec(num...  33.7 us
    dot_general x4, matrix products, per_device(): lax.dot_general(piece, gate_up_all, contract_last, preferred_element_type...  22.9 us
    dot_general x4, matrix products, per_device(): lax.dot_general(a, in_all, contract_last, preferred_element_type=f32)  22 us
  transfers between devices with their start and end apart: 53, of which 26 were waited for; matrix products, arithmetic and copies ran while one was open for 24% of the time, Pallas kernels for 19%

profile of v2, /device:TPU:1, one launch (start us, length us, event | category | flops | bytes accessed | tf_op | source)
XLA Modules:
  0.0 996.2 jit_solution(14029554549164842226)
XLA Ops:
  11.3 124.5 %shard_map.330 = (bf16[2048,1920]{1,0:T(8,128)(2,1)S(1)}, bf16[512,1024]{1,0:T(8,128)(2,1)S(1)}, bf16[1024,2048]{1,0:T(8,128)(2,1)S(1)}, bf16[256,2048]{1,0:T(8,128)(2,1)S(1)}) custom-call(bf16[256,1920]{1,0:T(8,128)(2,1)S(1)} %concatenate.54.in_ref, bf16[256,1024]{1,0:T(8,128)(2,1)S(1)} %pad_maximum_fusion.14.out_ref, bf16[256,2048]{1,0:T(8,128)(2,1)S(1)} %copy-done.2, ...), custom_call_target="tpu_custom_call" | custom-call | flops 4194304 | bytes 300000000 | tf_op jit(solution)/shard_map/pallas_call | solution.py:1005
  149.1 65.6 %collective-permute-done.7 = bf16[256,3072]{1,0:T(8,128)(2,1)} collective-permute-done((bf16[256,3072]{1,0:T(8,128)(2,1)S(1)}, bf16[256,3072]{1,0:T(8,128)(2,1)}, u32[]{:S(2)}, u32[]{:S(2)}) %collective-permute-start.7) | collective-permute-done | bytes 1572896 | tf_op jit(solution)/shard_map/ppermute | solution.py:641
  225.1 13.3 %fusion.95.q_ref.gate_ref.inner_ref.step_ref.before_ref = f32[1024,1920]{1,0:T(8,128)} fusion(bf16[1024,2048]{1,0:T(8,128)(2,1)S(1)} %copy-done.7, bf16[2048,1920]{1,0:T(8,128)(2,1)} %copy-done.5), kind=kOutput, calls=%fused_computation.212 | convolution fusion | flops 8053063680 | bytes 19922944 | tf_op jit(solution)/shard_map/dot_general | solution.py:1259
  257.8 15.5 %shard_map.332 = (bf16[1024,1024]{1,0:T(8,128)(2,1)}, f32[1024,768]{1,0:T(8,128)}, bf16[8,256,768]{2,1,0:T(8,128)(2,1)}) custom-call(s32[4]{0:T(128)} %fusion.72.order, f32[1024,1920]{1,0:T(8,128)} %fusion.95.q_ref.gate_ref.inner_ref.step_ref.before_ref, f32[1024,1920]{1,0:T(8,128)} %fusion.95.q_ref.gate_ref.inner_ref.step_ref.before_ref, ...), custom_call_target="tpu_custom_call" | custom-call | flops 3221225472 | bytes 15728640 | tf_op jit(solution)/shard_map/pallas_call | solution.py:480
  293.8 18.7 %collective-permute-done.3 = bf16[256,2048]{1,0:T(8,128)(2,1)} collective-permute-done((bf16[256,2048]{1,0:T(8,128)(2,1)}, bf16[256,2048]{1,0:T(8,128)(2,1)}, u32[]{:S(2)}, u32[]{:S(2)}) %collective-permute-start.3) | collective-permute-done | bytes 1048608 | tf_op jit(solution)/shard_map/ppermute | solution.py:641
  318.4 21.1 %collective-permute-done.5 = bf16[256,2048]{1,0:T(8,128)(2,1)S(1)} collective-permute-done((bf16[256,2048]{1,0:T(8,128)(2,1)S(1)}, bf16[256,2048]{1,0:T(8,128)(2,1)S(1)}, u32[]{:S(2)}, u32[]{:S(2)}) %collective-permute-start.5) | collective-permute-done | bytes 1048608 | tf_op jit(solution)/shard_map/ppermute | solution.py:641
  343.8 12.6 %fusion.35 = f32[1024,2048]{1,0:T(8,128)S(1)} fusion(bf16[2048,2048]{1,0:T(8,128)(2,1)} %all-gather.9.cloned.1.call-done, bf16[256,2048]{1,0:T(8,128)(2,1)} %collective-permute-done.6, bf16[256,2048]{1,0:T(8,128)(2,1)} %copy-done.56, bf16[256,2048]{1,0:T(8,128)(2,1)} %copy-done.58, bf16[256,2048]{1,0:T(8,128)(2,1)S(1)} %multiply_convert_fusion.3), kind=kOutput, calls=%fused_computation.104 | convolution fusion | flops 8606711808 | bytes 20971520 | tf_op jit(solution)/shard_map/dot_general | solution.py:1272
  386.5 11.3 %collective-permute-done.12 = bf16[256,2048]{1,0:T(8,128)(2,1)} collective-permute-done((bf16[256,2048]{1,0:T(8,128)(2,1)S(1)}, bf16[256,2048]{1,0:T(8,128)(2,1)}, u32[]{:S(2)}, u32[]{:S(2)}) %collective-permute-start.12) | collective-permute-done | bytes 1048608 | tf_op jit(solution)/shard_map/ppermute | solution.py:641
  397.8 17.4 %collective-permute-done.11 = bf16[256,2048]{1,0:T(8,128)(2,1)} collective-permute-done((bf16[256,2048]{1,0:T(8,128)(2,1)}, bf16[256,2048]{1,0:T(8,128)(2,1)}, u32[]{:S(2)}, u32[]{:S(2)}) %collective-permute-start.11) | collective-permute-done | bytes 1048608 | tf_op jit(solution)/shard_map/ppermute | solution.py:641
  422.2 23.0 %collective-permute-done.14 = bf16[256,2048]{1,0:T(8,128)(2,1)S(1)} collective-permute-done((bf16[256,2048]{1,0:T(8,128)(2,1)S(1)}, bf16[256,2048]{1,0:T(8,128)(2,1)S(1)}, u32[]{:S(2)}, u32[]{:S(2)}) %collective-permute-start.14) | collective-permute-done | bytes 1048608 | tf_op jit(solution)/shard_map/ppermute | solution.py:641
  449.3 11.5 %multiply_convert_fusion = (bf16[1024,1024]{1,0:T(8,128)(2,1)}, bf16[1024,1024]{1,0:T(8,128)(2,1)}) fusion(f32[1024,2048]{1,0:T(8,128)S(1)} %bitcast.77, bf16[2048,1024]{1,0:T(8,128)(2,1)} %all-gather.11.cloned.1.call-done, bf16[256,2048]{1,0:T(8,128)(2,1)} %collective-permute-done.15, bf16[256,2048]{1,0:T(8,128)(2,1)S(1)} %collective-permute-done.14, ...), kind=kOutput, calls=%fused_computation.17 | convolution fusion | flops 4325376000 | bytes 20971520 | tf_op jit(solution)/shard_map/dot_general | solution.py:1293
  469.7 13.8 %convolution_convert_fusion.1 = bf16[2048,2048]{1,0:T(8,128)(2,1)} fusion(bf16[1024,1024]{1,0:T(8,128)(2,1)} %get-tuple-element.118, bf16[1024,1024]{1,0:T(8,128)(2,1)} %get-tuple-element.119, bf16[256,2048]{1,0:T(8,128)(2,1)} %collective-permute-done.6, bf16[256,2048]{1,0:T(8,128)(2,1)S(1)} %copy-done.57, bf16[256,2048]{1,0:T(8,128)(2,1)S(1)} %copy-done.59, ...), kind=kOutput, calls=%fused_computation.1 | convolution fusion | flops 8619294720 | bytes 16777216 | tf_op jit(solution)/shard_map/dot_general | solution.py:1290
  526.1 22.1 %collective-permute-done.20 = bf16[256,2048]{1,0:T(8,128)(2,1)S(1)} collective-permute-done((bf16[256,2048]{1,0:T(8,128)(2,1)S(1)}, bf16[256,2048]{1,0:T(8,128)(2,1)S(1)}, u32[]{:S(2)}, u32[]{:S(2)}) %collective-permute-start.20) | collective-permute-done | bytes 1048608 | tf_op jit(solution)/shard_map/ppermute | solution.py:641
  562.8 9.6 reduce-scatter.10.cloned.1.call-done
  588.4 12.3 %collective-permute-done.38 = bf16[256,1024]{1,0:T(8,128)(2,1)S(1)} collective-permute-done((bf16[256,1024]{1,0:T(8,128)(2,1)S(1)}, bf16[256,1024]{1,0:T(8,128)(2,1)S(1)}, u32[]{:S(2)}, u32[]{:S(2)}) %collective-permute-start.38) | collective-permute-done | bytes 524320 | tf_op jit(solution)/shard_map/ppermute | solution.py:641
  604.3 12.0 %shard_map.333 = (bf16[1024,256]{1,0:T(8,128)(2,1)}, bf16[1024,256]{1,0:T(8,128)(2,1)}) custom-call(s32[4]{0:T(128)} %fusion.72.order, f32[1024,1920]{1,0:T(8,128)} %fusion.95.q_ref.gate_ref.inner_ref.step_ref.before_ref, f32[1024,768]{1,0:T(8,128)} %fusion.88.kv_ref.bc_ref.bcbefore_ref, f32[1024,128]{1,0:T(8,128)} %get-tuple-element.146.cos_ref.all_cos, ...), custom_call_target="tpu_custom_call" | custom-call | flops 2147483648 | bytes 5242880 | tf_op jit(solution)/shard_map/pallas_call | solution.py:442
  616.3 33.7 %shard_map.334 = (bf16[1024,1920]{1,0:T(8,128)(2,1)}, bf16[1024,768]{1,0:T(8,128)(2,1)}, f32[8,768]{1,0:T(8,128)}, f32[8,512]{1,0:T(8,128)}, f32[8,128]{1,0:T(8,128)}) custom-call(s32[4]{0:T(128)} %fusion.72.order, f32[1024,1920]{1,0:T(8,128)} %fusion.95.q_ref.gate_ref.inner_ref.step_ref.before_ref, ...), custom_call_target="tpu_custom_call" | custom-call | flops 8053063680 | bytes 31457280 | tf_op jit(solution)/shard_map/pallas_call | solution.py:549
  657.1 11.3 %convolution_convert_fusion = bf16[2048,1920]{1,0:T(8,128)(2,1)} fusion(bf16[1024,2048]{1,0:T(8,128)(2,1)S(1)} %copy-done.9, bf16[1024,1920]{1,0:T(8,128)(2,1)S(1)} %copy-done.52), kind=kOutput, calls=%fused_computation | convolution fusion | flops 8056995840 | bytes 15990784 | tf_op jit(solution)/shard_map/dot_general | solution.py:1290
  688.2 16.3 %collective-permute-done.40 = bf16[256,1024]{1,0:T(8,128)(2,1)} collective-permute-done((bf16[256,1024]{1,0:T(8,128)(2,1)}, bf16[256,1024]{1,0:T(8,128)(2,1)}, u32[]{:S(2)}, u32[]{:S(2)}) %collective-permute-start.40) | collective-permute-done | bytes 524320 | tf_op jit(solution)/shard_map/ppermute | solution.py:641
  707.1 36.0 %reduce-scatter.6.cloned.1.call-done = bf16[512,2048]{1,0:T(8,128)(2,1)} async-done(((bf16[2048,2048]{1,0:T(8,128)(2,1)}), bf16[512,2048]{1,0:T(8,128)(2,1)}) %reduce-scatter.6.cloned.1.call-update) | async-done | bytes 2097168 | tf_op jit(solution)/shard_map/reduce_scatter | solution.py:1068
  758.9 35.5 %collective-permute-done.33 = bf16[256,2048]{1,0:T(8,128)(2,1)S(1)} collective-permute-done((bf16[256,2048]{1,0:T(8,128)(2,1)S(1)}, bf16[256,2048]{1,0:T(8,128)(2,1)S(1)}, u32[]{:S(2)}, u32[]{:S(2)}) %collective-permute-start.33) | collective-permute-done | bytes 1048608 | tf_op jit(solution)/shard_map/ppermute | solution.py:641
  833.2 25.5 %collective-permute-done.25 = bf16[256,2048]{1,0:T(8,128)(2,1)} collective-permute-done((bf16[256,2048]{1,0:T(8,128)(2,1)}, bf16[256,2048]{1,0:T(8,128)(2,1)}, u32[]{:S(2)}, u32[]{:S(2)}) %collective-permute-start.25) | collective-permute-done | bytes 1048608 | tf_op jit(solution)/shard_map/ppermute | solution.py:641
  892.4 24.3 %collective-permute-done.41 = bf16[2,2,64,512]{3,2,0,1:T(8,128)(2,1)S(1)} collective-permute-done((bf16[2,2,64,512]{3,2,0,1:T(8,128)(2,1)S(1)}, bf16[2,2,64,512]{3,2,0,1:T(8,128)(2,1)S(1)}, u32[]{:S(2)}, u32[]{:S(2)}) %collective-permute-start.41) | collective-permute-done | bytes 262176 | tf_op jit(solution)/shard_map/ppermute | solution.py:641
  948.2 33.8 %collective-permute-done.35 = bf16[256,1920]{1,0:T(8,128)(2,1)} collective-permute-done((bf16[256,1920]{1,0:T(8,128)(2,1)}, bf16[256,1920]{1,0:T(8,128)(2,1)}, u32[]{:S(2)}, u32[]{:S(2)}) %collective-permute-start.35) | collective-permute-done | bytes 983072 | tf_op jit(solution)/shard_map/ppermute | solution.py:641
  (397 shorter events, 357.0 us)
Async XLA Ops:
  7.2 233.2 %all-gather.5.cloned.1.call-start = ((), (), s32[]{:S(2)}) async-start(), calls=%async_computation.5 | async-start | bytes 4325376 | tf_op jit(solution)/shard_map/all_gather | solution.py:1222
  8.0 265.3 %all-gather.7.cloned.1.call-start = ((), (), s32[]{:S(2)}) async-start(), calls=%async_computation.6 | async-start | bytes 5242880 | tf_op jit(solution)/shard_map/all_gather | solution.py:1064
  142.0 201.8 %all-gather.9.cloned.1.call-start = ((), (), s32[]{:S(2)}) async-start(), calls=%async_computation.7 | async-start | bytes 10485760 | tf_op jit(solution)/shard_map/all_gather | solution.py:1064
  145.0 69.7 %collective-permute-start.7 = (bf16[256,3072]{1,0:T(8,128)(2,1)S(1)}, bf16[256,3072]{1,0:T(8,128)(2,1)}, u32[]{:S(2)}, u32[]{:S(2)}) collective-permute-start(bf16[256,3072]{1,0:T(8,128)(2,1)S(1)} %pad_maximum_fusion.6), channel_id=1, source_target_pairs={{0,2},{1,3},{2,6},{3,7},{4,0},{5,1},{6,4},{7,5},{8,10},{9,11},{10,... | collective-permute-start | bytes 4718600 | tf_op jit(solution)/shard_map/ppermute | solution.py:641
  145.1 69.7 %collective-permute-start.8 = (bf16[256,3072]{1,0:T(8,128)(2,1)S(1)}, bf16[256,3072]{1,0:T(8,128)(2,1)}, u32[]{:S(2)}, u32[]{:S(2)}) collective-permute-start(bf16[256,3072]{1,0:T(8,128)(2,1)S(1)} %pad_maximum_fusion.6), channel_id=1, source_target_pairs={{2,4},{3,5},{4,2},{5,3},{10,12},{11,13},{12,10},{13,11},{18,20},{1... | collective-permute-start | bytes 4718600 | tf_op jit(solution)/shard_map/ppermute | solution.py:641
  219.7 145.0 %all-gather.11.cloned.1.call-start = ((), (), s32[]{:S(2)}) async-start(), calls=%async_computation.8 | async-start | bytes 5242880 | tf_op jit(solution)/shard_map/all_gather | solution.py:1064
  282.2 30.3 %collective-permute-start.3 = (bf16[256,2048]{1,0:T(8,128)(2,1)}, bf16[256,2048]{1,0:T(8,128)(2,1)}, u32[]{:S(2)}, u32[]{:S(2)}) collective-permute-start(bf16[256,2048]{1,0:T(8,128)(2,1)} %add_convert_fusion.3), channel_id=1, source_target_pairs={{0,1},{1,0},{2,3},{3,2},{4,5},{5,4},{6,7},{7,6},{8,9},{9,8},{10,11... | collective-permute-start | bytes 3145736 | tf_op jit(solution)/shard_map/ppermute | solution.py:641
  290.1 282.3 %reduce-scatter.10.cloned.1.call-start = ((), (), s32[]{:S(2)}) async-start(), calls=%async_computation.11 | async-start | bytes 5242880 | tf_op jit(solution)/shard_map/reduce_scatter | solution.py:1068
  369.2 28.6 %collective-permute-start.12 = (bf16[256,2048]{1,0:T(8,128)(2,1)S(1)}, bf16[256,2048]{1,0:T(8,128)(2,1)}, u32[]{:S(2)}, u32[]{:S(2)}) collective-permute-start(bf16[256,2048]{1,0:T(8,128)(2,1)S(1)} %copy-done.28), channel_id=1, source_target_pairs={{2,4},{3,5},{4,2},{5,3},{10,12},{11,13},{12,10},{13,11},{18,20},{1... | collective-permute-start | bytes 3145736 | tf_op jit(solution)/shard_map/ppermute | solution.py:641
  380.2 35.0 %collective-permute-start.11 = (bf16[256,2048]{1,0:T(8,128)(2,1)}, bf16[256,2048]{1,0:T(8,128)(2,1)}, u32[]{:S(2)}, u32[]{:S(2)}) collective-permute-start(bf16[256,2048]{1,0:T(8,128)(2,1)} %add_convert_fusion.2), channel_id=1, source_target_pairs={{0,1},{1,0},{2,3},{3,2},{4,5},{5,4},{6,7},{7,6},{8,9},{9,8},{10,11... | collective-permute-start | bytes 3145736 | tf_op jit(solution)/shard_map/ppermute | solution.py:641
  421.3 25.6 %collective-permute-start.13 = (bf16[256,2048]{1,0:T(8,128)(2,1)S(1)}, bf16[256,2048]{1,0:T(8,128)(2,1)S(1)}, u32[]{:S(2)}, u32[]{:S(2)}) collective-permute-start(bf16[256,2048]{1,0:T(8,128)(2,1)S(1)} %convert_element_type.241), channel_id=1, source_target_pairs={{0,4},{1,5},{2,6},{3,7},{4,0},{5,1},{6,2},{7,3},{8,12},{9,13},{10,... | collective-permute-start | bytes 3145736 | tf_op jit(solution)/shard_map/ppermute | solution.py:641
  465.6 40.5 %collective-permute-start.16 = (bf16[256,2048]{1,0:T(8,128)(2,1)}, bf16[256,2048]{1,0:T(8,128)(2,1)}, u32[]{:S(2)}, u32[]{:S(2)}) collective-permute-start(bf16[256,2048]{1,0:T(8,128)(2,1)} %convolution_convert_fusion.9), channel_id=1, source_target_pairs={{0,4},{1,5},{2,6},{3,7},{4,0},{5,1},{6,2},{7,3},{8,12},{9,13},{10,... | collective-permute-start | bytes 3145736 | tf_op jit(solution)/shard_map/ppermute | solution.py:641
  519.7 157.2 %reduce-scatter.12.cloned.1.call-start = ((), (), s32[]{:S(2)}) async-start(), calls=%async_computation.12 | async-start | bytes 5242880 | tf_op jit(solution)/shard_map/reduce_scatter | solution.py:1068
  524.6 25.6 %collective-permute-start.19 = (bf16[256,2048]{1,0:T(8,128)(2,1)S(1)}, bf16[256,2048]{1,0:T(8,128)(2,1)S(1)}, u32[]{:S(2)}, u32[]{:S(2)}) collective-permute-start(bf16[256,2048]{1,0:T(8,128)(2,1)S(1)} %get-tuple-element.114), channel_id=1, source_target_pairs={{0,4},{1,5},{2,6},{3,7},{4,0},{5,1},{6,2},{7,3},{8,12},{9,13},{10,... | collective-permute-start | bytes 3145736 | tf_op jit(solution)/shard_map/ppermute | solution.py:641
  602.0 141.2 %reduce-scatter.6.cloned.1.call-start = ((), (), s32[]{:S(2)}) async-start(), calls=%async_computation.9 | async-start | bytes 10485760 | tf_op jit(solution)/shard_map/reduce_scatter | solution.py:1068
  602.7 287.6 %reduce-scatter.14.cloned.1.call-start = ((), (), s32[]{:S(2)}) async-start(), calls=%async_computation.13 | async-start | bytes 2621440 | tf_op jit(solution)/shard_map/reduce_scatter | solution.py:1068
  679.1 25.4 %collective-permute-start.40 = (bf16[256,1024]{1,0:T(8,128)(2,1)}, bf16[256,1024]{1,0:T(8,128)(2,1)}, u32[]{:S(2)}, u32[]{:S(2)}) collective-permute-start(bf16[256,1024]{1,0:T(8,128)(2,1)} %get-tuple-element.105), channel_id=1, source_target_pairs={{2,4},{3,5},{4,2},{5,3},{10,12},{11,13},{12,10},{13,11},{18,20},{1... | collective-permute-start | bytes 1572872 | tf_op jit(solution)/shard_map/ppermute | solution.py:641
  707.1 222.8 %reduce-scatter.8.cloned.1.call-start = ((), (), s32[]{:S(2)}) async-start(), calls=%async_computation.10 | async-start | bytes 9830400 | tf_op jit(solution)/shard_map/reduce_scatter | solution.py:1068
  747.2 47.3 %collective-permute-start.33 = (bf16[256,2048]{1,0:T(8,128)(2,1)S(1)}, bf16[256,2048]{1,0:T(8,128)(2,1)S(1)}, u32[]{:S(2)}, u32[]{:S(2)}) collective-permute-start(bf16[256,2048]{1,0:T(8,128)(2,1)S(1)} %get-tuple-element.111), channel_id=1, source_target_pairs={{2,4},{3,5},{4,2},{5,3},{10,12},{11,13},{12,10},{13,11},{18,20},{1... | collective-permute-start | bytes 3145736 | tf_op jit(solution)/shard_map/ppermute | solution.py:641
  822.6 36.1 %collective-permute-start.25 = (bf16[256,2048]{1,0:T(8,128)(2,1)}, bf16[256,2048]{1,0:T(8,128)(2,1)}, u32[]{:S(2)}, u32[]{:S(2)}) collective-permute-start(bf16[256,2048]{1,0:T(8,128)(2,1)} %add_convert_fusion), channel_id=1, source_target_pairs={{0,1},{1,0},{2,3},{3,2},{4,5},{5,4},{6,7},{7,6},{8,9},{9,8},{10,11... | collective-permute-start | bytes 3145736 | tf_op jit(solution)/shard_map/ppermute | solution.py:641
  822.8 52.1 %collective-permute-start.22 = (bf16[256,2048]{1,0:T(8,128)(2,1)}, bf16[256,2048]{1,0:T(8,128)(2,1)}, u32[]{:S(2)}, u32[]{:S(2)}) collective-permute-start(bf16[256,2048]{1,0:T(8,128)(2,1)} %get-tuple-element.59), channel_id=1, source_target_pairs={{2,4},{3,5},{4,2},{5,3},{10,12},{11,13},{12,10},{13,11},{18,20},{1... | collective-permute-start | bytes 3145736 | tf_op jit(solution)/shard_map/ppermute | solution.py:641
  887.1 53.3 %collective-permute-start.31 = (bf16[256,2048]{1,0:T(8,128)(2,1)}, bf16[256,2048]{1,0:T(8,128)(2,1)}, u32[]{:S(2)}, u32[]{:S(2)}) collective-permute-start(bf16[256,2048]{1,0:T(8,128)(2,1)} %fusion.5), channel_id=1, source_target_pairs={{2,4},{3,5},{4,2},{5,3},{10,12},{11,13},{12,10},{13,11},{18,20},{1... | collective-permute-start | bytes 3145736 | tf_op jit(solution)/shard_map/ppermute | solution.py:641
  891.6 25.1 %collective-permute-start.41 = (bf16[2,2,64,512]{3,2,0,1:T(8,128)(2,1)S(1)}, bf16[2,2,64,512]{3,2,0,1:T(8,128)(2,1)S(1)}, u32[]{:S(2)}, u32[]{:S(2)}) collective-permute-start(bf16[2,2,64,512]{3,2,0,1:T(8,128)(2,1)S(1)} %fusion.61), channel_id=1, source_target_pairs={{0,2},{1,3},{2,0},{3,1},{4,6},{5,7},{6,4},{7,5},{8,10},{9,11},{10,... | collective-permute-start | bytes 786440 | tf_op jit(solution)/shard_map/ppermute | solution.py:641
  936.0 46.0 %collective-permute-start.35 = (bf16[256,1920]{1,0:T(8,128)(2,1)}, bf16[256,1920]{1,0:T(8,128)(2,1)}, u32[]{:S(2)}, u32[]{:S(2)}) collective-permute-start(bf16[256,1920]{1,0:T(8,128)(2,1)} %get-tuple-element.109), channel_id=1, source_target_pairs={{2,4},{3,5},{4,2},{5,3},{10,12},{11,13},{12,10},{13,11},{18,20},{1... | collective-permute-start | bytes 2949128 | tf_op jit(solution)/shard_map/ppermute | solution.py:641
  (108 other events, 1530.1 us)
Sparse Core Ops, SparseCore 0:
  11.1 117.9 all-gather.4
  142.1 52.8 all-gather.6
  219.8 89.8 all-gather.8
  311.9 52.6 all-gather.10
  519.8 52.5 reduce-scatter.9
  602.1 51.5 reduce-scatter.11
  656.8 86.3 reduce-scatter.5
  746.4 35.1 reduce-scatter.13
  795.3 82.1 reduce-scatter.7

commit v3 on v2

--- a/solution.py
+++ b/solution.py
@@ -740,14 +740,15 @@
 
 
 class Spread:
-    def __init__(self, lanes, full, rows, chunks, send_sems, recv_sems):
+    def __init__(self, lanes, full, rows, chunks, send_sems, recv_sems, cols=slice(None)):
         self.lanes, self.full, self.rows, self.chunks = lanes, full, rows, chunks
+        self.cols = cols
         self.piece = rows // chunks
         self.send_sems, self.recv_sems = send_sems, recv_sems
 
     def view(self, place, half, chunk):
         start = self.lanes.block(place) * (2 * self.rows) + half * self.rows + chunk * self.piece
-        return self.full.at[pl.ds(pl.multiple_of(start, self.piece), self.piece), :]
+        return self.full.at[pl.ds(pl.multiple_of(start, self.piece), self.piece), self.cols]
 
     def copy(self, place, half, chunk, bit):
         view = self.view(place, half, chunk)
@@ -797,10 +798,10 @@
 
 
 def front_body(
-    blocks, chunks, in_ref, out_ref, x_ref, gain_ref,
-    full_ref, pair_ref, act_ref, xr_ref,
+    blocks, chunks, in_ref, out_ref, shared_ref, x_ref, gain_ref,
+    full_ref, pair_ref, act_ref, xr_ref, sh_ref,
     x_s, act_s, home_sems, z_send, z_recv, o_sems, o_recv, send_sems, recv_sems, x_sems, a_send,
-    a_recv,
+    a_recv, line_send, line_recv, sh_send, sh_recv, swap_send, swap_recv,
 ):
     lanes = Lanes(blocks)
     rows = in_ref.shape[0]
@@ -809,6 +810,57 @@
     c, t = lanes.c, lanes.t
     lanes.greet()
     spread = Spread(lanes, full_ref, rows, chunks, send_sems, recv_sems)
+    few, wide = shared_ref.shape
+    side = wide // 2
+    mine = pl.ds(pl.multiple_of(c * side, side), side)
+    theirs = pl.ds(pl.multiple_of((1 - c) * side, side), side)
+
+    def line_view(half, at_t, cols):
+        start = lanes.k * (2 * rows) + half * rows + at_t * few
+        return sh_ref.at[pl.ds(pl.multiple_of(start, few), few), cols]
+
+    def line_own():
+        return pltpu.make_async_copy(
+            shared_ref.at[:, mine], line_view(c, t, mine), line_send.at[0]
+        )
+
+    def line_swap():
+        return remote(
+            shared_ref.at[:, theirs],
+            line_view(c, t, theirs),
+            line_send.at[1],
+            line_recv.at[0],
+            (lanes.other, t),
+        )
+
+    def line_swapped():
+        view = line_view(1 - c, t, mine)
+        return remote(view, view, line_send.at[1], line_recv.at[0], (lanes.other, t))
+
+    def line_near(half, came):
+        view = line_view(half, lanes.near if came else t, mine)
+        return remote(
+            view, view, line_send.at[2 + half], line_recv.at[1 + half], (lanes.d, lanes.near)
+        )
+
+    def line_far(half, near, came):
+        at_t = lanes.near if near else t
+        if came:
+            at_t = lax.rem(at_t + 2, 4)
+        view = line_view(half, at_t, mine)
+        place = 2 * near + half
+        return remote(
+            view, view, line_send.at[4 + place], line_recv.at[3 + place], (lanes.d, lanes.far)
+        )
+
+    shared_spread = Spread(lanes, sh_ref, rows, 1, sh_send, sh_recv, mine)
+
+    def swap_copy(place, half, came):
+        start = lanes.block(place) * (2 * rows) + half * rows
+        view = sh_ref.at[pl.ds(pl.multiple_of(start, rows), rows), theirs if came else mine]
+        return remote(
+            view, view, swap_send.at[half, place], swap_recv.at[half, place], (lanes.other, t)
+        )
 
     def slot(chunk):
         start = lanes.k * (2 * rows) + c * rows + chunk * piece
@@ -863,31 +915,6 @@
             first_copy(chunk, (lanes.other, t)).start()
             second_copy(chunk).start()
 
-    early = max(chunks // 2, 1)
-    for chunk in range(early):
-        send_first(chunk)
-
-    @pl.when(lanes.home)
-    def _():
-        x_home().start()
-
-    @pl.when(lanes.away)
-    def _():
-        x_away().start()
-
-    for chunk in range(early, chunks):
-        send_first(chunk)
-
-    @pl.when(lanes.home)
-    def _():
-        out_first((lanes.d, lanes.far)).start()
-        pltpu.make_async_copy(out_ref, out_slot(), o_sems.at[2]).start()
-
-    @pl.when(lanes.away)
-    def _():
-        out_first((lanes.other, t)).start()
-        out_second().start()
-
     def z_view(half, chunk):
         start = lanes.k * (2 * rows) + half * rows + chunk * piece
         return full_ref.at[pl.ds(pl.multiple_of(start, piece), piece), :]
@@ -898,23 +925,30 @@
             view, view, z_send.at[0, chunk], z_recv.at[half, chunk], (lanes.other, t)
         )
 
+    def arrive_home(chunk):
+        own_copy(chunk).wait()
+        start = lanes.k * (2 * rows) + (1 - c) * rows + chunk * piece
+        view = full_ref.at[pl.ds(pl.multiple_of(start, piece), piece), :]
+        remote(
+            view, view, z_send.at[0, chunk], z_recv.at[1 - c, chunk], (lanes.other, t)
+        ).wait_recv()
+        for half in range(2):
+            spread.give(0, half, chunk)
+
+    def arrive_away(chunk):
+        for half in range(2):
+            came(half, chunk).wait_recv()
+        for half in range(2):
+            spread.give(0, half, chunk)
+
     def arrive(chunk):
         @pl.when(lanes.home)
         def _():
-            own_copy(chunk).wait()
-            start = lanes.k * (2 * rows) + (1 - c) * rows + chunk * piece
-            view = full_ref.at[pl.ds(pl.multiple_of(start, piece), piece), :]
-            remote(
-                view, view, z_send.at[0, chunk], z_recv.at[1 - c, chunk], (lanes.other, t)
-            ).wait_recv()
+            arrive_home(chunk)
 
         @pl.when(lanes.away)
         def _():
-            for half in range(2):
-                came(half, chunk).wait_recv()
-
-        for half in range(2):
-            spread.give(0, half, chunk)
+            arrive_away(chunk)
 
     def act_slot(index):
         return act_ref.at[pl.ds(index * here, here), :]
@@ -949,20 +983,95 @@
         pltpu.make_async_copy(act_s, act_slot(0), a_send.at[3]).start()
         pltpu.make_async_copy(x_s, xr_ref, x_sems.at[3]).start()
 
-    for chunk in range(chunks):
+    early = list(range(max(chunks // 2, 1)))
+    late = list(range(len(early), chunks))
+    line_own().start()
+    line_swap().start()
+    for chunk in early:
+        send_first(chunk)
+
+    @pl.when(lanes.home)
+    def _():
+        x_home().start()
+
+    @pl.when(lanes.away)
+    def _():
+        x_away().start()
+
+    line_own().wait()
+    line_swapped().wait_recv()
+    for half in range(2):
+        line_near(half, False).start()
+    for chunk in early:
         arrive(chunk)
-        if chunk >= 1:
+        if chunk:
             spread.pass_on(chunk - 1)
-        if chunk == early:
-            norm()
-    if early >= chunks:
-        norm()
-    spread.pass_on(chunks - 1)
+    for half in range(2):
+        line_near(half, True).wait_recv()
+    for near in range(2):
+        for half in range(2):
+            line_far(half, near, False).start()
+    for chunk in late:
+        send_first(chunk)
+    spread.pass_on(early[-1])
+
+    @pl.when(lanes.home)
+    def _():
+        for chunk in late:
+            arrive_home(chunk)
+            spread.pass_on(chunk)
+
+    norm()
+
+    @pl.when(lanes.home)
+    def _():
+        out_first((lanes.d, lanes.far)).start()
+        pltpu.make_async_copy(out_ref, out_slot(), o_sems.at[2]).start()
+
+    @pl.when(lanes.away)
+    def _():
+        out_first((lanes.other, t)).start()
+        out_second().start()
+
+    for near in range(2):
+        for half in range(2):
+            line_far(half, near, True).wait_recv()
+    for half in range(2):
+        shared_spread.give(0, half, 0)
+        swap_copy(0, half, False).start()
+
+    @pl.when(lanes.away)
+    def _():
+        for chunk in late:
+            arrive_away(chunk)
+            if chunk > late[0]:
+                spread.pass_on(chunk - 1)
+
+    shared_spread.pass_on(0)
+
+    @pl.when(lanes.away)
+    def _():
+        for chunk in late[-1:]:
+            spread.pass_on(chunk)
+
+    shared_spread.finish(0)
+    for half in range(2):
+        for place in range(1, blocks):
+            swap_copy(place, half, False).start()
     act_far().wait_recv()
     act_both().start()
     act_core().wait_recv()
     for chunk in range(chunks):
         spread.finish(chunk)
+    for half in range(2):
+        for place in range(blocks):
+            swap_copy(place, half, True).wait_recv()
+            swap_copy(place, half, False).wait_send()
+    line_swap().wait_send()
+    for half in range(2):
+        line_near(half, False).wait_send()
+        for near in range(2):
+            line_far(half, near, False).wait_send()
     act_both().wait_recv()
     act_far().wait_send()
     act_core().wait_send()
@@ -993,7 +1102,7 @@
             remote(view, view, o_sems.at[0], o_recv.at[half], (lanes.other, t)).wait_recv()
 
 
-def front(in_pack, out_pack, layer_in, gain, at):
+def front(in_pack, out_pack, shared, layer_in, gain, at):
     bf16 = jnp.bfloat16
     rows = in_pack.shape[0]
     blocks = at.blocks
@@ -1004,13 +1113,14 @@
     total = 2 * blocks * rows
     return pl.pallas_call(
         functools.partial(front_body, blocks, chunks),
-        in_specs=[anywhere, anywhere, anywhere, pl.BlockSpec(memory_space=pltpu.VMEM)],
-        out_specs=[anywhere] * 4,
+        in_specs=[anywhere] * 4 + [pl.BlockSpec(memory_space=pltpu.VMEM)],
+        out_specs=[anywhere] * 5,
         out_shape=[
             jax.ShapeDtypeStruct((total, in_pack.shape[1]), bf16),
             jax.ShapeDtypeStruct((2 * rows, out_pack.shape[1]), bf16),
             jax.ShapeDtypeStruct((4 * here, features), bf16),
             jax.ShapeDtypeStruct((here, features), bf16),
+            jax.ShapeDtypeStruct((total, shared.shape[1]), bf16),
         ],
         scratch_shapes=[
             pltpu.VMEM((here, features), bf16),
@@ -1025,6 +1135,12 @@
             dma((4,)),
             dma((4,)),
             dma((3,)),
+            dma((8,)),
+            dma((7,)),
+            dma((2, blocks, 1)),
+            dma((2, blocks, 1)),
+            dma((2, blocks)),
+            dma((2, blocks)),
         ],
         compiler_params=pltpu.CompilerParams(
             collective_id=1, has_side_effects=True, vmem_limit_bytes=16 * 1024 * 1024
@@ -1032,7 +1148,469 @@
         cost_estimate=pl.CostEstimate(
             flops=here * features * 8, bytes_accessed=300_000_000, transcendentals=0
         ),
-    )(in_pack, out_pack, layer_in, gain.reshape(1, -1))
+    )(in_pack, out_pack, shared, layer_in, gain.reshape(1, -1))
+
+
+class Collect:
+    def __init__(self, lanes, part, rows, cols, send_s, recv_s, load_s, total_s, sems):
+        self.lanes, self.part, self.rows, self.cols = lanes, part, rows, cols
+        self.send_s, self.recv_s, self.load_s, self.total_s = send_s, recv_s, load_s, total_s
+        self.send_sems, self.recv_sems, self.load_sems = sems
+        self.loads = [
+            (half, place)
+            for half in range(2)
+            for place in range(lanes.blocks)
+            if onward(place, half, lanes.bits)
+        ]
+
+    def source(self, place, half, chunk):
+        start = self.lanes.block(place) * (2 * self.rows) + half * self.rows
+        return self.part.at[pl.ds(pl.multiple_of(start, self.rows), self.rows), self.cols[chunk]]
+
+    def bit_of(self, place, half):
+        bits = [bit for bit in range(self.lanes.bits) if (place >> bit) & 1]
+        return bits[-1] if half == 0 else bits[0]
+
+    def load(self, half, place):
+        index = self.loads.index((half, place))
+        start = self.lanes.block(place) * (2 * self.rows) + half * self.rows
+        view = self.part.at[pl.ds(pl.multiple_of(start, self.rows), self.rows), :]
+        return pltpu.make_async_copy(view, self.load_s.at[index], self.load_sems.at[index])
+
+    def copy(self, place, half, chunk):
+        if (half, place) in self.loads:
+            source = self.send_s.at[self.loads.index((half, place)), :, self.cols[chunk]]
+        else:
+            source = self.source(place, half, chunk)
+        return remote(
+            source,
+            self.recv_s.at[half, place, :, self.cols[chunk]],
+            self.send_sems.at[half, place, chunk],
+            self.recv_sems.at[half, place, chunk],
+            self.lanes.across(self.bit_of(place, half)),
+        )
+
+    def order(self, half):
+        places = list(range(1, self.lanes.blocks))
+        places.sort(key=lambda place: -len([b for b in range(8) if (place >> b) & 1]))
+        return places
+
+    def start(self):
+        for half, place in self.loads:
+            self.load(half, place).start()
+
+    def direct(self, chunk):
+        for half in range(2):
+            for place in self.order(half):
+                if (half, place) not in self.loads:
+                    self.copy(place, half, chunk).start()
+
+    def add(self, place, half, chunk):
+        cols = self.cols[chunk]
+        index = self.loads.index((half, place))
+        total = self.load_s[index, :, cols].astype(jnp.float32)
+        for bit in onward(place, half, self.lanes.bits):
+            came = place | (1 << bit)
+            self.copy(came, half, chunk).wait_recv()
+            total = total + self.recv_s[half, came, :, cols].astype(jnp.float32)
+        return total
+
+    def middle(self, chunk):
+        for half in range(2):
+            for place in self.order(half):
+                if (half, place) in self.loads:
+                    index = self.loads.index((half, place))
+                    if chunk == 0:
+                        self.load(half, place).wait()
+                    total = self.add(place, half, chunk)
+                    self.send_s[index, :, self.cols[chunk]] = total.astype(jnp.bfloat16)
+                    self.copy(place, half, chunk).start()
+
+    def last(self, chunk):
+        for half in range(2):
+            if chunk == 0:
+                self.load(half, 0).wait()
+            self.total_s[half, :, self.cols[chunk]] = self.add(0, half, chunk)
+
+    def finish(self):
+        for chunk in range(len(self.cols)):
+            for half in range(2):
+                for place in range(1, self.lanes.blocks):
+                    self.copy(place, half, chunk).wait_send()
+
+
+def back_body(
+    blocks, in_cols, small_row, part_ref, bc_ref, kv_ref, own_ref, far_ref, core_ref, both_ref,
+    resid_ref, x_ref, gain_ref, small_ref,
+    gin_ref, gsh_ref, gx_ref, sum_ref,
+    in_send, in_recv, in_load, in_total, settle_s, settle_r, sh_came, sh_part, sh_send, sh_recv,
+    sh_load, sh_total, line_s, line_r, near_s, near_r, swap_s, swap_r,
+    buf_both, buf_core, buf_far, pass_s, gx_s, gx_r, small_s, small_r,
+    in_ssem, in_rsem, in_lsem, sh_ssem, sh_rsem, sh_lsem, set_ssem, set_rsem, misc_s, misc_r,
+    pass_ssem, pass_rsem, small_ssem, small_rsem,
+):
+    f32, bf16 = jnp.float32, jnp.bfloat16
+    lanes = Lanes(blocks)
+    c, t = lanes.c, lanes.t
+    rows = gin_ref.shape[0]
+    here = own_ref.shape[0]
+    wide = bc_ref.shape[1]
+    few = gsh_ref.shape[0]
+    chunks = len(in_cols)
+    step = min(here, 32)
+    lanes.greet()
+    core_at = (lanes.other, t)
+    near_at = (lanes.d, lanes.near)
+    far_at = (lanes.d, lanes.far)
+    cross_at = (lanes.other, lanes.far)
+    first = c == 0
+    second = c == 1
+
+    collect = Collect(
+        lanes, part_ref, rows, in_cols, in_send, in_recv, in_load, in_total,
+        (in_ssem, in_rsem, in_lsem),
+    )
+    shared = Collect(
+        lanes, sh_part, rows, [slice(0, wide)], sh_send, sh_recv, sh_load, sh_total,
+        (sh_ssem, sh_rsem, sh_lsem),
+    )
+    half_kv = kv_ref.shape[1] // 2
+
+    def send_both():
+        return remote(both_ref, buf_both, misc_s.at[0], misc_r.at[0], core_at)
+
+    def send_core():
+        return remote(core_ref, buf_core, misc_s.at[1], misc_r.at[1], core_at)
+
+    def send_kv():
+        return remote(
+            kv_ref, sh_came.at[:, : 2 * half_kv], misc_s.at[2], misc_r.at[2], core_at
+        )
+
+    def send_bc():
+        return remote(bc_ref, sh_came, misc_s.at[3], misc_r.at[3], core_at)
+
+    send_both().start()
+    collect.start()
+    for chunk in range(chunks):
+        collect.direct(chunk)
+    send_core().start()
+
+    @pl.when(first)
+    def _():
+        send_kv().start()
+
+    @pl.when(second)
+    def _():
+        send_bc().start()
+
+    parts = 2 if here >= 64 else 1
+    share = here // parts
+
+    def send_pass(part):
+        view = pl.ds(part * share, share)
+        return remote(
+            pass_s.at[view, :], buf_far.at[view, :], pass_ssem.at[part], pass_rsem.at[part], near_at
+        )
+
+    send_both().wait_recv()
+    for part in range(parts):
+
+        @pl.loop(0, share // step)
+        def _(i, part=part):
+            view = pl.ds(pl.multiple_of(part * share + i * step, step), step)
+            pass_s[view, :] = (far_ref[view, :] + buf_both[view, :].astype(f32)).astype(bf16)
+
+        send_pass(part).start()
+
+    @pl.when(first)
+    def _():
+        send_bc().wait_recv()
+
+        @pl.loop(0, bc_ref.shape[0] // 64)
+        def _(i):
+            view = pl.ds(pl.multiple_of(i * 64, 64), 64)
+            total = bc_ref[view, :].astype(f32) + sh_came[view, :].astype(f32)
+            sh_part[view, :] = total.astype(bf16)
+
+    @pl.when(second)
+    def _():
+        send_kv().wait_recv()
+
+        @pl.loop(0, bc_ref.shape[0] // 64)
+        def _(i):
+            view = pl.ds(pl.multiple_of(i * 64, 64), 64)
+            for piece in range(2):
+                kept = pl.ds(piece * half_kv, half_kv)
+                sh_part[view, pl.ds(2 * piece * half_kv, half_kv)] = sh_came[view, kept]
+                sh_part[view, pl.ds((2 * piece + 1) * half_kv, half_kv)] = kv_ref[view, kept]
+
+    shared.start()
+    for chunk in range(chunks):
+        collect.middle(chunk)
+    shared.direct(0)
+
+    def send_x():
+        return remote(gx_s, gx_r, misc_s.at[4], misc_r.at[4], cross_at)
+
+    send_core().wait_recv()
+    for part in range(parts):
+        send_pass(part).wait_recv()
+    small_s[0] = small_ref[...]
+    features = gain_ref.shape[1]
+
+    def one_part(i, gains):
+        view = pl.ds(pl.multiple_of(i * step, step), step)
+        grad = own_ref[view, :] + buf_core[view, :].astype(f32) + buf_far[view, :].astype(f32)
+        x = x_ref[view, :].astype(f32)
+        scale = lax.rsqrt(jnp.mean(x * x, axis=1, keepdims=True) + EPS)
+        gains = gains + jnp.sum(grad * (x * scale), axis=0, keepdims=True)
+        grad = grad * gain_ref[...]
+        mean = jnp.mean(grad * x, axis=1, keepdims=True)
+        result = resid_ref[view, :] + scale * grad - x * (scale * scale * scale * mean)
+        gx_ref[view, :] = result
+        gx_s[view, :] = result.astype(bf16)
+        return gains
+
+    gains = lax.fori_loop(0, here // step, one_part, jnp.zeros((1, features), f32))
+    for i in range(features // WIDE):
+        small_s[0, small_row + i : small_row + i + 1, :] = gains[:, i * WIDE : (i + 1) * WIDE]
+
+    @pl.when(lanes.away)
+    def _():
+        send_x().start()
+
+    stops = [near_at, core_at, far_at] + [lanes.across(bit) for bit in range(lanes.bits)]
+
+    def send_small(index):
+        return remote(
+            small_s.at[index], small_r.at[index], small_ssem.at[index], small_rsem.at[index],
+            stops[index],
+        )
+
+    def step_small(index):
+        send_small(index).wait_recv()
+        small_s[index + 1] = small_s[index] + small_r[index]
+        if index + 1 < len(stops):
+            send_small(index + 1).start()
+
+    send_small(0).start()
+
+    def send_first(chunk, device):
+        cols = in_cols[chunk]
+        return remote(
+            settle_s.at[0, :, cols], settle_r.at[0, :, cols],
+            set_ssem.at[0, chunk], set_rsem.at[0, chunk], device,
+        )
+
+    def send_second(chunk):
+        cols = in_cols[chunk]
+        return remote(
+            settle_s.at[1, :, cols], settle_r.at[1, :, cols],
+            set_ssem.at[1, chunk], set_rsem.at[1, chunk], cross_at,
+        )
+
+    for chunk in range(chunks):
+        collect.last(chunk)
+        cols = in_cols[chunk]
+
+        @pl.when(lanes.home)
+        def _(chunk=chunk, cols=cols):
+            settle_s[0, :, cols] = in_total[1 - c, :, cols].astype(bf16)
+            send_first(chunk, core_at).start()
+
+        @pl.when(lanes.away)
+        def _(chunk=chunk, cols=cols):
+            settle_s[0, :, cols] = in_total[c, :, cols].astype(bf16)
+            send_first(chunk, far_at).start()
+            settle_s[1, :, cols] = in_total[1 - c, :, cols].astype(bf16)
+            send_second(chunk).start()
+
+        if chunk == 0:
+            step_small(0)
+            shared.middle(0)
+    step_small(1)
+    shared.last(0)
+
+    t_high, t_low = lax.div(t, 2), lax.rem(t, 2)
+    line = 2 * few
+
+    def send_line():
+        return remote(line_s, line_r, misc_s.at[5], misc_r.at[5], far_at)
+
+    def send_near():
+        return remote(near_s, near_r, misc_s.at[6], misc_r.at[6], near_at)
+
+    def send_swap():
+        return remote(swap_s, swap_r, misc_s.at[7], misc_r.at[7], core_at)
+
+    theirs = pl.ds(pl.multiple_of((1 - t_high) * line, line), line)
+    mine = pl.ds(pl.multiple_of(t_high * line, line), line)
+    for half in range(2):
+        line_s[half] = sh_total[half, theirs, :].astype(bf16)
+    send_line().start()
+    step_small(2)
+    send_line().wait_recv()
+    for half in range(2):
+        sh_total[half, mine, :] = sh_total[half, mine, :] + line_r[half].astype(f32)
+    theirs = pl.ds(pl.multiple_of(t_high * line + (1 - t_low) * few, few), few)
+    mine = pl.ds(pl.multiple_of(t_high * line + t_low * few, few), few)
+    for half in range(2):
+        near_s[half] = sh_total[half, theirs, :].astype(bf16)
+    send_near().start()
+    for index in range(3, len(stops)):
+        step_small(index)
+    send_near().wait_recv()
+    for half in range(2):
+        sh_total[half, mine, :] = sh_total[half, mine, :] + near_r[half].astype(f32)
+    swap_s[...] = sh_total[1 - c, mine, :].astype(bf16)
+    send_swap().start()
+    sum_ref[...] = small_s[len(stops)]
+
+    for chunk in range(chunks):
+        cols = in_cols[chunk]
+        send_first(chunk, core_at).wait_recv()
+
+        @pl.when(lanes.home)
+        def _(chunk=chunk, cols=cols):
+            gin_ref[:, cols] = in_total[c, :, cols] + settle_r[0, :, cols].astype(f32)
+
+        @pl.when(lanes.away)
+        def _(chunk=chunk, cols=cols):
+            send_second(chunk).wait_recv()
+            gin_ref[:, cols] = settle_r[0, :, cols].astype(f32) + settle_r[1, :, cols].astype(f32)
+
+    send_swap().wait_recv()
+
+    @pl.when(first)
+    def _():
+        gsh_ref[:, :wide] = sh_total[0, mine, :]
+        gsh_ref[:, wide:] = swap_r[...].astype(f32)
+
+    @pl.when(second)
+    def _():
+        gsh_ref[:, :wide] = swap_r[...].astype(f32)
+        gsh_ref[:, wide:] = sh_total[1, mine, :]
+
+    @pl.when(lanes.away)
+    def _():
+        send_x().wait_recv()
+
+        @pl.loop(0, here // step)
+        def _(i):
+            view = pl.ds(pl.multiple_of(i * step, step), step)
+            gx_ref[view, :] = gx_r[view, :].astype(f32)
+
+    collect.finish()
+    shared.finish()
+    send_both().wait_send()
+    send_core().wait_send()
+
+    @pl.when(first)
+    def _():
+        send_kv().wait_send()
+
+    @pl.when(second)
+    def _():
+        send_bc().wait_send()
+
+    for part in range(parts):
+        send_pass(part).wait_send()
+    for chunk in range(chunks):
+        send_first(chunk, core_at).wait_send()
+
+    @pl.when(lanes.away)
+    def _():
+        send_x().wait_send()
+        for chunk in range(chunks):
+            send_second(chunk).wait_send()
+
+    for index in range(len(stops)):
+        send_small(index).wait_send()
+    send_line().wait_send()
+    send_near().wait_send()
+    send_swap().wait_send()
+
+
+def back(part_in, bc, kv, act_parts, grad_resid, x, gain, small, small_row, few, at):
+    f32, bf16 = jnp.float32, jnp.bfloat16
+    own, core, far, both = act_parts
+    blocks = at.blocks
+    features, width = part_in.shape
+    rows = features // (2 * blocks)
+    here = own.shape[0]
+    wide = bc.shape[1]
+    chunks = 3
+    piece = width // chunks
+    in_cols = [slice(i * piece, (i + 1) * piece) for i in range(chunks)]
+    loads = sum(bool(onward(p, h, at.bits)) for h in range(2) for p in range(blocks))
+    steps = 3 + at.bits
+    parts = 2 if here >= 64 else 1
+    dma = pltpu.SemaphoreType.DMA
+    vmem = pl.BlockSpec(memory_space=pltpu.VMEM)
+    anywhere = pl.BlockSpec(memory_space=pl.ANY)
+    line = 2 * few
+    return pl.pallas_call(
+        functools.partial(back_body, blocks, in_cols, small_row),
+        in_specs=[anywhere, vmem, vmem, vmem, vmem, anywhere, anywhere, vmem, vmem, vmem, vmem],
+        out_specs=[vmem] * 4,
+        out_shape=[
+            jax.ShapeDtypeStruct((rows, width), f32),
+            jax.ShapeDtypeStruct((few, 2 * wide), f32),
+            jax.ShapeDtypeStruct((here, features), f32),
+            jax.ShapeDtypeStruct(small.shape, f32),
+        ],
+        scratch_shapes=[
+            pltpu.VMEM((loads, rows, width), bf16),
+            pltpu.VMEM((2, blocks, rows, width), bf16),
+            pltpu.VMEM((loads, rows, width), bf16),
+            pltpu.VMEM((2, rows, width), f32),
+            pltpu.VMEM((2, rows, width), bf16),
+            pltpu.VMEM((2, rows, width), bf16),
+            pltpu.VMEM((features, wide), bf16),
+            pltpu.VMEM((features, wide), bf16),
+            pltpu.VMEM((loads, rows, wide), bf16),
+            pltpu.VMEM((2, blocks, rows, wide), bf16),
+            pltpu.VMEM((loads, rows, wide), bf16),
+            pltpu.VMEM((2, rows, wide), f32),
+            pltpu.VMEM((2, line, wide), bf16),
+            pltpu.VMEM((2, line, wide), bf16),
+            pltpu.VMEM((2, few, wide), bf16),
+            pltpu.VMEM((2, few, wide), bf16),
+            pltpu.VMEM((few, wide), bf16),
+            pltpu.VMEM((few, wide), bf16),
+            pltpu.VMEM((here, features), bf16),
+            pltpu.VMEM((here, features), bf16),
+            pltpu.VMEM((here, features), bf16),
+            pltpu.VMEM((here, features), bf16),
+            pltpu.VMEM((here, features), bf16),
+            pltpu.VMEM((here, features), bf16),
+            pltpu.VMEM((steps + 1,) + small.shape, f32),
+            pltpu.VMEM((steps,) + small.shape, f32),
+            dma((2, blocks, chunks)),
+            dma((2, blocks, chunks)),
+            dma((loads,)),
+            dma((2, blocks, 1)),
+            dma((2, blocks, 1)),
+            dma((loads,)),
+            dma((2, chunks)),
+            dma((2, chunks)),
+            dma((8,)),
+            dma((8,)),
+            dma((parts,)),
+            dma((parts,)),
+            dma((steps,)),
+            dma((steps,)),
+        ],
+        compiler_params=pltpu.CompilerParams(
+            collective_id=2, has_side_effects=True, vmem_limit_bytes=58 * 1024 * 1024
+        ),
+        cost_estimate=pl.CostEstimate(
+            flops=here * features * 20, bytes_accessed=300_000_000, transcendentals=0
+        ),
+    )(
+        part_in, bc, kv, own, far, core, both, grad_resid, x, gain.reshape(1, -1), small,
+    )
 
 
 def after(values, *others):
@@ -1087,9 +1665,8 @@
     return gather_blocks(pair_weight(shard, at), at)
 
 
-def scatter_weight(grad, at):
+def settle_weight(mine, at):
     f32 = jnp.float32
-    mine = sum_blocks(grad, at)
     rows = mine.shape[0] // 2
     low, high = mine[:rows], mine[rows:]
     own = jnp.where(at.c == 0, low, high)
@@ -1219,7 +1796,19 @@
     quarters = jnp.arange(at.tp, dtype=jnp.int32)
     order = (at.c ^ (quarters // 2)) + 2 * (at.zq ^ (quarters % 2))
 
-    shared_full = lax.all_gather(shared_weight, ("dp", "tensor"), axis=0, tiled=True)
+    in_pack = jnp.concatenate(
+        [
+            mixer_in_weight.reshape(w_rows, 2 * width),
+            query_weight,
+            step_weight,
+            jnp.zeros((w_rows, WIDE - local_heads), bf16),
+        ],
+        axis=1,
+    )
+    out_pack = jnp.concatenate([mixer_out_weight, attn_out_weight], axis=1)
+    in_all, out_pair, act_all, inputs, shared_full = front(
+        in_pack, out_pack, shared_weight, layer_in, input_gain, at
+    )
     left, right = shared_full[:, :bc_width], shared_full[:, bc_width:]
     kv_index = at.column * (query_width // HD) // (QH // KVH)
     second = kv_index == 1
@@ -1231,23 +1820,12 @@
         ],
         axis=1,
     )
-    in_pack = jnp.concatenate(
-        [
-            mixer_in_weight.reshape(w_rows, 2 * width),
-            query_weight,
-            step_weight,
-            jnp.zeros((w_rows, WIDE - local_heads), bf16),
-        ],
-        axis=1,
-    )
-    out_pack = jnp.concatenate([mixer_out_weight, attn_out_weight], axis=1)
-    in_all, out_pair, act_all, inputs = front(in_pack, out_pack, layer_in, input_gain, at)
+    x_low = inputs
     inputs = inputs.astype(f32)
 
     def row_split(values):
         return [values[i * rows_here : (i + 1) * rows_here] for i in range(at.tp)]
 
-    _, norm_in_back = jax.vjp(rms_norm, inputs, input_gain)
     out_all = gather_blocks(out_pair, at)
     rest = jnp.concatenate(
         [gate_up_weight.reshape(w_rows, 2 * hidden_width), down_weight], axis=1
@@ -1301,8 +1879,8 @@
     part_gate_up = weight_grad(mid_all, grad_gu)
     grad_mid = sum_rows(grad_mid_parts, at)
     grad_mid, part_down, part_gate_up = lax.optimization_barrier((grad_mid, part_down, part_gate_up))
-    grad_down = scatter_weight(part_down, at)
-    grad_gate_up = scatter_weight(part_gate_up, at)
+    raw_down = sum_blocks(part_down, at)
+    raw_gate_up = sum_blocks(part_gate_up, at)
     grad_resid_norm, grad_middle_gain = norm_mid_back(grad_mid)
     grad_resid = error + grad_resid_norm
     mix_grad_all = jnp.concatenate(share_rows(grad_resid.astype(bf16), at), axis=0)
@@ -1310,8 +1888,7 @@
     part_out = weight_grad(mix_grad_all, heads_all)
     grad_heads, part_out = lax.optimization_barrier((grad_heads, part_out))
     layer_out = relocate(after(outputs.astype(bf16), grad_heads), at)
-    part_out = after(part_out, grad_down)
-    grad_out = scatter_weight(part_out, at)
+    raw_out = sum_blocks(after(part_out, raw_gate_up), at)
     dq, dkv = attn_backward(
         order, proj, proj_shared, cosine, sine, grad_heads, query_width, width, bc_width
     )
@@ -1319,58 +1896,52 @@
         order, proj, proj_shared, y, states, grad_heads, dq, dkv, lane_params, conv_shared,
         head_params, seg, query_width,
     )
-    grad_bc = lax.dot_general(
-        act_all, low_shared[:, :bc_width], contract_first, preferred_element_type=f32
-    )
-    grad_kv = lax.dot_general(
-        act_all, low_shared[:, bc_width:], contract_first, preferred_element_type=f32
-    )
-    part_in = weight_grad(act_all, low_pack)
-    low_pack, low_shared, part_in, grad_bc, grad_kv = lax.optimization_barrier(
-        (low_pack, low_shared, part_in, grad_bc, grad_kv)
-    )
-    grad_in = scatter_weight(after(part_in, grad_gate_up), at)
-    grad_shared_weight = scatter_shared(grad_bc, grad_kv, grad_out, at)
+    column = at.column
+    lanes_full = lax.dynamic_update_slice(
+        jnp.zeros((KC + 1, DI), f32), dlane[: KC + 1], (0, column * width)
+    )
+    head_stack = jnp.concatenate(
+        [dhead[:2, :local_heads], dlane[KC + 1].reshape(1, local_heads, head_dim).sum(2)], axis=0
+    )
+    heads_full = lax.dynamic_update_slice(
+        jnp.zeros((3, H), f32), head_stack, (0, column * local_heads)
+    )
+    small = (
+        jnp.zeros_like(input_gain),
+        grad_middle_gain,
+        lanes_full,
+        dconv[:KC],
+        heads_full,
+        err_local,
+    )
+    flat = jnp.concatenate([part.reshape(-1) for part in small])
+    padded = -(-flat.shape[0] // 1024) * 1024
+    flat = jnp.pad(flat, (0, padded - flat.shape[0])).reshape(-1, WIDE)
+
     grad_act_parts = [
         lax.dot_general(a, in_all, contract_last, preferred_element_type=f32)
         + lax.dot_general(b, shared_all, contract_last, preferred_element_type=f32)
         for a, b in zip(row_split(low_pack), row_split(low_shared))
     ]
-    grad_act = sum_rows(grad_act_parts, at)
-    grad_input_norm, grad_input_gain = norm_in_back(grad_act)
-    input_grad = grad_resid + grad_input_norm
-
-    column = at.column
-    convx_full = lax.dynamic_update_slice(
-        jnp.zeros((KC + 1, DI), f32), dlane[: KC + 1], (0, column * width)
-    )
-    head_stack = jnp.concatenate(
-        [dhead[:2, :local_heads], dlane[KC + 1].reshape(1, local_heads, head_dim).sum(2)], axis=0
-    )
-    heads_full = lax.dynamic_update_slice(
-        jnp.zeros((3, H), f32), head_stack, (0, column * local_heads)
-    )
-    small = (
-        convx_full,
-        dconv[:KC],
-        heads_full,
-        grad_input_gain,
-        grad_middle_gain,
-        err_local,
-    )
-    flat = jnp.concatenate([part.reshape(-1) for part in small])
-    length = flat.shape[0]
-    padded = -(-length // 1024) * 1024
-    flat = jnp.pad(flat, (0, padded - length)).reshape(-1, 128)
-    flat = sum_tensor(flat, at)
-    input_grad = relocate(after(input_grad.astype(bf16), flat), at).astype(f32)
-    flat = sum_data(flat, at).reshape(-1)
+    grad_act_parts[1] = grad_act_parts[1].astype(bf16)
+    grad_act_parts[3] = grad_act_parts[3].astype(bf16)
+    part_bc = weight_grad(act_all, low_shared[:, :bc_width])
+    part_kv = weight_grad(act_all, low_shared[:, bc_width:])
+    part_in = weight_grad(act_all, low_pack)
+    grad_rest = settle_weight(jnp.concatenate([raw_out, raw_gate_up, raw_down], axis=1), at)
+    grad_in, grad_shared_weight, input_grad, flat = back(
+        part_in, part_bc, part_kv, grad_act_parts, grad_resid, x_low, input_gain, flat, 0,
+        shared_weight.shape[0], at,
+    )
+    out_width = width + query_width
+    gate_up_to = out_width + 2 * hidden_width
+    flat = flat.reshape(-1)
     sums = []
     start = 0
     for part in small:
         sums.append(flat[start : start + part.size].reshape(part.shape))
         start += part.size
-    sum_lanes, sum_convs, sum_heads, sum_input_gain, sum_middle_gain, err_total = sums
+    sum_input_gain, sum_middle_gain, sum_lanes, sum_convs, sum_heads, err_total = sums
     lanes_local = lax.dynamic_slice_in_dim(sum_lanes, at.t * width, width, 1)
     heads_local = lax.dynamic_slice_in_dim(sum_heads, at.t * local_heads, local_heads, 1)
     loss = err_total / jnp.sum(lengths).astype(f32)
@@ -1391,11 +1962,11 @@
         heads_local[1],
         heads_local[2],
         lanes_local[KC],
-        grad_out[:, :width],
-        grad_out[:, width:],
+        grad_rest[:, :width],
+        grad_rest[:, width:out_width],
         sum_middle_gain,
-        grad_gate_up.reshape(w_rows, 2, hidden_width),
-        grad_down,
+        grad_rest[:, out_width:gate_up_to].reshape(w_rows, 2, hidden_width),
+        grad_rest[:, gate_up_to:],
     )
 
 

time: 1000 us -> 944 us (0.944)
  Pallas kernels: 194 us -> 359 us
  waiting for transfers between devices: 414 us -> 251 us
  starting transfers between devices: 76.1 us -> 34.7 us
  other arithmetic: 68.9 us -> 42.7 us
  local copies, waits for them, and re-layouts: 40.9 us -> 61 us
  matrix products: 184 us -> 169 us
    pallas_call x0 -> x1, Pallas kernels: none -> 173 us  [back(): pl.pallas_call(functools.partial(back_body, blocks, in_cols, small_row),...]
    ppermute x44 -> x25, waiting for transfers between devices: 365 us -> 198 us  [send(): return lax.ppermute(values, ('dp', 'tensor'), self.pairs(where_to))]
    ppermute x44 -> x25, starting transfers between devices: 75.7 us -> 34.5 us  [send(): return lax.ppermute(values, ('dp', 'tensor'), self.pairs(where_to))]
    convert_element_type x7 -> x0, other arithmetic: 14.7 us -> none  [the longest x2 6.9 us: per_device(): input_grad = relocate(after(input_grad.astype(bf16), flat), at).astype(f32)]
    unnamed x164 -> x152, local copies, waits for them, and re-layouts: 21 us -> 35.6 us
    dot_general x4 -> x6, matrix products: 42.3 us -> 45.4 us  [weight_grad(): lax.dot_general(left, right, contract_first, preferred_element_type=f32)]
    reduce_scatter x5 -> x3, waiting for transfers between devices: 45.7 us -> 45.1 us  [sum_blocks(): lax.psum_scatter(values, 'dp', scatter_dimension=0, tiled=True, axis_inde...]
  transfers between devices with their start and end apart: 53 -> 31, of which waited for: 26 -> 15; matrix products, arithmetic and copies ran while one was open for 24% -> 22% of each run, Pallas kernels for 19% -> 26%
where the time goes in v3:
time: 944 us; the launch traced here: 936 us
  Pallas kernels  359 us (38%)
  waiting for transfers between devices  251 us (27%)
  matrix products  169 us (18%)
  local copies, waits for them, and re-layouts  61 us (6%)
  other arithmetic  42.7 us (5%)
  starting transfers between devices  34.7 us (4%)
  between operations  18.5 us (2%)
    ppermute x25, waiting for transfers between devices, send(): return lax.ppermute(values, ('dp', 'tensor'), self.pairs(where_to))  198 us
    pallas_call x1, Pallas kernels, back(): pl.pallas_call(functools.partial(back_body, blocks, in_cols, small_row),...  173 us
    pallas_call x1, Pallas kernels, front(): pl.pallas_call(functools.partial(front_body, blocks, chunks), in_specs=[a...  117 us
    dot_general x6, matrix products, weight_grad(): lax.dot_general(left, right, contract_first, preferred_element_type=f32)  45.4 us
    reduce_scatter x3, waiting for transfers between devices, sum_blocks(): lax.psum_scatter(values, 'dp', scatter_dimension=0, tiled=True, axis_inde...  45.1 us
    unnamed x152, local copies, waits for them, and re-layouts  35.6 us
    ppermute x25, starting transfers between devices, send(): return lax.ppermute(values, ('dp', 'tensor'), self.pairs(where_to))  34.5 us
    pallas_call x1, Pallas kernels, mixer_backward(): pl.pallas_call(mixer_bwd_body, grid_spec=pltpu.PrefetchScalarGridSpec(num...  33.1 us
  transfers between devices with their start and end apart: 31, of which 15 were waited for; matrix products, arithmetic and copies ran while one was open for 22% of the time, Pallas kernels for 26%

profile of v3, /device:TPU:1, one launch (start us, length us, event | category | flops | bytes accessed | tf_op | source)
XLA Modules:
  0.0 935.7 jit_solution(8322862462207123692)
XLA Ops:
  12.9 116.9 %shard_map.330 = (bf16[2048,1920]{1,0:T(8,128)(2,1)S(1)}, bf16[512,1024]{1,0:T(8,128)(2,1)S(1)}, bf16[1024,2048]{1,0:T(8,128)(2,1)S(1)}, bf16[256,2048]{1,0:T(8,128)(2,1)S(1)}, bf16[2048,1024]{1,0:T(8,128)(2,1)S(1)}) custom-call(bf16[256,1920]{1,0:T(8,128)(2,1)S(1)} %concatenate.51.in_ref, bf16[256,1024]{1,0:T(8,128)(2,1)S(1)} %pad_maximum_fusion.14.out_ref, ...), custom_call_target="tpu_custom_call" | custom-call | flops 4194304 | bytes 300000000 | tf_op jit(solution)/shard_map/pallas_call | solution.py:1114
  142.4 67.9 %collective-permute-done.7 = bf16[256,3072]{1,0:T(8,128)(2,1)} collective-permute-done((bf16[256,3072]{1,0:T(8,128)(2,1)S(1)}, bf16[256,3072]{1,0:T(8,128)(2,1)}, u32[]{:S(2)}, u32[]{:S(2)}) %collective-permute-start.7) | collective-permute-done | bytes 1572896 | tf_op jit(solution)/shard_map/ppermute | solution.py:641
  228.9 11.2 %fusion.75.q_ref.gate_ref.inner_ref.step_ref.before_ref = f32[1024,1920]{1,0:T(8,128)} fusion(bf16[1024,2048]{1,0:T(8,128)(2,1)S(1)} %copy-done.9, bf16[2048,1920]{1,0:T(8,128)(2,1)S(1)} %bitcast.61), kind=kOutput, calls=%fused_computation.168 | convolution fusion | flops 8053063680 | bytes 19922944 | tf_op jit(solution)/shard_map/dot_general | solution.py:1837
  240.2 7.9 shard_map.331.attn_ref
  249.6 15.7 %shard_map.332 = (bf16[1024,1024]{1,0:T(8,128)(2,1)}, f32[1024,768]{1,0:T(8,128)}, bf16[8,256,768]{2,1,0:T(8,128)(2,1)}) custom-call(s32[4]{0:T(128)} %fusion.57.order, f32[1024,1920]{1,0:T(8,128)} %fusion.75.q_ref.gate_ref.inner_ref.step_ref.before_ref, f32[1024,1920]{1,0:T(8,128)} %fusion.75.q_ref.gate_ref.inner_ref.step_ref.before_ref, ...), custom_call_target="tpu_custom_call" | custom-call | flops 3221225472 | bytes 15728640 | tf_op jit(solution)/shard_map/pallas_call | solution.py:480
  281.4 18.7 %collective-permute-done.3 = bf16[256,2048]{1,0:T(8,128)(2,1)} collective-permute-done((bf16[256,2048]{1,0:T(8,128)(2,1)}, bf16[256,2048]{1,0:T(8,128)(2,1)}, u32[]{:S(2)}, u32[]{:S(2)}) %collective-permute-start.3) | collective-permute-done | bytes 1048608 | tf_op jit(solution)/shard_map/ppermute | solution.py:641
  305.4 21.2 %collective-permute-done.5 = bf16[256,2048]{1,0:T(8,128)(2,1)S(1)} collective-permute-done((bf16[256,2048]{1,0:T(8,128)(2,1)S(1)}, bf16[256,2048]{1,0:T(8,128)(2,1)S(1)}, u32[]{:S(2)}, u32[]{:S(2)}) %collective-permute-start.5) | collective-permute-done | bytes 1048608 | tf_op jit(solution)/shard_map/ppermute | solution.py:641
  330.7 12.8 %fusion.27 = f32[1024,2048]{1,0:T(8,128)S(1)} fusion(bf16[2048,2048]{1,0:T(8,128)(2,1)} %all-gather.6.cloned.1.call-done, bf16[256,2048]{1,0:T(8,128)(2,1)} %collective-permute-done.6, bf16[256,2048]{1,0:T(8,128)(2,1)} %copy-done.47, bf16[256,2048]{1,0:T(8,128)(2,1)} %copy-done.49, bf16[256,2048]{1,0:T(8,128)(2,1)S(1)} %multiply_convert_fusion.3), kind=kOutput, calls=%fused_computation.82 | convolution fusion | flops 8606711808 | bytes 20971520 | tf_op jit(solution)/shard_map/dot_general | solution.py:1850
  349.5 7.6 all-gather.8.cloned.1.call-done
  379.0 11.2 %collective-permute-done.12 = bf16[256,2048]{1,0:T(8,128)(2,1)} collective-permute-done((bf16[256,2048]{1,0:T(8,128)(2,1)S(1)}, bf16[256,2048]{1,0:T(8,128)(2,1)}, u32[]{:S(2)}, u32[]{:S(2)}) %collective-permute-start.12) | collective-permute-done | bytes 1048608 | tf_op jit(solution)/shard_map/ppermute | solution.py:641
  390.2 17.6 %collective-permute-done.11 = bf16[256,2048]{1,0:T(8,128)(2,1)} collective-permute-done((bf16[256,2048]{1,0:T(8,128)(2,1)}, bf16[256,2048]{1,0:T(8,128)(2,1)}, u32[]{:S(2)}, u32[]{:S(2)}) %collective-permute-start.11) | collective-permute-done | bytes 1048608 | tf_op jit(solution)/shard_map/ppermute | solution.py:641
  414.7 23.1 %collective-permute-done.14 = bf16[256,2048]{1,0:T(8,128)(2,1)S(1)} collective-permute-done((bf16[256,2048]{1,0:T(8,128)(2,1)S(1)}, bf16[256,2048]{1,0:T(8,128)(2,1)S(1)}, u32[]{:S(2)}, u32[]{:S(2)}) %collective-permute-start.14) | collective-permute-done | bytes 1048608 | tf_op jit(solution)/shard_map/ppermute | solution.py:641
  441.8 11.5 %multiply_convert_fusion = (bf16[1024,1024]{1,0:T(8,128)(2,1)}, bf16[1024,1024]{1,0:T(8,128)(2,1)}) fusion(f32[1024,2048]{1,0:T(8,128)S(1)} %bitcast.65, bf16[2048,1024]{1,0:T(8,128)(2,1)} %all-gather.8.cloned.1.call-done, bf16[256,2048]{1,0:T(8,128)(2,1)} %collective-permute-done.15, bf16[256,2048]{1,0:T(8,128)(2,1)S(1)} %collective-permute-done.14, ...), kind=kOutput, calls=%fused_computation.15 | convolution fusion | flops 4325376000 | bytes 20971520 | tf_op jit(solution)/shard_map/dot_general | solution.py:1871
  462.2 14.1 %convolution_convert_fusion.1 = bf16[2048,2048]{1,0:T(8,128)(2,1)} fusion(bf16[1024,1024]{1,0:T(8,128)(2,1)} %get-tuple-element.104, bf16[1024,1024]{1,0:T(8,128)(2,1)} %get-tuple-element.105, bf16[256,2048]{1,0:T(8,128)(2,1)} %collective-permute-done.6, bf16[256,2048]{1,0:T(8,128)(2,1)S(1)} %copy-done.48, bf16[256,2048]{1,0:T(8,128)(2,1)S(1)} %copy-done.50, ...), kind=kOutput, calls=%fused_computation.1 | convolution fusion | flops 8619294720 | bytes 16777216 | tf_op jit(solution)/shard_map/dot_general | solution.py:1868
  491.0 7.8 convolution_convert_fusion.3
  498.8 9.7 %collective-permute-done.18 = bf16[256,2048]{1,0:T(8,128)(2,1)} collective-permute-done((bf16[256,2048]{1,0:T(8,128)(2,1)}, bf16[256,2048]{1,0:T(8,128)(2,1)}, u32[]{:S(2)}, u32[]{:S(2)}) %collective-permute-start.18) | collective-permute-done | bytes 1048608 | tf_op jit(solution)/shard_map/ppermute | solution.py:641
  518.8 22.1 %collective-permute-done.20 = bf16[256,2048]{1,0:T(8,128)(2,1)S(1)} collective-permute-done((bf16[256,2048]{1,0:T(8,128)(2,1)S(1)}, bf16[256,2048]{1,0:T(8,128)(2,1)S(1)}, u32[]{:S(2)}, u32[]{:S(2)}) %collective-permute-start.20) | collective-permute-done | bytes 1048608 | tf_op jit(solution)/shard_map/ppermute | solution.py:641
  552.4 9.3 fusion.25.grad_ref
  561.8 37.1 %reduce-scatter.4.cloned.1.call-done = bf16[512,2048]{1,0:T(8,128)(2,1)} async-done(((bf16[2048,2048]{1,0:T(8,128)(2,1)}), bf16[512,2048]{1,0:T(8,128)(2,1)}) %reduce-scatter.4.cloned.1.call-update) | async-done | bytes 2097168 | tf_op jit(solution)/shard_map/reduce_scatter | solution.py:1646
  602.3 12.0 %shard_map.333 = (bf16[1024,256]{1,0:T(8,128)(2,1)}, bf16[1024,256]{1,0:T(8,128)(2,1)}) custom-call(s32[4]{0:T(128)} %fusion.57.order, f32[1024,1920]{1,0:T(8,128)} %fusion.75.q_ref.gate_ref.inner_ref.step_ref.before_ref, f32[1024,768]{1,0:T(8,128)} %fusion.72.kv_ref.bc_ref.bcbefore_ref, f32[1024,128]{1,0:T(8,128)} %get-tuple-element.123.cos_ref.all_cos, ...), custom_call_target="tpu_custom_call" | custom-call | flops 2147483648 | bytes 5242880 | tf_op jit(solution)/shard_map/pallas_call | solution.py:442
  614.3 33.1 %shard_map.334 = (bf16[1024,1920]{1,0:T(8,128)(2,1)}, bf16[1024,768]{1,0:T(8,128)(2,1)}, f32[8,768]{1,0:T(8,128)}, f32[8,512]{1,0:T(8,128)}, f32[8,128]{1,0:T(8,128)}) custom-call(s32[4]{0:T(128)} %fusion.57.order, f32[1024,1920]{1,0:T(8,128)} %fusion.75.q_ref.gate_ref.inner_ref.step_ref.before_ref, ...), custom_call_target="tpu_custom_call" | custom-call | flops 8053063680 | bytes 31457280 | tf_op jit(solution)/shard_map/pallas_call | solution.py:549
  685.4 11.1 %convolution_convert_fusion.part_ref = bf16[2048,1920]{1,0:T(8,128)(2,1)} fusion(bf16[1024,2048]{1,0:T(8,128)(2,1)S(1)} %copy-done.10, bf16[1024,1920]{1,0:T(8,128)(2,1)S(1)} %copy-done.42), kind=kOutput, calls=%fused_computation | convolution fusion | flops 8056995840 | bytes 15990784 | tf_op jit(solution)/shard_map/dot_general | solution.py:1868
  702.1 8.1 reduce-scatter.8.cloned.1.call-done
  727.5 173.2 %shard_map.335 = (f32[256,1920]{1,0:T(8,128)}, f32[64,1024]{1,0:T(8,128)}, f32[256,2048]{1,0:T(8,128)}, f32[176,128]{1,0:T(8,128)}) custom-call(bf16[2048,1920]{1,0:T(8,128)(2,1)} %convolution_convert_fusion.part_ref, bf16[2048,512]{1,0:T(8,128)(2,1)} %convolution_convert_fusion.4.bc_ref, bf16[2048,256]{1,0:T(8,128)(2,1)} %convolution_convert_fusion.5.kv_ref, ...), custom_call_target="tpu_custom_call" | custom-call | flops 10485760 | bytes 300000000 | tf_op jit(solution)/shard_map/pallas_call | solution.py:1553
  (316 shorter events, 236.5 us)
Async XLA Ops:
  7.2 258.1 %all-gather.4.cloned.1.call-start = ((), (), s32[]{:S(2)}) async-start(), calls=%async_computation.3 | async-start | bytes 5242880 | tf_op jit(solution)/shard_map/all_gather | solution.py:1642
  138.0 192.7 %all-gather.6.cloned.1.call-start = ((), (), s32[]{:S(2)}) async-start(), calls=%async_computation.4 | async-start | bytes 10485760 | tf_op jit(solution)/shard_map/all_gather | solution.py:1642
  140.0 70.3 %collective-permute-start.7 = (bf16[256,3072]{1,0:T(8,128)(2,1)S(1)}, bf16[256,3072]{1,0:T(8,128)(2,1)}, u32[]{:S(2)}, u32[]{:S(2)}) collective-permute-start(bf16[256,3072]{1,0:T(8,128)(2,1)S(1)} %pad_maximum_fusion.6), channel_id=1, source_target_pairs={{0,2},{1,3},{2,6},{3,7},{4,0},{5,1},{6,4},{7,5},{8,10},{9,11},{10,... | collective-permute-start | bytes 4718600 | tf_op jit(solution)/shard_map/ppermute | solution.py:641
  140.5 70.5 %collective-permute-start.8 = (bf16[256,3072]{1,0:T(8,128)(2,1)S(1)}, bf16[256,3072]{1,0:T(8,128)(2,1)}, u32[]{:S(2)}, u32[]{:S(2)}) collective-permute-start(bf16[256,3072]{1,0:T(8,128)(2,1)S(1)} %pad_maximum_fusion.6), channel_id=1, source_target_pairs={{2,4},{3,5},{4,2},{5,3},{10,12},{11,13},{12,10},{13,11},{18,20},{1... | collective-permute-start | bytes 4718600 | tf_op jit(solution)/shard_map/ppermute | solution.py:641
  215.8 141.3 %all-gather.8.cloned.1.call-start = ((), (), s32[]{:S(2)}) async-start(), calls=%async_computation.5 | async-start | bytes 5242880 | tf_op jit(solution)/shard_map/all_gather | solution.py:1642
  215.9 32.2 %collective-permute-start = (f32[3876]{0:T(1024)S(1)}, f32[3876]{0:T(1024)S(1)}, u32[]{:S(2)}, u32[]{:S(2)}) collective-permute-start(f32[3876]{0:T(1024)S(1)} %concatenate.56), channel_id=1, source_target_pairs={{2,4},{3,5},{4,2},{5,3},{10,12},{11,13},{12,10},{13,11},{18,20},{1... | collective-permute-start | bytes 46520 | tf_op jit(solution)/shard_map/ppermute | solution.py:641
  274.3 25.9 %collective-permute-start.3 = (bf16[256,2048]{1,0:T(8,128)(2,1)}, bf16[256,2048]{1,0:T(8,128)(2,1)}, u32[]{:S(2)}, u32[]{:S(2)}) collective-permute-start(bf16[256,2048]{1,0:T(8,128)(2,1)} %add_convert_fusion.2), channel_id=1, source_target_pairs={{0,1},{1,0},{2,3},{3,2},{4,5},{5,4},{6,7},{7,6},{8,9},{9,8},{10,11... | collective-permute-start | bytes 3145736 | tf_op jit(solution)/shard_map/ppermute | solution.py:641
  277.7 321.1 %reduce-scatter.4.cloned.1.call-start = ((), (), s32[]{:S(2)}) async-start(), calls=%async_computation.6 | async-start | bytes 10485760 | tf_op jit(solution)/shard_map/reduce_scatter | solution.py:1646
  302.6 23.9 %collective-permute-start.5 = (bf16[256,2048]{1,0:T(8,128)(2,1)S(1)}, bf16[256,2048]{1,0:T(8,128)(2,1)S(1)}, u32[]{:S(2)}, u32[]{:S(2)}) collective-permute-start(bf16[256,2048]{1,0:T(8,128)(2,1)S(1)} %multiply_convert_fusion.3), channel_id=1, source_target_pairs={{0,1},{1,0},{2,3},{3,2},{4,5},{5,4},{6,7},{7,6},{8,9},{9,8},{10,11... | collective-permute-start | bytes 3145736 | tf_op jit(solution)/shard_map/ppermute | solution.py:641
  303.8 24.4 %collective-permute-start.4 = (bf16[256,2048]{1,0:T(8,128)(2,1)S(1)}, bf16[256,2048]{1,0:T(8,128)(2,1)S(1)}, u32[]{:S(2)}, u32[]{:S(2)}) collective-permute-start(bf16[256,2048]{1,0:T(8,128)(2,1)S(1)} %multiply_convert_fusion.3), channel_id=1, source_target_pairs={{0,4},{1,5},{2,6},{3,7},{4,0},{5,1},{6,2},{7,3},{8,12},{9,13},{10,... | collective-permute-start | bytes 3145736 | tf_op jit(solution)/shard_map/ppermute | solution.py:641
  361.6 28.6 %collective-permute-start.12 = (bf16[256,2048]{1,0:T(8,128)(2,1)S(1)}, bf16[256,2048]{1,0:T(8,128)(2,1)}, u32[]{:S(2)}, u32[]{:S(2)}) collective-permute-start(bf16[256,2048]{1,0:T(8,128)(2,1)S(1)} %copy-done.22), channel_id=1, source_target_pairs={{2,4},{3,5},{4,2},{5,3},{10,12},{11,13},{12,10},{13,11},{18,20},{1... | collective-permute-start | bytes 3145736 | tf_op jit(solution)/shard_map/ppermute | solution.py:641
  370.5 19.7 %collective-permute-start.9 = (bf16[256,2048]{1,0:T(8,128)(2,1)}, bf16[256,2048]{1,0:T(8,128)(2,1)}, u32[]{:S(2)}, u32[]{:S(2)}) collective-permute-start(bf16[256,2048]{1,0:T(8,128)(2,1)} %convolution_convert_fusion.7), channel_id=1, source_target_pairs={{0,4},{1,5},{2,6},{3,7},{4,0},{5,1},{6,2},{7,3},{8,12},{9,13},{10,... | collective-permute-start | bytes 3145736 | tf_op jit(solution)/shard_map/ppermute | solution.py:641
  372.8 35.0 %collective-permute-start.11 = (bf16[256,2048]{1,0:T(8,128)(2,1)}, bf16[256,2048]{1,0:T(8,128)(2,1)}, u32[]{:S(2)}, u32[]{:S(2)}) collective-permute-start(bf16[256,2048]{1,0:T(8,128)(2,1)} %add_convert_fusion.1), channel_id=1, source_target_pairs={{0,1},{1,0},{2,3},{3,2},{4,5},{5,4},{6,7},{7,6},{8,9},{9,8},{10,11... | collective-permute-start | bytes 3145736 | tf_op jit(solution)/shard_map/ppermute | solution.py:641
  413.8 24.0 %collective-permute-start.14 = (bf16[256,2048]{1,0:T(8,128)(2,1)S(1)}, bf16[256,2048]{1,0:T(8,128)(2,1)S(1)}, u32[]{:S(2)}, u32[]{:S(2)}) collective-permute-start(bf16[256,2048]{1,0:T(8,128)(2,1)S(1)} %convert_element_type.163), channel_id=1, source_target_pairs={{0,1},{1,0},{2,3},{3,2},{4,5},{5,4},{6,7},{7,6},{8,9},{9,8},{10,11... | collective-permute-start | bytes 3145736 | tf_op jit(solution)/shard_map/ppermute | solution.py:641
  413.8 25.6 %collective-permute-start.13 = (bf16[256,2048]{1,0:T(8,128)(2,1)S(1)}, bf16[256,2048]{1,0:T(8,128)(2,1)S(1)}, u32[]{:S(2)}, u32[]{:S(2)}) collective-permute-start(bf16[256,2048]{1,0:T(8,128)(2,1)S(1)} %convert_element_type.163), channel_id=1, source_target_pairs={{0,4},{1,5},{2,6},{3,7},{4,0},{5,1},{6,2},{7,3},{8,12},{9,13},{10,... | collective-permute-start | bytes 3145736 | tf_op jit(solution)/shard_map/ppermute | solution.py:641
  458.2 40.6 %collective-permute-start.16 = (bf16[256,2048]{1,0:T(8,128)(2,1)}, bf16[256,2048]{1,0:T(8,128)(2,1)}, u32[]{:S(2)}, u32[]{:S(2)}) collective-permute-start(bf16[256,2048]{1,0:T(8,128)(2,1)} %convolution_convert_fusion.11), channel_id=1, source_target_pairs={{0,4},{1,5},{2,6},{3,7},{4,0},{5,1},{6,2},{7,3},{8,12},{9,13},{10,... | collective-permute-start | bytes 3145736 | tf_op jit(solution)/shard_map/ppermute | solution.py:641
  483.7 24.7 %collective-permute-start.18 = (bf16[256,2048]{1,0:T(8,128)(2,1)}, bf16[256,2048]{1,0:T(8,128)(2,1)}, u32[]{:S(2)}, u32[]{:S(2)}) collective-permute-start(bf16[256,2048]{1,0:T(8,128)(2,1)} %add_convert_fusion), channel_id=1, source_target_pairs={{0,1},{1,0},{2,3},{3,2},{4,5},{5,4},{6,7},{7,6},{8,9},{9,8},{10,11... | collective-permute-start | bytes 3145736 | tf_op jit(solution)/shard_map/ppermute | solution.py:641
  512.4 184.2 %reduce-scatter.6.cloned.1.call-start = ((), (), s32[]{:S(2)}) async-start(), calls=%async_computation.7 | async-start | bytes 5242880 | tf_op jit(solution)/shard_map/reduce_scatter | solution.py:1646
  517.3 23.6 %collective-permute-start.20 = (bf16[256,2048]{1,0:T(8,128)(2,1)S(1)}, bf16[256,2048]{1,0:T(8,128)(2,1)S(1)}, u32[]{:S(2)}, u32[]{:S(2)}) collective-permute-start(bf16[256,2048]{1,0:T(8,128)(2,1)S(1)} %get-tuple-element.100), channel_id=1, source_target_pairs={{0,1},{1,0},{2,3},{3,2},{4,5},{5,4},{6,7},{7,6},{8,9},{9,8},{10,11... | collective-permute-start | bytes 3145736 | tf_op jit(solution)/shard_map/ppermute | solution.py:641
  517.3 25.6 %collective-permute-start.19 = (bf16[256,2048]{1,0:T(8,128)(2,1)S(1)}, bf16[256,2048]{1,0:T(8,128)(2,1)S(1)}, u32[]{:S(2)}, u32[]{:S(2)}) collective-permute-start(bf16[256,2048]{1,0:T(8,128)(2,1)S(1)} %get-tuple-element.100), channel_id=1, source_target_pairs={{0,4},{1,5},{2,6},{3,7},{4,0},{5,1},{6,2},{7,3},{8,12},{9,13},{10,... | collective-permute-start | bytes 3145736 | tf_op jit(solution)/shard_map/ppermute | solution.py:641
  598.9 111.4 %reduce-scatter.8.cloned.1.call-start = ((), (), s32[]{:S(2)}) async-start(), calls=%async_computation.8 | async-start | bytes 5242880 | tf_op jit(solution)/shard_map/reduce_scatter | solution.py:1646
  650.9 261.3 %collective-permute-start.22 = (bf16[256,2048]{1,0:T(8,128)(2,1)}, bf16[256,2048]{1,0:T(8,128)(2,1)S(1)}, u32[]{:S(2)}, u32[]{:S(2)}) collective-permute-start(bf16[256,2048]{1,0:T(8,128)(2,1)} %get-tuple-element.57), channel_id=1, source_target_pairs={{2,4},{3,5},{4,2},{5,3},{10,12},{11,13},{12,10},{13,11},{18,20},{1... | collective-permute-start | bytes 3145736 | tf_op jit(solution)/shard_map/ppermute | solution.py:641
  717.3 195.9 %collective-permute-start.23 = (bf16[256,4096]{1,0:T(8,128)(2,1)}, bf16[256,4096]{1,0:T(8,128)(2,1)}, u32[]{:S(2)}, u32[]{:S(2)}) collective-permute-start(bf16[256,4096]{1,0:T(8,128)(2,1)} %get-tuple-element.96), channel_id=1, source_target_pairs={{0,4},{1,5},{2,0},{3,1},{4,6},{5,7},{6,2},{7,3},{8,12},{9,13},{10,... | collective-permute-start | bytes 6291464 | tf_op jit(solution)/shard_map/ppermute | solution.py:641
  719.4 193.8 %collective-permute-start.24 = (bf16[256,4096]{1,0:T(8,128)(2,1)}, bf16[256,4096]{1,0:T(8,128)(2,1)}, u32[]{:S(2)}, u32[]{:S(2)}) collective-permute-start(bf16[256,4096]{1,0:T(8,128)(2,1)} %get-tuple-element.97), channel_id=1, source_target_pairs={{2,4},{3,5},{4,2},{5,3},{10,12},{11,13},{12,10},{13,11},{18,20},{1... | collective-permute-start | bytes 6291464 | tf_op jit(solution)/shard_map/ppermute | solution.py:641
  (78 other events, 1030.7 us)
Sparse Core Ops, SparseCore 0:
  138.1 51.9 all-gather.3
  215.9 86.0 all-gather.5
  304.4 52.6 all-gather.7
  512.6 86.2 reduce-scatter.3
  601.9 52.7 reduce-scatter.5
  657.5 52.6 reduce-scatter.7

commit v4 on v3

--- a/solution.py
+++ b/solution.py
@@ -1151,6 +1151,529 @@
     )(in_pack, out_pack, shared, layer_in, gain.reshape(1, -1))
 
 
+class Stage:
+    def __init__(self, lanes, src, full, rows, cols, chunks, sems):
+        self.lanes, self.src, self.full, self.rows, self.cols = lanes, src, full, rows, cols
+        self.chunks = chunks
+        self.piece = rows // chunks
+        self.send_sems, self.recv_sems, self.home_sems, ssem, rsem = sems
+        self.spread = Spread(lanes, full, rows, chunks, ssem, rsem, cols)
+
+    def view(self, half, chunk):
+        start = self.lanes.k * (2 * self.rows) + half * self.rows + chunk * self.piece
+        return self.full.at[pl.ds(pl.multiple_of(start, self.piece), self.piece), self.cols]
+
+    def part(self, chunk):
+        return self.src.at[pl.ds(chunk * self.piece, self.piece), self.cols]
+
+    def own(self, chunk):
+        return pltpu.make_async_copy(
+            self.part(chunk), self.view(self.lanes.c, chunk), self.home_sems.at[chunk]
+        )
+
+    def first(self, chunk, device):
+        c = self.lanes.c
+        return remote(
+            self.part(chunk),
+            self.view(c, chunk),
+            self.send_sems.at[0, chunk],
+            self.recv_sems.at[c, chunk],
+            device,
+        )
+
+    def second(self, chunk):
+        c = self.lanes.c
+        return remote(
+            self.part(chunk),
+            self.view(c, chunk),
+            self.send_sems.at[1, chunk],
+            self.recv_sems.at[c, chunk],
+            (self.lanes.other, self.lanes.far),
+        )
+
+    def start(self):
+        lanes = self.lanes
+
+        @pl.when(lanes.home)
+        def _():
+            for chunk in range(self.chunks):
+                self.own(chunk).start()
+                self.first(chunk, (lanes.d, lanes.far)).start()
+
+        @pl.when(lanes.away)
+        def _():
+            for chunk in range(self.chunks):
+                self.first(chunk, (lanes.other, lanes.t)).start()
+                self.second(chunk).start()
+
+    def came(self, half, chunk):
+        view = self.view(half, chunk)
+        remote(
+            view,
+            view,
+            self.send_sems.at[0, chunk],
+            self.recv_sems.at[half, chunk],
+            (self.lanes.other, self.lanes.t),
+        ).wait_recv()
+
+    def give(self, chunk):
+        for half in range(2):
+            self.spread.give(0, half, chunk)
+
+    def arrive_home(self, chunk):
+        self.own(chunk).wait()
+        self.came(1 - self.lanes.c, chunk)
+        self.give(chunk)
+
+    def arrive_away(self, chunk):
+        for half in range(2):
+            self.came(half, chunk)
+        self.give(chunk)
+
+    def settle(self, place):
+        for half in range(2):
+            if not onward(place, half, self.lanes.bits):
+                for chunk in range(self.chunks):
+                    self.spread.take(place, half, chunk)
+
+    def finish(self):
+        lanes = self.lanes
+        for chunk in range(self.chunks):
+            for half in range(2):
+                for place in range(lanes.blocks):
+                    for bit in onward(place, half, lanes.bits):
+                        self.spread.copy(place, half, chunk, bit).wait_send()
+
+        @pl.when(lanes.home)
+        def _():
+            for chunk in range(self.chunks):
+                self.first(chunk, (lanes.d, lanes.far)).wait_send()
+
+        @pl.when(lanes.away)
+        def _():
+            for chunk in range(self.chunks):
+                self.first(chunk, (lanes.other, lanes.t)).wait_send()
+                self.second(chunk).wait_send()
+
+
+class Exchange:
+    def __init__(self, lanes, work, own, sends, recvs, ssem, rsem):
+        self.lanes, self.work, self.own = lanes, work, own
+        self.both_s, self.core_s, self.pass_s = sends
+        self.both_r, self.core_r, self.far_r = recvs
+        self.ssem, self.rsem = ssem, rsem
+        self.blocks, self.here, self.block = own.shape
+        self.step = min(self.here, 64)
+
+    def copies(self, index, place):
+        core, near = (self.lanes.other, self.lanes.t), (self.lanes.d, self.lanes.near)
+        table = (
+            (self.both_s, self.both_r, core),
+            (self.core_s, self.core_r, core),
+            (self.pass_s, self.far_r, near),
+        )
+
+        def copy(kind):
+            src, dst, device = table[kind]
+            return remote(
+                src.at[index], dst.at[index], self.ssem.at[kind, place], self.rsem.at[kind, place],
+                device,
+            )
+
+        return copy
+
+    def columns(self, place):
+        return slice(place * self.block, (place + 1) * self.block)
+
+    def rows(self, piece, i):
+        start = piece * self.here + i * self.step
+        return pl.ds(pl.multiple_of(start, self.step), self.step)
+
+    def give(self, index, place, left, weight):
+        bf16 = jnp.bfloat16
+        cols = self.columns(place)
+
+        @pl.loop(0, 4)
+        def _(piece):
+            rows = pl.ds(pl.multiple_of(piece * self.here, self.here), self.here)
+            self.work[rows, cols] = low_dot(left[rows, :], weight(), NT)
+
+        @pl.loop(0, self.here // self.step)
+        def _(i):
+            part = self.rows(0, i)
+            self.both_s[index, part, :] = self.work[self.rows(3, i), cols].astype(bf16)
+            self.core_s[index, part, :] = self.work[self.rows(1, i), cols].astype(bf16)
+            self.own[index, part, :] = self.work[part, cols]
+
+        copy = self.copies(index, place)
+        copy(0).start()
+        copy(1).start()
+
+    def pass_on(self, index, place):
+        copy = self.copies(index, place)
+        copy(0).wait_recv()
+        cols = self.columns(place)
+
+        @pl.loop(0, self.here // self.step)
+        def _(i):
+            part = self.rows(0, i)
+            total = self.work[self.rows(2, i), cols] + self.both_r[index, part, :].astype(
+                jnp.float32
+            )
+            self.pass_s[index, part, :] = total.astype(jnp.bfloat16)
+
+        copy(2).start()
+
+    def take(self, index, place):
+        copy = self.copies(index, place)
+        copy(1).wait_recv()
+        copy(2).wait_recv()
+
+    def total(self, index, rows):
+        f32 = jnp.float32
+        return (
+            self.own[index, rows, :]
+            + self.core_r[index, rows, :].astype(f32)
+            + self.far_r[index, rows, :].astype(f32)
+        )
+
+    def finish(self, index, place):
+        copy = self.copies(index, place)
+        for kind in range(3):
+            copy(kind).wait_send()
+
+
+def middle_body(
+    blocks, gu_chunks, down_chunks,
+    ff_ref, heads_ref, out_ref, x_ref, gain_ref, target_ref, live_ref,
+    full_ref, mid_ref, gate_ref, up_ref, hidden_ref, grads_ref, resid_ref, error_ref, low_ref,
+    loss_ref,
+    wbuf, mid_s, acc_s, hid_s, gate_s, up_s, own_s, both_s, core_s, pass_s,
+    both_r, core_r, far_r, both_q, core_q, far_q, err_s,
+    w_sems, one_s, one_r, two_s, two_r, mid_ssem, mid_rsem, err_ssem, err_rsem, keep_sems,
+    gz_s, gz_r, g_home, g_s, g_r, dz_s, dz_r, d_home, d_s, d_r,
+):
+    f32, bf16 = jnp.float32, jnp.bfloat16
+    lanes = Lanes(blocks)
+    rows = ff_ref.shape[0]
+    here = x_ref.shape[0]
+    block = 2 * rows
+    inner = heads_ref.shape[1]
+    hidden_width = hid_s.shape[1]
+    core_at = (lanes.other, lanes.t)
+    near_at = (lanes.d, lanes.near)
+    lanes.greet()
+    gate_up = Stage(
+        lanes, ff_ref, full_ref, rows, slice(0, 2 * hidden_width), gu_chunks,
+        (gz_s, gz_r, g_home, g_s, g_r),
+    )
+    down = Stage(
+        lanes, ff_ref, full_ref, rows, slice(2 * hidden_width, 3 * hidden_width), down_chunks,
+        (dz_s, dz_r, d_home, d_s, d_r),
+    )
+    sends = (both_s, core_s, pass_s)
+    one = Exchange(lanes, acc_s, own_s, sends, (both_r, core_r, far_r), one_s, one_r)
+    two = Exchange(lanes, acc_s, own_s, sends, (both_q, core_q, far_q), two_s, two_r)
+
+    def load(src, slot, width, cols):
+        return pltpu.make_async_copy(src, wbuf.at[slot, :, cols], w_sems.at[slot])
+
+    def out_load(index):
+        return load(
+            out_ref.at[pl.ds(index * block, block), :], index % 2, inner, pl.ds(0, inner)
+        )
+
+    gate_up.start()
+    out_load(0).start()
+    down.start()
+
+    for index in range(blocks):
+        if index + 1 < blocks:
+            out_load(index + 1).start()
+        out_load(index).wait()
+        one.give(index, index, heads_ref, lambda: wbuf[index % 2, :, :inner])
+        if index == 0:
+
+            @pl.when(lanes.home)
+            def _():
+                for chunk in range(gu_chunks):
+                    gate_up.arrive_home(chunk)
+
+    for index in range(blocks):
+        one.pass_on(index, index)
+
+    @pl.when(lanes.away)
+    def _():
+        for chunk in range(gu_chunks):
+            gate_up.arrive_away(chunk)
+            if chunk:
+                gate_up.spread.pass_on(chunk - 1)
+
+    @pl.when(lanes.home)
+    def _():
+        for chunk in range(gu_chunks - 1):
+            gate_up.spread.pass_on(chunk)
+
+    for index in range(blocks):
+        one.take(index, index)
+
+    step = min(here, 32)
+
+    def columns(index):
+        return slice(index * block, (index + 1) * block)
+
+    @pl.loop(0, here // step)
+    def _(i):
+        part = pl.ds(pl.multiple_of(i * step, step), step)
+        total = jnp.zeros((step, 1), f32)
+        for index in range(blocks):
+            resid = x_ref[part, columns(index)].astype(f32) + one.total(index, part)
+            resid_ref[part, columns(index)] = resid
+            total = total + jnp.sum(resid * resid, axis=1, keepdims=True)
+        scale = lax.rsqrt(total / (blocks * block) + EPS)
+        for index in range(blocks):
+            mid = resid_ref[part, columns(index)] * scale * gain_ref[:, columns(index)]
+            mid_s[index, part, :] = mid.astype(bf16)
+
+    def mid_view(slot):
+        return mid_s.at[:, pl.ds(slot * here, here), :]
+
+    def mid_near():
+        return remote(mid_view(0), mid_view(2), mid_ssem.at[0], mid_rsem.at[0], near_at)
+
+    def mid_core():
+        return remote(mid_view(0), mid_view(1), mid_ssem.at[1], mid_rsem.at[1], core_at)
+
+    def mid_both():
+        return remote(mid_view(2), mid_view(3), mid_ssem.at[2], mid_rsem.at[2], core_at)
+
+    mid_near().start()
+    mid_core().start()
+    gate_up.spread.pass_on(gu_chunks - 1)
+
+    @pl.when(lanes.home)
+    def _():
+        for chunk in range(down_chunks):
+            down.arrive_home(chunk)
+
+    @pl.when(lanes.away)
+    def _():
+        for chunk in range(down_chunks):
+            down.arrive_away(chunk)
+
+    def gu_load(place, slot):
+        start = lanes.block(place) * block
+        view = full_ref.at[pl.ds(pl.multiple_of(start, block), block), pl.ds(0, 2 * hidden_width)]
+        return load(view, slot, 2 * hidden_width, pl.ds(0, 2 * hidden_width))
+
+    def down_load(place, slot):
+        start = lanes.block(place) * block
+        view = full_ref.at[
+            pl.ds(pl.multiple_of(start, block), block), pl.ds(2 * hidden_width, hidden_width)
+        ]
+        return load(view, slot, hidden_width, pl.ds(0, hidden_width))
+
+    gu_load(0, 0).start()
+    mid_near().wait_recv()
+    mid_both().start()
+    mid_core().wait_recv()
+
+    wide = 2 * hidden_width
+    tile = min(wide, 512)
+
+    def accumulate(place, first, last):
+        slot = place % 2
+        index = lanes.block(place)
+
+        @pl.loop(first, last)
+        def _(piece):
+            part = pl.ds(pl.multiple_of(piece * here, here), here)
+            left = mid_s[index, part, :]
+            for col in range(0, wide, tile):
+                cols = slice(col, col + tile)
+                product = low_dot(left, wbuf[slot, :, cols], NN)
+                if place:
+                    product = product + acc_s[part, cols]
+                acc_s[part, cols] = product
+
+    for place in range(blocks):
+        if place + 1 < blocks:
+            gate_up.settle(place + 1)
+            gu_load(place + 1, (place + 1) % 2).start()
+        gu_load(place, place % 2).wait()
+        accumulate(place, 0, 3)
+        if place == 0:
+            mid_both().wait_recv()
+        accumulate(place, 3, 4)
+        if place < down_chunks:
+            down.spread.pass_on(place)
+
+    for chunk in range(blocks, down_chunks):
+        down.spread.pass_on(chunk)
+
+    down_load(0, 0).start()
+
+    @pl.loop(0, 4 * here // step)
+    def _(i):
+        part = pl.ds(pl.multiple_of(i * step, step), step)
+        gate = acc_s[part, :hidden_width]
+        up = acc_s[part, hidden_width : 2 * hidden_width]
+        gate_s[part, :] = gate.astype(bf16)
+        up_s[part, :] = up.astype(bf16)
+        hid_s[part, :] = (gate * sigmoid(gate) * up).astype(bf16)
+
+    kept = [
+        pltpu.make_async_copy(hid_s, hidden_ref, keep_sems.at[0]),
+        pltpu.make_async_copy(gate_s, gate_ref, keep_sems.at[1]),
+        pltpu.make_async_copy(up_s, up_ref, keep_sems.at[2]),
+    ] + [
+        pltpu.make_async_copy(
+            mid_s.at[index], mid_ref.at[:, pl.ds(index * block, block)], keep_sems.at[3 + index]
+        )
+        for index in range(blocks)
+    ]
+    for copy in kept:
+        copy.start()
+    for index in range(blocks):
+        one.finish(index, index)
+
+    for place in range(blocks):
+        index = lanes.block(place)
+        if place + 1 < blocks:
+            down.settle(place + 1)
+            down_load(place + 1, (place + 1) % 2).start()
+        down_load(place, place % 2).wait()
+        two.give(index, place, hid_s, lambda: wbuf[place % 2, :, :hidden_width])
+        if place:
+            two.pass_on(lanes.block(place - 1), place - 1)
+    two.pass_on(lanes.block(blocks - 1), blocks - 1)
+    for place in range(blocks):
+        two.take(lanes.block(place), place)
+
+    def output_part(i, loss):
+        part = pl.ds(pl.multiple_of(i * step, step), step)
+        live = live_ref[part, :]
+        for index in range(blocks):
+            cols = columns(index)
+            outputs = resid_ref[part, cols] + two.total(index, part)
+            low_ref[part, cols] = outputs.astype(bf16)
+            error = (outputs - target_ref[part, cols].astype(f32)) * live
+            error_ref[part, cols] = error
+            err_s[part, cols] = error.astype(bf16)
+            loss = loss + jnp.sum(error * error)
+        return loss
+
+    loss = lax.fori_loop(0, here // step, output_part, jnp.zeros((), f32))
+    loss_ref[...] = jnp.zeros((8, WIDE), f32) + 0.5 * loss
+
+    def grads_view(slot):
+        return grads_ref.at[pl.ds(slot * here, here), :]
+
+    def err_near():
+        return remote(err_s, grads_view(2), err_ssem.at[0], err_rsem.at[0], near_at)
+
+    def err_core():
+        return remote(err_s, grads_view(1), err_ssem.at[1], err_rsem.at[1], core_at)
+
+    def err_both():
+        return remote(grads_view(2), grads_view(3), err_ssem.at[2], err_rsem.at[2], core_at)
+
+    own_err = pltpu.make_async_copy(err_s, grads_view(0), err_ssem.at[3])
+    err_near().start()
+    err_core().start()
+    own_err.start()
+    for copy in kept:
+        copy.wait()
+    gate_up.finish()
+    down.finish()
+    for place in range(blocks):
+        two.finish(lanes.block(place), place)
+    for copy in (mid_near(), mid_core(), mid_both()):
+        copy.wait_send()
+    err_near().wait_recv()
+    err_both().start()
+    err_core().wait_recv()
+    err_both().wait_recv()
+    own_err.wait()
+    for copy in (err_near(), err_core(), err_both()):
+        copy.wait_send()
+
+
+def middle(ff_pack, heads_all, out_all, x, gain, target, live, at):
+    f32, bf16 = jnp.float32, jnp.bfloat16
+    rows = ff_pack.shape[0]
+    hidden_width = ff_pack.shape[1] // 3
+    slot, inner = heads_all.shape
+    here, features = x.shape
+    blocks = at.blocks
+    block = 2 * rows
+    gu_chunks = 4 if rows >= 256 else 1
+    down_chunks = 2 if rows >= 256 else 1
+    dma = pltpu.SemaphoreType.DMA
+    vmem = pl.BlockSpec(memory_space=pltpu.VMEM)
+    anywhere = pl.BlockSpec(memory_space=pl.ANY)
+
+    def stage_sems(chunks):
+        return [
+            dma((2, chunks)),
+            dma((2, chunks)),
+            dma((chunks,)),
+            dma((2, blocks, chunks)),
+            dma((2, blocks, chunks)),
+        ]
+
+    shape = jax.ShapeDtypeStruct
+    buffers = [pltpu.VMEM((blocks, here, block), bf16)]
+    return pl.pallas_call(
+        functools.partial(middle_body, blocks, gu_chunks, down_chunks),
+        in_specs=[anywhere, vmem, anywhere, vmem, vmem, vmem, vmem],
+        out_specs=[anywhere] * 6 + [vmem] * 4,
+        out_shape=[
+            shape((features, 3 * hidden_width), bf16),
+            shape((slot, features), bf16),
+            shape((slot, hidden_width), bf16),
+            shape((slot, hidden_width), bf16),
+            shape((slot, hidden_width), bf16),
+            shape((slot, features), bf16),
+            shape((here, features), f32),
+            shape((here, features), f32),
+            shape((here, features), bf16),
+            shape((8, WIDE), f32),
+        ],
+        scratch_shapes=[
+            pltpu.VMEM((2, block, 2 * hidden_width), bf16),
+            pltpu.VMEM((blocks, slot, block), bf16),
+            pltpu.VMEM((slot, max(2 * hidden_width, features)), f32),
+            pltpu.VMEM((slot, hidden_width), bf16),
+            pltpu.VMEM((slot, hidden_width), bf16),
+            pltpu.VMEM((slot, hidden_width), bf16),
+            pltpu.VMEM((blocks, here, block), f32),
+        ]
+        + buffers * 9
+        + [
+            pltpu.VMEM((here, features), bf16),
+            dma((2,)),
+            dma((3, blocks)),
+            dma((3, blocks)),
+            dma((3, blocks)),
+            dma((3, blocks)),
+            dma((3,)),
+            dma((3,)),
+            dma((4,)),
+            dma((3,)),
+            dma((3 + blocks,)),
+        ]
+        + stage_sems(gu_chunks)
+        + stage_sems(down_chunks),
+        compiler_params=pltpu.CompilerParams(
+            collective_id=3, has_side_effects=True, vmem_limit_bytes=58 * 1024 * 1024
+        ),
+        cost_estimate=pl.CostEstimate(
+            flops=slot * features * hidden_width * 8, bytes_accessed=400_000_000, transcendentals=0
+        ),
+    )(ff_pack, heads_all, out_all, x, gain.reshape(1, -1), target, live)
+
+
 class Collect:
     def __init__(self, lanes, part, rows, cols, send_s, recv_s, load_s, total_s, sems):
         self.lanes, self.part, self.rows, self.cols = lanes, part, rows, cols
@@ -1184,7 +1707,7 @@
             source = self.source(place, half, chunk)
         return remote(
             source,
-            self.recv_s.at[half, place, :, self.cols[chunk]],
+            self.recv_s.at[half, place - 1, :, self.cols[chunk]],
             self.send_sems.at[half, place, chunk],
             self.recv_sems.at[half, place, chunk],
             self.lanes.across(self.bit_of(place, half)),
@@ -1212,7 +1735,7 @@
         for bit in onward(place, half, self.lanes.bits):
             came = place | (1 << bit)
             self.copy(came, half, chunk).wait_recv()
-            total = total + self.recv_s[half, came, :, cols].astype(jnp.float32)
+            total = total + self.recv_s[half, came - 1, :, cols].astype(jnp.float32)
         return total
 
     def middle(self, chunk):
@@ -1241,13 +1764,13 @@
 
 def back_body(
     blocks, in_cols, small_row, part_ref, bc_ref, kv_ref, own_ref, far_ref, core_ref, both_ref,
-    resid_ref, x_ref, gain_ref, small_ref,
-    gin_ref, gsh_ref, gx_ref, sum_ref,
+    resid_ref, x_ref, gain_ref, small_ref, out_ref,
+    gin_ref, gsh_ref, gx_ref, sum_ref, gout_ref,
     in_send, in_recv, in_load, in_total, settle_s, settle_r, sh_came, sh_part, sh_send, sh_recv,
     sh_load, sh_total, line_s, line_r, near_s, near_r, swap_s, swap_r,
     buf_both, buf_core, buf_far, pass_s, gx_s, gx_r, small_s, small_r,
     in_ssem, in_rsem, in_lsem, sh_ssem, sh_rsem, sh_lsem, set_ssem, set_rsem, misc_s, misc_r,
-    pass_ssem, pass_rsem, small_ssem, small_rsem,
+    pass_ssem, pass_rsem, small_ssem, small_rsem, out_r, out_ssem, out_rsem,
 ):
     f32, bf16 = jnp.float32, jnp.bfloat16
     lanes = Lanes(blocks)
@@ -1290,7 +1813,26 @@
     def send_bc():
         return remote(bc_ref, sh_came, misc_s.at[3], misc_r.at[3], core_at)
 
+    def out_block(half):
+        return out_ref.at[pl.ds(pl.multiple_of(half * rows, rows), rows), :]
+
+    def out_first(half, device):
+        return remote(out_block(half), out_r.at[0], out_ssem.at[0], out_rsem.at[0], device)
+
+    def out_second():
+        return remote(out_block(1 - c), out_r.at[1], out_ssem.at[1], out_rsem.at[1], cross_at)
+
     send_both().start()
+
+    @pl.when(lanes.home)
+    def _():
+        out_first(1 - c, core_at).start()
+
+    @pl.when(lanes.away)
+    def _():
+        out_first(c, far_at).start()
+        out_second().start()
+
     collect.start()
     for chunk in range(chunks):
         collect.direct(chunk)
@@ -1480,6 +2022,21 @@
             send_second(chunk).wait_recv()
             gin_ref[:, cols] = settle_r[0, :, cols].astype(f32) + settle_r[1, :, cols].astype(f32)
 
+    out_first(0, core_at).wait_recv()
+
+    @pl.when(lanes.home)
+    def _():
+        own_rows = pl.ds(pl.multiple_of(c * rows, rows), rows)
+        gout_ref[...] = out_ref[own_rows, :].astype(f32) + out_r[0].astype(f32)
+        out_first(1 - c, core_at).wait_send()
+
+    @pl.when(lanes.away)
+    def _():
+        out_second().wait_recv()
+        gout_ref[...] = out_r[0].astype(f32) + out_r[1].astype(f32)
+        out_first(c, far_at).wait_send()
+        out_second().wait_send()
+
     send_swap().wait_recv()
 
     @pl.when(first)
@@ -1532,7 +2089,7 @@
     send_swap().wait_send()
 
 
-def back(part_in, bc, kv, act_parts, grad_resid, x, gain, small, small_row, few, at):
+def back(part_in, bc, kv, act_parts, grad_resid, x, gain, small, small_row, raw_out, few, at):
     f32, bf16 = jnp.float32, jnp.bfloat16
     own, core, far, both = act_parts
     blocks = at.blocks
@@ -1552,17 +2109,19 @@
     line = 2 * few
     return pl.pallas_call(
         functools.partial(back_body, blocks, in_cols, small_row),
-        in_specs=[anywhere, vmem, vmem, vmem, vmem, anywhere, anywhere, vmem, vmem, vmem, vmem],
-        out_specs=[vmem] * 4,
+        in_specs=[anywhere, vmem, vmem, vmem, vmem, anywhere, anywhere]
+        + [vmem] * 5,
+        out_specs=[vmem] * 5,
         out_shape=[
             jax.ShapeDtypeStruct((rows, width), f32),
             jax.ShapeDtypeStruct((few, 2 * wide), f32),
             jax.ShapeDtypeStruct((here, features), f32),
             jax.ShapeDtypeStruct(small.shape, f32),
+            jax.ShapeDtypeStruct((rows, raw_out.shape[1]), f32),
         ],
         scratch_shapes=[
             pltpu.VMEM((loads, rows, width), bf16),
-            pltpu.VMEM((2, blocks, rows, width), bf16),
+            pltpu.VMEM((2, blocks - 1, rows, width), bf16),
             pltpu.VMEM((loads, rows, width), bf16),
             pltpu.VMEM((2, rows, width), f32),
             pltpu.VMEM((2, rows, width), bf16),
@@ -1570,7 +2129,7 @@
             pltpu.VMEM((features, wide), bf16),
             pltpu.VMEM((features, wide), bf16),
             pltpu.VMEM((loads, rows, wide), bf16),
-            pltpu.VMEM((2, blocks, rows, wide), bf16),
+            pltpu.VMEM((2, blocks - 1, rows, wide), bf16),
             pltpu.VMEM((loads, rows, wide), bf16),
             pltpu.VMEM((2, rows, wide), f32),
             pltpu.VMEM((2, line, wide), bf16),
@@ -1601,6 +2160,9 @@
             dma((parts,)),
             dma((steps,)),
             dma((steps,)),
+            pltpu.VMEM((2, rows, raw_out.shape[1]), bf16),
+            dma((2,)),
+            dma((2,)),
         ],
         compiler_params=pltpu.CompilerParams(
             collective_id=2, has_side_effects=True, vmem_limit_bytes=58 * 1024 * 1024
@@ -1610,6 +2172,7 @@
         ),
     )(
         part_in, bc, kv, own, far, core, both, grad_resid, x, gain.reshape(1, -1), small,
+        raw_out,
     )
 
 
@@ -1665,14 +2228,16 @@
     return gather_blocks(pair_weight(shard, at), at)
 
 
-def settle_weight(mine, at):
+def settle_weight(mine, later, at):
     f32 = jnp.float32
     rows = mine.shape[0] // 2
     low, high = mine[:rows], mine[rows:]
     own = jnp.where(at.c == 0, low, high)
     other = jnp.where(at.c == 0, high, low)
-    first_in = at.column_back(jnp.where(at.home, other, own)).astype(f32)
-    second_in = at.swap_away(other).astype(f32)
+    first_in = at.column_back(jnp.where(at.home, other, own))
+    second_in = at.swap_away(other)
+    first_in, second_in, own, _ = lax.optimization_barrier((first_in, second_in, own, later))
+    first_in, second_in = first_in.astype(f32), second_in.astype(f32)
     return first_in + jnp.where(at.home, own.astype(f32), second_in)
 
 
@@ -1806,7 +2371,7 @@
         axis=1,
     )
     out_pack = jnp.concatenate([mixer_out_weight, attn_out_weight], axis=1)
-    in_all, out_pair, act_all, inputs, shared_full = front(
+    in_all, out_pair, act_all, x_low, shared_full = front(
         in_pack, out_pack, shared_weight, layer_in, input_gain, at
     )
     left, right = shared_full[:, :bc_width], shared_full[:, bc_width:]
@@ -1820,54 +2385,40 @@
         ],
         axis=1,
     )
-    x_low = inputs
-    inputs = inputs.astype(f32)
 
     def row_split(values):
         return [values[i * rows_here : (i + 1) * rows_here] for i in range(at.tp)]
 
     out_all = gather_blocks(out_pair, at)
-    rest = jnp.concatenate(
-        [gate_up_weight.reshape(w_rows, 2 * hidden_width), down_weight], axis=1
-    )
-    rest = pair_weight(after(rest, act_all), at)
-    gate_up_all = gather_blocks(rest[:, : 2 * hidden_width], at)
-    down_all = gather_blocks(rest[:, 2 * hidden_width :], at)
     proj_shared = jnp.dot(act_all, shared_all, preferred_element_type=f32)
     proj = jnp.dot(act_all, in_all, preferred_element_type=f32)
-    target = relocate(after(teacher, proj), at).astype(f32)
+    target = relocate(after(teacher, proj), at)
     attn_low = attn_forward(order, proj, proj_shared, cosine, sine, query_width, width, bc_width)
     heads_all, y, states = mixer_forward(
         order, proj, proj_shared, attn_low, lane_params, conv_shared, head_params
     )
-    mix_parts = [
-        lax.dot_general(piece, out_all, contract_last, preferred_element_type=f32)
-        for piece in row_split(heads_all)
-    ]
-    resid = inputs + sum_rows(mix_parts, at)
-    normed_mid, norm_mid_back = jax.vjp(rms_norm, resid, middle_gain)
-    mid_all = jnp.concatenate(share_rows(normed_mid.astype(bf16), at), axis=0)
-    gate_up = jnp.dot(mid_all, gate_up_all, preferred_element_type=f32)
-    gate_val = gate_up[:, :hidden_width]
-    up_val = gate_up[:, hidden_width:]
-    sigmoid_gate = jax.nn.sigmoid(gate_val)
-    hidden = (gate_val * sigmoid_gate * up_val).astype(bf16)
-    mlp_parts = [
-        lax.dot_general(piece, down_all, contract_last, preferred_element_type=f32)
-        for piece in row_split(hidden)
-    ]
-    outputs = resid + sum_rows(mlp_parts, at)
+    ff_pack = jnp.concatenate(
+        [gate_up_weight.reshape(w_rows, 2 * hidden_width), down_weight], axis=1
+    )
     seq_len = lax.dynamic_index_in_dim(lengths, at.slot, keepdims=False)
     positions = at.quarter * rows_here + jnp.arange(rows_here)
-    live = (positions < seq_len).astype(f32)
-    error = (outputs - target) * live[:, None]
-    err_local = 0.5 * jnp.sum(error * error)
-
-    grad_all = jnp.concatenate(share_rows(error.astype(bf16), at), axis=0)
+    live = (positions < seq_len).astype(f32)[:, None]
+    ff_all, mid_all, gate_low, up_low, hidden, grad_all, resid, error, outputs, loss_part = middle(
+        ff_pack, heads_all, out_all, x_low, middle_gain, target, live, at
+    )
+    err_local = loss_part[0, 0]
+    _, norm_mid_back = jax.vjp(rms_norm, resid, middle_gain)
+    gate_up_all = ff_all[:, : 2 * hidden_width]
+    down_all = ff_all[:, 2 * hidden_width :]
+    gate_val, up_val = gate_low.astype(f32), up_low.astype(f32)
+    sigmoid_gate = jax.nn.sigmoid(gate_val)
+
     def weight_grad(left, right):
         return lax.dot_general(left, right, contract_first, preferred_element_type=f32).astype(bf16)
 
     part_down = weight_grad(grad_all, hidden)
+    grad_all, part_down = lax.optimization_barrier((grad_all, part_down))
+    raw_down = sum_blocks(part_down, at)
     grad_hidden = jnp.dot(grad_all, down_all, preferred_element_type=f32)
     grad_gate = grad_hidden * up_val * sigmoid_gate * (1.0 + gate_val * (1.0 - sigmoid_gate))
     grad_up = grad_hidden * gate_val * sigmoid_gate
@@ -1878,17 +2429,15 @@
     ]
     part_gate_up = weight_grad(mid_all, grad_gu)
     grad_mid = sum_rows(grad_mid_parts, at)
-    grad_mid, part_down, part_gate_up = lax.optimization_barrier((grad_mid, part_down, part_gate_up))
-    raw_down = sum_blocks(part_down, at)
+    grad_mid, part_gate_up = lax.optimization_barrier((grad_mid, part_gate_up))
     raw_gate_up = sum_blocks(part_gate_up, at)
     grad_resid_norm, grad_middle_gain = norm_mid_back(grad_mid)
     grad_resid = error + grad_resid_norm
     mix_grad_all = jnp.concatenate(share_rows(grad_resid.astype(bf16), at), axis=0)
     grad_heads = jnp.dot(mix_grad_all, out_all, preferred_element_type=f32)
     part_out = weight_grad(mix_grad_all, heads_all)
-    grad_heads, part_out = lax.optimization_barrier((grad_heads, part_out))
-    layer_out = relocate(after(outputs.astype(bf16), grad_heads), at)
-    raw_out = sum_blocks(after(part_out, raw_gate_up), at)
+    grad_heads, part_out, raw_down = lax.optimization_barrier((grad_heads, part_out, raw_down))
+    layer_out = relocate(after(outputs, grad_heads), at)
     dq, dkv = attn_backward(
         order, proj, proj_shared, cosine, sine, grad_heads, query_width, width, bc_width
     )
@@ -1896,6 +2445,10 @@
         order, proj, proj_shared, y, states, grad_heads, dq, dkv, lane_params, conv_shared,
         head_params, seg, query_width,
     )
+    low_pack, low_shared, raw_gate_up, part_out = lax.optimization_barrier(
+        (low_pack, low_shared, raw_gate_up, part_out)
+    )
+    raw_out = sum_blocks(part_out, at)
     column = at.column
     lanes_full = lax.dynamic_update_slice(
         jnp.zeros((KC + 1, DI), f32), dlane[: KC + 1], (0, column * width)
@@ -1928,13 +2481,11 @@
     part_bc = weight_grad(act_all, low_shared[:, :bc_width])
     part_kv = weight_grad(act_all, low_shared[:, bc_width:])
     part_in = weight_grad(act_all, low_pack)
-    grad_rest = settle_weight(jnp.concatenate([raw_out, raw_gate_up, raw_down], axis=1), at)
-    grad_in, grad_shared_weight, input_grad, flat = back(
+    grad_in, grad_shared_weight, input_grad, flat, grad_out = back(
         part_in, part_bc, part_kv, grad_act_parts, grad_resid, x_low, input_gain, flat, 0,
-        shared_weight.shape[0], at,
-    )
-    out_width = width + query_width
-    gate_up_to = out_width + 2 * hidden_width
+        raw_out, shared_weight.shape[0], at,
+    )
+    grad_ff = settle_weight(jnp.concatenate([raw_gate_up, raw_down], axis=1), grad_in, at)
     flat = flat.reshape(-1)
     sums = []
     start = 0
@@ -1962,11 +2513,11 @@
         heads_local[1],
         heads_local[2],
         lanes_local[KC],
-        grad_rest[:, :width],
-        grad_rest[:, width:out_width],
+        grad_out[:, :width],
+        grad_out[:, width:],
         sum_middle_gain,
-        grad_rest[:, out_width:gate_up_to].reshape(w_rows, 2, hidden_width),
-        grad_rest[:, gate_up_to:],
+        grad_ff[:, : 2 * hidden_width].reshape(w_rows, 2, hidden_width),
+        grad_ff[:, 2 * hidden_width :],
     )
 
 

time: 944 us -> 828 us (0.88)
  waiting for transfers between devices: 251 us -> 35 us
  Pallas kernels: 359 us -> 535 us
  matrix products: 169 us -> 135 us
  other arithmetic: 42.7 us -> 23.2 us
  starting transfers between devices: 34.7 us -> 19.7 us
    pallas_call x0 -> x1, Pallas kernels: none -> 190 us  [middle(): pl.pallas_call(functools.partial(middle_body, blocks, gu_chunks, down_chu...]
    ppermute x25 -> x11, waiting for transfers between devices: 198 us -> 31.3 us  [send(): return lax.ppermute(values, ('dp', 'tensor'), self.pairs(where_to))]
    reduce_scatter x3, waiting for transfers between devices: 45.1 us -> 3.64 us  [sum_blocks(): lax.psum_scatter(values, 'dp', scatter_dimension=0, tiled=True, axis_inde...]
    dot_general x9 -> x0, matrix products: 39 us -> none  [the longest x4 14.3 us: per_device(): lax.dot_general(piece, down_all, contract_last, preferred_element_type=f32)]
    ppermute x25 -> x11, starting transfers between devices: 34.5 us -> 19.3 us  [send(): return lax.ppermute(values, ('dp', 'tensor'), self.pairs(where_to))]
    pallas_call x1, Pallas kernels: 173 us -> 158 us  [back(): pl.pallas_call(functools.partial(back_body, blocks, in_cols, small_row),...]
    unnamed x152 -> x105, local copies, waits for them, and re-layouts: 35.6 us -> 28.4 us
  transfers between devices with their start and end apart: 31 -> 15, of which waited for: 15 -> 3; matrix products, arithmetic and copies ran while one was open for 22% -> 19% of each run, Pallas kernels for 26% -> 28%
where the time goes in v4:
time: 828 us; the launch traced here: 819 us
  Pallas kernels  535 us (65%)
  matrix products  135 us (16%)
  local copies, waits for them, and re-layouts  53.8 us (6%)
  waiting for transfers between devices  35 us (4%)
  other arithmetic  23.2 us (3%)
  starting transfers between devices  19.7 us (2%)
  between operations  17.5 us (2%)
    pallas_call x1, Pallas kernels, middle(): pl.pallas_call(functools.partial(middle_body, blocks, gu_chunks, down_chu...  190 us
    pallas_call x1, Pallas kernels, back(): pl.pallas_call(functools.partial(back_body, blocks, in_cols, small_row),...  158 us
    pallas_call x1, Pallas kernels, front(): pl.pallas_call(functools.partial(front_body, blocks, chunks), in_specs=[a...  117 us
    dot_general x6, matrix products, weight_grad(): lax.dot_general(left, right, contract_first, preferred_element_type=f32)  49.8 us
    pallas_call x1, Pallas kernels, mixer_backward(): pl.pallas_call(mixer_bwd_body, grid_spec=pltpu.PrefetchScalarGridSpec(num...  33.3 us
    ppermute x11, waiting for transfers between devices, send(): return lax.ppermute(values, ('dp', 'tensor'), self.pairs(where_to))  31.3 us
    unnamed x105, local copies, waits for them, and re-layouts  28.4 us
    dot_general x4, matrix products, per_device(): lax.dot_general(piece, gate_up_all, contract_last, preferred_element_type...  24.6 us
  transfers between devices with their start and end apart: 15, of which 3 were waited for; matrix products, arithmetic and copies ran while one was open for 19% of the time, Pallas kernels for 28%

profile of v4, /device:TPU:1, one launch (start us, length us, event | category | flops | bytes accessed | tf_op | source)
XLA Modules:
  0.0 819.3 jit_solution(12492563909464690565)
XLA Ops:
  12.3 117.0 %shard_map.330 = (bf16[2048,1920]{1,0:T(8,128)(2,1)S(1)}, bf16[512,1024]{1,0:T(8,128)(2,1)}, bf16[1024,2048]{1,0:T(8,128)(2,1)S(1)}, bf16[256,2048]{1,0:T(8,128)(2,1)S(1)}, bf16[2048,1024]{1,0:T(8,128)(2,1)S(1)}) custom-call(bf16[256,1920]{1,0:T(8,128)(2,1)S(1)} %concatenate.43.in_ref, bf16[256,1024]{1,0:T(8,128)(2,1)S(1)} %pad_maximum_fusion.7.out_ref, ...), custom_call_target="tpu_custom_call" | custom-call | flops 4194304 | bytes 300000000 | tf_op jit(solution)/shard_map/pallas_call | solution.py:1114
  137.5 14.4 %fusion.85.q_ref.gate_ref.inner_ref.step_ref.before_ref = f32[1024,1920]{1,0:T(8,128)} fusion(bf16[1024,2048]{1,0:T(8,128)(2,1)} %copy-done.7, bf16[2048,1920]{1,0:T(8,128)(2,1)} %copy-done.6), kind=kOutput, calls=%fused_computation.147 | convolution fusion | flops 8053063680 | bytes 19922944 | tf_op jit(solution)/shard_map/dot_general | solution.py:2394
  153.9 4.5 collective-permute-start
  172.0 5.1 fusion.82.kv_ref.bc_ref.bcbefore_ref
  177.0 8.1 shard_map.331.attn_ref
  186.7 15.4 %shard_map.332 = (bf16[1024,1024]{1,0:T(8,128)(2,1)}, f32[1024,768]{1,0:T(8,128)}, bf16[8,256,768]{2,1,0:T(8,128)(2,1)}) custom-call(s32[4]{0:T(128)} %fusion.71.order, f32[1024,1920]{1,0:T(8,128)} %fusion.85.q_ref.gate_ref.inner_ref.step_ref.before_ref, f32[1024,1920]{1,0:T(8,128)} %fusion.85.q_ref.gate_ref.inner_ref.step_ref.before_ref, ...), custom_call_target="tpu_custom_call" | custom-call | flops 3221225472 | bytes 15728640 | tf_op jit(solution)/shard_map/pallas_call | solution.py:480
  204.4 190.4 %shard_map.333 = (bf16[2048,3072]{1,0:T(8,128)(2,1)}, bf16[1024,2048]{1,0:T(8,128)(2,1)}, bf16[1024,1024]{1,0:T(8,128)(2,1)}, bf16[1024,1024]{1,0:T(8,128)(2,1)}...) custom-call(bf16[256,3072]{1,0:T(8,128)(2,1)} %pad_maximum_fusion.4., ...), custom_call_target="tpu_custom_call" | custom-call | flops 17179869184 | bytes 400000000 | tf_op jit(solution)/shard_map/pallas_call | solution.py:1627
  394.8 9.4 %convolution_convert_fusion.3 = bf16[2048,1024]{1,0:T(8,128)(2,1)} fusion(bf16[1024,2048]{1,0:T(8,128)(2,1)} %get-tuple-element.76, bf16[1024,1024]{1,0:T(8,128)(2,1)} %get-tuple-element.75), kind=kOutput, calls=%fused_computation.34 | convolution fusion | flops 4297064448 | bytes 10485760 | tf_op jit(solution)/shard_map/dot_general | solution.py:2417
  405.8 9.9 %fusion.15 = (bf16[1024,1024]{1,0:T(8,128)(2,1)S(1)}, bf16[1024,1024]{1,0:T(8,128)(2,1)S(1)}) fusion(bf16[1024,1024]{1,0:T(8,128)(2,1)S(1)} %copy-done.42, bf16[1024,1024]{1,0:T(8,128)(2,1)} %get-tuple-element.78, bf16[1024,2048]{1,0:T(8,128)(2,1)} %get-tuple-element.76, bf16[2048,3072]{1,0:T(8,128)(2,1)} %get-tuple-element.77), kind=kOutput, calls=%fused_computation.29 | convolution fusion | flops 4310695936 | bytes 16777216 | tf_op jit(solution)/shard_map/dot_general | solution.py:2422
  415.7 7.6 fusion.35
  423.4 6.2 fusion.32
  435.2 13.9 %convolution_convert_fusion.1 = bf16[2048,2048]{1,0:T(8,128)(2,1)} fusion(bf16[1024,2048]{1,0:T(8,128)(2,1)} %get-tuple-element.80, bf16[1024,1024]{1,0:T(8,128)(2,1)S(1)} %get-tuple-element.156, bf16[1024,1024]{1,0:T(8,128)(2,1)S(1)} %get-tuple-element.157), kind=kOutput, calls=%fused_computation.1 | convolution fusion | flops 8602517504 | bytes 16777216 | tf_op jit(solution)/shard_map/dot_general | solution.py:2417
  449.1 9.7 %collective-permute-done.4 = bf16[256,2048]{1,0:T(8,128)(2,1)S(1)} collective-permute-done((bf16[256,2048]{1,0:T(8,128)(2,1)}, bf16[256,2048]{1,0:T(8,128)(2,1)S(1)}, u32[]{:S(2)}, u32[]{:S(2)}) %collective-permute-start.4) | collective-permute-done | bytes 1048608 | tf_op jit(solution)/shard_map/ppermute | solution.py:641
  458.8 7.5 fusion.24
  474.0 21.6 %collective-permute-done.6 = bf16[256,2048]{1,0:T(8,128)(2,1)S(1)} collective-permute-done((bf16[256,2048]{1,0:T(8,128)(2,1)S(1)}, bf16[256,2048]{1,0:T(8,128)(2,1)S(1)}, u32[]{:S(2)}, u32[]{:S(2)}) %collective-permute-start.6) | collective-permute-done | bytes 1048608 | tf_op jit(solution)/shard_map/ppermute | solution.py:641
  501.3 9.0 %convolution_convert_fusion.2 = bf16[2048,1024]{1,0:T(8,128)(2,1)} fusion(bf16[1024,1024]{1,0:T(8,128)(2,1)} %get-tuple-element.68.heads_ref, bf16[256,2048]{1,0:T(8,128)(2,1)} %collective-permute-done.7, bf16[256,2048]{1,0:T(8,128)(2,1)S(1)} %collective-permute-done.6, bf16[256,2048]{1,0:T(8,128)(2,1)S(1)} %collective-permute-done.5, ...), kind=kOutput, calls=%fused_computation.33 | convolution fusion | flops 4313841664 | bytes 10485760 | tf_op jit(solution)/shard_map/dot_general | solution.py:2417
  510.3 9.5 %fusion.56.grad_ref = f32[1024,1024]{1,0:T(8,128)} fusion(bf16[2048,1024]{1,0:T(8,128)(2,1)} %all-gather.2.cloned.1.call-done.out_ref, bf16[256,2048]{1,0:T(8,128)(2,1)} %collective-permute-done.7, bf16[256,2048]{1,0:T(8,128)(2,1)S(1)} %collective-permute-done.6, bf16[256,2048]{1,0:T(8,128)(2,1)} %copy-done.38, bf16[256,2048]{1,0:T(8,128)(2,1)S(1)} %get-tuple-element.154), kind=kOutput, calls=%fused_computation.77 | convolution fusion | flops 4311744512 | bytes 12582912 | tf_op jit(solution)/shard_map/dot_general | solution.py:2437
  519.8 4.3 collective-permute-start.8
  524.1 12.6 %shard_map.334 = (bf16[1024,256]{1,0:T(8,128)(2,1)}, bf16[1024,256]{1,0:T(8,128)(2,1)}) custom-call(s32[4]{0:T(128)} %fusion.71.order, f32[1024,1920]{1,0:T(8,128)} %fusion.85.q_ref.gate_ref.inner_ref.step_ref.before_ref, f32[1024,768]{1,0:T(8,128)} %fusion.82.kv_ref.bc_ref.bcbefore_ref, f32[1024,128]{1,0:T(8,128)} %get-tuple-element.172.cos_ref.all_cos, ...), custom_call_target="tpu_custom_call" | custom-call | flops 2147483648 | bytes 5242880 | tf_op jit(solution)/shard_map/pallas_call | solution.py:442
  536.7 33.3 %shard_map.335 = (bf16[1024,1920]{1,0:T(8,128)(2,1)}, bf16[1024,768]{1,0:T(8,128)(2,1)}, f32[8,768]{1,0:T(8,128)}, f32[8,512]{1,0:T(8,128)}, f32[8,128]{1,0:T(8,128)}) custom-call(s32[4]{0:T(128)} %fusion.71.order, f32[1024,1920]{1,0:T(8,128)} %fusion.85.q_ref.gate_ref.inner_ref.step_ref.before_ref, ...), custom_call_target="tpu_custom_call" | custom-call | flops 8053063680 | bytes 31457280 | tf_op jit(solution)/shard_map/pallas_call | solution.py:549
  584.4 5.8 fusion.52
  609.6 4.0 convolution_convert_fusion.4.bc_ref
  613.7 11.1 %convolution_convert_fusion.part_ref = bf16[2048,1920]{1,0:T(8,128)(2,1)} fusion(bf16[1024,2048]{1,0:T(8,128)(2,1)S(1)} %copy-done.9, bf16[1024,1920]{1,0:T(8,128)(2,1)S(1)} %copy-done.36), kind=kOutput, calls=%fused_computation | convolution fusion | flops 8056995840 | bytes 15990784 | tf_op jit(solution)/shard_map/dot_general | solution.py:2417
  628.4 158.5 %shard_map.336 = (f32[256,1920]{1,0:T(8,128)}, f32[64,1024]{1,0:T(8,128)}, f32[256,2048]{1,0:T(8,128)}, f32[176,128]{1,0:T(8,128)}, f32[256,1024]{1,0:T(8,128)}) custom-call(bf16[2048,1920]{1,0:T(8,128)(2,1)} %convolution_convert_fusion.part_ref, bf16[2048,512]{1,0:T(8,128)(2,1)} %convolution_convert_fusion.4.bc_ref, ...), custom_call_target="tpu_custom_call" | custom-call | flops 10485760 | bytes 300000000 | tf_op jit(solution)/shard_map/pallas_call | solution.py:2110
  (220 shorter events, 113.0 us)
Async XLA Ops:
  7.2 197.2 %all-gather.2.cloned.1.call-start = ((), (), s32[]{:S(2)}) async-start(), calls=%async_computation.3 | async-start | bytes 5242880 | tf_op jit(solution)/shard_map/all_gather | solution.py:2205
  137.4 382.4 %reduce-scatter.4.cloned.1.call-start = ((), (), s32[]{:S(2)}) async-start(), calls=%async_computation.4 | async-start | bytes 5242880 | tf_op jit(solution)/shard_map/reduce_scatter | solution.py:2209
  137.4 16.4 %copy-start.31 = (f32[4,768]{1,0:T(4,128)S(1)}, f32[4,768]{1,0:T(4,128)}, u32[]{:S(2)}) copy-start(f32[4,768]{1,0:T(4,128)} %param.27) | copy-start | bytes 36868
  137.4 16.4 %copy-start.32 = (f32[768]{0:T(1024)S(1)}, f32[768]{0:T(1024)}, u32[]{:S(2)}) copy-start(f32[768]{0:T(1024)} %param.32) | copy-start | bytes 9220
  137.4 16.4 %copy-start.33 = (f32[12]{0:T(128)S(1)}, f32[12]{0:T(128)}, u32[]{:S(2)}) copy-start(f32[12]{0:T(128)} %param.29) | copy-start | bytes 148
  137.5 16.4 %copy-start.34 = (f32[12]{0:T(128)S(1)}, f32[12]{0:T(128)}, u32[]{:S(2)}) copy-start(f32[12]{0:T(128)} %param.30) | copy-start | bytes 148
  137.5 16.4 %copy-start.35 = (f32[12]{0:T(128)S(1)}, f32[12]{0:T(128)}, u32[]{:S(2)}) copy-start(f32[12]{0:T(128)} %param.31) | copy-start | bytes 148
  151.9 50.2 %collective-permute-start.1 = (bf16[256,2048]{1,0:T(8,128)(2,1)}, bf16[256,2048]{1,0:T(8,128)(2,1)}, u32[]{:S(2)}, u32[]{:S(2)}) collective-permute-start(bf16[256,2048]{1,0:T(8,128)(2,1)} %param.20), channel_id=1, source_target_pairs={{2,4},{3,5},{4,2},{5,3},{10,12},{11,13},{12,10},{13,11},{18,20},{1... | collective-permute-start | bytes 3145736 | tf_op jit(solution)/shard_map/ppermute | solution.py:641
  153.9 31.2 %collective-permute-start = (f32[3876]{0:T(1024)S(1)}, f32[3876]{0:T(1024)S(1)}, u32[]{:S(2)}, u32[]{:S(2)}) collective-permute-start(f32[3876]{0:T(1024)S(1)} %concatenate.48), channel_id=1, source_target_pairs={{2,4},{3,5},{4,2},{5,3},{10,12},{11,13},{12,10},{13,11},{18,20},{1... | collective-permute-start | bytes 46520 | tf_op jit(solution)/shard_map/ppermute | solution.py:641
  404.2 171.8 %reduce-scatter.6.cloned.1.call-start = ((), (), s32[]{:S(2)}) async-start(), calls=%async_computation.5 | async-start | bytes 10485760 | tf_op jit(solution)/shard_map/reduce_scatter | solution.py:2209
  415.7 19.5 %copy-start.40 = (bf16[1024,1024]{1,0:T(8,128)(2,1)}, bf16[1024,1024]{1,0:T(8,128)(2,1)S(1)}, u32[]{:S(2)}) copy-start(bf16[1024,1024]{1,0:T(8,128)(2,1)S(1)} %get-tuple-element.156) | copy-start | bytes 6291460
  415.7 19.5 %copy-start.41 = (bf16[1024,1024]{1,0:T(8,128)(2,1)}, bf16[1024,1024]{1,0:T(8,128)(2,1)S(1)}, u32[]{:S(2)}) copy-start(bf16[1024,1024]{1,0:T(8,128)(2,1)S(1)} %get-tuple-element.157) | copy-start | bytes 6291460
  415.7 14.7 %slice-start.3 = ((s8[12582912]{0:T(1024)(128)(4,1)}), s8[4194304]{0:T(1024)(128)(4,1)S(1)}, s32[]{:S(2)}) async-start(s8[12582912]{0:T(1024)(128)(4,1)} %bitcast.62), calls=%async_computation.10 | async-start | bytes 8388608
  423.3 7.1 collective-permute-start.3
  429.6 19.5 %collective-permute-start.2 = (bf16[256,2048]{1,0:T(8,128)(2,1)S(1)}, bf16[256,2048]{1,0:T(8,128)(2,1)S(1)}, u32[]{:S(2)}, u32[]{:S(2)}) collective-permute-start(bf16[256,2048]{1,0:T(8,128)(2,1)S(1)} %fusion.32), channel_id=1, source_target_pairs={{0,4},{1,5},{2,6},{3,7},{4,0},{5,1},{6,2},{7,3},{8,12},{9,13},{10,... | collective-permute-start | bytes 3145736 | tf_op jit(solution)/shard_map/ppermute | solution.py:641
  433.9 25.0 %collective-permute-start.4 = (bf16[256,2048]{1,0:T(8,128)(2,1)}, bf16[256,2048]{1,0:T(8,128)(2,1)S(1)}, u32[]{:S(2)}, u32[]{:S(2)}) collective-permute-start(bf16[256,2048]{1,0:T(8,128)(2,1)} %fusion.27), channel_id=1, source_target_pairs={{0,1},{1,0},{2,3},{3,2},{4,5},{5,4},{6,7},{7,6},{8,9},{9,8},{10,11... | collective-permute-start | bytes 3145736 | tf_op jit(solution)/shard_map/ppermute | solution.py:641
  466.3 162.1 %reduce-scatter.8.cloned.1.call-start = ((), (), s32[]{:S(2)}) async-start(), calls=%async_computation.6 | async-start | bytes 5242880 | tf_op jit(solution)/shard_map/reduce_scatter | solution.py:2209
  471.6 24.0 %collective-permute-start.6 = (bf16[256,2048]{1,0:T(8,128)(2,1)S(1)}, bf16[256,2048]{1,0:T(8,128)(2,1)S(1)}, u32[]{:S(2)}, u32[]{:S(2)}) collective-permute-start(bf16[256,2048]{1,0:T(8,128)(2,1)S(1)} %get-tuple-element.154), channel_id=1, source_target_pairs={{0,1},{1,0},{2,3},{3,2},{4,5},{5,4},{6,7},{7,6},{8,9},{9,8},{10,11... | collective-permute-start | bytes 3145736 | tf_op jit(solution)/shard_map/ppermute | solution.py:641
  472.9 28.4 %collective-permute-start.5 = (bf16[256,2048]{1,0:T(8,128)(2,1)S(1)}, bf16[256,2048]{1,0:T(8,128)(2,1)S(1)}, u32[]{:S(2)}, u32[]{:S(2)}) collective-permute-start(bf16[256,2048]{1,0:T(8,128)(2,1)S(1)} %get-tuple-element.154), channel_id=1, source_target_pairs={{0,4},{1,5},{2,6},{3,7},{4,0},{5,1},{6,2},{7,3},{8,12},{9,13},{10,... | collective-permute-start | bytes 3145736 | tf_op jit(solution)/shard_map/ppermute | solution.py:641
  495.6 5.7 collective-permute-start.7
  519.8 55.1 %collective-permute-start.8 = (bf16[256,2048]{1,0:T(8,128)(2,1)S(1)}, bf16[256,2048]{1,0:T(8,128)(2,1)S(1)}, u32[]{:S(2)}, u32[]{:S(2)}) collective-permute-start(bf16[256,2048]{1,0:T(8,128)(2,1)S(1)} %copy-done.22), channel_id=1, source_target_pairs={{2,4},{3,5},{4,2},{5,3},{10,12},{11,13},{12,10},{13,11},{18,20},{1... | collective-permute-start | bytes 3145736 | tf_op jit(solution)/shard_map/ppermute | solution.py:641
  582.0 205.0 %collective-permute-start.10 = (bf16[256,3072]{1,0:T(8,128)(2,1)}, bf16[256,3072]{1,0:T(8,128)(2,1)S(1)}, u32[]{:S(2)}, u32[]{:S(2)}) collective-permute-start(bf16[256,3072]{1,0:T(8,128)(2,1)} %get-tuple-element.153), channel_id=1, source_target_pairs={{2,4},{3,5},{4,2},{5,3},{10,12},{11,13},{12,10},{13,11},{18,20},{1... | collective-permute-start | bytes 4718600 | tf_op jit(solution)/shard_map/ppermute | solution.py:641
  584.0 202.9 %collective-permute-start.9 = (bf16[256,3072]{1,0:T(8,128)(2,1)}, bf16[256,3072]{1,0:T(8,128)(2,1)S(1)}, u32[]{:S(2)}, u32[]{:S(2)}) collective-permute-start(bf16[256,3072]{1,0:T(8,128)(2,1)} %get-tuple-element.151), channel_id=1, source_target_pairs={{0,4},{1,5},{2,0},{3,1},{4,6},{5,7},{6,2},{7,3},{8,12},{9,13},{10,... | collective-permute-start | bytes 4718600 | tf_op jit(solution)/shard_map/ppermute | solution.py:641
  628.4 160.2 %copy-start.13 = (bf16[256,3072]{1,0:T(8,128)(2,1)S(1)}, bf16[256,3072]{1,0:T(8,128)(2,1)}, u32[]{:S(2)}) copy-start(bf16[256,3072]{1,0:T(8,128)(2,1)} %get-tuple-element.109) | copy-start | bytes 4718596
  (40 other events, 192.5 us)
Sparse Core Ops, SparseCore 0:
  137.5 51.9 all-gather.1
  404.4 52.6 reduce-scatter.3
  466.4 86.8 reduce-scatter.5
  577.9 50.4 reduce-scatter.7

commit v5 on v4

--- a/solution.py
+++ b/solution.py
@@ -740,9 +740,9 @@
 
 
 class Spread:
-    def __init__(self, lanes, full, rows, chunks, send_sems, recv_sems, cols=slice(None)):
+    def __init__(self, lanes, full, rows, chunks, send_sems, recv_sems, cols=slice(None), first=None):
         self.lanes, self.full, self.rows, self.chunks = lanes, full, rows, chunks
-        self.cols = cols
+        self.cols, self.first = cols, first
         self.piece = rows // chunks
         self.send_sems, self.recv_sems = send_sems, recv_sems
 
@@ -753,8 +753,12 @@
     def copy(self, place, half, chunk, bit):
         view = self.view(place, half, chunk)
         to = place | (1 << bit)
+        source = view
+        if place == 0 and self.first is not None:
+            start = half * self.rows + chunk * self.piece
+            source = self.first.at[pl.ds(start, self.piece), self.cols]
         return remote(
-            view,
+            source,
             view,
             self.send_sems.at[half, to, chunk],
             self.recv_sems.at[half, to, chunk],
@@ -798,10 +802,10 @@
 
 
 def front_body(
-    blocks, chunks, in_ref, out_ref, shared_ref, x_ref, gain_ref,
-    full_ref, pair_ref, act_ref, xr_ref, sh_ref,
+    blocks, chunks, in_ref, out_ref, shared_ref, x_ref, gain_ref, par_ref,
+    full_ref, pair_ref, act_ref, xr_ref, sh_ref, parr_ref,
     x_s, act_s, home_sems, z_send, z_recv, o_sems, o_recv, send_sems, recv_sems, x_sems, a_send,
-    a_recv, line_send, line_recv, sh_send, sh_recv, swap_send, swap_recv,
+    a_recv, line_send, line_recv, sh_send, sh_recv, swap_send, swap_recv, par_sems,
 ):
     lanes = Lanes(blocks)
     rows = in_ref.shape[0]
@@ -982,6 +986,19 @@
         act_core().start()
         pltpu.make_async_copy(act_s, act_slot(0), a_send.at[3]).start()
         pltpu.make_async_copy(x_s, xr_ref, x_sems.at[3]).start()
+
+    def par_away():
+        return remote(
+            par_ref, parr_ref, par_sems.at[0], par_sems.at[1], (lanes.other, lanes.far)
+        )
+
+    @pl.when(lanes.home)
+    def _():
+        parr_ref[...] = par_ref[...]
+
+    @pl.when(lanes.away)
+    def _():
+        par_away().start()
 
     early = list(range(max(chunks // 2, 1)))
     late = list(range(len(early), chunks))
@@ -1091,6 +1108,8 @@
 
     @pl.when(lanes.away)
     def _():
+        par_away().wait_recv()
+        par_away().wait_send()
         x_away().wait_send()
         for chunk in range(chunks):
             first_copy(chunk, (lanes.other, t)).wait_send()
@@ -1102,7 +1121,7 @@
             remote(view, view, o_sems.at[0], o_recv.at[half], (lanes.other, t)).wait_recv()
 
 
-def front(in_pack, out_pack, shared, layer_in, gain, at):
+def front(in_pack, out_pack, shared, layer_in, gain, params, at):
     bf16 = jnp.bfloat16
     rows = in_pack.shape[0]
     blocks = at.blocks
@@ -1113,14 +1132,15 @@
     total = 2 * blocks * rows
     return pl.pallas_call(
         functools.partial(front_body, blocks, chunks),
-        in_specs=[anywhere] * 4 + [pl.BlockSpec(memory_space=pltpu.VMEM)],
-        out_specs=[anywhere] * 5,
+        in_specs=[pl.BlockSpec(memory_space=pltpu.VMEM)] * 6,
+        out_specs=[anywhere] * 5 + [pl.BlockSpec(memory_space=pltpu.VMEM)],
         out_shape=[
             jax.ShapeDtypeStruct((total, in_pack.shape[1]), bf16),
             jax.ShapeDtypeStruct((2 * rows, out_pack.shape[1]), bf16),
             jax.ShapeDtypeStruct((4 * here, features), bf16),
             jax.ShapeDtypeStruct((here, features), bf16),
             jax.ShapeDtypeStruct((total, shared.shape[1]), bf16),
+            jax.ShapeDtypeStruct(params.shape, jnp.float32),
         ],
         scratch_shapes=[
             pltpu.VMEM((here, features), bf16),
@@ -1141,6 +1161,7 @@
             dma((2, blocks, 1)),
             dma((2, blocks)),
             dma((2, blocks)),
+            dma((2,)),
         ],
         compiler_params=pltpu.CompilerParams(
             collective_id=1, has_side_effects=True, vmem_limit_bytes=16 * 1024 * 1024
@@ -1148,87 +1169,25 @@
         cost_estimate=pl.CostEstimate(
             flops=here * features * 8, bytes_accessed=300_000_000, transcendentals=0
         ),
-    )(in_pack, out_pack, shared, layer_in, gain.reshape(1, -1))
+    )(in_pack, out_pack, shared, layer_in, gain.reshape(1, -1), params)
 
 
 class Stage:
-    def __init__(self, lanes, src, full, rows, cols, chunks, sems):
-        self.lanes, self.src, self.full, self.rows, self.cols = lanes, src, full, rows, cols
+    def __init__(self, lanes, pair, full, rows, cols, chunks, sems):
+        self.lanes, self.pair, self.full, self.rows, self.cols = lanes, pair, full, rows, cols
         self.chunks = chunks
-        self.piece = rows // chunks
-        self.send_sems, self.recv_sems, self.home_sems, ssem, rsem = sems
-        self.spread = Spread(lanes, full, rows, chunks, ssem, rsem, cols)
-
-    def view(self, half, chunk):
-        start = self.lanes.k * (2 * self.rows) + half * self.rows + chunk * self.piece
-        return self.full.at[pl.ds(pl.multiple_of(start, self.piece), self.piece), self.cols]
-
-    def part(self, chunk):
-        return self.src.at[pl.ds(chunk * self.piece, self.piece), self.cols]
-
-    def own(self, chunk):
-        return pltpu.make_async_copy(
-            self.part(chunk), self.view(self.lanes.c, chunk), self.home_sems.at[chunk]
-        )
-
-    def first(self, chunk, device):
-        c = self.lanes.c
-        return remote(
-            self.part(chunk),
-            self.view(c, chunk),
-            self.send_sems.at[0, chunk],
-            self.recv_sems.at[c, chunk],
-            device,
-        )
-
-    def second(self, chunk):
-        c = self.lanes.c
-        return remote(
-            self.part(chunk),
-            self.view(c, chunk),
-            self.send_sems.at[1, chunk],
-            self.recv_sems.at[c, chunk],
-            (self.lanes.other, self.lanes.far),
-        )
-
-    def start(self):
-        lanes = self.lanes
-
-        @pl.when(lanes.home)
-        def _():
-            for chunk in range(self.chunks):
-                self.own(chunk).start()
-                self.first(chunk, (lanes.d, lanes.far)).start()
-
-        @pl.when(lanes.away)
-        def _():
-            for chunk in range(self.chunks):
-                self.first(chunk, (lanes.other, lanes.t)).start()
-                self.second(chunk).start()
-
-    def came(self, half, chunk):
-        view = self.view(half, chunk)
-        remote(
-            view,
-            view,
-            self.send_sems.at[0, chunk],
-            self.recv_sems.at[half, chunk],
-            (self.lanes.other, self.lanes.t),
-        ).wait_recv()
-
-    def give(self, chunk):
-        for half in range(2):
-            self.spread.give(0, half, chunk)
-
-    def arrive_home(self, chunk):
-        self.own(chunk).wait()
-        self.came(1 - self.lanes.c, chunk)
-        self.give(chunk)
-
-    def arrive_away(self, chunk):
-        for half in range(2):
-            self.came(half, chunk)
-        self.give(chunk)
+        self.own_sem, ssem, rsem = sems
+        self.spread = Spread(lanes, full, rows, chunks, ssem, rsem, cols, pair)
+
+    def own(self):
+        start = self.lanes.k * (2 * self.rows)
+        view = self.full.at[pl.ds(pl.multiple_of(start, 2 * self.rows), 2 * self.rows), self.cols]
+        return pltpu.make_async_copy(self.pair.at[:, self.cols], view, self.own_sem.at[0])
+
+    def give(self):
+        for chunk in range(self.chunks):
+            for half in range(2):
+                self.spread.give(0, half, chunk)
 
     def settle(self, place):
         for half in range(2):
@@ -1237,23 +1196,11 @@
                     self.spread.take(place, half, chunk)
 
     def finish(self):
-        lanes = self.lanes
         for chunk in range(self.chunks):
             for half in range(2):
-                for place in range(lanes.blocks):
-                    for bit in onward(place, half, lanes.bits):
+                for place in range(self.lanes.blocks):
+                    for bit in onward(place, half, self.lanes.bits):
                         self.spread.copy(place, half, chunk, bit).wait_send()
-
-        @pl.when(lanes.home)
-        def _():
-            for chunk in range(self.chunks):
-                self.first(chunk, (lanes.d, lanes.far)).wait_send()
-
-        @pl.when(lanes.away)
-        def _():
-            for chunk in range(self.chunks):
-                self.first(chunk, (lanes.other, lanes.t)).wait_send()
-                self.second(chunk).wait_send()
 
 
 class Exchange:
@@ -1289,14 +1236,14 @@
         start = piece * self.here + i * self.step
         return pl.ds(pl.multiple_of(start, self.step), self.step)
 
-    def give(self, index, place, left, weight):
+    def give(self, index, place, product):
         bf16 = jnp.bfloat16
         cols = self.columns(place)
 
         @pl.loop(0, 4)
         def _(piece):
             rows = pl.ds(pl.multiple_of(piece * self.here, self.here), self.here)
-            self.work[rows, cols] = low_dot(left[rows, :], weight(), NT)
+            self.work[rows, cols] = product(rows)
 
         @pl.loop(0, self.here // self.step)
         def _(i):
@@ -1345,17 +1292,17 @@
 
 def middle_body(
     blocks, gu_chunks, down_chunks,
-    ff_ref, heads_ref, out_ref, x_ref, gain_ref, target_ref, live_ref,
+    pair_ref, heads_ref, out_ref, teacher_ref, x_ref, gain_ref, live_ref,
     full_ref, mid_ref, gate_ref, up_ref, hidden_ref, grads_ref, resid_ref, error_ref, low_ref,
     loss_ref,
     wbuf, mid_s, acc_s, hid_s, gate_s, up_s, own_s, both_s, core_s, pass_s,
     both_r, core_r, far_r, both_q, core_q, far_q, err_s,
     w_sems, one_s, one_r, two_s, two_r, mid_ssem, mid_rsem, err_ssem, err_rsem, keep_sems,
-    gz_s, gz_r, g_home, g_s, g_r, dz_s, dz_r, d_home, d_s, d_r,
+    g_home, g_s, g_r, d_home, d_s, d_r, target_ref, t_sems, out_s,
 ):
     f32, bf16 = jnp.float32, jnp.bfloat16
     lanes = Lanes(blocks)
-    rows = ff_ref.shape[0]
+    rows = pair_ref.shape[0] // 2
     here = x_ref.shape[0]
     block = 2 * rows
     inner = heads_ref.shape[1]
@@ -1364,13 +1311,22 @@
     near_at = (lanes.d, lanes.near)
     lanes.greet()
     gate_up = Stage(
-        lanes, ff_ref, full_ref, rows, slice(0, 2 * hidden_width), gu_chunks,
-        (gz_s, gz_r, g_home, g_s, g_r),
+        lanes, pair_ref, full_ref, rows, slice(0, 2 * hidden_width), gu_chunks,
+        (g_home, g_s, g_r),
     )
     down = Stage(
-        lanes, ff_ref, full_ref, rows, slice(2 * hidden_width, 3 * hidden_width), down_chunks,
-        (dz_s, dz_r, d_home, d_s, d_r),
-    )
+        lanes, pair_ref, full_ref, rows, slice(2 * hidden_width, 3 * hidden_width), down_chunks,
+        (d_home, d_s, d_r),
+    )
+
+    def target_away():
+        return remote(
+            teacher_ref, target_ref, t_sems.at[0], t_sems.at[1], (lanes.other, lanes.far)
+        )
+
+    def target_home():
+        return pltpu.make_async_copy(teacher_ref, target_ref, t_sems.at[2])
+
     sends = (both_s, core_s, pass_s)
     one = Exchange(lanes, acc_s, own_s, sends, (both_r, core_r, far_r), one_s, one_r)
     two = Exchange(lanes, acc_s, own_s, sends, (both_q, core_q, far_q), two_s, two_r)
@@ -1383,36 +1339,26 @@
             out_ref.at[pl.ds(index * block, block), :], index % 2, inner, pl.ds(0, inner)
         )
 
-    gate_up.start()
     out_load(0).start()
-    down.start()
+    gate_up.give()
+    gate_up.own().start()
+    down.own().start()
 
     for index in range(blocks):
         if index + 1 < blocks:
             out_load(index + 1).start()
         out_load(index).wait()
-        one.give(index, index, heads_ref, lambda: wbuf[index % 2, :, :inner])
-        if index == 0:
-
-            @pl.when(lanes.home)
-            def _():
-                for chunk in range(gu_chunks):
-                    gate_up.arrive_home(chunk)
-
+        one.give(
+            index,
+            index,
+            lambda rows: low_dot(heads_ref[rows, :], wbuf[index % 2, :, :inner], NT),
+        )
     for index in range(blocks):
         one.pass_on(index, index)
 
-    @pl.when(lanes.away)
-    def _():
-        for chunk in range(gu_chunks):
-            gate_up.arrive_away(chunk)
-            if chunk:
-                gate_up.spread.pass_on(chunk - 1)
-
-    @pl.when(lanes.home)
-    def _():
-        for chunk in range(gu_chunks - 1):
-            gate_up.spread.pass_on(chunk)
+    for chunk in range(gu_chunks):
+        gate_up.spread.pass_on(chunk)
+    down.give()
 
     for index in range(blocks):
         one.take(index, index)
@@ -1449,17 +1395,14 @@
 
     mid_near().start()
     mid_core().start()
-    gate_up.spread.pass_on(gu_chunks - 1)
 
     @pl.when(lanes.home)
     def _():
-        for chunk in range(down_chunks):
-            down.arrive_home(chunk)
+        target_home().start()
 
     @pl.when(lanes.away)
     def _():
-        for chunk in range(down_chunks):
-            down.arrive_away(chunk)
+        target_away().start()
 
     def gu_load(place, slot):
         start = lanes.block(place) * block
@@ -1473,6 +1416,7 @@
         ]
         return load(view, slot, hidden_width, pl.ds(0, hidden_width))
 
+    gate_up.own().wait()
     gu_load(0, 0).start()
     mid_near().wait_recv()
     mid_both().start()
@@ -1511,6 +1455,7 @@
     for chunk in range(blocks, down_chunks):
         down.spread.pass_on(chunk)
 
+    down.own().wait()
     down_load(0, 0).start()
 
     @pl.loop(0, 4 * here // step)
@@ -1543,12 +1488,25 @@
             down.settle(place + 1)
             down_load(place + 1, (place + 1) % 2).start()
         down_load(place, place % 2).wait()
-        two.give(index, place, hid_s, lambda: wbuf[place % 2, :, :hidden_width])
+        two.give(
+            index,
+            place,
+            lambda rows: low_dot(hid_s[rows, :], wbuf[place % 2, :, :hidden_width], NT),
+        )
         if place:
             two.pass_on(lanes.block(place - 1), place - 1)
     two.pass_on(lanes.block(blocks - 1), blocks - 1)
     for place in range(blocks):
         two.take(lanes.block(place), place)
+
+    @pl.when(lanes.home)
+    def _():
+        target_home().wait()
+
+    @pl.when(lanes.away)
+    def _():
+        target_away().wait_recv()
+        target_away().wait_send()
 
     def output_part(i, loss):
         part = pl.ds(pl.multiple_of(i * step, step), step)
@@ -1556,7 +1514,7 @@
         for index in range(blocks):
             cols = columns(index)
             outputs = resid_ref[part, cols] + two.total(index, part)
-            low_ref[part, cols] = outputs.astype(bf16)
+            out_s[part, cols] = outputs.astype(bf16)
             error = (outputs - target_ref[part, cols].astype(f32)) * live
             error_ref[part, cols] = error
             err_s[part, cols] = error.astype(bf16)
@@ -1582,6 +1540,21 @@
     err_near().start()
     err_core().start()
     own_err.start()
+
+    def out_home():
+        return pltpu.make_async_copy(out_s, low_ref, t_sems.at[5])
+
+    def out_away():
+        return remote(out_s, low_ref, t_sems.at[3], t_sems.at[4], (lanes.other, lanes.far))
+
+    @pl.when(lanes.home)
+    def _():
+        out_home().start()
+
+    @pl.when(lanes.away)
+    def _():
+        out_away().start()
+
     for copy in kept:
         copy.wait()
     gate_up.finish()
@@ -1595,14 +1568,23 @@
     err_core().wait_recv()
     err_both().wait_recv()
     own_err.wait()
+
+    @pl.when(lanes.home)
+    def _():
+        out_home().wait()
+
+    @pl.when(lanes.away)
+    def _():
+        out_away().wait()
+
     for copy in (err_near(), err_core(), err_both()):
         copy.wait_send()
 
 
-def middle(ff_pack, heads_all, out_all, x, gain, target, live, at):
+def middle(pair, heads_all, out_all, x, gain, teacher, live, at):
     f32, bf16 = jnp.float32, jnp.bfloat16
-    rows = ff_pack.shape[0]
-    hidden_width = ff_pack.shape[1] // 3
+    rows = pair.shape[0] // 2
+    hidden_width = pair.shape[1] // 3
     slot, inner = heads_all.shape
     here, features = x.shape
     blocks = at.blocks
@@ -1614,19 +1596,13 @@
     anywhere = pl.BlockSpec(memory_space=pl.ANY)
 
     def stage_sems(chunks):
-        return [
-            dma((2, chunks)),
-            dma((2, chunks)),
-            dma((chunks,)),
-            dma((2, blocks, chunks)),
-            dma((2, blocks, chunks)),
-        ]
+        return [dma((1,)), dma((2, blocks, chunks)), dma((2, blocks, chunks))]
 
     shape = jax.ShapeDtypeStruct
     buffers = [pltpu.VMEM((blocks, here, block), bf16)]
     return pl.pallas_call(
         functools.partial(middle_body, blocks, gu_chunks, down_chunks),
-        in_specs=[anywhere, vmem, anywhere, vmem, vmem, vmem, vmem],
+        in_specs=[vmem, vmem, anywhere, anywhere, vmem, vmem, vmem],
         out_specs=[anywhere] * 6 + [vmem] * 4,
         out_shape=[
             shape((features, 3 * hidden_width), bf16),
@@ -1664,14 +1640,232 @@
             dma((3 + blocks,)),
         ]
         + stage_sems(gu_chunks)
-        + stage_sems(down_chunks),
+        + stage_sems(down_chunks)
+        + [pltpu.VMEM((here, features), bf16), dma((6,)), pltpu.VMEM((here, features), bf16)],
         compiler_params=pltpu.CompilerParams(
             collective_id=3, has_side_effects=True, vmem_limit_bytes=58 * 1024 * 1024
         ),
         cost_estimate=pl.CostEstimate(
             flops=slot * features * hidden_width * 8, bytes_accessed=400_000_000, transcendentals=0
         ),
-    )(ff_pack, heads_all, out_all, x, gain.reshape(1, -1), target, live)
+    )(
+        pair, heads_all, out_all, teacher, x, gain.reshape(1, -1), live,
+    )
+
+
+def turn_body(
+    blocks, low_ref, lowsh_ref, act_ref, in_ref, sh_ref, rawgu_ref, rawdown_ref,
+    part_ref, bc_ref, kv_ref, sum_ref, gu_ref, down_ref,
+    win_s, wsh_s, work_s, own_s, both_s, core_s, pass_s, both_r, core_r, far_r, stage_s,
+    gu_r, down_r, w_sems, x_ssem, x_rsem, stage_sems, ff_ssem, ff_rsem,
+):
+    f32, bf16 = jnp.float32, jnp.bfloat16
+    lanes = Lanes(blocks)
+    c, t = lanes.c, lanes.t
+    here = sum_ref.shape[0]
+    rows = rawgu_ref.shape[0] // 2
+    block = 2 * rows
+    width = low_ref.shape[1]
+    bc_width = bc_ref.shape[1]
+    features = act_ref.shape[1]
+    core_at, far_at, cross_at = (
+        (lanes.other, t), (lanes.d, lanes.far), (lanes.other, lanes.far),
+    )
+    lanes.greet()
+
+    def ff_copies(kind, half, device):
+        view = pl.ds(pl.multiple_of(half * rows, rows), rows)
+        return [
+            remote(
+                src.at[view, :], dst.at[kind], ff_ssem.at[kind, i], ff_rsem.at[kind, i], device
+            )
+            for i, (src, dst) in enumerate(((rawgu_ref, gu_r), (rawdown_ref, down_r)))
+        ]
+
+    def first_home():
+        return ff_copies(0, 1 - c, core_at)
+
+    def first_away():
+        return ff_copies(0, c, far_at)
+
+    def second_away():
+        return ff_copies(1, 1 - c, cross_at)
+
+    def load(index):
+        slot = index % 2
+        view = pl.ds(index * block, block)
+        return (
+            pltpu.make_async_copy(in_ref.at[view, :], win_s.at[slot], w_sems.at[slot, 0]),
+            pltpu.make_async_copy(sh_ref.at[view, :], wsh_s.at[slot], w_sems.at[slot, 1]),
+        )
+
+    for copy in load(0):
+        copy.start()
+
+    @pl.when(lanes.home)
+    def _():
+        for copy in first_home():
+            copy.start()
+
+    @pl.when(lanes.away)
+    def _():
+        for one, two in zip(first_away(), second_away()):
+            one.start()
+            two.start()
+
+    exchange = Exchange(
+        lanes, work_s, own_s, (both_s, core_s, pass_s), (both_r, core_r, far_r), x_ssem, x_rsem
+    )
+    for index in range(blocks):
+        slot = index % 2
+        if index + 1 < blocks:
+            for copy in load(index + 1):
+                copy.start()
+        for copy in load(index):
+            copy.wait()
+        exchange.give(
+            index,
+            index,
+            lambda part: low_dot(low_ref[part, :], win_s[slot], NT)
+            + low_dot(lowsh_ref[part, :], wsh_s[slot], NT),
+        )
+        if index:
+            exchange.pass_on(index - 1, index - 1)
+    exchange.pass_on(blocks - 1, blocks - 1)
+
+    tall = 256
+    steps = features // tall
+
+    def out_copies(i, slot):
+        view = pl.ds(pl.multiple_of(i * tall, tall), tall)
+        kv_from = width + bc_width
+        return (
+            pltpu.make_async_copy(
+                stage_s.at[slot, :, :width], part_ref.at[view, :], stage_sems.at[slot, 0]
+            ),
+            pltpu.make_async_copy(
+                stage_s.at[slot, :, width:kv_from], bc_ref.at[view, :], stage_sems.at[slot, 1]
+            ),
+            pltpu.make_async_copy(
+                stage_s.at[slot, :, kv_from:], kv_ref.at[view, :], stage_sems.at[slot, 2]
+            ),
+        )
+
+    @pl.loop(0, steps)
+    def _(i):
+        slot = lax.rem(i, 2)
+
+        @pl.when(i >= 2)
+        def _():
+            for copy in out_copies(i - 2, slot):
+                copy.wait()
+
+        left = act_ref[:, pl.ds(pl.multiple_of(i * tall, tall), tall)]
+        for src, base in ((low_ref, 0), (lowsh_ref, width)):
+            total = src.shape[1]
+            tile = total // 3
+            for col in range(0, total, tile):
+                product = low_dot(left, src[:, col : col + tile], TN)
+                stage_s[slot, :, base + col : base + col + tile] = product.astype(bf16)
+        for copy in out_copies(i, slot):
+            copy.start()
+
+    for index in range(blocks):
+        exchange.take(index, index)
+    step = min(here, 32)
+
+    @pl.loop(0, here // step)
+    def _(i):
+        part = pl.ds(pl.multiple_of(i * step, step), step)
+        for index in range(blocks):
+            sum_ref[part, index * block : (index + 1) * block] = exchange.total(index, part)
+
+    for i in (steps - 2, steps - 1):
+        for copy in out_copies(i, i % 2):
+            copy.wait()
+    for index in range(blocks):
+        exchange.finish(index, index)
+    for copy in first_home():
+        copy.wait_recv()
+    span = min(rows, 32)
+
+    @pl.when(lanes.home)
+    def _():
+        for copy in first_home():
+            copy.wait_send()
+
+        @pl.loop(0, rows // span)
+        def _(i):
+            part = pl.ds(pl.multiple_of(i * span, span), span)
+            mine = pl.ds(pl.multiple_of(c * rows + i * span, span), span)
+            gu_ref[part, :] = rawgu_ref[mine, :].astype(f32) + gu_r[0, part, :].astype(f32)
+            down_ref[part, :] = rawdown_ref[mine, :].astype(f32) + down_r[0, part, :].astype(f32)
+
+    @pl.when(lanes.away)
+    def _():
+        for copy in second_away():
+            copy.wait_recv()
+        for copy in first_away() + second_away():
+            copy.wait_send()
+
+        @pl.loop(0, rows // span)
+        def _(i):
+            part = pl.ds(pl.multiple_of(i * span, span), span)
+            gu_ref[part, :] = gu_r[0, part, :].astype(f32) + gu_r[1, part, :].astype(f32)
+            down_ref[part, :] = down_r[0, part, :].astype(f32) + down_r[1, part, :].astype(f32)
+
+
+def turn(low_pack, low_shared, act_all, in_all, shared_all, raw_gate_up, raw_down, bc_width, at):
+    f32, bf16 = jnp.float32, jnp.bfloat16
+    slot, width = low_pack.shape
+    shared_width = low_shared.shape[1]
+    features = act_all.shape[1]
+    here = slot // 4
+    blocks = at.blocks
+    rows = raw_gate_up.shape[0] // 2
+    block = 2 * rows
+    gu_width, down_width = raw_gate_up.shape[1], raw_down.shape[1]
+    dma = pltpu.SemaphoreType.DMA
+    vmem = pl.BlockSpec(memory_space=pltpu.VMEM)
+    anywhere = pl.BlockSpec(memory_space=pl.ANY)
+    shape = jax.ShapeDtypeStruct
+    return pl.pallas_call(
+        functools.partial(turn_body, blocks),
+        in_specs=[vmem] * 3 + [anywhere] * 2 + [vmem] * 2,
+        out_specs=[anywhere] * 3 + [vmem] * 3,
+        out_shape=[
+            shape((features, width), bf16),
+            shape((features, bc_width), bf16),
+            shape((features, shared_width - bc_width), bf16),
+            shape((here, features), f32),
+            shape((rows, gu_width), f32),
+            shape((rows, down_width), f32),
+        ],
+        scratch_shapes=[
+            pltpu.VMEM((2, block, width), bf16),
+            pltpu.VMEM((2, block, shared_width), bf16),
+            pltpu.VMEM((slot, features), f32),
+            pltpu.VMEM((blocks, here, block), f32),
+        ]
+        + [pltpu.VMEM((blocks, here, block), bf16)] * 6
+        + [
+            pltpu.VMEM((2, 256, width + shared_width), bf16),
+            pltpu.VMEM((2, rows, gu_width), bf16),
+            pltpu.VMEM((2, rows, down_width), bf16),
+            dma((2, 2)),
+            dma((3, blocks)),
+            dma((3, blocks)),
+            dma((2, 3)),
+            dma((2, 2)),
+            dma((2, 2)),
+        ],
+        compiler_params=pltpu.CompilerParams(
+            collective_id=4, has_side_effects=True, vmem_limit_bytes=58 * 1024 * 1024
+        ),
+        cost_estimate=pl.CostEstimate(
+            flops=slot * features * width * 5, bytes_accessed=60_000_000, transcendentals=0
+        ),
+    )(low_pack, low_shared, act_all, in_all, shared_all, raw_gate_up, raw_down)
 
 
 class Collect:
@@ -1763,20 +1957,20 @@
 
 
 def back_body(
-    blocks, in_cols, small_row, part_ref, bc_ref, kv_ref, own_ref, far_ref, core_ref, both_ref,
+    blocks, in_cols, small_row, part_ref, bc_ref, kv_ref, act_ref,
     resid_ref, x_ref, gain_ref, small_ref, out_ref,
     gin_ref, gsh_ref, gx_ref, sum_ref, gout_ref,
     in_send, in_recv, in_load, in_total, settle_s, settle_r, sh_came, sh_part, sh_send, sh_recv,
     sh_load, sh_total, line_s, line_r, near_s, near_r, swap_s, swap_r,
-    buf_both, buf_core, buf_far, pass_s, gx_s, gx_r, small_s, small_r,
+    gx_s, gx_r, small_s, small_r,
     in_ssem, in_rsem, in_lsem, sh_ssem, sh_rsem, sh_lsem, set_ssem, set_rsem, misc_s, misc_r,
-    pass_ssem, pass_rsem, small_ssem, small_rsem, out_r, out_ssem, out_rsem,
+    small_ssem, small_rsem, out_r, out_ssem, out_rsem,
 ):
     f32, bf16 = jnp.float32, jnp.bfloat16
     lanes = Lanes(blocks)
     c, t = lanes.c, lanes.t
     rows = gin_ref.shape[0]
-    here = own_ref.shape[0]
+    here = act_ref.shape[0]
     wide = bc_ref.shape[1]
     few = gsh_ref.shape[0]
     chunks = len(in_cols)
@@ -1799,12 +1993,6 @@
     )
     half_kv = kv_ref.shape[1] // 2
 
-    def send_both():
-        return remote(both_ref, buf_both, misc_s.at[0], misc_r.at[0], core_at)
-
-    def send_core():
-        return remote(core_ref, buf_core, misc_s.at[1], misc_r.at[1], core_at)
-
     def send_kv():
         return remote(
             kv_ref, sh_came.at[:, : 2 * half_kv], misc_s.at[2], misc_r.at[2], core_at
@@ -1822,22 +2010,9 @@
     def out_second():
         return remote(out_block(1 - c), out_r.at[1], out_ssem.at[1], out_rsem.at[1], cross_at)
 
-    send_both().start()
-
-    @pl.when(lanes.home)
-    def _():
-        out_first(1 - c, core_at).start()
-
-    @pl.when(lanes.away)
-    def _():
-        out_first(c, far_at).start()
-        out_second().start()
-
     collect.start()
     for chunk in range(chunks):
         collect.direct(chunk)
-    send_core().start()
-
     @pl.when(first)
     def _():
         send_kv().start()
@@ -1845,65 +2020,16 @@
     @pl.when(second)
     def _():
         send_bc().start()
-
-    parts = 2 if here >= 64 else 1
-    share = here // parts
-
-    def send_pass(part):
-        view = pl.ds(part * share, share)
-        return remote(
-            pass_s.at[view, :], buf_far.at[view, :], pass_ssem.at[part], pass_rsem.at[part], near_at
-        )
-
-    send_both().wait_recv()
-    for part in range(parts):
-
-        @pl.loop(0, share // step)
-        def _(i, part=part):
-            view = pl.ds(pl.multiple_of(part * share + i * step, step), step)
-            pass_s[view, :] = (far_ref[view, :] + buf_both[view, :].astype(f32)).astype(bf16)
-
-        send_pass(part).start()
-
-    @pl.when(first)
-    def _():
-        send_bc().wait_recv()
-
-        @pl.loop(0, bc_ref.shape[0] // 64)
-        def _(i):
-            view = pl.ds(pl.multiple_of(i * 64, 64), 64)
-            total = bc_ref[view, :].astype(f32) + sh_came[view, :].astype(f32)
-            sh_part[view, :] = total.astype(bf16)
-
-    @pl.when(second)
-    def _():
-        send_kv().wait_recv()
-
-        @pl.loop(0, bc_ref.shape[0] // 64)
-        def _(i):
-            view = pl.ds(pl.multiple_of(i * 64, 64), 64)
-            for piece in range(2):
-                kept = pl.ds(piece * half_kv, half_kv)
-                sh_part[view, pl.ds(2 * piece * half_kv, half_kv)] = sh_came[view, kept]
-                sh_part[view, pl.ds((2 * piece + 1) * half_kv, half_kv)] = kv_ref[view, kept]
-
-    shared.start()
-    for chunk in range(chunks):
-        collect.middle(chunk)
-    shared.direct(0)
 
     def send_x():
         return remote(gx_s, gx_r, misc_s.at[4], misc_r.at[4], cross_at)
 
-    send_core().wait_recv()
-    for part in range(parts):
-        send_pass(part).wait_recv()
     small_s[0] = small_ref[...]
     features = gain_ref.shape[1]
 
     def one_part(i, gains):
         view = pl.ds(pl.multiple_of(i * step, step), step)
-        grad = own_ref[view, :] + buf_core[view, :].astype(f32) + buf_far[view, :].astype(f32)
+        grad = act_ref[view, :]
         x = x_ref[view, :].astype(f32)
         scale = lax.rsqrt(jnp.mean(x * x, axis=1, keepdims=True) + EPS)
         gains = gains + jnp.sum(grad * (x * scale), axis=0, keepdims=True)
@@ -1918,11 +2044,7 @@
     for i in range(features // WIDE):
         small_s[0, small_row + i : small_row + i + 1, :] = gains[:, i * WIDE : (i + 1) * WIDE]
 
-    @pl.when(lanes.away)
-    def _():
-        send_x().start()
-
-    stops = [near_at, core_at, far_at] + [lanes.across(bit) for bit in range(lanes.bits)]
+    stops = [far_at, near_at, core_at] + [lanes.across(bit) for bit in range(lanes.bits)]
 
     def send_small(index):
         return remote(
@@ -1937,6 +2059,46 @@
             send_small(index + 1).start()
 
     send_small(0).start()
+
+    @pl.when(lanes.away)
+    def _():
+        send_x().start()
+
+    @pl.when(lanes.home)
+    def _():
+        out_first(1 - c, core_at).start()
+
+    @pl.when(lanes.away)
+    def _():
+        out_first(c, far_at).start()
+        out_second().start()
+
+    @pl.when(first)
+    def _():
+        send_bc().wait_recv()
+
+        @pl.loop(0, bc_ref.shape[0] // 64)
+        def _(i):
+            view = pl.ds(pl.multiple_of(i * 64, 64), 64)
+            total = bc_ref[view, :].astype(f32) + sh_came[view, :].astype(f32)
+            sh_part[view, :] = total.astype(bf16)
+
+    @pl.when(second)
+    def _():
+        send_kv().wait_recv()
+
+        @pl.loop(0, bc_ref.shape[0] // 64)
+        def _(i):
+            view = pl.ds(pl.multiple_of(i * 64, 64), 64)
+            for piece in range(2):
+                kept = pl.ds(piece * half_kv, half_kv)
+                sh_part[view, pl.ds(2 * piece * half_kv, half_kv)] = sh_came[view, kept]
+                sh_part[view, pl.ds((2 * piece + 1) * half_kv, half_kv)] = kv_ref[view, kept]
+
+    shared.start()
+    for chunk in range(chunks):
+        collect.middle(chunk)
+    shared.direct(0)
 
     def send_first(chunk, device):
         cols = in_cols[chunk]
@@ -1971,7 +2133,9 @@
         if chunk == 0:
             step_small(0)
             shared.middle(0)
-    step_small(1)
+        if chunk == 1:
+            step_small(1)
+    step_small(2)
     shared.last(0)
 
     t_high, t_low = lax.div(t, 2), lax.rem(t, 2)
@@ -1991,7 +2155,7 @@
     for half in range(2):
         line_s[half] = sh_total[half, theirs, :].astype(bf16)
     send_line().start()
-    step_small(2)
+    step_small(3)
     send_line().wait_recv()
     for half in range(2):
         sh_total[half, mine, :] = sh_total[half, mine, :] + line_r[half].astype(f32)
@@ -2000,7 +2164,7 @@
     for half in range(2):
         near_s[half] = sh_total[half, theirs, :].astype(bf16)
     send_near().start()
-    for index in range(3, len(stops)):
+    for index in range(4, len(stops)):
         step_small(index)
     send_near().wait_recv()
     for half in range(2):
@@ -2060,8 +2224,6 @@
 
     collect.finish()
     shared.finish()
-    send_both().wait_send()
-    send_core().wait_send()
 
     @pl.when(first)
     def _():
@@ -2071,8 +2233,6 @@
     def _():
         send_bc().wait_send()
 
-    for part in range(parts):
-        send_pass(part).wait_send()
     for chunk in range(chunks):
         send_first(chunk, core_at).wait_send()
 
@@ -2089,28 +2249,25 @@
     send_swap().wait_send()
 
 
-def back(part_in, bc, kv, act_parts, grad_resid, x, gain, small, small_row, raw_out, few, at):
+def back(part_in, bc, kv, grad_act, grad_resid, x, gain, small, small_row, raw_out, few, at):
     f32, bf16 = jnp.float32, jnp.bfloat16
-    own, core, far, both = act_parts
     blocks = at.blocks
     features, width = part_in.shape
     rows = features // (2 * blocks)
-    here = own.shape[0]
+    here = grad_act.shape[0]
     wide = bc.shape[1]
     chunks = 3
     piece = width // chunks
     in_cols = [slice(i * piece, (i + 1) * piece) for i in range(chunks)]
     loads = sum(bool(onward(p, h, at.bits)) for h in range(2) for p in range(blocks))
     steps = 3 + at.bits
-    parts = 2 if here >= 64 else 1
     dma = pltpu.SemaphoreType.DMA
     vmem = pl.BlockSpec(memory_space=pltpu.VMEM)
     anywhere = pl.BlockSpec(memory_space=pl.ANY)
     line = 2 * few
     return pl.pallas_call(
         functools.partial(back_body, blocks, in_cols, small_row),
-        in_specs=[anywhere, vmem, vmem, vmem, vmem, anywhere, anywhere]
-        + [vmem] * 5,
+        in_specs=[anywhere] + [vmem] * 8,
         out_specs=[vmem] * 5,
         out_shape=[
             jax.ShapeDtypeStruct((rows, width), f32),
@@ -2140,10 +2297,6 @@
             pltpu.VMEM((few, wide), bf16),
             pltpu.VMEM((here, features), bf16),
             pltpu.VMEM((here, features), bf16),
-            pltpu.VMEM((here, features), bf16),
-            pltpu.VMEM((here, features), bf16),
-            pltpu.VMEM((here, features), bf16),
-            pltpu.VMEM((here, features), bf16),
             pltpu.VMEM((steps + 1,) + small.shape, f32),
             pltpu.VMEM((steps,) + small.shape, f32),
             dma((2, blocks, chunks)),
@@ -2156,8 +2309,6 @@
             dma((2, chunks)),
             dma((8,)),
             dma((8,)),
-            dma((parts,)),
-            dma((parts,)),
             dma((steps,)),
             dma((steps,)),
             pltpu.VMEM((2, rows, raw_out.shape[1]), bf16),
@@ -2168,10 +2319,10 @@
             collective_id=2, has_side_effects=True, vmem_limit_bytes=58 * 1024 * 1024
         ),
         cost_estimate=pl.CostEstimate(
-            flops=here * features * 20, bytes_accessed=300_000_000, transcendentals=0
+            flops=here, bytes_accessed=here, transcendentals=0
         ),
     )(
-        part_in, bc, kv, own, far, core, both, grad_resid, x, gain.reshape(1, -1), small,
+        part_in, bc, kv, grad_act, grad_resid, x, gain.reshape(1, -1), small,
         raw_out,
     )
 
@@ -2228,17 +2379,18 @@
     return gather_blocks(pair_weight(shard, at), at)
 
 
-def settle_weight(mine, later, at):
-    f32 = jnp.float32
+def send_settle(mine, at):
     rows = mine.shape[0] // 2
     low, high = mine[:rows], mine[rows:]
     own = jnp.where(at.c == 0, low, high)
     other = jnp.where(at.c == 0, high, low)
-    first_in = at.column_back(jnp.where(at.home, other, own))
-    second_in = at.swap_away(other)
-    first_in, second_in, own, _ = lax.optimization_barrier((first_in, second_in, own, later))
-    first_in, second_in = first_in.astype(f32), second_in.astype(f32)
-    return first_in + jnp.where(at.home, own.astype(f32), second_in)
+    return at.column_back(jnp.where(at.home, other, own)), at.swap_away(other), own
+
+
+def end_settle(moves, at):
+    first_in, second_in, own = moves
+    f32 = jnp.float32
+    return first_in.astype(f32) + jnp.where(at.home, own, second_in).astype(f32)
 
 
 def gather_shared(shard, at):
@@ -2333,21 +2485,6 @@
     bc_width = conv_shared.shape[1]
     w_rows = step_weight.shape[0]
 
-    column_params = jnp.concatenate(
-        [conv_inner.reshape(-1), inner_gain, step_bias, decay_log, skip_gain]
-    )
-    column_params = relocate(column_params, at)
-    lane_params = jnp.concatenate(
-        [
-            column_params[: (KC + 1) * width].reshape(KC + 1, width),
-            jnp.repeat(column_params[(KC + 1) * width + 2 * local_heads :], head_dim)[None],
-            jnp.zeros((2, width), f32),
-        ],
-        axis=0,
-    )
-    head_rows = column_params[(KC + 1) * width :][: 2 * local_heads].reshape(2, local_heads)
-    head_rows = jnp.concatenate([head_rows[:1], -jnp.exp(head_rows[1:])], axis=0)
-    head_params = jnp.pad(head_rows, ((0, 6), (0, WIDE - local_heads)))
     seg = (
         lax.broadcasted_iota(jnp.int32, (width, WIDE), 0) // head_dim
         == lax.broadcasted_iota(jnp.int32, (width, WIDE), 1)
@@ -2371,9 +2508,25 @@
         axis=1,
     )
     out_pack = jnp.concatenate([mixer_out_weight, attn_out_weight], axis=1)
-    in_all, out_pair, act_all, x_low, shared_full = front(
-        in_pack, out_pack, shared_weight, layer_in, input_gain, at
-    )
+    column_params = jnp.concatenate(
+        [conv_inner.reshape(-1), inner_gain, step_bias, decay_log, skip_gain]
+    )
+    params = jnp.pad(column_params, (0, -column_params.shape[0] % 1024)).reshape(-1, WIDE)
+    in_all, out_pair, act_all, x_low, shared_full, params = front(
+        in_pack, out_pack, shared_weight, layer_in, input_gain, params, at
+    )
+    column_params = params.reshape(-1)[: column_params.shape[0]]
+    lane_params = jnp.concatenate(
+        [
+            column_params[: (KC + 1) * width].reshape(KC + 1, width),
+            jnp.repeat(column_params[(KC + 1) * width + 2 * local_heads :], head_dim)[None],
+            jnp.zeros((2, width), f32),
+        ],
+        axis=0,
+    )
+    head_rows = column_params[(KC + 1) * width :][: 2 * local_heads].reshape(2, local_heads)
+    head_rows = jnp.concatenate([head_rows[:1], -jnp.exp(head_rows[1:])], axis=0)
+    head_params = jnp.pad(head_rows, ((0, 6), (0, WIDE - local_heads)))
     left, right = shared_full[:, :bc_width], shared_full[:, bc_width:]
     kv_index = at.column * (query_width // HD) // (QH // KVH)
     second = kv_index == 1
@@ -2392,7 +2545,6 @@
     out_all = gather_blocks(out_pair, at)
     proj_shared = jnp.dot(act_all, shared_all, preferred_element_type=f32)
     proj = jnp.dot(act_all, in_all, preferred_element_type=f32)
-    target = relocate(after(teacher, proj), at)
     attn_low = attn_forward(order, proj, proj_shared, cosine, sine, query_width, width, bc_width)
     heads_all, y, states = mixer_forward(
         order, proj, proj_shared, attn_low, lane_params, conv_shared, head_params
@@ -2403,8 +2555,9 @@
     seq_len = lax.dynamic_index_in_dim(lengths, at.slot, keepdims=False)
     positions = at.quarter * rows_here + jnp.arange(rows_here)
     live = (positions < seq_len).astype(f32)[:, None]
-    ff_all, mid_all, gate_low, up_low, hidden, grad_all, resid, error, outputs, loss_part = middle(
-        ff_pack, heads_all, out_all, x_low, middle_gain, target, live, at
+    ff_pair = pair_weight(ff_pack, at)
+    ff_all, mid_all, gate_low, up_low, hidden, grad_all, resid, error, layer_out, loss_part = middle(
+        ff_pair, heads_all, out_all, x_low, middle_gain, teacher, live, at
     )
     err_local = loss_part[0, 0]
     _, norm_mid_back = jax.vjp(rms_norm, resid, middle_gain)
@@ -2437,7 +2590,6 @@
     grad_heads = jnp.dot(mix_grad_all, out_all, preferred_element_type=f32)
     part_out = weight_grad(mix_grad_all, heads_all)
     grad_heads, part_out, raw_down = lax.optimization_barrier((grad_heads, part_out, raw_down))
-    layer_out = relocate(after(outputs, grad_heads), at)
     dq, dkv = attn_backward(
         order, proj, proj_shared, cosine, sine, grad_heads, query_width, width, bc_width
     )
@@ -2471,21 +2623,13 @@
     padded = -(-flat.shape[0] // 1024) * 1024
     flat = jnp.pad(flat, (0, padded - flat.shape[0])).reshape(-1, WIDE)
 
-    grad_act_parts = [
-        lax.dot_general(a, in_all, contract_last, preferred_element_type=f32)
-        + lax.dot_general(b, shared_all, contract_last, preferred_element_type=f32)
-        for a, b in zip(row_split(low_pack), row_split(low_shared))
-    ]
-    grad_act_parts[1] = grad_act_parts[1].astype(bf16)
-    grad_act_parts[3] = grad_act_parts[3].astype(bf16)
-    part_bc = weight_grad(act_all, low_shared[:, :bc_width])
-    part_kv = weight_grad(act_all, low_shared[:, bc_width:])
-    part_in = weight_grad(act_all, low_pack)
+    part_in, part_bc, part_kv, grad_act, grad_gate_up, grad_down = turn(
+        low_pack, low_shared, act_all, in_all, shared_all, raw_gate_up, raw_down, bc_width, at
+    )
     grad_in, grad_shared_weight, input_grad, flat, grad_out = back(
-        part_in, part_bc, part_kv, grad_act_parts, grad_resid, x_low, input_gain, flat, 0,
+        part_in, part_bc, part_kv, grad_act, grad_resid, x_low, input_gain, flat, 0,
         raw_out, shared_weight.shape[0], at,
     )
-    grad_ff = settle_weight(jnp.concatenate([raw_gate_up, raw_down], axis=1), grad_in, at)
     flat = flat.reshape(-1)
     sums = []
     start = 0
@@ -2516,8 +2660,8 @@
         grad_out[:, :width],
         grad_out[:, width:],
         sum_middle_gain,
-        grad_ff[:, : 2 * hidden_width].reshape(w_rows, 2, hidden_width),
-        grad_ff[:, 2 * hidden_width :],
+        grad_gate_up.reshape(w_rows, 2, hidden_width),
+        grad_down,
     )
 
 

time: 828 us -> 801 us (0.967)
  matrix products: 135 us -> 85.6 us
  Pallas kernels: 535 us -> 567 us
  starting transfers between devices: 19.7 us -> 6.06 us
  waiting for transfers between devices: 35 us -> 45.2 us
    pallas_call x1 -> x2, Pallas kernels: 117 us -> 197 us  [the longest x1 117 us: front(): pl.pallas_call(functools.partial(front_body, blocks, chunks), in_specs=[p...]
    pallas_call x1, Pallas kernels: 158 us -> 126 us  [back(): pl.pallas_call(functools.partial(back_body, blocks, in_cols, small_row),...]
    dot_general x6 -> x3, matrix products: 49.8 us -> 27.3 us  [weight_grad(): lax.dot_general(left, right, contract_first, preferred_element_type=f32)]
    dot_general x8 -> x0, matrix products: 21.5 us -> none  [the longest x4 12.9 us: per_device(): lax.dot_general(a, in_all, contract_last, preferred_element_type=f32)]
    pallas_call x1, Pallas kernels: 190 us -> 175 us  [middle(): pl.pallas_call(functools.partial(middle_body, blocks, gu_chunks, down_chu...]
    ppermute x11 -> x8, waiting for transfers between devices: 31.3 us -> 45.1 us  [send(): return lax.ppermute(values, ('dp', 'tensor'), self.pairs(where_to))]
    ppermute x11 -> x8, starting transfers between devices: 19.3 us -> 5.9 us  [send(): return lax.ppermute(values, ('dp', 'tensor'), self.pairs(where_to))]
    unnamed x105 -> x85, local copies, waits for them, and re-layouts: 28.4 us -> 22.2 us
  transfers between devices with their start and end apart: 15 -> 12, of which waited for: 3 -> 5; matrix products, arithmetic and copies ran while one was open for 19% -> 14% of each run, Pallas kernels for 28% -> 19%
where the time goes in v5:
time: 801 us; the launch traced here: 794 us
  Pallas kernels  567 us (71%)
  matrix products  85.6 us (11%)
  local copies, waits for them, and re-layouts  48.7 us (6%)
  waiting for transfers between devices  45.2 us (6%)
  other arithmetic  24.5 us (3%)
  between operations  17.1 us (2%)
    pallas_call x1, Pallas kernels, middle(): pl.pallas_call(functools.partial(middle_body, blocks, gu_chunks, down_chu...  175 us
    pallas_call x1, Pallas kernels, back(): pl.pallas_call(functools.partial(back_body, blocks, in_cols, small_row),...  126 us
    pallas_call x1, Pallas kernels, front(): pl.pallas_call(functools.partial(front_body, blocks, chunks), in_specs=[p...  117 us
    pallas_call x1, Pallas kernels, turn(): pl.pallas_call(functools.partial(turn_body, blocks), in_specs=[vmem] * 3...  79.2 us
    ppermute x8, waiting for transfers between devices, send(): return lax.ppermute(values, ('dp', 'tensor'), self.pairs(where_to))  45.1 us
    pallas_call x1, Pallas kernels, mixer_backward(): pl.pallas_call(mixer_bwd_body, grid_spec=pltpu.PrefetchScalarGridSpec(num...  33.1 us
    dot_general x3, matrix products, weight_grad(): lax.dot_general(left, right, contract_first, preferred_element_type=f32)  27.3 us
    unnamed x85, local copies, waits for them, and re-layouts  22.2 us
  transfers between devices with their start and end apart: 12, of which 5 were waited for; matrix products, arithmetic and copies ran while one was open for 14% of the time, Pallas kernels for 19%

profile of v5, /device:TPU:1, one launch (start us, length us, event | category | flops | bytes accessed | tf_op | source)
XLA Modules:
  0.0 794.0 jit_solution(2246882473003379507)
XLA Ops:
  14.5 117.5 %shard_map.330 = (bf16[2048,1920]{1,0:T(8,128)(2,1)S(1)}, bf16[512,1024]{1,0:T(8,128)(2,1)}, bf16[1024,2048]{1,0:T(8,128)(2,1)S(1)}, bf16[256,2048]{1,0:T(8,128)...) custom-call(bf16[256,1920]{1,0:T(8,128)(2,1)S(1)} %concatenate.44.in_ref, ...), custom_call_target="tpu_custom_call" | custom-call | flops 4194304 | bytes 300000000 | tf_op jit(solution)/shard_map/pallas_call | solution.py:1133
  152.7 15.4 %fusion.61.q_ref.gate_ref.inner_ref.step_ref.before_ref = f32[1024,1920]{1,0:T(8,128)} fusion(bf16[1024,2048]{1,0:T(8,128)(2,1)} %copy-done.7, bf16[2048,1920]{1,0:T(8,128)(2,1)} %copy-done.6), kind=kOutput, calls=%fused_computation.120 | convolution fusion | flops 8053063680 | bytes 19922944 | tf_op jit(solution)/shard_map/dot_general | solution.py:2547
  168.1 5.0 fusion.58.kv_ref.bc_ref.bcbefore_ref
  173.1 7.9 shard_map.331.attn_ref
  183.6 15.7 %shard_map.332 = (bf16[1024,1024]{1,0:T(8,128)(2,1)}, f32[1024,768]{1,0:T(8,128)}, bf16[8,256,768]{2,1,0:T(8,128)(2,1)}) custom-call(s32[4]{0:T(128)} %fusion.47.order, f32[1024,1920]{1,0:T(8,128)} %fusion.61.q_ref.gate_ref.inner_ref.step_ref.before_ref, f32[1024,1920]{1,0:T(8,128)} %fusion.61.q_ref.gate_ref.inner_ref.step_ref.before_ref, ...), custom_call_target="tpu_custom_call" | custom-call | flops 3221225472 | bytes 15728640 | tf_op jit(solution)/shard_map/pallas_call | solution.py:480
  199.3 14.5 %collective-permute-done = bf16[256,3072]{1,0:T(8,128)(2,1)} collective-permute-done((bf16[256,3072]{1,0:T(8,128)(2,1)}, bf16[256,3072]{1,0:T(8,128)(2,1)}, u32[]{:S(2)}, u32[]{:S(2)}) %collective-permute-start) | collective-permute-done | bytes 1572896 | tf_op jit(solution)/shard_map/ppermute | solution.py:641
  218.5 174.8 %shard_map.333 = (bf16[2048,3072]{1,0:T(8,128)(2,1)}, bf16[1024,2048]{1,0:T(8,128)(2,1)}, bf16[1024,1024]{1,0:T(8,128)(2,1)}, bf16[1024,1024]{1,0:T(8,128)(2,1)}...) custom-call(bf16[512,3072]{1,0:T(8,128)(2,1)} %pad_maximum_fusion.3., ...), custom_call_target="tpu_custom_call" | custom-call | flops 17179869184 | bytes 400000000 | tf_op jit(solution)/shard_map/pallas_call | solution.py:1603
  393.4 9.4 %convolution_convert_fusion.2 = bf16[2048,1024]{1,0:T(8,128)(2,1)} fusion(bf16[1024,2048]{1,0:T(8,128)(2,1)} %get-tuple-element.80, bf16[1024,1024]{1,0:T(8,128)(2,1)} %get-tuple-element.79), kind=kOutput, calls=%fused_computation.33 | convolution fusion | flops 4297064448 | bytes 10485760 | tf_op jit(solution)/shard_map/dot_general | solution.py:2570
  402.8 7.7 fusion.16
  412.7 7.1 fusion.21
  420.0 3.4 fusion.18
  423.8 3.4 add_convert_fusion
  427.2 11.8 %convolution_convert_fusion = bf16[2048,2048]{1,0:T(8,128)(2,1)} fusion(bf16[1024,2048]{1,0:T(8,128)(2,1)S(1)} %copy-done.33, bf16[1024,1024]{1,0:T(8,128)(2,1)S(1)} %get-tuple-element.157, bf16[1024,1024]{1,0:T(8,128)(2,1)S(1)} %get-tuple-element.158), kind=kOutput, calls=%fused_computation | convolution fusion | flops 8602517504 | bytes 16777216 | tf_op jit(solution)/shard_map/dot_general | solution.py:2570
  439.0 6.3 fusion.6
  445.4 6.8 collective-permute-done.4
  452.1 3.4 convert_add_fusion
  462.1 22.5 %collective-permute-done.6 = bf16[256,2048]{1,0:T(8,128)(2,1)S(1)} collective-permute-done((bf16[256,2048]{1,0:T(8,128)(2,1)S(1)}, bf16[256,2048]{1,0:T(8,128)(2,1)S(1)}, u32[]{:S(2)}, u32[]{:S(2)}) %collective-permute-start.6) | collective-permute-done | bytes 1048608 | tf_op jit(solution)/shard_map/ppermute | solution.py:641
  490.0 6.1 convolution_convert_fusion.1
  496.1 9.9 %fusion.37.grad_ref = f32[1024,1024]{1,0:T(8,128)} fusion(bf16[2048,1024]{1,0:T(8,128)(2,1)} %all-gather.2.cloned.1.call-done.out_ref, bf16[256,2048]{1,0:T(8,128)(2,1)} %copy-done.30, bf16[256,2048]{1,0:T(8,128)(2,1)S(1)} %collective-permute-done.6, bf16[256,2048]{1,0:T(8,128)(2,1)} %copy-done.29, bf16[256,2048]{1,0:T(8,128)(2,1)} %copy-done.18), kind=kOutput, calls=%fused_computation.55 | convolution fusion | flops 4311744512 | bytes 12582912 | tf_op jit(solution)/shard_map/dot_general | solution.py:2590
  506.0 12.4 %shard_map.334 = (bf16[1024,256]{1,0:T(8,128)(2,1)}, bf16[1024,256]{1,0:T(8,128)(2,1)}) custom-call(s32[4]{0:T(128)} %fusion.47.order, f32[1024,1920]{1,0:T(8,128)} %fusion.61.q_ref.gate_ref.inner_ref.step_ref.before_ref, f32[1024,768]{1,0:T(8,128)} %fusion.58.kv_ref.bc_ref.bcbefore_ref, f32[1024,128]{1,0:T(8,128)} %get-tuple-element.175.cos_ref.all_cos, ...), custom_call_target="tpu_custom_call" | custom-call | flops 2147483648 | bytes 5242880 | tf_op jit(solution)/shard_map/pallas_call | solution.py:442
  518.4 33.1 %shard_map.335 = (bf16[1024,1920]{1,0:T(8,128)(2,1)}, bf16[1024,768]{1,0:T(8,128)(2,1)}, f32[8,768]{1,0:T(8,128)}, f32[8,512]{1,0:T(8,128)}, f32[8,128]{1,0:T(8,128)}) custom-call(s32[4]{0:T(128)} %fusion.47.order, f32[1024,1920]{1,0:T(8,128)} %fusion.61.q_ref.gate_ref.inner_ref.step_ref.before_ref, ...), custom_call_target="tpu_custom_call" | custom-call | flops 8053063680 | bytes 31457280 | tf_op jit(solution)/shard_map/pallas_call | solution.py:549
  559.3 79.2 %shard_map.336 = (bf16[2048,1920]{1,0:T(8,128)(2,1)}, bf16[2048,512]{1,0:T(8,128)(2,1)}, bf16[2048,256]{1,0:T(8,128)(2,1)}, f32[256,2048]{1,0:T(8,128)}, f32[256,2048]{1,0:T(8,128)}, /*index=5*/f32[256,1024]{1,0:T(8,128)}) custom-call(bf16[1024,1920]{1,0:T(8,128)(2,1)} %get-tuple-element.95.low_ref, bf16[1024,768]{1,0:T(8,128)(2,1)} %get-tuple-element.96.lowsh_ref, ...), custom_call_target="tpu_custom_call" | custom-call | flops 20132659200 | bytes 60000000 | tf_op jit(solution)/shard_map/pallas_call | solution.py:1832
  638.5 4.0 reshape.170
  642.5 126.3 %shard_map.337 = (f32[256,1920]{1,0:T(8,128)}, f32[64,1024]{1,0:T(8,128)}, f32[256,2048]{1,0:T(8,128)}, f32[176,128]{1,0:T(8,128)}, f32[256,1024]{1,0:T(8,128)}) custom-call(bf16[2048,1920]{1,0:T(8,128)(2,1)} %get-tuple-element.99.part_ref, bf16[2048,512]{1,0:T(8,128)(2,1)} %get-tuple-element.100.bc_ref, bf16[2048,256]{1,0:T(8,128)(2,1)} %get-tuple-element.101.kv_ref, ...), custom_call_target="tpu_custom_call" | custom-call | flops 256 | bytes 256 | tf_op jit(solution)/shard_map/pallas_call | solution.py:2268
  (180 shorter events, 73.2 us)
Async XLA Ops:
  7.2 7.2 copy-start.4
  7.2 211.3 %all-gather.2.cloned.1.call-start = ((), (), s32[]{:S(2)}) async-start(), calls=%async_computation.3 | async-start | bytes 5242880 | tf_op jit(solution)/shard_map/all_gather | solution.py:2356
  139.9 366.0 %reduce-scatter.4.cloned.1.call-start = ((), (), s32[]{:S(2)}) async-start(), calls=%async_computation.4 | async-start | bytes 5242880 | tf_op jit(solution)/shard_map/reduce_scatter | solution.py:2360
  143.4 70.4 %collective-permute-start = (bf16[256,3072]{1,0:T(8,128)(2,1)}, bf16[256,3072]{1,0:T(8,128)(2,1)}, u32[]{:S(2)}, u32[]{:S(2)}) collective-permute-start(bf16[256,3072]{1,0:T(8,128)(2,1)} %constant_dynamic-update-slice_fusion), channel_id=1, source_target_pairs={{0,2},{1,3},{2,6},{3,7},{4,0},{5,1},{6,4},{7,5},{8,10},{9,11},{10,... | collective-permute-start | bytes 4718600 | tf_op jit(solution)/shard_map/ppermute | solution.py:641
  143.8 70.7 %collective-permute-start.1 = (bf16[256,3072]{1,0:T(8,128)(2,1)}, bf16[256,3072]{1,0:T(8,128)(2,1)}, u32[]{:S(2)}, u32[]{:S(2)}) collective-permute-start(bf16[256,3072]{1,0:T(8,128)(2,1)} %constant_dynamic-update-slice_fusion), channel_id=1, source_target_pairs={{2,4},{3,5},{4,2},{5,3},{10,12},{11,13},{12,10},{13,11},{18,20},{1... | collective-permute-start | bytes 4718600 | tf_op jit(solution)/shard_map/ppermute | solution.py:641
  147.7 20.3 %copy-start.11 = (bf16[2048,512]{1,0:T(8,128)(2,1)}, bf16[2048,512]{1,0:T(8,128)(2,1)S(1)}, u32[]{:S(2)}) copy-start(bf16[2048,512]{1,0:T(8,128)(2,1)S(1)} %slice.135) | copy-start | bytes 6291460
  152.7 15.4 %copy-start.8 = (bf16[1024,2048]{1,0:T(8,128)(2,1)S(1)}, bf16[1024,2048]{1,0:T(8,128)(2,1)}, u32[]{:S(2)}) copy-start(bf16[1024,2048]{1,0:T(8,128)(2,1)} %copy-done.7) | copy-start | bytes 12582916
  402.8 148.8 %reduce-scatter.6.cloned.1.call-start = ((), (), s32[]{:S(2)}) async-start(), calls=%async_computation.5 | async-start | bytes 10485760 | tf_op jit(solution)/shard_map/reduce_scatter | solution.py:2360
  402.8 7.7 copy-start.16
  402.8 7.7 copy-start.17
  410.5 9.4 %slice-start = ((s8[12582912]{0:T(1024)(128)(4,1)}), s8[4194304]{0:T(1024)(128)(4,1)S(1)}, s32[]{:S(2)}) async-start(s8[12582912]{0:T(1024)(128)(4,1)} %bitcast.56), calls=%async_computation.7 | async-start | bytes 8388608
  410.5 9.4 %slice-start.1 = ((s8[12582912]{0:T(1024)(128)(4,1)}), s8[4194304]{0:T(1024)(128)(4,1)S(1)}, s32[]{:S(2)}) async-start(s8[12582912]{0:T(1024)(128)(4,1)} %bitcast.56), calls=%async_computation.8 | async-start | bytes 8388608
  412.7 14.6 %copy-start.15 = (bf16[1024,1024]{1,0:T(8,128)(2,1)}, bf16[1024,1024]{1,0:T(8,128)(2,1)S(1)}, u32[]{:S(2)}) copy-start(bf16[1024,1024]{1,0:T(8,128)(2,1)S(1)} %get-tuple-element.158) | copy-start | bytes 6291460
  412.7 7.3 slice-start.2
  419.8 4.0 collective-permute-start.3
  423.4 22.0 %collective-permute-start.2 = (bf16[256,2048]{1,0:T(8,128)(2,1)}, bf16[256,2048]{1,0:T(8,128)(2,1)}, u32[]{:S(2)}, u32[]{:S(2)}) collective-permute-start(bf16[256,2048]{1,0:T(8,128)(2,1)} %fusion.18), channel_id=1, source_target_pairs={{0,4},{1,5},{2,6},{3,7},{4,0},{5,1},{6,2},{7,3},{8,12},{9,13},{10,... | collective-permute-start | bytes 3145736 | tf_op jit(solution)/shard_map/ppermute | solution.py:641
  427.2 24.9 %collective-permute-start.4 = (bf16[256,2048]{1,0:T(8,128)(2,1)}, bf16[256,2048]{1,0:T(8,128)(2,1)}, u32[]{:S(2)}, u32[]{:S(2)}) collective-permute-start(bf16[256,2048]{1,0:T(8,128)(2,1)} %add_convert_fusion), channel_id=1, source_target_pairs={{0,1},{1,0},{2,3},{3,2},{4,5},{5,4},{6,7},{7,6},{8,9},{9,8},{10,11... | collective-permute-start | bytes 3145736 | tf_op jit(solution)/shard_map/ppermute | solution.py:641
  455.5 187.0 %reduce-scatter.8.cloned.1.call-start = ((), (), s32[]{:S(2)}) async-start(), calls=%async_computation.6 | async-start | bytes 5242880 | tf_op jit(solution)/shard_map/reduce_scatter | solution.py:2360
  458.8 31.1 %copy-start.28 = (bf16[1024,1024]{1,0:T(8,128)(2,1)S(1)}, bf16[1024,1024]{1,0:T(8,128)(2,1)}, u32[]{:S(2)}) copy-start(bf16[1024,1024]{1,0:T(8,128)(2,1)} %get-tuple-element.71.heads_ref) | copy-start | bytes 6291460
  460.8 27.9 %copy-start.18 = (bf16[256,2048]{1,0:T(8,128)(2,1)}, bf16[256,2048]{1,0:T(8,128)(2,1)S(1)}, u32[]{:S(2)}) copy-start(bf16[256,2048]{1,0:T(8,128)(2,1)S(1)} %get-tuple-element.155) | copy-start | bytes 3145732
  460.8 23.8 %collective-permute-start.6 = (bf16[256,2048]{1,0:T(8,128)(2,1)S(1)}, bf16[256,2048]{1,0:T(8,128)(2,1)S(1)}, u32[]{:S(2)}, u32[]{:S(2)}) collective-permute-start(bf16[256,2048]{1,0:T(8,128)(2,1)S(1)} %get-tuple-element.155), channel_id=1, source_target_pairs={{0,1},{1,0},{2,3},{3,2},{4,5},{5,4},{6,7},{7,6},{8,9},{9,8},{10,11... | collective-permute-start | bytes 3145736 | tf_op jit(solution)/shard_map/ppermute | solution.py:641
  461.1 27.0 %collective-permute-start.5 = (bf16[256,2048]{1,0:T(8,128)(2,1)S(1)}, bf16[256,2048]{1,0:T(8,128)(2,1)S(1)}, u32[]{:S(2)}, u32[]{:S(2)}) collective-permute-start(bf16[256,2048]{1,0:T(8,128)(2,1)S(1)} %get-tuple-element.155), channel_id=1, source_target_pairs={{0,4},{1,5},{2,6},{3,7},{4,0},{5,1},{6,2},{7,3},{8,12},{9,13},{10,... | collective-permute-start | bytes 3145736 | tf_op jit(solution)/shard_map/ppermute | solution.py:641
  484.6 4.1 collective-permute-start.7
  771.4 10.8 %copy-start.20 = (bf16[256,2048]{1,0:T(8,128)(2,1)S(1)}, bf16[256,2048]{1,0:T(8,128)(2,1)}, u32[]{:S(2)}) copy-start(bf16[256,2048]{1,0:T(8,128)(2,1)} %get-tuple-element.198) | copy-start | bytes 3145732
  (25 other events, 77.0 us)
Sparse Core Ops, SparseCore 0:
  140.1 51.9 all-gather.1
  402.9 50.9 reduce-scatter.3
  457.3 86.3 reduce-scatter.5
  551.7 51.5 reduce-scatter.7

commit v6 on v5

--- a/solution.py
+++ b/solution.py
@@ -242,7 +242,7 @@
 
 def mixer_bwd_body(
     order, gate_ref, inner_ref, before_ref, step_ref, bc_ref, bcbefore_ref, y_ref, state_ref,
-    grad_ref, dq_ref, dkv_ref, lane_ref, conv_ref, head_ref, seg_ref,
+    grad_ref, dq_ref, dkv_ref, lane_ref, conv_ref, head_ref, seg_ref, first_ref, second_ref,
     low_ref, lowsh_ref, dlane_ref, dconv_ref, dhead_ref,
     ext_s, extbc_s, pre_s, prebc_s, x_s, bc_s, g_s, dx_s, dbc_s, dpre_s, dprebc_s, dstate_s,
     z_s, rows_s,
@@ -520,7 +520,7 @@
 
 def mixer_backward(
     order, proj, proj_shared, y, states, grad_heads, dq, dkv, lane_params, conv_shared,
-    head_params, seg, query_width,
+    head_params, seg, query_width, moved,
 ):
     slot = proj.shape[0]
     f32, bf16 = jnp.float32, jnp.bfloat16
@@ -567,6 +567,8 @@
                 whole_at(conv_shared.shape),
                 whole_at(head_params.shape),
                 whole_at(seg.shape),
+                pl.BlockSpec(memory_space=pl.ANY),
+                pl.BlockSpec(memory_space=pl.ANY),
             ],
             out_specs=[
                 back(ROWS, 2 * width + query_width + WIDE, 0),
@@ -607,7 +609,7 @@
         ),
     )(
         order, proj, proj, proj, proj, proj_shared, proj_shared, y, states, grad_heads, dq, dkv,
-        lane_params, conv_shared, head_params, seg,
+        lane_params, conv_shared, head_params, seg, *moved,
     )
 
 
@@ -740,9 +742,9 @@
 
 
 class Spread:
-    def __init__(self, lanes, full, rows, chunks, send_sems, recv_sems, cols=slice(None), first=None):
+    def __init__(self, lanes, full, rows, chunks, send_sems, recv_sems, cols=slice(None), first=None, first_cols=None):
         self.lanes, self.full, self.rows, self.chunks = lanes, full, rows, chunks
-        self.cols, self.first = cols, first
+        self.cols, self.first, self.first_cols = cols, first, first_cols
         self.piece = rows // chunks
         self.send_sems, self.recv_sems = send_sems, recv_sems
 
@@ -756,7 +758,7 @@
         source = view
         if place == 0 and self.first is not None:
             start = half * self.rows + chunk * self.piece
-            source = self.first.at[pl.ds(start, self.piece), self.cols]
+            source = self.first.at[pl.ds(start, self.piece), self.first_cols]
         return remote(
             source,
             view,
@@ -790,11 +792,13 @@
                     self.take(place, half, chunk)
                     self.give(place, half, chunk)
 
-    def finish(self, chunk):
+    def settle(self, place):
         for half in range(2):
-            for place in range(1, self.lanes.blocks):
-                if not onward(place, half, self.lanes.bits):
+            if not onward(place, half, self.lanes.bits):
+                for chunk in range(self.chunks):
                     self.take(place, half, chunk)
+
+    def sent(self, chunk):
         for half in range(2):
             for place in range(self.lanes.blocks):
                 for bit in onward(place, half, self.lanes.bits):
@@ -802,10 +806,11 @@
 
 
 def front_body(
-    blocks, chunks, in_ref, out_ref, shared_ref, x_ref, gain_ref, par_ref,
-    full_ref, pair_ref, act_ref, xr_ref, sh_ref, parr_ref,
+    blocks, chunks, in_ref, out_ref, down_ref, shared_ref, x_ref, gain_ref, par_ref,
+    full_ref, pair_ref, dpair_ref, act_ref, xr_ref, sh_ref, parr_ref, proj_ref, projsh_ref, shall_ref,
     x_s, act_s, home_sems, z_send, z_recv, o_sems, o_recv, send_sems, recv_sems, x_sems, a_send,
     a_recv, line_send, line_recv, sh_send, sh_recv, swap_send, swap_recv, par_sems,
+    win_s, wsh_s, acc_s, w_sems, keep_sems, out_sems,
 ):
     lanes = Lanes(blocks)
     rows = in_ref.shape[0]
@@ -893,14 +898,25 @@
             in_ref.at[pl.ds(chunk * piece, piece), :], slot(chunk), home_sems.at[chunk]
         )
 
-    def out_slot():
-        return pair_ref.at[pl.ds(pl.multiple_of(c * rows, rows), rows), :]
-
-    def out_first(device):
-        return remote(out_ref, out_slot(), o_sems.at[0], o_recv.at[c], device)
-
-    def out_second():
-        return remote(out_ref, out_slot(), o_sems.at[1], o_recv.at[c], (lanes.other, lanes.far))
+    riders = ((out_ref, pair_ref), (down_ref, dpair_ref))
+
+    def out_slot(i):
+        return riders[i][1].at[pl.ds(pl.multiple_of(c * rows, rows), rows), :]
+
+    def out_first(i, device):
+        return remote(riders[i][0], out_slot(i), o_sems.at[i, 0], o_recv.at[i, c], device)
+
+    def out_second(i):
+        return remote(
+            riders[i][0], out_slot(i), o_sems.at[i, 1], o_recv.at[i, c], (lanes.other, lanes.far)
+        )
+
+    def out_own(i):
+        return pltpu.make_async_copy(riders[i][0], out_slot(i), o_sems.at[i, 2])
+
+    def out_came(i, half):
+        view = riders[i][1].at[pl.ds(pl.multiple_of(half * rows, rows), rows), :]
+        remote(view, view, o_sems.at[i, 0], o_recv.at[i, half], (lanes.other, t)).wait_recv()
 
     def x_away():
         return remote(x_ref, x_s, x_sems.at[0], x_sems.at[1], (lanes.other, lanes.far))
@@ -954,14 +970,18 @@
         def _():
             arrive_away(chunk)
 
+    block = 2 * rows
+
     def act_slot(index):
-        return act_ref.at[pl.ds(index * here, here), :]
+        return act_s.at[:, pl.ds(index * here, here), :]
 
     def act_far():
-        return remote(act_s, act_slot(2), a_send.at[0], a_recv.at[0], (lanes.d, lanes.near))
+        return remote(
+            act_slot(0), act_slot(2), a_send.at[0], a_recv.at[0], (lanes.d, lanes.near)
+        )
 
     def act_core():
-        return remote(act_s, act_slot(1), a_send.at[1], a_recv.at[1], (lanes.other, t))
+        return remote(act_slot(0), act_slot(1), a_send.at[1], a_recv.at[1], (lanes.other, t))
 
     def act_both():
         return remote(act_slot(2), act_slot(3), a_send.at[2], a_recv.at[2], (lanes.other, t))
@@ -980,11 +1000,12 @@
             part = pl.ds(pl.multiple_of(step * 32, 32), 32)
             x = x_s[part, :].astype(jnp.float32)
             scale = lax.rsqrt(jnp.mean(x * x, axis=1, keepdims=True) + EPS)
-            act_s[part, :] = (x * scale * gain_ref[...]).astype(jnp.bfloat16)
+            act = (x * scale * gain_ref[...]).astype(jnp.bfloat16)
+            for index in range(blocks):
+                act_s[index, part, :] = act[:, index * block : (index + 1) * block]
 
         act_far().start()
         act_core().start()
-        pltpu.make_async_copy(act_s, act_slot(0), a_send.at[3]).start()
         pltpu.make_async_copy(x_s, xr_ref, x_sems.at[3]).start()
 
     def par_away():
@@ -1040,15 +1061,17 @@
 
     norm()
 
-    @pl.when(lanes.home)
-    def _():
-        out_first((lanes.d, lanes.far)).start()
-        pltpu.make_async_copy(out_ref, out_slot(), o_sems.at[2]).start()
-
-    @pl.when(lanes.away)
-    def _():
-        out_first((lanes.other, t)).start()
-        out_second().start()
+    for i in range(2):
+
+        @pl.when(lanes.home)
+        def _(i=i):
+            out_first(i, (lanes.d, lanes.far)).start()
+            out_own(i).start()
+
+        @pl.when(lanes.away)
+        def _(i=i):
+            out_first(i, (lanes.other, t)).start()
+            out_second(i).start()
 
     for near in range(2):
         for half in range(2):
@@ -1071,40 +1094,138 @@
         for chunk in late[-1:]:
             spread.pass_on(chunk)
 
-    shared_spread.finish(0)
+    for place in range(1, blocks):
+        shared_spread.settle(place)
     for half in range(2):
         for place in range(1, blocks):
             swap_copy(place, half, False).start()
+
+    width = full_ref.shape[1]
+    narrow = wsh_s.shape[2]
+    kv = (narrow - side) // 2
+
+    def weight_copies(place, slot):
+        start = lanes.block(place) * block
+        view = pl.ds(pl.multiple_of(start, block), block)
+        key = pl.ds(pl.multiple_of(side + c * kv, kv), kv)
+        value = pl.ds(pl.multiple_of(side + 2 * kv + c * kv, kv), kv)
+        return [
+            pltpu.make_async_copy(src, dst, w_sems.at[slot, i])
+            for i, (src, dst) in enumerate(
+                (
+                    (full_ref.at[view, :], win_s.at[slot]),
+                    (sh_ref.at[view, pl.ds(0, side)], wsh_s.at[slot, :, pl.ds(0, side)]),
+                    (sh_ref.at[view, key], wsh_s.at[slot, :, pl.ds(side, kv)]),
+                    (sh_ref.at[view, value], wsh_s.at[slot, :, pl.ds(side + kv, kv)]),
+                )
+            )
+        ]
+
+    def shared_copy(place, slot):
+        start = lanes.block(place) * block
+        view = pl.ds(pl.multiple_of(start, block), block)
+        return pltpu.make_async_copy(wsh_s.at[slot], shall_ref.at[view, :], keep_sems.at[slot])
+
+    def fetch(place):
+        if place:
+            spread.settle(place)
+        for half in range(2):
+            swap_copy(place, half, True).wait_recv()
+        if place >= 2:
+            shared_copy(place - 2, place % 2).wait()
+        for copy in weight_copies(place, place % 2):
+            copy.start()
+
+    def accumulate(place, first, last):
+        slot = place % 2
+        index = lanes.block(place)
+
+        @pl.loop(first, last)
+        def _(part):
+            at_rows = pl.ds(pl.multiple_of(part * here, here), here)
+            left = act_s[index, at_rows, :]
+            for src, base in ((win_s, 0), (wsh_s, width)):
+                total = src.shape[2]
+                tile = total // 3
+                for col in range(0, total, tile):
+                    cols = slice(base + col, base + col + tile)
+                    product = low_dot(left, src[slot, :, col : col + tile], NN)
+                    if place:
+                        product = product + acc_s[at_rows, cols]
+                    acc_s[at_rows, cols] = product
+
+    def out_copies(part):
+        at_rows = pl.ds(part * here, here)
+        return [
+            pltpu.make_async_copy(
+                acc_s.at[at_rows, pl.ds(0, width)], proj_ref.at[at_rows, :], out_sems.at[0, part]
+            ),
+            pltpu.make_async_copy(
+                acc_s.at[at_rows, pl.ds(width, narrow)],
+                projsh_ref.at[at_rows, :],
+                out_sems.at[1, part],
+            ),
+        ]
+
     act_far().wait_recv()
     act_both().start()
+    fetch(0)
     act_core().wait_recv()
+    act_both().wait_recv()
+    act_copies = [
+        pltpu.make_async_copy(
+            act_s.at[index],
+            act_ref.at[:, pl.ds(index * block, block)],
+            keep_sems.at[2 + index],
+        )
+        for index in range(blocks)
+    ]
+    for copy in act_copies:
+        copy.start()
+    for place in range(blocks):
+        if place + 1 < blocks:
+            fetch(place + 1)
+        for copy in weight_copies(place, place % 2):
+            copy.wait()
+        shared_copy(place, place % 2).start()
+        if place + 1 < blocks:
+            accumulate(place, 0, 4)
+        else:
+            for part in range(4):
+                accumulate(place, part, part + 1)
+                for copy in out_copies(part):
+                    copy.start()
+    for place in range(max(blocks - 2, 0), blocks):
+        shared_copy(place, place % 2).wait()
+    for copy in act_copies:
+        copy.wait()
     for chunk in range(chunks):
-        spread.finish(chunk)
+        spread.sent(chunk)
+    shared_spread.sent(0)
     for half in range(2):
         for place in range(blocks):
-            swap_copy(place, half, True).wait_recv()
             swap_copy(place, half, False).wait_send()
     line_swap().wait_send()
     for half in range(2):
         line_near(half, False).wait_send()
         for near in range(2):
             line_far(half, near, False).wait_send()
-    act_both().wait_recv()
     act_far().wait_send()
     act_core().wait_send()
     act_both().wait_send()
-    pltpu.make_async_copy(act_s, act_slot(0), a_send.at[3]).wait()
+    for part in range(4):
+        for copy in out_copies(part):
+            copy.wait()
     pltpu.make_async_copy(x_s, xr_ref, x_sems.at[3]).wait()
 
     @pl.when(lanes.home)
     def _():
         for chunk in range(chunks):
             first_copy(chunk, (lanes.d, lanes.far)).wait_send()
-        out_first((lanes.d, lanes.far)).wait_send()
-        pltpu.make_async_copy(out_ref, out_slot(), o_sems.at[2]).wait()
-        start = (1 - c) * rows
-        view = pair_ref.at[pl.ds(pl.multiple_of(start, rows), rows), :]
-        remote(view, view, o_sems.at[0], o_recv.at[1 - c], (lanes.other, t)).wait_recv()
+        for i in range(2):
+            out_first(i, (lanes.d, lanes.far)).wait_send()
+            out_own(i).wait()
+            out_came(i, 1 - c)
 
     @pl.when(lanes.away)
     def _():
@@ -1114,14 +1235,14 @@
         for chunk in range(chunks):
             first_copy(chunk, (lanes.other, t)).wait_send()
             second_copy(chunk).wait_send()
-        out_first((lanes.other, t)).wait_send()
-        out_second().wait_send()
-        for half in range(2):
-            view = pair_ref.at[pl.ds(half * rows, rows), :]
-            remote(view, view, o_sems.at[0], o_recv.at[half], (lanes.other, t)).wait_recv()
-
-
-def front(in_pack, out_pack, shared, layer_in, gain, params, at):
+        for i in range(2):
+            out_first(i, (lanes.other, t)).wait_send()
+            out_second(i).wait_send()
+            for half in range(2):
+                out_came(i, half)
+
+
+def front(in_pack, out_pack, down, shared, layer_in, gain, params, kv_width, at):
     bf16 = jnp.bfloat16
     rows = in_pack.shape[0]
     blocks = at.blocks
@@ -1130,26 +1251,31 @@
     anywhere = pl.BlockSpec(memory_space=pl.ANY)
     here, features = layer_in.shape
     total = 2 * blocks * rows
+    narrow = shared.shape[1] // 2 + 2 * kv_width
     return pl.pallas_call(
         functools.partial(front_body, blocks, chunks),
-        in_specs=[pl.BlockSpec(memory_space=pltpu.VMEM)] * 6,
-        out_specs=[anywhere] * 5 + [pl.BlockSpec(memory_space=pltpu.VMEM)],
+        in_specs=[pl.BlockSpec(memory_space=pltpu.VMEM)] * 7,
+        out_specs=[anywhere] * 6 + [pl.BlockSpec(memory_space=pltpu.VMEM)] + [anywhere] * 3,
         out_shape=[
             jax.ShapeDtypeStruct((total, in_pack.shape[1]), bf16),
             jax.ShapeDtypeStruct((2 * rows, out_pack.shape[1]), bf16),
+            jax.ShapeDtypeStruct((2 * rows, down.shape[1]), bf16),
             jax.ShapeDtypeStruct((4 * here, features), bf16),
             jax.ShapeDtypeStruct((here, features), bf16),
             jax.ShapeDtypeStruct((total, shared.shape[1]), bf16),
             jax.ShapeDtypeStruct(params.shape, jnp.float32),
+            jax.ShapeDtypeStruct((4 * here, in_pack.shape[1]), jnp.float32),
+            jax.ShapeDtypeStruct((4 * here, narrow), jnp.float32),
+            jax.ShapeDtypeStruct((total, narrow), bf16),
         ],
         scratch_shapes=[
             pltpu.VMEM((here, features), bf16),
-            pltpu.VMEM((here, features), bf16),
+            pltpu.VMEM((blocks, 4 * here, 2 * rows), bf16),
             dma((chunks,)),
             dma((2, chunks)),
             dma((2, chunks)),
-            dma((3,)),
-            dma((2,)),
+            dma((2, 3)),
+            dma((2, 2)),
             dma((2, blocks, chunks)),
             dma((2, blocks, chunks)),
             dma((4,)),
@@ -1162,27 +1288,34 @@
             dma((2, blocks)),
             dma((2, blocks)),
             dma((2,)),
+            pltpu.VMEM((2, 2 * rows, in_pack.shape[1]), bf16),
+            pltpu.VMEM((2, 2 * rows, narrow), bf16),
+            pltpu.VMEM((4 * here, in_pack.shape[1] + narrow), jnp.float32),
+            dma((2, 4)),
+            dma((2 + blocks,)),
+            dma((2, 4)),
         ],
         compiler_params=pltpu.CompilerParams(
-            collective_id=1, has_side_effects=True, vmem_limit_bytes=16 * 1024 * 1024
+            collective_id=1, has_side_effects=True, vmem_limit_bytes=52 * 1024 * 1024
         ),
         cost_estimate=pl.CostEstimate(
             flops=here * features * 8, bytes_accessed=300_000_000, transcendentals=0
         ),
-    )(in_pack, out_pack, shared, layer_in, gain.reshape(1, -1), params)
+    )(in_pack, out_pack, down, shared, layer_in, gain.reshape(1, -1), params)
 
 
 class Stage:
     def __init__(self, lanes, pair, full, rows, cols, chunks, sems):
+        pair_cols = slice(0, pair.shape[1])
         self.lanes, self.pair, self.full, self.rows, self.cols = lanes, pair, full, rows, cols
         self.chunks = chunks
         self.own_sem, ssem, rsem = sems
-        self.spread = Spread(lanes, full, rows, chunks, ssem, rsem, cols, pair)
+        self.spread = Spread(lanes, full, rows, chunks, ssem, rsem, cols, pair, pair_cols)
 
     def own(self):
         start = self.lanes.k * (2 * self.rows)
         view = self.full.at[pl.ds(pl.multiple_of(start, 2 * self.rows), 2 * self.rows), self.cols]
-        return pltpu.make_async_copy(self.pair.at[:, self.cols], view, self.own_sem.at[0])
+        return pltpu.make_async_copy(self.pair, view, self.own_sem.at[0])
 
     def give(self):
         for chunk in range(self.chunks):
@@ -1292,7 +1425,7 @@
 
 def middle_body(
     blocks, gu_chunks, down_chunks,
-    pair_ref, heads_ref, out_ref, teacher_ref, x_ref, gain_ref, live_ref,
+    pair_ref, dpair_ref, heads_ref, out_ref, teacher_ref, x_ref, gain_ref, live_ref,
     full_ref, mid_ref, gate_ref, up_ref, hidden_ref, grads_ref, resid_ref, error_ref, low_ref,
     loss_ref,
     wbuf, mid_s, acc_s, hid_s, gate_s, up_s, own_s, both_s, core_s, pass_s,
@@ -1315,7 +1448,7 @@
         (g_home, g_s, g_r),
     )
     down = Stage(
-        lanes, pair_ref, full_ref, rows, slice(2 * hidden_width, 3 * hidden_width), down_chunks,
+        lanes, dpair_ref, full_ref, rows, slice(2 * hidden_width, 3 * hidden_width), down_chunks,
         (d_home, d_s, d_r),
     )
 
@@ -1581,10 +1714,10 @@
         copy.wait_send()
 
 
-def middle(pair, heads_all, out_all, x, gain, teacher, live, at):
+def middle(pair, down_pair, heads_all, out_all, x, gain, teacher, live, at):
     f32, bf16 = jnp.float32, jnp.bfloat16
     rows = pair.shape[0] // 2
-    hidden_width = pair.shape[1] // 3
+    hidden_width = down_pair.shape[1]
     slot, inner = heads_all.shape
     here, features = x.shape
     blocks = at.blocks
@@ -1602,7 +1735,7 @@
     buffers = [pltpu.VMEM((blocks, here, block), bf16)]
     return pl.pallas_call(
         functools.partial(middle_body, blocks, gu_chunks, down_chunks),
-        in_specs=[vmem, vmem, anywhere, anywhere, vmem, vmem, vmem],
+        in_specs=[vmem] * 3 + [anywhere, anywhere, vmem, vmem, vmem],
         out_specs=[anywhere] * 6 + [vmem] * 4,
         out_shape=[
             shape((features, 3 * hidden_width), bf16),
@@ -1649,15 +1782,15 @@
             flops=slot * features * hidden_width * 8, bytes_accessed=400_000_000, transcendentals=0
         ),
     )(
-        pair, heads_all, out_all, teacher, x, gain.reshape(1, -1), live,
+        pair, down_pair, heads_all, out_all, teacher, x, gain.reshape(1, -1), live,
     )
 
 
 def turn_body(
-    blocks, low_ref, lowsh_ref, act_ref, in_ref, sh_ref, rawgu_ref, rawdown_ref,
-    part_ref, bc_ref, kv_ref, sum_ref, gu_ref, down_ref,
+    blocks, low_ref, lowsh_ref, act_ref, in_ref, sh_ref, rawgu_ref,
+    part_ref, bc_ref, kv_ref, sum_ref, gu_ref,
     win_s, wsh_s, work_s, own_s, both_s, core_s, pass_s, both_r, core_r, far_r, stage_s,
-    gu_r, down_r, w_sems, x_ssem, x_rsem, stage_sems, ff_ssem, ff_rsem,
+    gu_r, w_sems, x_ssem, x_rsem, stage_sems, ff_ssem, ff_rsem,
 ):
     f32, bf16 = jnp.float32, jnp.bfloat16
     lanes = Lanes(blocks)
@@ -1679,7 +1812,7 @@
             remote(
                 src.at[view, :], dst.at[kind], ff_ssem.at[kind, i], ff_rsem.at[kind, i], device
             )
-            for i, (src, dst) in enumerate(((rawgu_ref, gu_r), (rawdown_ref, down_r)))
+            for i, (src, dst) in enumerate(((rawgu_ref, gu_r),))
         ]
 
     def first_home():
@@ -1788,6 +1921,7 @@
     for copy in first_home():
         copy.wait_recv()
     span = min(rows, 32)
+    side_width = gu_ref.shape[2]
 
     @pl.when(lanes.home)
     def _():
@@ -1798,8 +1932,10 @@
         def _(i):
             part = pl.ds(pl.multiple_of(i * span, span), span)
             mine = pl.ds(pl.multiple_of(c * rows + i * span, span), span)
-            gu_ref[part, :] = rawgu_ref[mine, :].astype(f32) + gu_r[0, part, :].astype(f32)
-            down_ref[part, :] = rawdown_ref[mine, :].astype(f32) + down_r[0, part, :].astype(f32)
+            for side in range(2):
+                cols = slice(side * side_width, (side + 1) * side_width)
+                total = rawgu_ref[mine, cols].astype(f32) + gu_r[0, part, cols].astype(f32)
+                gu_ref[part, side, :] = total
 
     @pl.when(lanes.away)
     def _():
@@ -1811,11 +1947,13 @@
         @pl.loop(0, rows // span)
         def _(i):
             part = pl.ds(pl.multiple_of(i * span, span), span)
-            gu_ref[part, :] = gu_r[0, part, :].astype(f32) + gu_r[1, part, :].astype(f32)
-            down_ref[part, :] = down_r[0, part, :].astype(f32) + down_r[1, part, :].astype(f32)
-
-
-def turn(low_pack, low_shared, act_all, in_all, shared_all, raw_gate_up, raw_down, bc_width, at):
+            for side in range(2):
+                cols = slice(side * side_width, (side + 1) * side_width)
+                total = gu_r[0, part, cols].astype(f32) + gu_r[1, part, cols].astype(f32)
+                gu_ref[part, side, :] = total
+
+
+def turn(low_pack, low_shared, act_all, in_all, shared_all, raw_gate_up, bc_width, at):
     f32, bf16 = jnp.float32, jnp.bfloat16
     slot, width = low_pack.shape
     shared_width = low_shared.shape[1]
@@ -1824,22 +1962,21 @@
     blocks = at.blocks
     rows = raw_gate_up.shape[0] // 2
     block = 2 * rows
-    gu_width, down_width = raw_gate_up.shape[1], raw_down.shape[1]
+    gu_width = raw_gate_up.shape[1]
     dma = pltpu.SemaphoreType.DMA
     vmem = pl.BlockSpec(memory_space=pltpu.VMEM)
     anywhere = pl.BlockSpec(memory_space=pl.ANY)
     shape = jax.ShapeDtypeStruct
     return pl.pallas_call(
         functools.partial(turn_body, blocks),
-        in_specs=[vmem] * 3 + [anywhere] * 2 + [vmem] * 2,
-        out_specs=[anywhere] * 3 + [vmem] * 3,
+        in_specs=[vmem] * 3 + [anywhere] * 2 + [vmem],
+        out_specs=[anywhere] * 3 + [vmem] * 2,
         out_shape=[
             shape((features, width), bf16),
             shape((features, bc_width), bf16),
             shape((features, shared_width - bc_width), bf16),
             shape((here, features), f32),
-            shape((rows, gu_width), f32),
-            shape((rows, down_width), f32),
+            shape((rows, 2, gu_width // 2), f32),
         ],
         scratch_shapes=[
             pltpu.VMEM((2, block, width), bf16),
@@ -1851,13 +1988,12 @@
         + [
             pltpu.VMEM((2, 256, width + shared_width), bf16),
             pltpu.VMEM((2, rows, gu_width), bf16),
-            pltpu.VMEM((2, rows, down_width), bf16),
             dma((2, 2)),
             dma((3, blocks)),
             dma((3, blocks)),
             dma((2, 3)),
-            dma((2, 2)),
-            dma((2, 2)),
+            dma((2, 1)),
+            dma((2, 1)),
         ],
         compiler_params=pltpu.CompilerParams(
             collective_id=4, has_side_effects=True, vmem_limit_bytes=58 * 1024 * 1024
@@ -1865,7 +2001,7 @@
         cost_estimate=pl.CostEstimate(
             flops=slot * features * width * 5, bytes_accessed=60_000_000, transcendentals=0
         ),
-    )(low_pack, low_shared, act_all, in_all, shared_all, raw_gate_up, raw_down)
+    )(low_pack, low_shared, act_all, in_all, shared_all, raw_gate_up)
 
 
 class Collect:
@@ -1959,7 +2095,7 @@
 def back_body(
     blocks, in_cols, small_row, part_ref, bc_ref, kv_ref, act_ref,
     resid_ref, x_ref, gain_ref, small_ref, out_ref,
-    gin_ref, gsh_ref, gx_ref, sum_ref, gout_ref,
+    gmix_ref, gquery_ref, gstep_ref, gsh_ref, gx_ref, sum_ref, gout_ref, gattn_ref,
     in_send, in_recv, in_load, in_total, settle_s, settle_r, sh_came, sh_part, sh_send, sh_recv,
     sh_load, sh_total, line_s, line_r, near_s, near_r, swap_s, swap_r,
     gx_s, gx_r, small_s, small_r,
@@ -1969,7 +2105,9 @@
     f32, bf16 = jnp.float32, jnp.bfloat16
     lanes = Lanes(blocks)
     c, t = lanes.c, lanes.t
-    rows = gin_ref.shape[0]
+    rows = gquery_ref.shape[0]
+    width = gmix_ref.shape[2]
+    query_width = gquery_ref.shape[1]
     here = act_ref.shape[0]
     wide = bc_ref.shape[1]
     few = gsh_ref.shape[0]
@@ -2173,31 +2311,48 @@
     send_swap().start()
     sum_ref[...] = small_s[len(stops)]
 
+    bounds = [
+        (0, gmix_ref.at[:, 0, :], width),
+        (width, gmix_ref.at[:, 1, :], width),
+        (2 * width, gquery_ref, query_width),
+        (2 * width + query_width, gstep_ref, gstep_ref.shape[1]),
+    ]
+
+    def put_in(cols, other, kind):
+        for start, dst, size in bounds:
+            low, high = max(cols.start, start), min(cols.stop, start + size)
+            if low < high:
+                part = slice(low, high)
+                total = settle_r[kind, :, part].astype(f32) + other(part)
+                dst[:, low - start : high - start] = total
+
     for chunk in range(chunks):
         cols = in_cols[chunk]
         send_first(chunk, core_at).wait_recv()
 
         @pl.when(lanes.home)
         def _(chunk=chunk, cols=cols):
-            gin_ref[:, cols] = in_total[c, :, cols] + settle_r[0, :, cols].astype(f32)
+            put_in(cols, lambda part: in_total[c, :, part], 0)
 
         @pl.when(lanes.away)
         def _(chunk=chunk, cols=cols):
             send_second(chunk).wait_recv()
-            gin_ref[:, cols] = settle_r[0, :, cols].astype(f32) + settle_r[1, :, cols].astype(f32)
+            put_in(cols, lambda part: settle_r[1, :, part].astype(f32), 0)
 
     out_first(0, core_at).wait_recv()
 
     @pl.when(lanes.home)
     def _():
         own_rows = pl.ds(pl.multiple_of(c * rows, rows), rows)
-        gout_ref[...] = out_ref[own_rows, :].astype(f32) + out_r[0].astype(f32)
+        gout_ref[...] = out_ref[own_rows, :width].astype(f32) + out_r[0, :, :width].astype(f32)
+        gattn_ref[...] = out_ref[own_rows, width:].astype(f32) + out_r[0, :, width:].astype(f32)
         out_first(1 - c, core_at).wait_send()
 
     @pl.when(lanes.away)
     def _():
         out_second().wait_recv()
-        gout_ref[...] = out_r[0].astype(f32) + out_r[1].astype(f32)
+        gout_ref[...] = out_r[0, :, :width].astype(f32) + out_r[1, :, :width].astype(f32)
+        gattn_ref[...] = out_r[0, :, width:].astype(f32) + out_r[1, :, width:].astype(f32)
         out_first(c, far_at).wait_send()
         out_second().wait_send()
 
@@ -2249,10 +2404,11 @@
     send_swap().wait_send()
 
 
-def back(part_in, bc, kv, grad_act, grad_resid, x, gain, small, small_row, raw_out, few, at):
+def back(part_in, bc, kv, grad_act, grad_resid, x, gain, small, small_row, raw_out, few, mixer_width, at):
     f32, bf16 = jnp.float32, jnp.bfloat16
     blocks = at.blocks
     features, width = part_in.shape
+    query_width = width - 2 * mixer_width - WIDE
     rows = features // (2 * blocks)
     here = grad_act.shape[0]
     wide = bc.shape[1]
@@ -2268,13 +2424,16 @@
     return pl.pallas_call(
         functools.partial(back_body, blocks, in_cols, small_row),
         in_specs=[anywhere] + [vmem] * 8,
-        out_specs=[vmem] * 5,
+        out_specs=[vmem] * 8,
         out_shape=[
-            jax.ShapeDtypeStruct((rows, width), f32),
+            jax.ShapeDtypeStruct((rows, 2, mixer_width), f32),
+            jax.ShapeDtypeStruct((rows, query_width), f32),
+            jax.ShapeDtypeStruct((rows, WIDE), f32),
             jax.ShapeDtypeStruct((few, 2 * wide), f32),
             jax.ShapeDtypeStruct((here, features), f32),
             jax.ShapeDtypeStruct(small.shape, f32),
-            jax.ShapeDtypeStruct((rows, raw_out.shape[1]), f32),
+            jax.ShapeDtypeStruct((rows, mixer_width), f32),
+            jax.ShapeDtypeStruct((rows, raw_out.shape[1] - mixer_width), f32),
         ],
         scratch_shapes=[
             pltpu.VMEM((loads, rows, width), bf16),
@@ -2512,8 +2671,8 @@
         [conv_inner.reshape(-1), inner_gain, step_bias, decay_log, skip_gain]
     )
     params = jnp.pad(column_params, (0, -column_params.shape[0] % 1024)).reshape(-1, WIDE)
-    in_all, out_pair, act_all, x_low, shared_full, params = front(
-        in_pack, out_pack, shared_weight, layer_in, input_gain, params, at
+    in_all, out_pair, down_pair, act_all, x_low, _, params, proj, proj_shared, shared_all = front(
+        in_pack, out_pack, down_weight, shared_weight, layer_in, input_gain, params, HD, at
     )
     column_params = params.reshape(-1)[: column_params.shape[0]]
     lane_params = jnp.concatenate(
@@ -2527,37 +2686,20 @@
     head_rows = column_params[(KC + 1) * width :][: 2 * local_heads].reshape(2, local_heads)
     head_rows = jnp.concatenate([head_rows[:1], -jnp.exp(head_rows[1:])], axis=0)
     head_params = jnp.pad(head_rows, ((0, 6), (0, WIDE - local_heads)))
-    left, right = shared_full[:, :bc_width], shared_full[:, bc_width:]
-    kv_index = at.column * (query_width // HD) // (QH // KVH)
-    second = kv_index == 1
-    shared_all = jnp.concatenate(
-        [
-            left,
-            jnp.where(second, right[:, HD : 2 * HD], right[:, :HD]),
-            jnp.where(second, right[:, 3 * HD :], right[:, 2 * HD : 3 * HD]),
-        ],
-        axis=1,
-    )
-
     def row_split(values):
         return [values[i * rows_here : (i + 1) * rows_here] for i in range(at.tp)]
 
     out_all = gather_blocks(out_pair, at)
-    proj_shared = jnp.dot(act_all, shared_all, preferred_element_type=f32)
-    proj = jnp.dot(act_all, in_all, preferred_element_type=f32)
     attn_low = attn_forward(order, proj, proj_shared, cosine, sine, query_width, width, bc_width)
     heads_all, y, states = mixer_forward(
         order, proj, proj_shared, attn_low, lane_params, conv_shared, head_params
     )
-    ff_pack = jnp.concatenate(
-        [gate_up_weight.reshape(w_rows, 2 * hidden_width), down_weight], axis=1
-    )
     seq_len = lax.dynamic_index_in_dim(lengths, at.slot, keepdims=False)
     positions = at.quarter * rows_here + jnp.arange(rows_here)
     live = (positions < seq_len).astype(f32)[:, None]
-    ff_pair = pair_weight(ff_pack, at)
+    ff_pair = pair_weight(gate_up_weight.reshape(w_rows, 2 * hidden_width), at)
     ff_all, mid_all, gate_low, up_low, hidden, grad_all, resid, error, layer_out, loss_part = middle(
-        ff_pair, heads_all, out_all, x_low, middle_gain, teacher, live, at
+        ff_pair, down_pair, heads_all, out_all, x_low, middle_gain, teacher, live, at
     )
     err_local = loss_part[0, 0]
     _, norm_mid_back = jax.vjp(rms_norm, resid, middle_gain)
@@ -2572,6 +2714,7 @@
     part_down = weight_grad(grad_all, hidden)
     grad_all, part_down = lax.optimization_barrier((grad_all, part_down))
     raw_down = sum_blocks(part_down, at)
+    down_moves = send_settle(raw_down, at)
     grad_hidden = jnp.dot(grad_all, down_all, preferred_element_type=f32)
     grad_gate = grad_hidden * up_val * sigmoid_gate * (1.0 + gate_val * (1.0 - sigmoid_gate))
     grad_up = grad_hidden * gate_val * sigmoid_gate
@@ -2589,13 +2732,13 @@
     mix_grad_all = jnp.concatenate(share_rows(grad_resid.astype(bf16), at), axis=0)
     grad_heads = jnp.dot(mix_grad_all, out_all, preferred_element_type=f32)
     part_out = weight_grad(mix_grad_all, heads_all)
-    grad_heads, part_out, raw_down = lax.optimization_barrier((grad_heads, part_out, raw_down))
+    grad_heads, part_out = lax.optimization_barrier((grad_heads, part_out))
     dq, dkv = attn_backward(
         order, proj, proj_shared, cosine, sine, grad_heads, query_width, width, bc_width
     )
     low_pack, low_shared, dlane, dconv, dhead = mixer_backward(
         order, proj, proj_shared, y, states, grad_heads, dq, dkv, lane_params, conv_shared,
-        head_params, seg, query_width,
+        head_params, seg, query_width, down_moves[:2],
     )
     low_pack, low_shared, raw_gate_up, part_out = lax.optimization_barrier(
         (low_pack, low_shared, raw_gate_up, part_out)
@@ -2623,12 +2766,13 @@
     padded = -(-flat.shape[0] // 1024) * 1024
     flat = jnp.pad(flat, (0, padded - flat.shape[0])).reshape(-1, WIDE)
 
-    part_in, part_bc, part_kv, grad_act, grad_gate_up, grad_down = turn(
-        low_pack, low_shared, act_all, in_all, shared_all, raw_gate_up, raw_down, bc_width, at
-    )
-    grad_in, grad_shared_weight, input_grad, flat, grad_out = back(
+    grad_down = end_settle(down_moves, at)
+    part_in, part_bc, part_kv, grad_act, grad_gate_up = turn(
+        low_pack, low_shared, act_all, in_all, shared_all, raw_gate_up, bc_width, at
+    )
+    grad_mix, grad_query, grad_step, grad_shared_weight, input_grad, flat, grad_out, grad_attn = back(
         part_in, part_bc, part_kv, grad_act, grad_resid, x_low, input_gain, flat, 0,
-        raw_out, shared_weight.shape[0], at,
+        raw_out, shared_weight.shape[0], width, at,
     )
     flat = flat.reshape(-1)
     sums = []
@@ -2647,9 +2791,9 @@
         loss,
         input_grad,
         sum_input_gain,
-        grad_in[:, :query_from].reshape(w_rows, 2, width),
-        grad_in[:, step_from : step_from + local_heads],
-        grad_in[:, query_from:step_from],
+        grad_mix,
+        grad_step[:, :local_heads],
+        grad_query,
         grad_shared_weight,
         lanes_local[:KC],
         sum_convs,
@@ -2657,10 +2801,10 @@
         heads_local[1],
         heads_local[2],
         lanes_local[KC],
-        grad_out[:, :width],
-        grad_out[:, width:],
+        grad_out,
+        grad_attn,
         sum_middle_gain,
-        grad_gate_up.reshape(w_rows, 2, hidden_width),
+        grad_gate_up,
         grad_down,
     )
 

time: 801 us -> 784 us (0.979)
  matrix products: 85.6 us -> 67.2 us
  local copies, waits for them, and re-layouts: 48.7 us -> 32.4 us
  Pallas kernels: 567 us -> 576 us
    pallas_call x1, Pallas kernels: 117 us -> 139 us  [front(): pl.pallas_call(functools.partial(front_body, blocks, chunks), in_specs=[p...]
    dot_general x2 -> x0, matrix products: 20.5 us -> none  [the longest x1 15.4 us: per_device(): proj = jnp.dot(act_all, in_all, preferred_element_type=f32)]
    pallas_call x1, Pallas kernels: 79.2 us -> 64.5 us  [turn(): pl.pallas_call(functools.partial(turn_body, blocks), in_specs=[vmem] * 3...]
    unnamed x85 -> x82, local copies, waits for them, and re-layouts: 22.2 us -> 17.7 us
    ppermute x8 -> x10, waiting for transfers between devices: 45.1 us -> 43.8 us  [send(): return lax.ppermute(values, ('dp', 'tensor'), self.pairs(where_to))]
  transfers between devices with their start and end apart: 12 -> 14, of which waited for: 5 -> 7; matrix products, arithmetic and copies ran while one was open for 14% -> 11% of each run, Pallas kernels for 19% -> 17%
where the time goes in v6:
time: 784 us; the launch traced here: 774 us
  Pallas kernels  576 us (73%)
  matrix products  67.2 us (9%)
  waiting for transfers between devices  45.9 us (6%)
  local copies, waits for them, and re-layouts  32.4 us (4%)
  other arithmetic  24.2 us (3%)
  between operations  17.3 us (2%)
  starting transfers between devices  10.8 us (1%)
    pallas_call x1, Pallas kernels, middle(): pl.pallas_call(functools.partial(middle_body, blocks, gu_chunks, down_chu...  177 us
    pallas_call x1, Pallas kernels, front(): pl.pallas_call(functools.partial(front_body, blocks, chunks), in_specs=[p...  139 us
    pallas_call x1, Pallas kernels, back(): pl.pallas_call(functools.partial(back_body, blocks, in_cols, small_row),...  127 us
    pallas_call x1, Pallas kernels, turn(): pl.pallas_call(functools.partial(turn_body, blocks), in_specs=[vmem] * 3...  64.5 us
    ppermute x10, waiting for transfers between devices, send(): return lax.ppermute(values, ('dp', 'tensor'), self.pairs(where_to))  43.8 us
    pallas_call x1, Pallas kernels, mixer_backward(): pl.pallas_call(mixer_bwd_body, grid_spec=pltpu.PrefetchScalarGridSpec(num...  33.1 us
    dot_general x3, matrix products, weight_grad(): lax.dot_general(left, right, contract_first, preferred_element_type=f32)  30.4 us
    dot_general x4, matrix products, per_device(): lax.dot_general(piece, gate_up_all, contract_last, preferred_element_type...  20 us
  transfers between devices with their start and end apart: 14, of which 7 were waited for; matrix products, arithmetic and copies ran while one was open for 11% of the time, Pallas kernels for 17%

profile of v6, /device:TPU:1, one launch (start us, length us, event | category | flops | bytes accessed | tf_op | source)
XLA Modules:
  0.0 773.5 jit_solution(1889205598736563072)
XLA Ops:
  14.1 138.6 %shard_map.330 = (bf16[2048,1920]{1,0:T(8,128)(2,1)}, bf16[512,1024]{1,0:T(8,128)(2,1)}, bf16[512,1024]{1,0:T(8,128)(2,1)}, bf16[1024,2048]{1,0:T(8,128)(2,1)}, ...) custom-call(bf16[256,1920]{1,0:T(8,128)(2,1)} %concatenate.37.in_ref, ...), custom_call_target="tpu_custom_call" | custom-call | flops 4194304 | bytes 300000000 | tf_op jit(solution)/shard_map/pallas_call | solution.py:1255
  160.8 8.3 %shard_map.331.attn_ref = bf16[1024,256]{1,0:T(8,128)(2,1)} custom-call(s32[4]{0:T(128)} %fusion.47.order, f32[1024,1920]{1,0:T(8,128)} %get-tuple-element.72.q_ref.gate_ref.inner_ref.step_ref.before_ref, f32[1024,768]{1,0:T(8,128)} %get-tuple-element.73.kv_ref.bc_ref.bcbefore_ref, f32[1024,128]{1,0:T(8,128)} %get-tuple-element.183.cos_ref.all_cos, ...), custom_call_target="tpu_custom_call" | custom-call | flops 805306368 | bytes 3145728 | tf_op jit(solution)/shard_map/pallas_call | solution.py:416
  171.7 15.3 %shard_map.332 = (bf16[1024,1024]{1,0:T(8,128)(2,1)}, f32[1024,768]{1,0:T(8,128)}, bf16[8,256,768]{2,1,0:T(8,128)(2,1)}) custom-call(s32[4]{0:T(128)} %fusion.47.order, f32[1024,1920]{1,0:T(8,128)} %get-tuple-element.72.q_ref.gate_ref.inner_ref.step_ref.before_ref, f32[1024,1920]{1,0:T(8,128)} %get-tuple-element.72.q_ref.gate_ref.inner_ref.step_ref.before_ref, ...), custom_call_target="tpu_custom_call" | custom-call | flops 3221225472 | bytes 15728640 | tf_op jit(solution)/shard_map/pallas_call | solution.py:480
  187.0 12.7 %collective-permute-done = bf16[256,2048]{1,0:T(8,128)(2,1)S(1)} collective-permute-done((bf16[256,2048]{1,0:T(8,128)(2,1)S(1)}, bf16[256,2048]{1,0:T(8,128)(2,1)S(1)}, u32[]{:S(2)}, u32[]{:S(2)}) %collective-permute-start) | collective-permute-done | bytes 1048608 | tf_op jit(solution)/shard_map/ppermute | solution.py:643
  203.5 177.2 %shard_map.333 = (bf16[2048,3072]{1,0:T(8,128)(2,1)}, bf16[1024,2048]{1,0:T(8,128)(2,1)}, bf16[1024,1024]{1,0:T(8,128)(2,1)}, bf16[1024,1024]{1,0:T(8,128)(2,1)}...) custom-call(bf16[512,2048]{1,0:T(8,128)(2,1)} %pad_maximum_fusion.3., ...), custom_call_target="tpu_custom_call" | custom-call | flops 17179869184 | bytes 400000000 | tf_op jit(solution)/shard_map/pallas_call | solution.py:1736
  380.7 9.4 %convolution_convert_fusion.2 = bf16[2048,1024]{1,0:T(8,128)(2,1)} fusion(bf16[1024,2048]{1,0:T(8,128)(2,1)} %get-tuple-element.84, bf16[1024,1024]{1,0:T(8,128)(2,1)} %get-tuple-element.83), kind=kOutput, calls=%fused_computation.33 | convolution fusion | flops 4297064448 | bytes 10485760 | tf_op jit(solution)/shard_map/dot_general | solution.py:2712
  390.1 7.9 %fusion.16 = f32[1024,1024]{1,0:T(8,128)S(1)} fusion(bf16[1024,2048]{1,0:T(8,128)(2,1)} %get-tuple-element.84, bf16[2048,3072]{1,0:T(8,128)(2,1)} %get-tuple-element.85), kind=kOutput, calls=%fused_computation.30 | convolution fusion | flops 4294967296 | bytes 12582912 | tf_op jit(solution)/shard_map/dot_general | solution.py:2718
  400.2 7.2 fusion.21
  407.6 3.4 fusion.18
  411.5 3.4 add_convert_fusion
  414.9 11.9 %convolution_convert_fusion = bf16[2048,2048]{1,0:T(8,128)(2,1)} fusion(bf16[1024,2048]{1,0:T(8,128)(2,1)S(1)} %copy-done.30, bf16[1024,1024]{1,0:T(8,128)(2,1)S(1)} %get-tuple-element.167, bf16[1024,1024]{1,0:T(8,128)(2,1)S(1)} %get-tuple-element.168), kind=kOutput, calls=%fused_computation | convolution fusion | flops 8602517504 | bytes 16777216 | tf_op jit(solution)/shard_map/dot_general | solution.py:2712
  426.9 5.9 fusion.6
  432.8 7.2 collective-permute-done.4
  440.0 3.1 convert_add_fusion
  444.9 2.2 multiply_reduce_fusion
  450.1 22.9 %collective-permute-done.6 = bf16[256,2048]{1,0:T(8,128)(2,1)S(1)} collective-permute-done((bf16[256,2048]{1,0:T(8,128)(2,1)S(1)}, bf16[256,2048]{1,0:T(8,128)(2,1)S(1)}, u32[]{:S(2)}, u32[]{:S(2)}) %collective-permute-start.6) | collective-permute-done | bytes 1048608 | tf_op jit(solution)/shard_map/ppermute | solution.py:643
  478.4 8.8 %fusion.37.grad_ref = f32[1024,1024]{1,0:T(8,128)} fusion(bf16[2048,1024]{1,0:T(8,128)(2,1)S(1)} %copy-done.25, bf16[256,2048]{1,0:T(8,128)(2,1)S(1)} %collective-permute-done.7, bf16[256,2048]{1,0:T(8,128)(2,1)S(1)} %collective-permute-done.6, bf16[256,2048]{1,0:T(8,128)(2,1)S(1)} %collective-permute-done.5, bf16[256,2048]{1,0:T(8,128)(2,1)S(1)} %get-tuple-element.165), kind=kOutput, calls=%fused_computation.55 | convolution fusion | flops 4311744512 | bytes 12582912 | tf_op jit(solution)/shard_map/dot_general | solution.py:2733
  488.7 4.3 collective-permute-start.9
  493.1 9.1 %convolution_convert_fusion.1 = bf16[2048,1024]{1,0:T(8,128)(2,1)} fusion(bf16[1024,1024]{1,0:T(8,128)(2,1)} %get-tuple-element.75.heads_ref, bf16[256,2048]{1,0:T(8,128)(2,1)} %copy-done.28, bf16[256,2048]{1,0:T(8,128)(2,1)} %copy-done.26, bf16[256,2048]{1,0:T(8,128)(2,1)} %copy-done.27, bf16[256,2048]{1,0:T(8,128)(2,1)S(1)} %get-tuple-element.165), kind=kOutput, calls=%fused_computation.32 | convolution fusion | flops 4313841664 | bytes 10485760 | tf_op jit(solution)/shard_map/dot_general | solution.py:2712
  502.2 12.2 %shard_map.334 = (bf16[1024,256]{1,0:T(8,128)(2,1)}, bf16[1024,256]{1,0:T(8,128)(2,1)}) custom-call(s32[4]{0:T(128)} %fusion.47.order, f32[1024,1920]{1,0:T(8,128)} %get-tuple-element.72.q_ref.gate_ref.inner_ref.step_ref.before_ref, f32[1024,768]{1,0:T(8,128)} %get-tuple-element.73.kv_ref.bc_ref.bcbefore_ref, ...), custom_call_target="tpu_custom_call" | custom-call | flops 2147483648 | bytes 5242880 | tf_op jit(solution)/shard_map/pallas_call | solution.py:442
  515.6 33.1 %shard_map.335 = (bf16[1024,1920]{1,0:T(8,128)(2,1)}, bf16[1024,768]{1,0:T(8,128)(2,1)}, f32[8,768]{1,0:T(8,128)}, f32[8,512]{1,0:T(8,128)}, f32[8,128]{1,0:T(8,128)}) custom-call(s32[4]{0:T(128)} %fusion.47.order, f32[1024,1920]{1,0:T(8,128)} %get-tuple-element.72.q_ref.gate_ref.inner_ref.step_ref.before_ref, ...), custom_call_target="tpu_custom_call" | custom-call | flops 8053063680 | bytes 31457280 | tf_op jit(solution)/shard_map/pallas_call | solution.py:549
  555.4 64.5 %shard_map.336 = (bf16[2048,1920]{1,0:T(8,128)(2,1)}, bf16[2048,512]{1,0:T(8,128)(2,1)}, bf16[2048,256]{1,0:T(8,128)(2,1)}, f32[256,2048]{1,0:T(8,128)}, f32[256,2,1024]{2,1,0:T(2,128)}) custom-call(bf16[1024,1920]{1,0:T(8,128)(2,1)} %get-tuple-element.99.low_ref, bf16[1024,768]{1,0:T(8,128)(2,1)} %get-tuple-element.100.lowsh_ref, ...), custom_call_target="tpu_custom_call" | custom-call | flops 20132659200 | bytes 60000000 | tf_op jit(solution)/shard_map/pallas_call | solution.py:1970
  619.9 126.6 %shard_map.337 = (f32[256,2,768]{2,1,0:T(2,128)}, f32[256,256]{1,0:T(8,128)}, f32[256,128]{1,0:T(8,128)}, f32[64,1024]{1,0:T(8,128)}, f32[256,2048]{1,0:T(8,128)...) custom-call(bf16[2048,1920]{1,0:T(8,128)(2,1)} %get-tuple-element.105.part_ref, ...), custom_call_target="tpu_custom_call" | custom-call | flops 256 | bytes 256 | tf_op jit(solution)/shard_map/pallas_call | solution.py:2424
  756.6 3.3 copy.62
  (170 shorter events, 57.7 us)
Async XLA Ops:
  7.2 196.3 %all-gather.2.cloned.1.call-start = ((), (), s32[]{:S(2)}) async-start(), calls=%async_computation.3 | async-start | bytes 5242880 | tf_op jit(solution)/shard_map/all_gather | solution.py:2515
  8.6 144.2 %copy-start.16 = (bf16[256,2,1024]{2,1,0:T(2,128)(2,1)S(1)}, bf16[256,2,1024]{2,1,0:T(2,128)(2,1)}, u32[]{:S(2)}) copy-start(bf16[256,2,1024]{2,1,0:T(2,128)(2,1)} %param.36) | copy-start | bytes 3145732
  12.1 144.2 %copy-start.29 = (s32[8]{0:T(128)S(1)}, s32[8]{0:T(128)}, u32[]{:S(2)}) copy-start(s32[8]{0:T(128)} %param.21) | copy-start | bytes 100
  152.7 334.6 %reduce-scatter.4.cloned.1.call-start = ((), (), s32[]{:S(2)}) async-start(), calls=%async_computation.4 | async-start | bytes 5242880 | tf_op jit(solution)/shard_map/reduce_scatter | solution.py:2519
  153.0 46.6 %collective-permute-start = (bf16[256,2048]{1,0:T(8,128)(2,1)S(1)}, bf16[256,2048]{1,0:T(8,128)(2,1)S(1)}, u32[]{:S(2)}, u32[]{:S(2)}) collective-permute-start(bf16[256,2048]{1,0:T(8,128)(2,1)S(1)} %bitcast.45), channel_id=1, source_target_pairs={{0,2},{1,3},{2,6},{3,7},{4,0},{5,1},{6,4},{7,5},{8,10},{9,11},{10,... | collective-permute-start | bytes 3145736 | tf_op jit(solution)/shard_map/ppermute | solution.py:643
  154.1 45.6 %collective-permute-start.1 = (bf16[256,2048]{1,0:T(8,128)(2,1)S(1)}, bf16[256,2048]{1,0:T(8,128)(2,1)S(1)}, u32[]{:S(2)}, u32[]{:S(2)}) collective-permute-start(bf16[256,2048]{1,0:T(8,128)(2,1)S(1)} %bitcast.46), channel_id=1, source_target_pairs={{2,4},{3,5},{4,2},{5,3},{10,12},{11,13},{12,10},{13,11},{18,20},{1... | collective-permute-start | bytes 3145736 | tf_op jit(solution)/shard_map/ppermute | solution.py:643
  390.1 158.7 %reduce-scatter.6.cloned.1.call-start = ((), (), s32[]{:S(2)}) async-start(), calls=%async_computation.5 | async-start | bytes 10485760 | tf_op jit(solution)/shard_map/reduce_scatter | solution.py:2519
  390.1 7.9 %copy-start.13 = (bf16[1024,1024]{1,0:T(8,128)(2,1)S(1)}, bf16[1024,1024]{1,0:T(8,128)(2,1)}, u32[]{:S(2)}) copy-start(bf16[1024,1024]{1,0:T(8,128)(2,1)} %get-tuple-element.87) | copy-start | bytes 6291460
  390.1 7.9 %copy-start.14 = (bf16[1024,1024]{1,0:T(8,128)(2,1)S(1)}, bf16[1024,1024]{1,0:T(8,128)(2,1)}, u32[]{:S(2)}) copy-start(bf16[1024,1024]{1,0:T(8,128)(2,1)} %get-tuple-element.86) | copy-start | bytes 6291460
  398.1 9.5 %slice-start = ((s8[12582912]{0:T(1024)(128)(4,1)}), s8[4194304]{0:T(1024)(128)(4,1)S(1)}, s32[]{:S(2)}) async-start(s8[12582912]{0:T(1024)(128)(4,1)} %bitcast.57), calls=%async_computation.7 | async-start | bytes 8388608
  398.1 9.5 %slice-start.1 = ((s8[12582912]{0:T(1024)(128)(4,1)}), s8[4194304]{0:T(1024)(128)(4,1)S(1)}, s32[]{:S(2)}) async-start(s8[12582912]{0:T(1024)(128)(4,1)} %bitcast.57), calls=%async_computation.8 | async-start | bytes 8388608
  400.2 14.7 %copy-start.12 = (bf16[1024,1024]{1,0:T(8,128)(2,1)}, bf16[1024,1024]{1,0:T(8,128)(2,1)S(1)}, u32[]{:S(2)}) copy-start(bf16[1024,1024]{1,0:T(8,128)(2,1)S(1)} %get-tuple-element.168) | copy-start | bytes 6291460
  407.5 4.0 collective-permute-start.3
  411.0 21.8 %collective-permute-start.2 = (bf16[256,2048]{1,0:T(8,128)(2,1)}, bf16[256,2048]{1,0:T(8,128)(2,1)S(1)}, u32[]{:S(2)}, u32[]{:S(2)}) collective-permute-start(bf16[256,2048]{1,0:T(8,128)(2,1)} %fusion.18), channel_id=1, source_target_pairs={{0,4},{1,5},{2,6},{3,7},{4,0},{5,1},{6,2},{7,3},{8,12},{9,13},{10,... | collective-permute-start | bytes 3145736 | tf_op jit(solution)/shard_map/ppermute | solution.py:643
  414.9 25.1 %collective-permute-start.4 = (bf16[256,2048]{1,0:T(8,128)(2,1)}, bf16[256,2048]{1,0:T(8,128)(2,1)}, u32[]{:S(2)}, u32[]{:S(2)}) collective-permute-start(bf16[256,2048]{1,0:T(8,128)(2,1)} %add_convert_fusion), channel_id=1, source_target_pairs={{0,1},{1,0},{2,3},{3,2},{4,5},{5,4},{6,7},{7,6},{8,9},{9,8},{10,11... | collective-permute-start | bytes 3145736 | tf_op jit(solution)/shard_map/ppermute | solution.py:643
  443.1 176.9 %reduce-scatter.8.cloned.1.call-start = ((), (), s32[]{:S(2)}) async-start(), calls=%async_computation.6 | async-start | bytes 5242880 | tf_op jit(solution)/shard_map/reduce_scatter | solution.py:2519
  447.1 31.3 %copy-start.25 = (bf16[2048,1024]{1,0:T(8,128)(2,1)S(1)}, bf16[2048,1024]{1,0:T(8,128)(2,1)}, u32[]{:S(2)}) copy-start(bf16[2048,1024]{1,0:T(8,128)(2,1)} %all-gather.2.cloned.1.call-done.out_ref) | copy-start | bytes 12582916
  449.1 24.0 %collective-permute-start.6 = (bf16[256,2048]{1,0:T(8,128)(2,1)S(1)}, bf16[256,2048]{1,0:T(8,128)(2,1)S(1)}, u32[]{:S(2)}, u32[]{:S(2)}) collective-permute-start(bf16[256,2048]{1,0:T(8,128)(2,1)S(1)} %get-tuple-element.165), channel_id=1, source_target_pairs={{0,1},{1,0},{2,3},{3,2},{4,5},{5,4},{6,7},{7,6},{8,9},{9,8},{10,11... | collective-permute-start | bytes 3145736 | tf_op jit(solution)/shard_map/ppermute | solution.py:643
  449.2 27.2 %collective-permute-start.5 = (bf16[256,2048]{1,0:T(8,128)(2,1)S(1)}, bf16[256,2048]{1,0:T(8,128)(2,1)S(1)}, u32[]{:S(2)}, u32[]{:S(2)}) collective-permute-start(bf16[256,2048]{1,0:T(8,128)(2,1)S(1)} %get-tuple-element.165), channel_id=1, source_target_pairs={{0,4},{1,5},{2,6},{3,7},{4,0},{5,1},{6,2},{7,3},{8,12},{9,13},{10,... | collective-permute-start | bytes 3145736 | tf_op jit(solution)/shard_map/ppermute | solution.py:643
  473.0 3.9 collective-permute-start.7
  488.7 25.6 %collective-permute-start.8 = (bf16[256,1024]{1,0:T(8,128)(2,1)S(1)}, bf16[256,1024]{1,0:T(8,128)(2,1)S(1)}, u32[]{:S(2)}, u32[]{:S(2)}) collective-permute-start(bf16[256,1024]{1,0:T(8,128)(2,1)S(1)} %get-tuple-element.163), channel_id=1, source_target_pairs={{0,4},{1,5},{2,0},{3,1},{4,6},{5,7},{6,2},{7,3},{8,12},{9,13},{10,... | collective-permute-start | bytes 1572872 | tf_op jit(solution)/shard_map/ppermute | solution.py:643
  488.7 26.1 %collective-permute-start.9 = (bf16[256,1024]{1,0:T(8,128)(2,1)S(1)}, bf16[256,1024]{1,0:T(8,128)(2,1)S(1)}, u32[]{:S(2)}, u32[]{:S(2)}) collective-permute-start(bf16[256,1024]{1,0:T(8,128)(2,1)S(1)} %get-tuple-element.164), channel_id=1, source_target_pairs={{2,4},{3,5},{4,2},{5,3},{10,12},{11,13},{12,10},{13,11},{18,20},{1... | collective-permute-start | bytes 1572872 | tf_op jit(solution)/shard_map/ppermute | solution.py:643
  619.9 135.7 %copy-start.17 = (bf16[256,2048]{1,0:T(8,128)(2,1)S(1)}, bf16[256,2048]{1,0:T(8,128)(2,1)}, u32[]{:S(2)}) copy-start(bf16[256,2048]{1,0:T(8,128)(2,1)} %get-tuple-element.206) | copy-start | bytes 3145732
  746.6 13.4 %copy-start.15 = (f32[256,2,768]{2,1,0:T(2,128)S(1)}, f32[256,2,768]{2,1,0:T(2,128)}, u32[]{:S(2)}) copy-start(f32[256,2,768]{2,1,0:T(2,128)} %get-tuple-element.210) | copy-start | bytes 4718596
  (24 other events, 102.7 us)
Sparse Core Ops, SparseCore 0:
  152.8 50.6 all-gather.1
  390.2 50.3 reduce-scatter.3
  444.0 86.3 reduce-scatter.5
  548.9 50.1 reduce-scatter.7

commit v7 on v6

--- a/solution.py
+++ b/solution.py
@@ -1893,12 +1893,12 @@
             for copy in out_copies(i - 2, slot):
                 copy.wait()
 
-        left = act_ref[:, pl.ds(pl.multiple_of(i * tall, tall), tall)]
+        left = act_ref[:, pl.ds(pl.multiple_of(i * tall, tall), tall)].T
         for src, base in ((low_ref, 0), (lowsh_ref, width)):
             total = src.shape[1]
             tile = total // 3
             for col in range(0, total, tile):
-                product = low_dot(left, src[:, col : col + tile], TN)
+                product = low_dot(left, src[:, col : col + tile], NN)
                 stage_s[slot, :, base + col : base + col + tile] = product.astype(bf16)
         for copy in out_copies(i, slot):
             copy.start()
@@ -2412,9 +2412,9 @@
     rows = features // (2 * blocks)
     here = grad_act.shape[0]
     wide = bc.shape[1]
-    chunks = 3
-    piece = width // chunks
-    in_cols = [slice(i * piece, (i + 1) * piece) for i in range(chunks)]
+    cut = -(-width // (2 * WIDE)) * WIDE
+    in_cols = [slice(0, cut), slice(cut, width)]
+    chunks = len(in_cols)
     loads = sum(bool(onward(p, h, at.bits)) for h in range(2) for p in range(blocks))
     steps = 3 + at.bits
     dma = pltpu.SemaphoreType.DMA

time: 784 us -> 782 us (level)
  no operation moved by 1% of the time
where the time goes in v7:
time: 782 us; the launch traced here: 772 us
  Pallas kernels  575 us (74%)
  matrix products  67.2 us (9%)
  waiting for transfers between devices  45.9 us (6%)
  local copies, waits for them, and re-layouts  32.4 us (4%)
  other arithmetic  24.2 us (3%)
  between operations  17.3 us (2%)
  starting transfers between devices  10.8 us (1%)
    pallas_call x1, Pallas kernels, middle(): pl.pallas_call(functools.partial(middle_body, blocks, gu_chunks, down_chu...  177 us
    pallas_call x1, Pallas kernels, front(): pl.pallas_call(functools.partial(front_body, blocks, chunks), in_specs=[p...  139 us
    pallas_call x1, Pallas kernels, back(): pl.pallas_call(functools.partial(back_body, blocks, in_cols, small_row),...  126 us
    pallas_call x1, Pallas kernels, turn(): pl.pallas_call(functools.partial(turn_body, blocks), in_specs=[vmem] * 3...  64.5 us
    ppermute x10, waiting for transfers between devices, send(): return lax.ppermute(values, ('dp', 'tensor'), self.pairs(where_to))  43.8 us
    pallas_call x1, Pallas kernels, mixer_backward(): pl.pallas_call(mixer_bwd_body, grid_spec=pltpu.PrefetchScalarGridSpec(num...  33.1 us
    dot_general x3, matrix products, weight_grad(): lax.dot_general(left, right, contract_first, preferred_element_type=f32)  30.4 us
    dot_general x4, matrix products, per_device(): lax.dot_general(piece, gate_up_all, contract_last, preferred_element_type...  20 us
  transfers between devices with their start and end apart: 14, of which 7 were waited for; matrix products, arithmetic and copies ran while one was open for 11% of the time, Pallas kernels for 17%

profile of v7, /device:TPU:1, one launch (start us, length us, event | category | flops | bytes accessed | tf_op | source)
XLA Modules:
  0.0 772.5 jit_solution(15402223430692248857)
XLA Ops:
  14.1 138.6 %shard_map.330 = (bf16[2048,1920]{1,0:T(8,128)(2,1)}, bf16[512,1024]{1,0:T(8,128)(2,1)}, bf16[512,1024]{1,0:T(8,128)(2,1)}, bf16[1024,2048]{1,0:T(8,128)(2,1)}, ...) custom-call(bf16[256,1920]{1,0:T(8,128)(2,1)} %concatenate.37.in_ref, ...), custom_call_target="tpu_custom_call" | custom-call | flops 4194304 | bytes 300000000 | tf_op jit(solution)/shard_map/pallas_call | solution.py:1255
  160.8 8.3 %shard_map.331.attn_ref = bf16[1024,256]{1,0:T(8,128)(2,1)} custom-call(s32[4]{0:T(128)} %fusion.47.order, f32[1024,1920]{1,0:T(8,128)} %get-tuple-element.72.q_ref.gate_ref.inner_ref.step_ref.before_ref, f32[1024,768]{1,0:T(8,128)} %get-tuple-element.73.kv_ref.bc_ref.bcbefore_ref, f32[1024,128]{1,0:T(8,128)} %get-tuple-element.183.cos_ref.all_cos, ...), custom_call_target="tpu_custom_call" | custom-call | flops 805306368 | bytes 3145728 | tf_op jit(solution)/shard_map/pallas_call | solution.py:416
  171.7 15.3 %shard_map.332 = (bf16[1024,1024]{1,0:T(8,128)(2,1)}, f32[1024,768]{1,0:T(8,128)}, bf16[8,256,768]{2,1,0:T(8,128)(2,1)}) custom-call(s32[4]{0:T(128)} %fusion.47.order, f32[1024,1920]{1,0:T(8,128)} %get-tuple-element.72.q_ref.gate_ref.inner_ref.step_ref.before_ref, f32[1024,1920]{1,0:T(8,128)} %get-tuple-element.72.q_ref.gate_ref.inner_ref.step_ref.before_ref, ...), custom_call_target="tpu_custom_call" | custom-call | flops 3221225472 | bytes 15728640 | tf_op jit(solution)/shard_map/pallas_call | solution.py:480
  187.0 12.7 %collective-permute-done = bf16[256,2048]{1,0:T(8,128)(2,1)S(1)} collective-permute-done((bf16[256,2048]{1,0:T(8,128)(2,1)S(1)}, bf16[256,2048]{1,0:T(8,128)(2,1)S(1)}, u32[]{:S(2)}, u32[]{:S(2)}) %collective-permute-start) | collective-permute-done | bytes 1048608 | tf_op jit(solution)/shard_map/ppermute | solution.py:643
  203.5 177.2 %shard_map.333 = (bf16[2048,3072]{1,0:T(8,128)(2,1)}, bf16[1024,2048]{1,0:T(8,128)(2,1)}, bf16[1024,1024]{1,0:T(8,128)(2,1)}, bf16[1024,1024]{1,0:T(8,128)(2,1)}...) custom-call(bf16[512,2048]{1,0:T(8,128)(2,1)} %pad_maximum_fusion.3., ...), custom_call_target="tpu_custom_call" | custom-call | flops 17179869184 | bytes 400000000 | tf_op jit(solution)/shard_map/pallas_call | solution.py:1736
  380.7 9.4 %convolution_convert_fusion.2 = bf16[2048,1024]{1,0:T(8,128)(2,1)} fusion(bf16[1024,2048]{1,0:T(8,128)(2,1)} %get-tuple-element.84, bf16[1024,1024]{1,0:T(8,128)(2,1)} %get-tuple-element.83), kind=kOutput, calls=%fused_computation.33 | convolution fusion | flops 4297064448 | bytes 10485760 | tf_op jit(solution)/shard_map/dot_general | solution.py:2712
  390.1 7.9 %fusion.16 = f32[1024,1024]{1,0:T(8,128)S(1)} fusion(bf16[1024,2048]{1,0:T(8,128)(2,1)} %get-tuple-element.84, bf16[2048,3072]{1,0:T(8,128)(2,1)} %get-tuple-element.85), kind=kOutput, calls=%fused_computation.30 | convolution fusion | flops 4294967296 | bytes 12582912 | tf_op jit(solution)/shard_map/dot_general | solution.py:2718
  400.2 7.2 fusion.21
  407.6 3.4 fusion.18
  411.5 3.4 add_convert_fusion
  414.9 11.9 %convolution_convert_fusion = bf16[2048,2048]{1,0:T(8,128)(2,1)} fusion(bf16[1024,2048]{1,0:T(8,128)(2,1)S(1)} %copy-done.30, bf16[1024,1024]{1,0:T(8,128)(2,1)S(1)} %get-tuple-element.167, bf16[1024,1024]{1,0:T(8,128)(2,1)S(1)} %get-tuple-element.168), kind=kOutput, calls=%fused_computation | convolution fusion | flops 8602517504 | bytes 16777216 | tf_op jit(solution)/shard_map/dot_general | solution.py:2712
  426.9 5.9 fusion.6
  432.8 7.2 collective-permute-done.4
  440.0 3.1 convert_add_fusion
  444.9 2.2 multiply_reduce_fusion
  450.1 22.9 %collective-permute-done.6 = bf16[256,2048]{1,0:T(8,128)(2,1)S(1)} collective-permute-done((bf16[256,2048]{1,0:T(8,128)(2,1)S(1)}, bf16[256,2048]{1,0:T(8,128)(2,1)S(1)}, u32[]{:S(2)}, u32[]{:S(2)}) %collective-permute-start.6) | collective-permute-done | bytes 1048608 | tf_op jit(solution)/shard_map/ppermute | solution.py:643
  478.4 8.8 %fusion.37.grad_ref = f32[1024,1024]{1,0:T(8,128)} fusion(bf16[2048,1024]{1,0:T(8,128)(2,1)S(1)} %copy-done.25, bf16[256,2048]{1,0:T(8,128)(2,1)S(1)} %collective-permute-done.7, bf16[256,2048]{1,0:T(8,128)(2,1)S(1)} %collective-permute-done.6, bf16[256,2048]{1,0:T(8,128)(2,1)S(1)} %collective-permute-done.5, bf16[256,2048]{1,0:T(8,128)(2,1)S(1)} %get-tuple-element.165), kind=kOutput, calls=%fused_computation.55 | convolution fusion | flops 4311744512 | bytes 12582912 | tf_op jit(solution)/shard_map/dot_general | solution.py:2733
  488.7 4.3 collective-permute-start.9
  493.1 9.1 %convolution_convert_fusion.1 = bf16[2048,1024]{1,0:T(8,128)(2,1)} fusion(bf16[1024,1024]{1,0:T(8,128)(2,1)} %get-tuple-element.75.heads_ref, bf16[256,2048]{1,0:T(8,128)(2,1)} %copy-done.28, bf16[256,2048]{1,0:T(8,128)(2,1)} %copy-done.26, bf16[256,2048]{1,0:T(8,128)(2,1)} %copy-done.27, bf16[256,2048]{1,0:T(8,128)(2,1)S(1)} %get-tuple-element.165), kind=kOutput, calls=%fused_computation.32 | convolution fusion | flops 4313841664 | bytes 10485760 | tf_op jit(solution)/shard_map/dot_general | solution.py:2712
  502.2 12.2 %shard_map.334 = (bf16[1024,256]{1,0:T(8,128)(2,1)}, bf16[1024,256]{1,0:T(8,128)(2,1)}) custom-call(s32[4]{0:T(128)} %fusion.47.order, f32[1024,1920]{1,0:T(8,128)} %get-tuple-element.72.q_ref.gate_ref.inner_ref.step_ref.before_ref, f32[1024,768]{1,0:T(8,128)} %get-tuple-element.73.kv_ref.bc_ref.bcbefore_ref, ...), custom_call_target="tpu_custom_call" | custom-call | flops 2147483648 | bytes 5242880 | tf_op jit(solution)/shard_map/pallas_call | solution.py:442
  515.6 33.1 %shard_map.335 = (bf16[1024,1920]{1,0:T(8,128)(2,1)}, bf16[1024,768]{1,0:T(8,128)(2,1)}, f32[8,768]{1,0:T(8,128)}, f32[8,512]{1,0:T(8,128)}, f32[8,128]{1,0:T(8,128)}) custom-call(s32[4]{0:T(128)} %fusion.47.order, f32[1024,1920]{1,0:T(8,128)} %get-tuple-element.72.q_ref.gate_ref.inner_ref.step_ref.before_ref, ...), custom_call_target="tpu_custom_call" | custom-call | flops 8053063680 | bytes 31457280 | tf_op jit(solution)/shard_map/pallas_call | solution.py:549
  555.4 64.5 %shard_map.336 = (bf16[2048,1920]{1,0:T(8,128)(2,1)}, bf16[2048,512]{1,0:T(8,128)(2,1)}, bf16[2048,256]{1,0:T(8,128)(2,1)}, f32[256,2048]{1,0:T(8,128)}, f32[256,2,1024]{2,1,0:T(2,128)}) custom-call(bf16[1024,1920]{1,0:T(8,128)(2,1)} %get-tuple-element.99.low_ref, bf16[1024,768]{1,0:T(8,128)(2,1)} %get-tuple-element.100.lowsh_ref, ...), custom_call_target="tpu_custom_call" | custom-call | flops 20132659200 | bytes 60000000 | tf_op jit(solution)/shard_map/pallas_call | solution.py:1970
  619.9 125.6 %shard_map.337 = (f32[256,2,768]{2,1,0:T(2,128)}, f32[256,256]{1,0:T(8,128)}, f32[256,128]{1,0:T(8,128)}, f32[64,1024]{1,0:T(8,128)}, f32[256,2048]{1,0:T(8,128)...) custom-call(bf16[2048,1920]{1,0:T(8,128)(2,1)} %get-tuple-element.105.part_ref, ...), custom_call_target="tpu_custom_call" | custom-call | flops 256 | bytes 256 | tf_op jit(solution)/shard_map/pallas_call | solution.py:2424
  755.6 3.3 copy.62
  (170 shorter events, 57.7 us)
Async XLA Ops:
  7.2 196.3 %all-gather.2.cloned.1.call-start = ((), (), s32[]{:S(2)}) async-start(), calls=%async_computation.3 | async-start | bytes 5242880 | tf_op jit(solution)/shard_map/all_gather | solution.py:2515
  8.6 144.2 %copy-start.16 = (bf16[256,2,1024]{2,1,0:T(2,128)(2,1)S(1)}, bf16[256,2,1024]{2,1,0:T(2,128)(2,1)}, u32[]{:S(2)}) copy-start(bf16[256,2,1024]{2,1,0:T(2,128)(2,1)} %param.36) | copy-start | bytes 3145732
  12.1 144.2 %copy-start.29 = (s32[8]{0:T(128)S(1)}, s32[8]{0:T(128)}, u32[]{:S(2)}) copy-start(s32[8]{0:T(128)} %param.21) | copy-start | bytes 100
  152.7 334.6 %reduce-scatter.4.cloned.1.call-start = ((), (), s32[]{:S(2)}) async-start(), calls=%async_computation.4 | async-start | bytes 5242880 | tf_op jit(solution)/shard_map/reduce_scatter | solution.py:2519
  153.0 46.6 %collective-permute-start = (bf16[256,2048]{1,0:T(8,128)(2,1)S(1)}, bf16[256,2048]{1,0:T(8,128)(2,1)S(1)}, u32[]{:S(2)}, u32[]{:S(2)}) collective-permute-start(bf16[256,2048]{1,0:T(8,128)(2,1)S(1)} %bitcast.45), channel_id=1, source_target_pairs={{0,2},{1,3},{2,6},{3,7},{4,0},{5,1},{6,4},{7,5},{8,10},{9,11},{10,... | collective-permute-start | bytes 3145736 | tf_op jit(solution)/shard_map/ppermute | solution.py:643
  154.1 45.6 %collective-permute-start.1 = (bf16[256,2048]{1,0:T(8,128)(2,1)S(1)}, bf16[256,2048]{1,0:T(8,128)(2,1)S(1)}, u32[]{:S(2)}, u32[]{:S(2)}) collective-permute-start(bf16[256,2048]{1,0:T(8,128)(2,1)S(1)} %bitcast.46), channel_id=1, source_target_pairs={{2,4},{3,5},{4,2},{5,3},{10,12},{11,13},{12,10},{13,11},{18,20},{1... | collective-permute-start | bytes 3145736 | tf_op jit(solution)/shard_map/ppermute | solution.py:643
  390.1 158.7 %reduce-scatter.6.cloned.1.call-start = ((), (), s32[]{:S(2)}) async-start(), calls=%async_computation.5 | async-start | bytes 10485760 | tf_op jit(solution)/shard_map/reduce_scatter | solution.py:2519
  390.1 7.9 %copy-start.13 = (bf16[1024,1024]{1,0:T(8,128)(2,1)S(1)}, bf16[1024,1024]{1,0:T(8,128)(2,1)}, u32[]{:S(2)}) copy-start(bf16[1024,1024]{1,0:T(8,128)(2,1)} %get-tuple-element.87) | copy-start | bytes 6291460
  390.1 7.9 %copy-start.14 = (bf16[1024,1024]{1,0:T(8,128)(2,1)S(1)}, bf16[1024,1024]{1,0:T(8,128)(2,1)}, u32[]{:S(2)}) copy-start(bf16[1024,1024]{1,0:T(8,128)(2,1)} %get-tuple-element.86) | copy-start | bytes 6291460
  398.1 9.5 %slice-start = ((s8[12582912]{0:T(1024)(128)(4,1)}), s8[4194304]{0:T(1024)(128)(4,1)S(1)}, s32[]{:S(2)}) async-start(s8[12582912]{0:T(1024)(128)(4,1)} %bitcast.57), calls=%async_computation.7 | async-start | bytes 8388608
  398.1 9.5 %slice-start.1 = ((s8[12582912]{0:T(1024)(128)(4,1)}), s8[4194304]{0:T(1024)(128)(4,1)S(1)}, s32[]{:S(2)}) async-start(s8[12582912]{0:T(1024)(128)(4,1)} %bitcast.57), calls=%async_computation.8 | async-start | bytes 8388608
  400.2 14.7 %copy-start.12 = (bf16[1024,1024]{1,0:T(8,128)(2,1)}, bf16[1024,1024]{1,0:T(8,128)(2,1)S(1)}, u32[]{:S(2)}) copy-start(bf16[1024,1024]{1,0:T(8,128)(2,1)S(1)} %get-tuple-element.168) | copy-start | bytes 6291460
  407.5 4.0 collective-permute-start.3
  411.0 21.8 %collective-permute-start.2 = (bf16[256,2048]{1,0:T(8,128)(2,1)}, bf16[256,2048]{1,0:T(8,128)(2,1)S(1)}, u32[]{:S(2)}, u32[]{:S(2)}) collective-permute-start(bf16[256,2048]{1,0:T(8,128)(2,1)} %fusion.18), channel_id=1, source_target_pairs={{0,4},{1,5},{2,6},{3,7},{4,0},{5,1},{6,2},{7,3},{8,12},{9,13},{10,... | collective-permute-start | bytes 3145736 | tf_op jit(solution)/shard_map/ppermute | solution.py:643
  414.9 25.1 %collective-permute-start.4 = (bf16[256,2048]{1,0:T(8,128)(2,1)}, bf16[256,2048]{1,0:T(8,128)(2,1)}, u32[]{:S(2)}, u32[]{:S(2)}) collective-permute-start(bf16[256,2048]{1,0:T(8,128)(2,1)} %add_convert_fusion), channel_id=1, source_target_pairs={{0,1},{1,0},{2,3},{3,2},{4,5},{5,4},{6,7},{7,6},{8,9},{9,8},{10,11... | collective-permute-start | bytes 3145736 | tf_op jit(solution)/shard_map/ppermute | solution.py:643
  443.1 176.9 %reduce-scatter.8.cloned.1.call-start = ((), (), s32[]{:S(2)}) async-start(), calls=%async_computation.6 | async-start | bytes 5242880 | tf_op jit(solution)/shard_map/reduce_scatter | solution.py:2519
  447.1 31.3 %copy-start.25 = (bf16[2048,1024]{1,0:T(8,128)(2,1)S(1)}, bf16[2048,1024]{1,0:T(8,128)(2,1)}, u32[]{:S(2)}) copy-start(bf16[2048,1024]{1,0:T(8,128)(2,1)} %all-gather.2.cloned.1.call-done.out_ref) | copy-start | bytes 12582916
  449.1 24.0 %collective-permute-start.6 = (bf16[256,2048]{1,0:T(8,128)(2,1)S(1)}, bf16[256,2048]{1,0:T(8,128)(2,1)S(1)}, u32[]{:S(2)}, u32[]{:S(2)}) collective-permute-start(bf16[256,2048]{1,0:T(8,128)(2,1)S(1)} %get-tuple-element.165), channel_id=1, source_target_pairs={{0,1},{1,0},{2,3},{3,2},{4,5},{5,4},{6,7},{7,6},{8,9},{9,8},{10,11... | collective-permute-start | bytes 3145736 | tf_op jit(solution)/shard_map/ppermute | solution.py:643
  449.2 27.2 %collective-permute-start.5 = (bf16[256,2048]{1,0:T(8,128)(2,1)S(1)}, bf16[256,2048]{1,0:T(8,128)(2,1)S(1)}, u32[]{:S(2)}, u32[]{:S(2)}) collective-permute-start(bf16[256,2048]{1,0:T(8,128)(2,1)S(1)} %get-tuple-element.165), channel_id=1, source_target_pairs={{0,4},{1,5},{2,6},{3,7},{4,0},{5,1},{6,2},{7,3},{8,12},{9,13},{10,... | collective-permute-start | bytes 3145736 | tf_op jit(solution)/shard_map/ppermute | solution.py:643
  473.0 3.9 collective-permute-start.7
  488.7 25.6 %collective-permute-start.8 = (bf16[256,1024]{1,0:T(8,128)(2,1)S(1)}, bf16[256,1024]{1,0:T(8,128)(2,1)S(1)}, u32[]{:S(2)}, u32[]{:S(2)}) collective-permute-start(bf16[256,1024]{1,0:T(8,128)(2,1)S(1)} %get-tuple-element.163), channel_id=1, source_target_pairs={{0,4},{1,5},{2,0},{3,1},{4,6},{5,7},{6,2},{7,3},{8,12},{9,13},{10,... | collective-permute-start | bytes 1572872 | tf_op jit(solution)/shard_map/ppermute | solution.py:643
  488.7 26.1 %collective-permute-start.9 = (bf16[256,1024]{1,0:T(8,128)(2,1)S(1)}, bf16[256,1024]{1,0:T(8,128)(2,1)S(1)}, u32[]{:S(2)}, u32[]{:S(2)}) collective-permute-start(bf16[256,1024]{1,0:T(8,128)(2,1)S(1)} %get-tuple-element.164), channel_id=1, source_target_pairs={{2,4},{3,5},{4,2},{5,3},{10,12},{11,13},{12,10},{13,11},{18,20},{1... | collective-permute-start | bytes 1572872 | tf_op jit(solution)/shard_map/ppermute | solution.py:643
  619.9 134.7 %copy-start.17 = (bf16[256,2048]{1,0:T(8,128)(2,1)S(1)}, bf16[256,2048]{1,0:T(8,128)(2,1)}, u32[]{:S(2)}) copy-start(bf16[256,2048]{1,0:T(8,128)(2,1)} %get-tuple-element.206) | copy-start | bytes 3145732
  745.5 13.4 %copy-start.15 = (f32[256,2,768]{2,1,0:T(2,128)S(1)}, f32[256,2,768]{2,1,0:T(2,128)}, u32[]{:S(2)}) copy-start(f32[256,2,768]{2,1,0:T(2,128)} %get-tuple-element.210) | copy-start | bytes 4718596
  (24 other events, 102.7 us)
Sparse Core Ops, SparseCore 0:
  152.8 50.6 all-gather.1
  390.2 50.3 reduce-scatter.3
  444.0 86.3 reduce-scatter.5
  548.9 50.1 reduce-scatter.7
